TPU v7x, 32 devices: a whole 2x2x4 slice. The times are simulated.
32 devices in a mesh: seq: 8 (over z, y), exp: 4 (over x, core).
Axes of the slice: x: 2, y: 2, z: 4, core: 2. Of those that a mesh axis runs over, the one named last changes fastest.
Arguments:
- projected: bfloat16 [4096, 3, 8192], P('seq', None, 'exp'), may hold values from -6 to 6
- log_decay: float32 [4096, 64], P('seq', 'exp'), may hold values from -2.5 to 0, as said below
- norm_gain: float32 [8192], P('exp'), may hold values from 0.1 to 1.9
- moe_tokens: bfloat16 [256, 6144], P(('seq', 'exp')), may hold values from -6 to 6
- expert_ids: int32 [256, 2], P(('seq', 'exp')), may hold values from 0 to 3, all different within a row; in each aligned block of 8 rows (0 to 7, 8 to 15, ...) at most 4 rows name the same one
- route_probs: float32 [256, 2], P(('seq', 'exp')), may hold values from 0.1 to 1
- w_in: bfloat16 [4, 6144, 2, 4608], P('exp', None, None, 'seq'), may hold values from -0.078125 to 0.078125
- w_out: bfloat16 [4, 4608, 6144], P('exp', 'seq'), may hold values from -0.09375 to 0.09375
Outputs:
- attn_out: bfloat16 [4096, 8192], P('seq', 'exp')
- moe_out: bfloat16 [256, 6144], P(('seq', 'exp'))
Inputs may be any that keep to these rules, and one draw needn't show every extreme that they name: `log_decay`: negative in every entry. `expert_ids`: A token names 2 different experts. In the rows of one device (aligned blocks of 8 tokens) no expert is named more than 4 times, a bound that some block reaches.
All inputs are finite; a program needn't handle non-finite values.
Results may differ from a plain program's by a relative error of at most 0.025.
Values may be sent and summed in bfloat16 or wider, within the bound.
No kernel may reach another device: no remote copies, remote signals or barrier semaphores. Data moves between devices by JAX's collectives and lax.ppermute only.
A program may use at most 128 MiB of HBM per device.

v0:
```python
import jax
import jax.numpy as jnp
from jax import lax
from jax.sharding import PartitionSpec as P

CAP = 4


EPS = 1e-06
HIGH = lax.Precision.HIGHEST


def prefix(shard, axis, join, neutral):
    place = lax.axis_index(axis)
    gathered = jax.tree.map(
        lambda a, kind: lax.all_gather(a.astype(kind), axis), shard, (jnp.bfloat16, jnp.bfloat16)
    )
    state = jax.tree.map(lambda a, e: jnp.zeros_like(a) + jnp.asarray(e, a.dtype), shard, neutral)

    def one(turn, state):
        return join(
            state,
            jax.tree.map(
                lambda a, own: lax.dynamic_index_in_dim(a, turn, 0, False).astype(own.dtype),
                gathered,
                shard,
            ),
        )

    return lax.fori_loop(0, place, one, state)


def combine_states(earlier, later):
    return (earlier[0] * later[0], later[0][:, None, None] * earlier[1] + later[1])


def on_device(projected, log_decay, norm_gain, moe_tokens, expert_ids, route_probs, w_in, w_out):
    rows = projected.shape[0]
    heads = log_decay.shape[1]
    width = projected.shape[2] // heads
    queries = projected[:, 0].reshape(rows, heads, width)
    key_rows = projected[:, 1].reshape(rows, heads, width)
    values = projected[:, 2].reshape(rows, heads, width)
    running = jnp.cumsum(log_decay, axis=0)
    last = running[-1]
    weighted = key_rows.astype(jnp.float32) * jnp.exp(last[None] - running)[:, :, None]
    block_state = jnp.einsum("thi,thj->hij", weighted, values.astype(jnp.float32), precision=HIGH)
    identity = (jnp.ones_like(last), jnp.zeros_like(block_state))
    _, carried = prefix((jnp.exp(last), block_state), "seq", combine_states, identity)
    scores = jnp.einsum("thd,uhd->htu", queries, key_rows, preferred_element_type=jnp.float32)
    turned = running.T
    gap = turned[:, :, None] - turned[:, None, :]
    causal = (jnp.arange(rows)[:, None] >= jnp.arange(rows)[None, :])[None]
    decay = jnp.exp(jnp.where(causal, gap, -jnp.inf))
    weights = (scores * decay).astype(jnp.bfloat16)
    local_part = jnp.einsum("htu,uhd->thd", weights, values, preferred_element_type=jnp.float32)
    carried_part = jnp.einsum(
        "thd,hde->the",
        queries.astype(jnp.float32) * jnp.exp(running)[:, :, None],
        carried,
        precision=HIGH,
    )
    mixed = local_part + carried_part
    scaled = mixed * lax.rsqrt(jnp.mean(mixed * mixed, axis=-1, keepdims=True) + EPS)
    attn_out = (scaled.reshape(rows, heads * width) * norm_gain).astype(jnp.bfloat16)
    count_tok = moe_tokens.shape[0]
    model_width = moe_tokens.shape[1]
    topk = expert_ids.shape[1]
    experts = w_in.shape[0] * lax.axis_size("exp")
    assigned = expert_ids.reshape(-1)
    onehot = (assigned[:, None] == jnp.arange(experts, dtype=jnp.int32)[None]).astype(jnp.int32)
    slot = jnp.sum((jnp.cumsum(onehot, axis=0) - onehot) * onehot, axis=1)
    target = assigned * CAP + slot
    pick = (target[None, :] == jnp.arange(experts * CAP, dtype=jnp.int32)[:, None]).astype(
        jnp.bfloat16
    )
    local_units = w_in.shape[3]
    joined_in = w_in.reshape(model_width, 2 * local_units)
    down = w_out[0]
    spread_rows = jnp.repeat(moe_tokens, topk, axis=0)
    outgoing = (
        jnp.dot(pick, spread_rows, preferred_element_type=jnp.float32)
        .astype(jnp.bfloat16)
        .reshape(experts, CAP, model_width)
    )
    arrived = lax.all_to_all(outgoing, "exp", split_axis=0, concat_axis=0, tiled=True)
    both = jnp.dot(
        lax.all_gather(arrived.reshape(experts * CAP, model_width), "seq", axis=0, tiled=True),
        joined_in,
        preferred_element_type=jnp.float32,
    )
    hidden = (jax.nn.silu(both[:, :local_units]) * both[:, local_units:]).astype(jnp.bfloat16)
    summed = lax.psum_scatter(
        jnp.dot(hidden, down, preferred_element_type=jnp.float32).astype(jnp.bfloat16),
        "seq",
        scatter_dimension=0,
        tiled=True,
    )
    results = summed.reshape(experts, CAP, model_width)
    returned = lax.all_to_all(results, "exp", split_axis=0, concat_axis=0, tiled=True)
    picked = jnp.dot(
        pick.T, returned.reshape(experts * CAP, model_width), preferred_element_type=jnp.float32
    )
    scaled_rows = picked * route_probs.reshape(-1)[:, None]
    moe_out = jnp.sum(scaled_rows.reshape(count_tok, topk, model_width), axis=1).astype(
        jnp.bfloat16
    )
    return (attn_out, moe_out)


def solution(mesh):
    in_specs = (
        P("seq", None, "exp"),
        P("seq", "exp"),
        P("exp"),
        P(("seq", "exp"), None),
        P(("seq", "exp"), None),
        P(("seq", "exp"), None),
        P("exp", None, None, "seq"),
        P("exp", "seq", None),
    )
    out_specs = (P("seq", "exp"), P(("seq", "exp"), None))
    return jax.shard_map(
        on_device, mesh=mesh, in_specs=in_specs, out_specs=out_specs, check_vma=False
    )
```

profile of v0, /device:TPU:31, one launch (start us, length us, event | category | flops | bytes accessed | tf_op | source)
XLA Modules:
  0.0 248.3 jit_solution(5509535321156864374)
XLA Ops:
  7.2 0.8 copy.66
  8.4 1.0 broadcast_in_dim.21
  9.7 6.6 %all_to_all.10 = bf16[4,4,6144]{2,1,0:T(4,128)(2,1)S(1)} all-to-all(bf16[4,4,6144]{2,1,0:T(4,128)(2,1)S(1)} %reshape.109), channel_id=1, replica_groups=mesh['seq'=8,'exp'=4] {'exp'}, dimensions={0} | all-to-all | bytes 393216 | tf_op jit(solution)/shard_map/all_to_all | solution.py:86
  16.3 0.7 reshape.110
  17.1 43.5 %all-gather.5.cloned.1.call-done = bf16[128,6144]{1,0:T(8,128)(2,1)} async-done(((bf16[16,6144]{1,0:T(8,128)(2,1)}), bf16[128,6144]{1,0:T(8,128)(2,1)}) %all-gather.5.cloned.1.call-update) | async-done | bytes 1572880 | tf_op jit(solution)/shard_map/all_gather | solution.py:88
  60.6 10.1 %fusion.26 = f32[128,1152]{1,0:T(8,128)S(1)} fusion(bf16[128,6144]{1,0:T(8,128)(2,1)} %all-gather.5.cloned.1.call-done, bf16[6144,1152]{0,1:T(8,128)(2,1)} %bitcast.59), kind=kOutput, calls=%fused_computation.47 | convolution fusion | flops 1811939328 | bytes 16318464 | tf_op jit(solution)/shard_map/dot_general | solution.py:87
  70.8 5.6 %convolution_convert_fusion = bf16[128,6144]{1,0:T(8,128)(2,1)} fusion(bf16[1,576,6144]{2,1,0:T(8,128)(2,1)} %param.17, f32[128,1152]{1,0:T(8,128)S(1)} %fusion.26), kind=kOutput, calls=%fused_computation.3 | convolution fusion | flops 907198464 | bytes 9306112 | tf_op jit(solution)/shard_map/dot_general | solution.py:94
  76.5 1.2 reduce-window.6
  77.8 5.8 %fusion.25 = (bf16[512,1,2048]{2,0,1:T(8,128)(2,1)}, bf16[512,1,2048]{2,0,1:T(8,128)(2,1)}, bf16[512,1,2048]{2,0,1:T(8,128)(2,1)S(1)}) fusion(bf16[512,3,2048]{2,0,1:T(8,128)(2,1)} %param.10), kind=kLoop, calls=%fused_computation.46 | loop fusion | bytes 12582912 | tf_op jit(solution)/shard_map/slice | solution.py:42
  83.7 3.9 %copy.75 = bf16[512,1,2048]{0,2,1:T(8,128)(2,1)} copy(bf16[512,1,2048]{2,0,1:T(8,128)(2,1)} %get-tuple-element.57) | data formatting | bytes 4194304
  87.6 2.5 %copy.61 = bf16[512,1,2048]{0,2,1:T(8,128)(2,1)} copy(bf16[512,1,2048]{2,0,1:T(8,128)(2,1)S(1)} %get-tuple-element.59) | data formatting | bytes 4194304 | tf_op jit(solution)/shard_map/slice | solution.py:43
  90.5 5.3 %fusion.12 = bf16[16,128,128]{2,1,0:T(8,128)(2,1)} fusion(bf16[512,16,128]{0,2,1:T(8,128)(2,1)} %bitcast.64, bf16[512,16,128]{0,2,1:T(8,128)(2,1)} %bitcast.62, f32[512,16]{0,1:T(8,128)S(1)} %get-tuple-element.61), kind=kOutput, calls=%fused_computation.20 | convolution fusion | flops 1612972032 | bytes 4751360 | tf_op jit(solution)/shard_map/thi,thj->hij/dot_general | solution.py:47
  95.8 2.9 %copy.74 = bf16[512,1,2048]{0,2,1:T(8,128)(2,1)S(1)} copy(bf16[512,1,2048]{2,0,1:T(8,128)(2,1)} %get-tuple-element.58) | data formatting | bytes 4194304
  98.7 40.0 %reduce-scatter.2.cloned.1.call-done = bf16[16,6144]{1,0:T(8,128)(2,1)} async-done(((bf16[128,6144]{1,0:T(8,128)(2,1)}), bf16[16,6144]{1,0:T(8,128)(2,1)}) %reduce-scatter.2.cloned.1.call-update) | async-done | bytes 196624 | tf_op jit(solution)/shard_map/reduce_scatter | solution.py:93
  138.7 1.7 reshape.112
  140.4 5.7 %all-to-all-start.1 = ((bf16[4,4,6144]{2,1,0:T(4,128)(2,1)}), bf16[4,4,6144]{2,1,0:T(4,128)(2,1)S(1)}, u32[]{:S(2)}, u32[]{:S(2)}) async-start(bf16[4,4,6144]{2,1,0:T(4,128)(2,1)} %reshape.112), calls=%async_computation.2 | async-start | bytes 393216 | tf_op jit(solution)/shard_map/all_to_all | solution.py:100
  146.2 10.7 %fusion.11 = f32[16,512,128]{1,2,0:T(8,128)} fusion(bf16[512,16,128]{0,2,1:T(8,128)(2,1)} %bitcast.65, bf16[512,16,128]{0,2,1:T(8,128)(2,1)S(1)} %bitcast.60, bf16[512,16,128]{0,2,1:T(8,128)(2,1)} %bitcast.63, f32[16,512]{1,0:T(8,128)S(1)} %get-tuple-element.63, pred[512,512]{1,0:T(8,128)(4,1)S(1)} %iota_compare_fusion), kind=kOutput, calls=%fused_computation.19 | convolution fusion | flops 2164260864 | bytes 10780672 | tf_op jit(solution)/shard_map/htu,uhd->thd/dot_general | solution.py:56
  157.0 13.0 %all-gather.1 = bf16[8,1,16]{2,1,0:T(2,128)(2,1)S(1)} all-gather(bf16[1,1,16]{2,1,0:T(2,128)(2,1)S(1)} %bitcast.68), channel_id=1, replica_groups=mesh['seq'=8,'exp'=4] {'seq'}, dimensions={0}, use_global_device_ids=true | all-gather | bytes 288 | tf_op jit(solution)/shard_map/all_gather | solution.py:16
  170.8 1.1 reduce_sum.29
  171.9 42.6 %all-gather.7.cloned.1.call-done = bf16[128,128,128]{2,1,0:T(8,128)(2,1)} async-done(((bf16[16,128,128]{2,1,0:T(8,128)(2,1)}), bf16[128,128,128]{2,1,0:T(8,128)(2,1)}) %all-gather.7.cloned.1.call-update) | async-done | bytes 4194320 | tf_op jit(solution)/shard_map/all_gather | solution.py:16
  214.6 9.4 %while.12 = (s32[]{:T(128)}, f32[16,128,128]{2,1,0:T(8,128)S(1)}, s32[]{:T(128)}, bf16[8,16]{1,0:T(8,128)(2,1)S(1)}, bf16[8,16,128,128]{3,2,1,0:T(8,128)(2,1)}, /*index=5*/s32[]{:T(128)}, s32[]{:T(128)}, s32[]{:T(128)}) while((s32[]{:T(128)}, f32[16,128,128]{2,1,0:T(8,128)S(1)}, s32[]{:T(128)}, bf16[8,16]{1,0:T(8,128)(2,1)S(1)}, ...), condition=%wide.region_3.4_spmd, body=%wide.region_2.3_spmd.sunk | while | flops 786453 | bytes 2621727 | solution.py:30
  214.6 1.3 convert_add_fusion.2
  216.0 1.3 convert_add_fusion.2
  217.3 1.3 convert_add_fusion.2
  218.7 1.3 convert_add_fusion.2
  220.0 1.3 convert_add_fusion.2
  221.4 1.3 convert_add_fusion.2
  222.7 1.3 convert_add_fusion.2
  224.0 5.8 %multiply_reduce_fusion = (f32[512,16]{0,1:T(8,128)S(1)}, f32[512,16,128]{0,2,1:T(8,128)S(1)}) fusion(f32[16,128,128]{2,1,0:T(8,128)S(1)} %get-tuple-element.46, bf16[512,16,128]{0,2,1:T(8,128)(2,1)S(1)} %bitcast.61, f32[512,16]{0,1:T(8,128)S(1)} %get-tuple-element.60, f32[16,512,128]{1,2,0:T(8,128)} %fusion.11), kind=kOutput, calls=%fused_computation.9 | convolution fusion | flops 1615847424 | bytes 11599872 | tf_op jit(solution)/shard_map/thd,hde->the/dot_general | solution.py:57
  229.8 2.5 %broadcast_multiply_fusion = f32[512,16,128]{0,2,1:T(8,128)} fusion(f32[512,16,128]{0,2,1:T(8,128)S(1)} %get-tuple-element.65, f32[512,16]{0,1:T(8,128)S(1)} %add_rsqrt_fusion), kind=kLoop, calls=%fused_computation.16 | loop fusion | flops 1048576 | bytes 8421376 | tf_op jit(solution)/shard_map/mul | solution.py:64
  232.3 5.4 %copy.65 = f32[512,2048]{1,0:T(8,128)} copy(f32[512,2048]{0,1:T(8,128)} %bitcast.58) | data formatting | bytes 8388608 | tf_op jit(solution)/shard_map/reshape | solution.py:65
  237.8 4.0 %multiply_convert_fusion.1 = bf16[512,2048]{1,0:T(8,128)(2,1)} fusion(f32[512,2048]{1,0:T(8,128)} %copy.65, f32[2048]{0:T(1024)S(1)} %copy-done.2), kind=kLoop, calls=%fused_computation.8 | loop fusion | flops 2097152 | bytes 6299648 | tf_op jit(solution)/shard_map/convert_element_type | solution.py:65
  (47 shorter events, 2.6 us)
Async XLA Ops:
  7.2 69.3 %copy-start = (f32[512,16]{0,1:T(8,128)S(1)}, f32[512,16]{0,1:T(8,128)}, u32[]{:S(2)}) copy-start(f32[512,16]{0,1:T(8,128)} %param.11) | copy-start | bytes 98308
  7.2 53.4 %all-gather.5.cloned.1.call-start = ((), (), s32[]{:S(2)}) async-start(), calls=%async_computation.3 | async-start | bytes 1769472 | tf_op jit(solution)/shard_map/all_gather | solution.py:88
  17.1 121.7 %reduce-scatter.2.cloned.1.call-start = ((), (), s32[]{:S(2)}) async-start(), calls=%async_computation.4 | async-start | bytes 1769472 | tf_op jit(solution)/shard_map/reduce_scatter | solution.py:93
  76.4 138.1 %all-gather.7.cloned.1.call-start = ((), (), s32[]{:S(2)}) async-start(), calls=%async_computation.5 | async-start | bytes 4718592 | tf_op jit(solution)/shard_map/all_gather | solution.py:16
  140.4 29.8 %all-to-all-start.1 = ((bf16[4,4,6144]{2,1,0:T(4,128)(2,1)}), bf16[4,4,6144]{2,1,0:T(4,128)(2,1)S(1)}, u32[]{:S(2)}, u32[]{:S(2)}) async-start(bf16[4,4,6144]{2,1,0:T(4,128)(2,1)} %reshape.112), calls=%async_computation.2 | async-start | bytes 393216 | tf_op jit(solution)/shard_map/all_to_all | solution.py:100
  146.2 23.9 %copy-start.3 = (f32[8,2]{0,1:T(2,128)S(1)}, f32[8,2]{0,1:T(2,128)}, u32[]{:S(2)}) copy-start(f32[8,2]{0,1:T(2,128)} %param.15) | copy-start | bytes 196
  232.3 5.4 %copy-start.2 = (f32[2048]{0:T(1024)S(1)}, f32[2048]{0:T(1024)}, u32[]{:S(2)}) copy-start(f32[2048]{0:T(1024)} %param.12) | copy-start | bytes 24580
  232.3 9.4 %copy-start.1 = (f32[512,16]{0,1:T(8,128)S(1)}, f32[512,16]{0,1:T(8,128)}, u32[]{:S(2)}) copy-start(f32[512,16]{0,1:T(8,128)} %param.11) | copy-start | bytes 98308
Sparse Core Ops, SparseCore 0:
  17.2 43.3 all-gather.4
  76.5 62.1 reduce-scatter.1
  141.1 73.3 all-gather.6
where the time goes:
time: 249 us; the launch traced here: 248 us
  waiting for transfers between devices  126 us (51%)
  matrix products  37.9 us (15%)
  local copies, waits for them, and re-layouts  25.9 us (10%)
  blocking collectives  19.6 us (8%)
  other arithmetic  18.7 us (8%)
  between operations  13.9 us (6%)
  starting transfers between devices  5.84 us (2%)
    all_gather x1, waiting for transfers between devices, on_device(): lax.all_gather(arrived.reshape(experts * CAP, model_width), 'seq', axis=0...  43.5 us
    all_gather x1, waiting for transfers between devices, prefix(): lax.all_gather(a.astype(kind), axis)  42.6 us
    reduce_scatter x1, waiting for transfers between devices, on_device(): lax.psum_scatter(jnp.dot(hidden, down, preferred_element_type=jnp.float32...  40 us
    all_gather x1, blocking collectives, prefix(): lax.all_gather(a.astype(kind), axis)  13 us
    dot_general x1, matrix products, on_device(): jnp.einsum('htu,uhd->thd', weights, values, preferred_element_type=jnp.fl...  10.7 us
    dot_general x1, matrix products, on_device(): jnp.dot(lax.all_gather(arrived.reshape(experts * CAP, model_width), 'seq'...  10.1 us
    add x7, other arithmetic, combine_states(): later[0][:, None, None] * earlier[1] + later[1]  9.08 us
    unnamed x13, local copies, waits for them, and re-layouts  7.68 us
  transfers between devices with their start and end apart: 4, of which 3 were waited for; matrix products, arithmetic and copies ran while one was open for 15% of the time, Pallas kernels for 0%

commit v1 on v0

v1 whole, which is shorter than its diff:
```python
import functools
import jax
import jax.numpy as jnp
from jax import lax
from jax.experimental import pallas as pl
from jax.experimental.pallas import tpu as pltpu
from jax.sharding import PartitionSpec as P

EPS = 1e-06
CHUNK = 128
PIECES = 3
F32 = jnp.float32
BF16 = jnp.bfloat16
NT = (((1,), (1,)), ((), ()))
TN = (((0,), (0,)), ((), ()))
NN = (((1,), (0,)), ((), ()))


def factors(size):
    bits = size.bit_length() - 1
    inner = 2 ** (bits // 2)
    return size // inner, inner


class Axis:
    def __init__(self, name, n, inner, outer):
        self.name, self.n, self.inner, self.outer = name, n, inner, outer

    def index(self):
        return (lax.axis_index(self.name) // self.inner) % self.n

    def flat(self, o, i, j):
        return (o * self.n + i) * self.inner + j

    def turn(self, k):
        return [
            (self.flat(o, i, j), self.flat(o, (i + k) % self.n, j))
            for o in range(self.outer)
            for i in range(self.n)
            for j in range(self.inner)
        ]

    def hop(self, i):
        return [
            (self.flat(o, i, j), self.flat(o, i + 1, j))
            for o in range(self.outer)
            for j in range(self.inner)
        ]

    def send(self, a, k):
        return lax.ppermute(a, self.name, self.turn(k))


def gather(axis, a):
    return jnp.concatenate([a] + [axis.send(a, k) for k in range(1, axis.n)], 0)


def total(parts):
    s = parts[0].astype(F32)
    for p in parts[1:]:
        s = s + p.astype(F32)
    return s.astype(BF16)


def scatter(axis, parts):
    return total([parts[0]] + [axis.send(parts[k], axis.n - k) for k in range(1, axis.n)])


def rows_split(a, n):
    m = a.shape[0] // n
    return [a[i * m : (i + 1) * m] for i in range(n)]


def pieces_of(x):
    out = []
    for _ in range(PIECES):
        hi = lax.reduce_precision(x, 8, 7)
        out.append(hi)
        x = x - hi
    return out


def params(limit=56):
    return pltpu.CompilerParams(vmem_limit_bytes=limit * 2**20)


def prep_kernel(heads, rows, d_ref, run_ref, cols_ref):
    run = d_ref[...]
    lane = lax.broadcasted_iota(jnp.int32, (heads, rows), 1)
    step = 1
    while step < rows:
        run = run + jnp.where(lane >= step, pltpu.roll(run, step, 1), 0.0)
        step *= 2
    enter = jnp.zeros((heads, 1), F32)
    before, after = [], []
    for i in range(rows // CHUNK):
        leave = run[:, (i + 1) * CHUNK - 1 : (i + 1) * CHUNK]
        before.append(jnp.broadcast_to(enter, (heads, CHUNK)))
        after.append(jnp.broadcast_to(leave, (heads, CHUNK)))
        enter = leave
    eq = jnp.exp(run - jnp.concatenate(before, 1))
    ek = jnp.exp(jnp.concatenate(after, 1) - run)
    run_ref[...] = run
    tall = jnp.concatenate([run, eq, ek, jnp.exp(run)], 0)
    if 4 * heads < 128:
        tall = jnp.concatenate([tall, jnp.zeros((128 - 4 * heads, rows), F32)], 0)
    cols_ref[...] = tall.T


def prepare(log_decay):
    rows, heads = log_decay.shape
    return pl.pallas_call(
        functools.partial(prep_kernel, heads, rows),
        out_shape=(
            jax.ShapeDtypeStruct((heads, rows), F32),
            jax.ShapeDtypeStruct((rows, 128), F32),
        ),
        compiler_params=params(),
        name="prepare",
    )(log_decay.T)


def local_kernel(heads, group, base, q_ref, k_ref, v_ref, run_ref, cols_ref, mixed_ref, state_ref):
    rows, width = q_ref.shape[1], q_ref.shape[2] // group
    first = base + pl.program_id(0) * group
    cols = pltpu.roll(cols_ref[...], 128 - first, 1)
    ri = lax.broadcasted_iota(jnp.int32, (CHUNK, CHUNK), 0)
    ci = lax.broadcasted_iota(jnp.int32, (CHUNK, CHUNK), 1)
    causal = ri >= ci
    for g in range(group):
        lanes = slice(g * width, (g + 1) * width)
        run_row = run_ref[pl.ds(first + g, 1), :]
        state = None
        for i in range(rows // CHUNK):
            part = slice(i * CHUNK, (i + 1) * CHUNK)
            q, k, v = q_ref[0, part, lanes], k_ref[0, part, lanes], v_ref[0, part, lanes]
            run_col = cols[part, g : g + 1]
            eq = cols[part, heads + g : heads + g + 1]
            ek = cols[part, 2 * heads + g : 2 * heads + g + 1]
            scores = lax.dot_general(q, k, NT, preferred_element_type=F32)
            decay = jnp.exp(jnp.where(causal, run_col - run_row[:, part], -jnp.inf))
            weights = (scores * decay).astype(BF16)
            out = lax.dot_general(weights, v, NN, preferred_element_type=F32)
            faded = (k.astype(F32) * ek).astype(BF16)
            fresh = lax.dot_general(faded, v, TN, preferred_element_type=F32)
            if state is None:
                state = fresh
            else:
                out = out + eq * lax.dot_general(
                    q, state.astype(BF16), NN, preferred_element_type=F32
                )
                state = eq[CHUNK - 1 :, :] * state + fresh
            mixed_ref[part, lanes] = out.astype(mixed_ref.dtype)
        state_ref[g] = state.astype(BF16)


def local_pass(qkv, run, cols, heads, base, count, group=2):
    rows, width = qkv.shape[1], qkv.shape[2] // heads
    start = base // group

    def take(which):
        return pl.BlockSpec((1, rows, group * width), lambda h: (which, 0, start + h))

    return pl.pallas_call(
        functools.partial(local_kernel, heads, group, base),
        grid=(count // group,),
        in_specs=[
            take(0),
            take(1),
            take(2),
            pl.BlockSpec(run.shape, lambda h: (0, 0)),
            pl.BlockSpec(cols.shape, lambda h: (0, 0)),
        ],
        out_specs=(
            pl.BlockSpec((rows, group * width), lambda h: (0, h)),
            pl.BlockSpec((group, width, width), lambda h: (h, 0, 0)),
        ),
        out_shape=(
            jax.ShapeDtypeStruct((rows, count * width), F32),
            jax.ShapeDtypeStruct((count, width, width), BF16),
        ),
        compiler_params=params(),
        cost_estimate=pl.CostEstimate(
            flops=8 * count * rows * width * CHUNK,
            bytes_accessed=count * rows * width * 10,
            transcendentals=count * rows * CHUNK,
        ),
        name="local_pass",
    )(qkv, qkv, qkv, run, cols)


def final_kernel(heads, group, base, q_ref, mixed_ref, cols_ref, carried_ref, gain_ref, out_ref):
    width = q_ref.shape[2] // group
    first = base + pl.program_id(0) * group
    cols = pltpu.roll(cols_ref[...], 128 - first, 1)
    for g in range(group):
        lanes = slice(g * width, (g + 1) * width)
        er = cols[:, 3 * heads + g : 3 * heads + g + 1]
        far = lax.dot_general(q_ref[0, :, lanes], carried_ref[g], NN, preferred_element_type=F32)
        mixed = mixed_ref[:, lanes] + er * far
        mean = jnp.mean(mixed * mixed, axis=-1, keepdims=True)
        out_ref[:, lanes] = (mixed * lax.rsqrt(mean + EPS) * gain_ref[:, lanes]).astype(BF16)


def final_pass(qkv, mixed, cols, carried, gain, heads, group=2):
    rows, width = qkv.shape[1], qkv.shape[2] // heads
    return pl.pallas_call(
        functools.partial(final_kernel, heads, group, 0),
        grid=(heads // group,),
        in_specs=[
            pl.BlockSpec((1, rows, group * width), lambda h: (0, 0, h)),
            pl.BlockSpec((rows, group * width), lambda h: (0, h)),
            pl.BlockSpec(cols.shape, lambda h: (0, 0)),
            pl.BlockSpec((group, width, width), lambda h: (h, 0, 0)),
            pl.BlockSpec((1, group * width), lambda h: (0, h)),
        ],
        out_specs=pl.BlockSpec((rows, group * width), lambda h: (0, h)),
        out_shape=jax.ShapeDtypeStruct((rows, heads * width), BF16),
        compiler_params=params(),
        cost_estimate=pl.CostEstimate(
            flops=2 * heads * rows * width * width,
            bytes_accessed=heads * rows * width * 8,
            transcendentals=0,
        ),
        name="final_pass",
    )(qkv, mixed, cols, carried, gain)


def carry_scan(state, last, z_axis, y_axis):
    heads, width = state.shape[0], state.shape[1]
    ny, y = y_axis.n, y_axis.index()
    share = heads // ny
    pad = 16

    def packed(k):
        at = ((y + k) % ny) * share
        body = lax.dynamic_slice_in_dim(state, at, share, 0).reshape(share * width, width)
        fade = jnp.exp(lax.dynamic_slice_in_dim(last, at, share, 0))
        rows = jnp.stack(pieces_of(fade), 0)
        rows = jnp.pad(rows, ((0, pad - PIECES), (0, width - share)))
        return jnp.concatenate([body, rows.astype(BF16)], 0)

    got = [packed(0)] + [y_axis.send(packed(k), k) for k in range(1, ny)]
    states = [g[: share * width].reshape(share, width, width).astype(F32) for g in got]
    fades = [jnp.sum(g[share * width :, :share].astype(F32), 0) for g in got]
    places = [(y - k) % ny for k in range(ny)]

    def reach(k, end):
        r = jnp.where(places[k] < end, 1.0, 0.0) * jnp.ones((share,), F32)
        for m in range(ny):
            if m != k:
                r = r * jnp.where((places[m] > places[k]) & (places[m] < end), fades[m], 1.0)
        return r[:, None, None]

    def whole(end):
        r = jnp.ones((share,), F32)
        for m in range(ny):
            r = r * jnp.where(places[m] < end, fades[m], 1.0)
        return r[:, None, None]

    inner = sum(reach(k, ny) * states[k] for k in range(ny))
    through = whole(ny)
    carried = jnp.zeros((share, width, width), F32)
    for i in range(z_axis.n - 1):
        out = (through * carried + inner).astype(BF16)
        carried = carried + lax.ppermute(out, z_axis.name, z_axis.hop(i)).astype(F32)

    def entering(j):
        end = (y + j) % ny
        return (
            whole(end) * carried + sum(reach(k, end) * states[k] for k in range(ny))
        ).astype(BF16)

    back = [entering(0)] + [y_axis.send(entering(j), j) for j in range(1, ny)]
    both = jnp.stack(back, 0)
    order = [(y - p) % ny for p in range(ny)]
    return jnp.concatenate([lax.dynamic_index_in_dim(both, o, 0, False) for o in order], 0)


def hidden_kernel(steps, split, *refs):
    xs, w_ref, h_ref, gate, up = refs[:4], refs[4], refs[5], refs[6], refs[7]
    step = pl.program_id(0)

    @pl.when(step == 0)
    def _():
        gate[...] = jnp.zeros_like(gate)
        up[...] = jnp.zeros_like(up)

    def add(pair):
        x = jnp.concatenate([pair[0][...], pair[1][...]], 0)
        gate[...] += lax.dot_general(w_ref[0], x, NT, preferred_element_type=F32)
        up[...] += lax.dot_general(w_ref[1], x, NT, preferred_element_type=F32)

    pl.when(step < split)(lambda: add(xs[:2]))
    pl.when(step >= split)(lambda: add(xs[2:]))

    @pl.when(step == steps - 1)
    def _():
        g = gate[...]
        h_ref[...] = (g / (1.0 + jnp.exp(-g)) * up[...]).T.astype(BF16)


def hidden_pass(xs, w_in, block=1024):
    units, wide = w_in.shape[1], w_in.shape[2]
    tokens = xs[0].shape[0] * 2
    steps = wide // block
    split = steps // 2
    half = tokens // 2
    first = pl.BlockSpec((half, block), lambda s: (0, jnp.minimum(s, split - 1)))
    second = pl.BlockSpec((half, block), lambda s: (0, jnp.maximum(s - split, 0)))
    return pl.pallas_call(
        functools.partial(hidden_kernel, steps, split),
        grid=(steps,),
        in_specs=[first, first, second, second]
        + [pl.BlockSpec((2, units, block), lambda s: (0, 0, s))],
        out_specs=pl.BlockSpec((tokens, units), lambda s: (0, 0)),
        out_shape=jax.ShapeDtypeStruct((tokens, units), BF16),
        scratch_shapes=[pltpu.VMEM((units, tokens), F32), pltpu.VMEM((units, tokens), F32)],
        compiler_params=params(),
        cost_estimate=pl.CostEstimate(
            flops=4 * units * wide * tokens,
            bytes_accessed=4 * units * wide + 2 * tokens * wide,
            transcendentals=units * tokens,
        ),
        name="hidden_pass",
    )(*xs, w_in)


def down_kernel(h_ref, w_ref, p0_ref, p1_ref, o0_ref, o1_ref):
    half = o0_ref.shape[0]
    out = lax.dot_general(h_ref[...], w_ref[...], NN, preferred_element_type=F32)
    o0_ref[...] = (out[:half] * p0_ref[...]).astype(BF16)
    o1_ref[...] = (out[half:] * p1_ref[...]).astype(BF16)


def down_pass(h, w_out, probs, start, width, block=1024):
    tokens, units = h.shape
    half = tokens // 2
    off = start // block
    out = jax.ShapeDtypeStruct((half, width), BF16)
    spec = pl.BlockSpec((half, block), lambda s: (0, s))
    weight = pl.BlockSpec((half, 1), lambda s: (0, 0))
    return pl.pallas_call(
        down_kernel,
        grid=(width // block,),
        in_specs=[
            pl.BlockSpec((tokens, units), lambda s: (0, 0)),
            pl.BlockSpec((units, block), lambda s: (0, off + s)),
            weight,
            weight,
        ],
        out_specs=(spec, spec),
        out_shape=(out, out),
        compiler_params=params(),
        cost_estimate=pl.CostEstimate(
            flops=2 * units * width * tokens,
            bytes_accessed=2 * units * width + 2 * tokens * width,
            transcendentals=0,
        ),
        name="down_pass",
    )(h, w_out, *probs)


def experts_layer(tokens, ids, probs, w_in, w_out, axes):
    x_axis, core, z_axis, y_axis = axes
    count, wide = tokens.shape
    experts = w_in.shape[0] * lax.axis_size("exp")
    units = w_in.shape[3]
    half = wide // 2
    named = ids[:, :, None] == jnp.arange(experts, dtype=jnp.int32)[None, None]
    weight = jnp.sum(jnp.where(named, probs[:, :, None], 0.0), axis=1)
    route = jnp.concatenate(pieces_of(weight), 1)
    route = jnp.pad(route, ((0, 0), (0, 128 - route.shape[1]))).astype(BF16)
    z = gather(z_axis, jnp.concatenate([tokens, route], 1))
    a, b = z[:, :half], z[:, half:]
    a, b = gather(y_axis, a), gather(x_axis, b)
    a, b = gather(x_axis, a), gather(y_axis, b)
    nx, ny = x_axis.n, y_axis.n
    b = b.reshape(ny, nx, -1, b.shape[1]).transpose(1, 0, 2, 3).reshape(b.shape)
    a2, b2 = core.send(a, 1), core.send(b, 1)
    own = lax.axis_index("exp")

    def weights_of(rows):
        r = rows[:, half : half + PIECES * experts].astype(F32).reshape(-1, PIECES, experts)
        mine = jnp.arange(experts)[None, None] == own
        return jnp.sum(jnp.where(mine, r, 0.0), axis=(1, 2))[:, None]

    flow = (weights_of(b), weights_of(b2))
    h = hidden_pass((a, a2, b, b2), w_in[0].transpose(1, 2, 0))
    pa = down_pass(h, w_out[0], flow, 0, half)
    pb = down_pass(h, w_out[0], flow, half, half)
    a = scatter(core, pa)
    b = scatter(core, pb)
    b = b.reshape(nx, ny, -1, half).transpose(1, 0, 2, 3).reshape(b.shape)
    a, b = scatter(x_axis, rows_split(a, nx)), scatter(y_axis, rows_split(b, ny))
    a, b = scatter(y_axis, rows_split(a, ny)), scatter(x_axis, rows_split(b, nx))
    return scatter(z_axis, rows_split(jnp.concatenate([a, b], 1), z_axis.n))


def on_device(axes, projected, log_decay, norm_gain, moe_tokens, expert_ids, route_probs, w_in, w_out):
    x_axis, core, z_axis, y_axis = axes
    heads = log_decay.shape[1]
    qkv = projected.transpose(1, 0, 2)
    run, cols = prepare(log_decay)
    mixed, state = local_pass(qkv, run, cols, heads, 0, heads)
    moe_out = experts_layer(moe_tokens, expert_ids, route_probs, w_in, w_out, axes)
    carried = carry_scan(state, run[:, -1], z_axis, y_axis)
    attn_out = final_pass(qkv, mixed, cols, carried, norm_gain[None], heads)
    return attn_out, moe_out


def solution(mesh):
    nz, ny = factors(mesh.shape["seq"])
    nx = mesh.shape["exp"] // 2
    axes = (
        Axis("exp", nx, 2, 1),
        Axis("exp", 2, 1, nx),
        Axis("seq", nz, ny, 1),
        Axis("seq", ny, 1, nz),
    )
    in_specs = (
        P("seq", None, "exp"),
        P("seq", "exp"),
        P("exp"),
        P(("seq", "exp"), None),
        P(("seq", "exp"), None),
        P(("seq", "exp"), None),
        P("exp", None, None, "seq"),
        P("exp", "seq", None),
    )
    out_specs = (P("seq", "exp"), P(("seq", "exp"), None))
    return jax.shard_map(
        functools.partial(on_device, axes),
        mesh=mesh,
        in_specs=in_specs,
        out_specs=out_specs,
        check_vma=False,
    )
```

time: 249 us -> 121 us (0.49)
  the two profiles are of different devices: /device:TPU:31 before, /device:TPU:0 now
where the time goes in v1:
time: 121 us; the launch traced here: 120 us
  Pallas kernels  43.5 us (36%)
  starting transfers between devices  36.5 us (30%)
  waiting for transfers between devices  29 us (24%)
  other arithmetic  6.48 us (5%)
  local copies, waits for them, and re-layouts  3.76 us (3%)
    ppermute x20, starting transfers between devices, send(): return lax.ppermute(a, self.name, self.turn(k))  30.8 us
    ppermute x20, waiting for transfers between devices, send(): return lax.ppermute(a, self.name, self.turn(k))  29 us
    pallas_call x1, Pallas kernels, local_pass(): pl.pallas_call(functools.partial(local_kernel, heads, group, base), grid=...  12.9 us
    pallas_call x1, Pallas kernels, hidden_pass(): pl.pallas_call(functools.partial(hidden_kernel, steps, split), grid=(step...  10.4 us
    pallas_call x2, Pallas kernels, down_pass(): pl.pallas_call(down_kernel, grid=(width // block,), in_specs=[pl.BlockSpe...  9.43 us
    pallas_call x1, Pallas kernels, final_pass(): pl.pallas_call(functools.partial(final_kernel, heads, group, 0), grid=(he...  8.61 us
    ppermute x3, starting transfers between devices, carry_scan(): lax.ppermute(out, z_axis.name, z_axis.hop(i)).astype(F32)  5.75 us
  transfers between devices with their start and end apart: 23, of which 9 were waited for; matrix products, arithmetic and copies ran while one was open for 6% of the time, Pallas kernels for 36%

profile of v1, /device:TPU:0, one launch (start us, length us, event | category | flops | bytes accessed | tf_op | source)
XLA Modules:
  0.0 120.3 jit_solution(4414516288880769933)
XLA Ops:
  1.5 0.9 pad_maximum_fusion.11
  2.4 5.0 %collective-permute-start.7 = (bf16[8,6272]{1,0:T(8,128)(2,1)S(1)}, bf16[8,6272]{1,0:T(8,128)(2,1)S(1)}, u32[]{:S(2)}, u32[]{:S(2)}) collective-permute-start(bf16[8,6272]{1,0:T(8,128)(2,1)S(1)} %pad_maximum_fusion.11), channel_id=1, source_target_pairs={{0,24},{4,28},{8,0},{12,4},{16,8},{20,12},{24,16},{28,20},{1,25},{... | collective-permute-start | bytes 301064 | tf_op jit(solution)/shard_map/ppermute | solution.py:51
  7.5 1.0 collective-permute-start.5
  8.5 2.2 %prepare.1 = (f32[16,512]{1,0:T(8,128)}, f32[512,128]{1,0:T(8,128)}) custom-call(f32[16,512]{1,0:T(8,128)} %bitcast.63), custom_call_target="tpu_custom_call" | custom-call | tf_op jit(solution)/shard_map/prepare/pallas_call | solution.py:112
  10.7 0.8 slice.64
  11.4 12.9 %local_pass.1 = (f32[512,2048]{1,0:T(8,128)}, bf16[16,128,128]{2,1,0:T(8,128)(2,1)}) custom-call(bf16[3,512,2048]{2,1,0:T(8,128)(2,1)} %bitcast.44, bf16[3,512,2048]{2,1,0:T(8,128)(2,1)} %bitcast.45, bf16[3,512,2048]{2,1,0:T(8,128)(2,1)} %bitcast.46, f32[16,512]{1,0:T(8,128)} %get-tuple-element.10.run_ref, f32[512,128]{1,0:T(8,128)} %get-tuple-element.11.cols_ref), custom_call_target="tpu_custom_call" | custom-call | flops 1073741824 | bytes 10485760 | tf_op jit(solution)/shard_map/local_pass/pallas_call | solution.py:164
  24.3 1.0 constant_dynamic-slice_fusion
  25.6 1.6 %collective-permute-start = (bf16[1040,128]{1,0:T(8,128)(2,1)S(1)}, bf16[1040,128]{1,0:T(8,128)(2,1)S(1)}, u32[]{:S(2)}, u32[]{:S(2)}) collective-permute-start(bf16[1040,128]{1,0:T(8,128)(2,1)S(1)} %pad_maximum_fusion.5), channel_id=1, source_target_pairs={{0,4},{4,0},{8,12},{12,8},{16,20},{20,16},{24,28},{28,24},{1,5},{5... | collective-permute-start | bytes 798728 | tf_op jit(solution)/shard_map/ppermute | solution.py:51
  27.9 1.6 %collective-permute-start.11 = (bf16[32,3200]{1,0:T(8,128)(2,1)S(1)}, bf16[32,3200]{1,0:T(8,128)(2,1)S(1)}, u32[]{:S(2)}, u32[]{:S(2)}) collective-permute-start(bf16[32,3200]{1,0:T(8,128)(2,1)S(1)} %pad_maximum_fusion.6), channel_id=1, source_target_pairs={{0,2},{1,3},{2,0},{3,1},{4,6},{5,7},{6,4},{7,5},{8,10},{9,11},{10,... | collective-permute-start | bytes 614408 | tf_op jit(solution)/shard_map/ppermute | solution.py:51
  29.4 5.5 %collective-permute-done = bf16[1040,128]{1,0:T(8,128)(2,1)S(1)} collective-permute-done((bf16[1040,128]{1,0:T(8,128)(2,1)S(1)}, bf16[1040,128]{1,0:T(8,128)(2,1)S(1)}, u32[]{:S(2)}, u32[]{:S(2)}) %collective-permute-start) | collective-permute-done | bytes 266272 | tf_op jit(solution)/shard_map/ppermute | solution.py:51
  35.1 1.6 %collective-permute-start.12 = (bf16[64,3200]{1,0:T(8,128)(2,1)S(1)}, bf16[64,3200]{1,0:T(8,128)(2,1)S(1)}, u32[]{:S(2)}, u32[]{:S(2)}) collective-permute-start(bf16[64,3200]{1,0:T(8,128)(2,1)S(1)} %pad_maximum_fusion.3), channel_id=1, source_target_pairs={{0,4},{4,0},{8,12},{12,8},{16,20},{20,16},{24,28},{28,24},{1,5},{5... | collective-permute-start | bytes 1228808 | tf_op jit(solution)/shard_map/ppermute | solution.py:51
  36.9 4.4 %collective-permute-start.1 = (bf16[8,128,128]{2,1,0:T(8,128)(2,1)S(1)}, bf16[8,128,128]{2,1,0:T(8,128)(2,1)S(1)}, u32[]{:S(2)}, u32[]{:S(2)}) collective-permute-start(bf16[8,128,128]{2,1,0:T(8,128)(2,1)S(1)} %add_convert_fusion.4), channel_id=1, source_target_pairs={{0,8},{4,12},{1,9},{5,13},{2,10},{6,14},{3,11},{7,15}} | collective-permute-start | bytes 786440 | tf_op jit(solution)/shard_map/ppermute | solution.py:266
  41.3 1.6 %collective-permute-start.9 = (bf16[64,3072]{1,0:T(8,128)(2,1)S(1)}, bf16[64,3072]{1,0:T(8,128)(2,1)S(1)}, u32[]{:S(2)}, u32[]{:S(2)}) collective-permute-start(bf16[64,3072]{1,0:T(8,128)(2,1)S(1)} %pad_maximum_fusion.4), channel_id=1, source_target_pairs={{0,2},{1,3},{2,0},{3,1},{4,6},{5,7},{6,4},{7,5},{8,10},{9,11},{10,... | collective-permute-start | bytes 1179656 | tf_op jit(solution)/shard_map/ppermute | solution.py:51
  42.9 3.0 %collective-permute-done.12 = bf16[64,3200]{1,0:T(8,128)(2,1)S(1)} collective-permute-done((bf16[64,3200]{1,0:T(8,128)(2,1)S(1)}, bf16[64,3200]{1,0:T(8,128)(2,1)S(1)}, u32[]{:S(2)}, u32[]{:S(2)}) %collective-permute-start.12) | collective-permute-done | bytes 409632 | tf_op jit(solution)/shard_map/ppermute | solution.py:51
  46.1 3.0 %collective-permute-done.9 = bf16[64,3072]{1,0:T(8,128)(2,1)S(1)} collective-permute-done((bf16[64,3072]{1,0:T(8,128)(2,1)S(1)}, bf16[64,3072]{1,0:T(8,128)(2,1)S(1)}, u32[]{:S(2)}, u32[]{:S(2)}) %collective-permute-start.9) | collective-permute-done | bytes 393248 | tf_op jit(solution)/shard_map/ppermute | solution.py:51
  51.7 10.4 %hidden_pass.1.h_ref = bf16[256,576]{1,0:T(8,128)(2,1)} custom-call(bf16[128,3072]{1,0:T(8,128)(2,1)} %copy-done.2, bf16[128,3072]{1,0:T(8,128)(2,1)} %collective-permute-done.10.refs_1_, bf16[128,3200]{1,0:T(8,128)(2,1)} %bitcast.56, bf16[128,3200]{1,0:T(8,128)(2,1)} %collective-permute-done.13.refs_3_, bf16[2,576,6144]{2,1,0:T(8,128)(2,1)} %bitcast.50), custom_call_target="tpu_custom_call" | custom-call | flops 3623878656 | bytes 17301504 | tf_op jit(solution)/shard_map/hidden_pass/pallas_call | solution.py:311
  62.1 0.9 select_reduce_fusion
  63.0 0.8 copy.27.p0_ref
  64.5 4.7 %down_pass.2 = (bf16[128,3072]{1,0:T(8,128)(2,1)}, bf16[128,3072]{1,0:T(8,128)(2,1)}) custom-call(bf16[256,576]{1,0:T(8,128)(2,1)} %hidden_pass.1.h_ref, bf16[576,6144]{1,0:T(8,128)(2,1)} %bitcast.48, f32[128,1]{1,0:T(8,128)} %copy.27.p0_ref, f32[128,1]{1,0:T(8,128)} %copy.28.p1_ref), custom_call_target="tpu_custom_call" | custom-call | flops 905969664 | bytes 5111808 | tf_op jit(solution)/shard_map/down_pass/pallas_call | solution.py:343
  70.4 4.7 %down_pass.3 = (bf16[128,3072]{1,0:T(8,128)(2,1)}, bf16[128,3072]{1,0:T(8,128)(2,1)}) custom-call(bf16[256,576]{1,0:T(8,128)(2,1)} %hidden_pass.1.h_ref, bf16[576,6144]{1,0:T(8,128)(2,1)} %bitcast.49, f32[128,1]{1,0:T(8,128)} %copy.27.p0_ref, f32[128,1]{1,0:T(8,128)} %copy.28.p1_ref), custom_call_target="tpu_custom_call" | custom-call | flops 905969664 | bytes 5111808 | tf_op jit(solution)/shard_map/down_pass/pallas_call | solution.py:343
  75.2 3.2 %collective-permute-done.4 = bf16[8,128,128]{2,1,0:T(8,128)(2,1)S(1)} collective-permute-done((bf16[8,128,128]{2,1,0:T(8,128)(2,1)S(1)}, bf16[8,128,128]{2,1,0:T(8,128)(2,1)S(1)}, u32[]{:S(2)}, u32[]{:S(2)}) %collective-permute-start.4) | collective-permute-done | bytes 262176 | tf_op jit(solution)/shard_map/ppermute | solution.py:51
  78.9 1.6 %collective-permute-start.15 = (bf16[64,3072]{1,0:T(8,128)(2,1)S(1)}, bf16[64,3072]{1,0:T(8,128)(2,1)S(1)}, u32[]{:S(2)}, u32[]{:S(2)}) collective-permute-start(bf16[64,3072]{1,0:T(8,128)(2,1)S(1)} %slice.90), channel_id=1, source_target_pairs={{0,2},{1,3},{2,0},{3,1},{4,6},{5,7},{6,4},{7,5},{8,10},{9,11},{10,... | collective-permute-start | bytes 1179656 | tf_op jit(solution)/shard_map/ppermute | solution.py:51
  81.3 8.3 %collective-permute-done.15 = bf16[64,3072]{1,0:T(8,128)(2,1)S(1)} collective-permute-done((bf16[64,3072]{1,0:T(8,128)(2,1)S(1)}, bf16[64,3072]{1,0:T(8,128)(2,1)S(1)}, u32[]{:S(2)}, u32[]{:S(2)}) %collective-permute-start.15) | collective-permute-done | bytes 393248 | tf_op jit(solution)/shard_map/ppermute | solution.py:51
  90.2 0.9 collective-permute-done.18
  91.3 1.1 collective-permute-start.19
  92.4 3.0 %collective-permute-done.16 = bf16[32,3072]{1,0:T(8,128)(2,1)S(1)} collective-permute-done((bf16[32,3072]{1,0:T(8,128)(2,1)S(1)}, bf16[32,3072]{1,0:T(8,128)(2,1)S(1)}, u32[]{:S(2)}, u32[]{:S(2)}) %collective-permute-start.16) | collective-permute-done | bytes 196640 | tf_op jit(solution)/shard_map/ppermute | solution.py:51
  95.4 1.6 %collective-permute-done.19 = bf16[32,3072]{1,0:T(8,128)(2,1)S(1)} collective-permute-done((bf16[32,3072]{1,0:T(8,128)(2,1)S(1)}, bf16[32,3072]{1,0:T(8,128)(2,1)S(1)}, u32[]{:S(2)}, u32[]{:S(2)}) %collective-permute-start.19) | collective-permute-done | bytes 196640 | tf_op jit(solution)/shard_map/ppermute | solution.py:51
  97.1 7.6 %collective-permute-start.22 = (bf16[8,6144]{1,0:T(8,128)(2,1)S(1)}, bf16[8,6144]{1,0:T(8,128)(2,1)S(1)}, u32[]{:S(2)}, u32[]{:S(2)}) collective-permute-start(bf16[8,6144]{1,0:T(8,128)(2,1)S(1)} %get-tuple-element.31), channel_id=1, source_target_pairs={{0,8},{4,12},{8,16},{12,20},{16,24},{20,28},{24,0},{28,4},{1,9},{5... | collective-permute-start | bytes 294920 | tf_op jit(solution)/shard_map/ppermute | solution.py:51
  104.7 2.6 %collective-permute-start.21 = (bf16[8,6144]{1,0:T(8,128)(2,1)S(1)}, bf16[8,6144]{1,0:T(8,128)(2,1)S(1)}, u32[]{:S(2)}, u32[]{:S(2)}) collective-permute-start(bf16[8,6144]{1,0:T(8,128)(2,1)S(1)} %get-tuple-element.32), channel_id=1, source_target_pairs={{0,16},{4,20},{8,24},{12,28},{16,0},{20,4},{24,8},{28,12},{1,17},{... | collective-permute-start | bytes 294920 | tf_op jit(solution)/shard_map/ppermute | solution.py:51
  107.3 2.8 %collective-permute-start.20 = (bf16[8,6144]{1,0:T(8,128)(2,1)S(1)}, bf16[8,6144]{1,0:T(8,128)(2,1)S(1)}, u32[]{:S(2)}, u32[]{:S(2)}) collective-permute-start(bf16[8,6144]{1,0:T(8,128)(2,1)S(1)} %get-tuple-element.30), channel_id=1, source_target_pairs={{0,24},{4,28},{8,0},{12,4},{16,8},{20,12},{24,16},{28,20},{1,25},{... | collective-permute-start | bytes 294920 | tf_op jit(solution)/shard_map/ppermute | solution.py:51
  110.2 0.8 pad_maximum_fusion.2.carried_ref
  111.0 8.6 %final_pass.1 = bf16[512,2048]{1,0:T(8,128)(2,1)} custom-call(bf16[3,512,2048]{2,1,0:T(8,128)(2,1)} %bitcast.47, f32[512,2048]{1,0:T(8,128)} %get-tuple-element.12.mixed_ref, f32[512,128]{1,0:T(8,128)} %get-tuple-element.11.cols_ref, bf16[16,128,128]{2,1,0:T(8,128)(2,1)} %pad_maximum_fusion.2.carried_ref, f32[1,2048]{1,0:T(1,128)} %bitcast.64), custom_call_target="tpu_custom_call" | custom-call | flops 268435456 | bytes 8388608 | tf_op jit(solution)/shard_map/final_pass/pallas_call | solution.py:207
  (79 shorter events, 9.6 us)
Async XLA Ops:
  2.4 24.8 %collective-permute-start.7 = (bf16[8,6272]{1,0:T(8,128)(2,1)S(1)}, bf16[8,6272]{1,0:T(8,128)(2,1)S(1)}, u32[]{:S(2)}, u32[]{:S(2)}) collective-permute-start(bf16[8,6272]{1,0:T(8,128)(2,1)S(1)} %pad_maximum_fusion.11), channel_id=1, source_target_pairs={{0,24},{4,28},{8,0},{12,4},{16,8},{20,12},{24,16},{28,20},{1,25},{... | collective-permute-start | bytes 301064 | tf_op jit(solution)/shard_map/ppermute | solution.py:51
  7.5 19.8 %collective-permute-start.6 = (bf16[8,6272]{1,0:T(8,128)(2,1)S(1)}, bf16[8,6272]{1,0:T(8,128)(2,1)S(1)}, u32[]{:S(2)}, u32[]{:S(2)}) collective-permute-start(bf16[8,6272]{1,0:T(8,128)(2,1)S(1)} %pad_maximum_fusion.11), channel_id=1, source_target_pairs={{0,16},{4,20},{8,24},{12,28},{16,0},{20,4},{24,8},{28,12},{1,17},{... | collective-permute-start | bytes 301064 | tf_op jit(solution)/shard_map/ppermute | solution.py:51
  7.5 19.8 %collective-permute-start.5 = (bf16[8,6272]{1,0:T(8,128)(2,1)S(1)}, bf16[8,6272]{1,0:T(8,128)(2,1)S(1)}, u32[]{:S(2)}, u32[]{:S(2)}) collective-permute-start(bf16[8,6272]{1,0:T(8,128)(2,1)S(1)} %pad_maximum_fusion.11), channel_id=1, source_target_pairs={{0,8},{4,12},{8,16},{12,20},{16,24},{20,28},{24,0},{28,4},{1,9},{5... | collective-permute-start | bytes 301064 | tf_op jit(solution)/shard_map/ppermute | solution.py:51
  11.4 15.8 %copy-start.3 = (bf16[8,6144]{1,0:T(8,128)(2,1)S(1)}, bf16[8,6144]{1,0:T(8,128)(2,1)}, u32[]{:S(2)}) copy-start(bf16[8,6144]{1,0:T(8,128)(2,1)} %param.11) | copy-start | bytes 294916
  25.5 11.1 %copy-start.1 = (bf16[16,128,128]{2,1,0:T(8,128)(2,1)S(1)}, bf16[16,128,128]{2,1,0:T(8,128)(2,1)}, u32[]{:S(2)}) copy-start(bf16[16,128,128]{2,1,0:T(8,128)(2,1)} %get-tuple-element.13) | copy-start | bytes 1572868
  25.6 9.4 %collective-permute-start = (bf16[1040,128]{1,0:T(8,128)(2,1)S(1)}, bf16[1040,128]{1,0:T(8,128)(2,1)S(1)}, u32[]{:S(2)}, u32[]{:S(2)}) collective-permute-start(bf16[1040,128]{1,0:T(8,128)(2,1)S(1)} %pad_maximum_fusion.5), channel_id=1, source_target_pairs={{0,4},{4,0},{8,12},{12,8},{16,20},{20,16},{24,28},{28,24},{1,5},{5... | collective-permute-start | bytes 798728 | tf_op jit(solution)/shard_map/ppermute | solution.py:51
  27.3 14.0 %collective-permute-start.8 = (bf16[32,3072]{1,0:T(8,128)(2,1)S(1)}, bf16[32,3072]{1,0:T(8,128)(2,1)S(1)}, u32[]{:S(2)}, u32[]{:S(2)}) collective-permute-start(bf16[32,3072]{1,0:T(8,128)(2,1)S(1)} %pad_maximum_fusion.10), channel_id=1, source_target_pairs={{0,4},{4,0},{8,12},{12,8},{16,20},{20,16},{24,28},{28,24},{1,5},{5... | collective-permute-start | bytes 589832 | tf_op jit(solution)/shard_map/ppermute | solution.py:51
  27.9 7.2 %collective-permute-start.11 = (bf16[32,3200]{1,0:T(8,128)(2,1)S(1)}, bf16[32,3200]{1,0:T(8,128)(2,1)S(1)}, u32[]{:S(2)}, u32[]{:S(2)}) collective-permute-start(bf16[32,3200]{1,0:T(8,128)(2,1)S(1)} %pad_maximum_fusion.6), channel_id=1, source_target_pairs={{0,2},{1,3},{2,0},{3,1},{4,6},{5,7},{6,4},{7,5},{8,10},{9,11},{10,... | collective-permute-start | bytes 614408 | tf_op jit(solution)/shard_map/ppermute | solution.py:51
  35.1 10.8 %collective-permute-start.12 = (bf16[64,3200]{1,0:T(8,128)(2,1)S(1)}, bf16[64,3200]{1,0:T(8,128)(2,1)S(1)}, u32[]{:S(2)}, u32[]{:S(2)}) collective-permute-start(bf16[64,3200]{1,0:T(8,128)(2,1)S(1)} %pad_maximum_fusion.3), channel_id=1, source_target_pairs={{0,4},{4,0},{8,12},{12,8},{16,20},{20,16},{24,28},{28,24},{1,5},{5... | collective-permute-start | bytes 1228808 | tf_op jit(solution)/shard_map/ppermute | solution.py:51
  36.9 12.4 %collective-permute-start.1 = (bf16[8,128,128]{2,1,0:T(8,128)(2,1)S(1)}, bf16[8,128,128]{2,1,0:T(8,128)(2,1)S(1)}, u32[]{:S(2)}, u32[]{:S(2)}) collective-permute-start(bf16[8,128,128]{2,1,0:T(8,128)(2,1)S(1)} %add_convert_fusion.4), channel_id=1, source_target_pairs={{0,8},{4,12},{1,9},{5,13},{2,10},{6,14},{3,11},{7,15}} | collective-permute-start | bytes 786440 | tf_op jit(solution)/shard_map/ppermute | solution.py:266
  41.3 7.8 %collective-permute-start.9 = (bf16[64,3072]{1,0:T(8,128)(2,1)S(1)}, bf16[64,3072]{1,0:T(8,128)(2,1)S(1)}, u32[]{:S(2)}, u32[]{:S(2)}) collective-permute-start(bf16[64,3072]{1,0:T(8,128)(2,1)S(1)} %pad_maximum_fusion.4), channel_id=1, source_target_pairs={{0,2},{1,3},{2,0},{3,1},{4,6},{5,7},{6,4},{7,5},{8,10},{9,11},{10,... | collective-permute-start | bytes 1179656 | tf_op jit(solution)/shard_map/ppermute | solution.py:51
  46.0 4.5 %copy-start = (bf16[2,2,32,3200]{3,2,0,1:T(8,128)(2,1)}, bf16[2,2,32,3200]{3,2,0,1:T(8,128)(2,1)S(1)}, u32[]{:S(2)}) copy-start(bf16[2,2,32,3200]{3,2,0,1:T(8,128)(2,1)S(1)} %copy.26) | copy-start | bytes 2457604
  46.0 5.7 %collective-permute-start.13 = (bf16[128,3200]{1,0:T(8,128)(2,1)S(1)}, bf16[128,3200]{1,0:T(8,128)(2,1)}, u32[]{:S(2)}, u32[]{:S(2)}) collective-permute-start(bf16[128,3200]{1,0:T(8,128)(2,1)S(1)} %bitcast.55), channel_id=1, source_target_pairs={{0,1},{1,0},{2,3},{3,2},{4,5},{5,4},{6,7},{7,6},{8,9},{9,8},{10,11... | collective-permute-start | bytes 2457608 | tf_op jit(solution)/shard_map/ppermute | solution.py:51
  49.2 2.5 %copy-start.2 = (bf16[128,3072]{1,0:T(8,128)(2,1)}, bf16[128,3072]{1,0:T(8,128)(2,1)S(1)}, u32[]{:S(2)}) copy-start(bf16[128,3072]{1,0:T(8,128)(2,1)S(1)} %pad_maximum_fusion.1.refs_0_) | copy-start | bytes 2359300
  49.2 2.5 %collective-permute-start.10 = (bf16[128,3072]{1,0:T(8,128)(2,1)S(1)}, bf16[128,3072]{1,0:T(8,128)(2,1)}, u32[]{:S(2)}, u32[]{:S(2)}) collective-permute-start(bf16[128,3072]{1,0:T(8,128)(2,1)S(1)} %pad_maximum_fusion.1.refs_0_), channel_id=1, source_target_pairs={{0,1},{1,0},{2,3},{3,2},{4,5},{5,4},{6,7},{7,6},{8,9},{9,8},{10,11... | collective-permute-start | bytes 2359304 | tf_op jit(solution)/shard_map/ppermute | solution.py:51
  49.5 0.8 collective-permute-start.2
  50.6 18.7 %collective-permute-start.3 = (bf16[8,128,128]{2,1,0:T(8,128)(2,1)S(1)}, bf16[8,128,128]{2,1,0:T(8,128)(2,1)S(1)}, u32[]{:S(2)}, u32[]{:S(2)}) collective-permute-start(bf16[8,128,128]{2,1,0:T(8,128)(2,1)S(1)} %add_convert_fusion.3), channel_id=1, source_target_pairs={{16,24},{20,28},{17,25},{21,29},{18,26},{22,30},{19,27},{23,31}} | collective-permute-start | bytes 786440 | tf_op jit(solution)/shard_map/ppermute | solution.py:266
  69.2 9.5 %collective-permute-start.14 = (bf16[128,3072]{1,0:T(8,128)(2,1)}, bf16[128,3072]{1,0:T(8,128)(2,1)S(1)}, u32[]{:S(2)}, u32[]{:S(2)}) collective-permute-start(bf16[128,3072]{1,0:T(8,128)(2,1)} %get-tuple-element.15), channel_id=1, source_target_pairs={{0,1},{1,0},{2,3},{3,2},{4,5},{5,4},{6,7},{7,6},{8,9},{9,8},{10,11... | collective-permute-start | bytes 2359304 | tf_op jit(solution)/shard_map/ppermute | solution.py:51
  69.8 8.6 %collective-permute-start.4 = (bf16[8,128,128]{2,1,0:T(8,128)(2,1)S(1)}, bf16[8,128,128]{2,1,0:T(8,128)(2,1)S(1)}, u32[]{:S(2)}, u32[]{:S(2)}) collective-permute-start(bf16[8,128,128]{2,1,0:T(8,128)(2,1)S(1)} %get-tuple-element.24), channel_id=1, source_target_pairs={{0,4},{4,0},{8,12},{12,8},{16,20},{20,16},{24,28},{28,24},{1,5},{5... | collective-permute-start | bytes 786440 | tf_op jit(solution)/shard_map/ppermute | solution.py:51
  75.1 3.5 %copy-start.4 = (bf16[128,3072]{1,0:T(8,128)(2,1)S(1)}, bf16[128,3072]{1,0:T(8,128)(2,1)}, u32[]{:S(2)}) copy-start(bf16[128,3072]{1,0:T(8,128)(2,1)} %get-tuple-element.14) | copy-start | bytes 2359300
  75.1 5.3 %collective-permute-start.17 = (bf16[128,3072]{1,0:T(8,128)(2,1)}, bf16[128,3072]{1,0:T(8,128)(2,1)S(1)}, u32[]{:S(2)}, u32[]{:S(2)}) collective-permute-start(bf16[128,3072]{1,0:T(8,128)(2,1)} %get-tuple-element.17), channel_id=1, source_target_pairs={{0,1},{1,0},{2,3},{3,2},{4,5},{5,4},{6,7},{7,6},{8,9},{9,8},{10,11... | collective-permute-start | bytes 2359304 | tf_op jit(solution)/shard_map/ppermute | solution.py:51
  78.7 1.8 %copy-start.5 = (bf16[128,3072]{1,0:T(8,128)(2,1)S(1)}, bf16[128,3072]{1,0:T(8,128)(2,1)}, u32[]{:S(2)}) copy-start(bf16[128,3072]{1,0:T(8,128)(2,1)} %get-tuple-element.16) | copy-start | bytes 2359300
  78.9 10.6 %collective-permute-start.15 = (bf16[64,3072]{1,0:T(8,128)(2,1)S(1)}, bf16[64,3072]{1,0:T(8,128)(2,1)S(1)}, u32[]{:S(2)}, u32[]{:S(2)}) collective-permute-start(bf16[64,3072]{1,0:T(8,128)(2,1)S(1)} %slice.90), channel_id=1, source_target_pairs={{0,2},{1,3},{2,0},{3,1},{4,6},{5,7},{6,4},{7,5},{8,10},{9,11},{10,... | collective-permute-start | bytes 1179656 | tf_op jit(solution)/shard_map/ppermute | solution.py:51
  80.7 10.4 %collective-permute-start.18 = (bf16[64,3072]{1,0:T(8,128)(2,1)S(1)}, bf16[64,3072]{1,0:T(8,128)(2,1)S(1)}, u32[]{:S(2)}, u32[]{:S(2)}) collective-permute-start(bf16[64,3072]{1,0:T(8,128)(2,1)S(1)} %bitcast.61), channel_id=1, source_target_pairs={{0,4},{4,0},{8,12},{12,8},{16,20},{20,16},{24,28},{28,24},{1,5},{5... | collective-permute-start | bytes 1179656 | tf_op jit(solution)/shard_map/ppermute | solution.py:51
  89.7 5.7 %collective-permute-start.16 = (bf16[32,3072]{1,0:T(8,128)(2,1)S(1)}, bf16[32,3072]{1,0:T(8,128)(2,1)S(1)}, u32[]{:S(2)}, u32[]{:S(2)}) collective-permute-start(bf16[32,3072]{1,0:T(8,128)(2,1)S(1)} %slice.92), channel_id=1, source_target_pairs={{0,4},{4,0},{8,12},{12,8},{16,20},{20,16},{24,28},{28,24},{1,5},{5... | collective-permute-start | bytes 589832 | tf_op jit(solution)/shard_map/ppermute | solution.py:51
  91.3 5.7 %collective-permute-start.19 = (bf16[32,3072]{1,0:T(8,128)(2,1)S(1)}, bf16[32,3072]{1,0:T(8,128)(2,1)S(1)}, u32[]{:S(2)}, u32[]{:S(2)}) collective-permute-start(bf16[32,3072]{1,0:T(8,128)(2,1)S(1)} %slice.96), channel_id=1, source_target_pairs={{0,2},{1,3},{2,0},{3,1},{4,6},{5,7},{6,4},{7,5},{8,10},{9,11},{10,... | collective-permute-start | bytes 589832 | tf_op jit(solution)/shard_map/ppermute | solution.py:51
  97.1 22.6 %collective-permute-start.22 = (bf16[8,6144]{1,0:T(8,128)(2,1)S(1)}, bf16[8,6144]{1,0:T(8,128)(2,1)S(1)}, u32[]{:S(2)}, u32[]{:S(2)}) collective-permute-start(bf16[8,6144]{1,0:T(8,128)(2,1)S(1)} %get-tuple-element.31), channel_id=1, source_target_pairs={{0,8},{4,12},{8,16},{12,20},{16,24},{20,28},{24,0},{28,4},{1,9},{5... | collective-permute-start | bytes 294920 | tf_op jit(solution)/shard_map/ppermute | solution.py:51
  104.7 14.9 %collective-permute-start.21 = (bf16[8,6144]{1,0:T(8,128)(2,1)S(1)}, bf16[8,6144]{1,0:T(8,128)(2,1)S(1)}, u32[]{:S(2)}, u32[]{:S(2)}) collective-permute-start(bf16[8,6144]{1,0:T(8,128)(2,1)S(1)} %get-tuple-element.32), channel_id=1, source_target_pairs={{0,16},{4,20},{8,24},{12,28},{16,0},{20,4},{24,8},{28,12},{1,17},{... | collective-permute-start | bytes 294920 | tf_op jit(solution)/shard_map/ppermute | solution.py:51
  107.3 12.3 %collective-permute-start.20 = (bf16[8,6144]{1,0:T(8,128)(2,1)S(1)}, bf16[8,6144]{1,0:T(8,128)(2,1)S(1)}, u32[]{:S(2)}, u32[]{:S(2)}) collective-permute-start(bf16[8,6144]{1,0:T(8,128)(2,1)S(1)} %get-tuple-element.30), channel_id=1, source_target_pairs={{0,24},{4,28},{8,0},{12,4},{16,8},{20,12},{24,16},{28,20},{1,25},{... | collective-permute-start | bytes 294920 | tf_op jit(solution)/shard_map/ppermute | solution.py:51

commit v2 on v1

--- a/solution.py
+++ b/solution.py
@@ -7,7 +7,8 @@
 from jax.sharding import PartitionSpec as P
 
 EPS = 1e-06
-CHUNK = 128
+CHUNK = 256
+PARTS = 4
 PIECES = 3
 F32 = jnp.float32
 BF16 = jnp.bfloat16
@@ -80,7 +81,7 @@
     return out
 
 
-def params(limit=56):
+def params(limit=16):
     return pltpu.CompilerParams(vmem_limit_bytes=limit * 2**20)
 
 
@@ -120,7 +121,9 @@
     )(log_decay.T)
 
 
-def local_kernel(heads, group, base, q_ref, k_ref, v_ref, run_ref, cols_ref, mixed_ref, state_ref):
+def local_kernel(heads, group, base, *refs):
+    q_ref, k_ref, v_ref, run_ref, cols_ref = refs[:5]
+    mixed_ref, state_ref = refs[-2:]
     rows, width = q_ref.shape[1], q_ref.shape[2] // group
     first = base + pl.program_id(0) * group
     cols = pltpu.roll(cols_ref[...], 128 - first, 1)
@@ -154,8 +157,9 @@
         state_ref[g] = state.astype(BF16)
 
 
-def local_pass(qkv, run, cols, heads, base, count, group=2):
+def local_pass(qkv, run, cols, heads, base, count, behind, group=4):
     rows, width = qkv.shape[1], qkv.shape[2] // heads
+    group = min(group, count)
     start = base // group
 
     def take(which):
@@ -170,26 +174,30 @@
             take(2),
             pl.BlockSpec(run.shape, lambda h: (0, 0)),
             pl.BlockSpec(cols.shape, lambda h: (0, 0)),
-        ],
+        ]
+        + [pl.BlockSpec(memory_space=pl.ANY)] * len(behind),
         out_specs=(
             pl.BlockSpec((rows, group * width), lambda h: (0, h)),
             pl.BlockSpec((group, width, width), lambda h: (h, 0, 0)),
         ),
         out_shape=(
-            jax.ShapeDtypeStruct((rows, count * width), F32),
+            jax.ShapeDtypeStruct((rows, count * width), BF16),
             jax.ShapeDtypeStruct((count, width, width), BF16),
         ),
-        compiler_params=params(),
+        compiler_params=params(56),
         cost_estimate=pl.CostEstimate(
             flops=8 * count * rows * width * CHUNK,
-            bytes_accessed=count * rows * width * 10,
+            bytes_accessed=count * rows * width * 8,
             transcendentals=count * rows * CHUNK,
         ),
         name="local_pass",
-    )(qkv, qkv, qkv, run, cols)
-
-
-def final_kernel(heads, group, base, q_ref, mixed_ref, cols_ref, carried_ref, gain_ref, out_ref):
+    )(qkv, qkv, qkv, run, cols, *behind)
+
+
+def final_kernel(heads, group, base, *refs):
+    q_ref, mixed_ref, cols_ref, carried_ref, gain_ref = refs[:5]
+    out_ref, mark_ref = refs[-2:]
+    mark_ref[...] = jnp.zeros_like(mark_ref)
     width = q_ref.shape[2] // group
     first = base + pl.program_id(0) * group
     cols = pltpu.roll(cols_ref[...], 128 - first, 1)
@@ -197,33 +205,47 @@
         lanes = slice(g * width, (g + 1) * width)
         er = cols[:, 3 * heads + g : 3 * heads + g + 1]
         far = lax.dot_general(q_ref[0, :, lanes], carried_ref[g], NN, preferred_element_type=F32)
-        mixed = mixed_ref[:, lanes] + er * far
+        mixed = mixed_ref[:, lanes].astype(F32) + er * far
         mean = jnp.mean(mixed * mixed, axis=-1, keepdims=True)
         out_ref[:, lanes] = (mixed * lax.rsqrt(mean + EPS) * gain_ref[:, lanes]).astype(BF16)
 
 
-def final_pass(qkv, mixed, cols, carried, gain, heads, group=2):
+def final_pass(qkv, mixed, cols, carried, gain, heads, base, count, done, behind, group=4):
     rows, width = qkv.shape[1], qkv.shape[2] // heads
+    group = min(group, count)
+    start = base // group
+    args = [qkv, mixed, cols, carried, gain]
+    specs = [
+        pl.BlockSpec((1, rows, group * width), lambda h: (0, 0, start + h)),
+        pl.BlockSpec((rows, group * width), lambda h: (0, h)),
+        pl.BlockSpec(cols.shape, lambda h: (0, 0)),
+        pl.BlockSpec((group, width, width), lambda h: (start + h, 0, 0)),
+        pl.BlockSpec((1, group * width), lambda h: (0, start + h)),
+    ]
+    more = ([] if done is None else [done]) + list(behind)
+    args += more
+    specs += [pl.BlockSpec(memory_space=pl.ANY)] * len(more)
     return pl.pallas_call(
-        functools.partial(final_kernel, heads, group, 0),
-        grid=(heads // group,),
-        in_specs=[
-            pl.BlockSpec((1, rows, group * width), lambda h: (0, 0, h)),
-            pl.BlockSpec((rows, group * width), lambda h: (0, h)),
-            pl.BlockSpec(cols.shape, lambda h: (0, 0)),
-            pl.BlockSpec((group, width, width), lambda h: (h, 0, 0)),
-            pl.BlockSpec((1, group * width), lambda h: (0, h)),
-        ],
-        out_specs=pl.BlockSpec((rows, group * width), lambda h: (0, h)),
-        out_shape=jax.ShapeDtypeStruct((rows, heads * width), BF16),
-        compiler_params=params(),
+        functools.partial(final_kernel, heads, group, base),
+        grid=(count // group,),
+        in_specs=specs,
+        out_specs=(
+            pl.BlockSpec((rows, group * width), lambda h: (0, start + h)),
+            pl.BlockSpec((8, 128), lambda h: (0, 0)),
+        ),
+        out_shape=(
+            jax.ShapeDtypeStruct((rows, heads * width), BF16),
+            jax.ShapeDtypeStruct((8, 128), F32),
+        ),
+        input_output_aliases={} if done is None else {5: 0},
+        compiler_params=params(56),
         cost_estimate=pl.CostEstimate(
-            flops=2 * heads * rows * width * width,
-            bytes_accessed=heads * rows * width * 8,
+            flops=2 * count * rows * width * width,
+            bytes_accessed=count * rows * width * 6,
             transcendentals=0,
         ),
         name="final_pass",
-    )(qkv, mixed, cols, carried, gain)
+    )(*args)
 
 
 def carry_scan(state, last, z_axis, y_axis):
@@ -316,7 +338,7 @@
         out_specs=pl.BlockSpec((tokens, units), lambda s: (0, 0)),
         out_shape=jax.ShapeDtypeStruct((tokens, units), BF16),
         scratch_shapes=[pltpu.VMEM((units, tokens), F32), pltpu.VMEM((units, tokens), F32)],
-        compiler_params=params(),
+        compiler_params=params(56),
         cost_estimate=pl.CostEstimate(
             flops=4 * units * wide * tokens,
             bytes_accessed=4 * units * wide + 2 * tokens * wide,
@@ -351,7 +373,7 @@
         ],
         out_specs=(spec, spec),
         out_shape=(out, out),
-        compiler_params=params(),
+        compiler_params=params(56),
         cost_estimate=pl.CostEstimate(
             flops=2 * units * width * tokens,
             bytes_accessed=2 * units * width + 2 * tokens * width,
@@ -361,51 +383,232 @@
     )(h, w_out, *probs)
 
 
-def experts_layer(tokens, ids, probs, w_in, w_out, axes):
-    x_axis, core, z_axis, y_axis = axes
-    count, wide = tokens.shape
-    experts = w_in.shape[0] * lax.axis_size("exp")
-    units = w_in.shape[3]
+def ordered(ref, lanes, outer, inner):
+    m = ref.shape[0] // (outer * inner)
+    blocks = [(i * outer + o) * m for o in range(outer) for i in range(inner)]
+    return jnp.concatenate([ref[at : at + m, lanes] for at in blocks], 0)
+
+
+def store_ordered(ref, lanes, value, outer, inner):
+    m = ref.shape[0] // (outer * inner)
+    for o in range(outer):
+        for i in range(inner):
+            src, dst = (o * inner + i) * m, (i * outer + o) * m
+            ref[dst : dst + m, lanes] = value[src : src + m]
+
+
+def own_weights(ref, lanes, experts, outer, inner):
+    r = ordered(ref, lanes, outer, inner).astype(F32)
+    lane = lax.broadcasted_iota(jnp.int32, r.shape, 1)
+    mine = (lane % experts == lax.axis_index("exp")) & (lane < PIECES * experts)
+    return jnp.sum(jnp.where(mine, r, 0.0), axis=1, keepdims=True)
+
+
+class Stream:
+    def __init__(self, copies, depth):
+        self.copies, self.depth, self.at = copies, depth, 0
+        for c in copies[:depth]:
+            c.start()
+
+    def next(self):
+        self.copies[self.at].wait()
+        ahead = self.at + self.depth
+        if ahead < len(self.copies):
+            self.copies[ahead].start()
+        self.at += 1
+
+
+def chunks(w, scratch, sems, start, width, block, first):
+    out = []
+    for j, at in enumerate(range(0, width, block)):
+        src = w.at[(slice(None),) * (len(w.shape) - 1) + (pl.ds(start + at, block),)]
+        out.append(pltpu.make_async_copy(src, scratch.at[j], sems.at[first + j]))
+    return out
+
+
+def lead_kernel(experts, nx, ny, block, depth, a, a2, b, b2, w_in, w_out, o, o2, h, flow, acc, wi, wo, sems):
+    units, wide = w_in.shape[1], w_in.shape[2]
     half = wide // 2
+    rows = a.shape[0]
+    copies = chunks(w_in, wi, sems, 0, wide, block, 0)
+    copies += chunks(w_out, wo, sems, 0, half, block, len(copies))
+    stream = Stream(copies, depth)
+    lanes = slice(half, half + 128)
+    flow[:rows] = jnp.broadcast_to(own_weights(b, lanes, experts, nx, ny), (rows, 128))
+    flow[rows:] = jnp.broadcast_to(own_weights(b2, lanes, experts, nx, ny), (rows, 128))
+    for j, at in enumerate(range(0, wide, block)):
+        stream.next()
+        if at < half:
+            x = jnp.concatenate([a[:, at : at + block], a2[:, at : at + block]], 0)
+        else:
+            lanes = slice(at - half, at - half + block)
+            x = jnp.concatenate([ordered(b, lanes, nx, ny), ordered(b2, lanes, nx, ny)], 0)
+        w = wi[j].reshape(2 * units, block)
+        d = lax.dot_general(w, x, NT, preferred_element_type=F32)
+        if at == 0:
+            acc[...] = d
+        else:
+            acc[...] += d
+    g = acc[:units]
+    h[...] = (g / (1.0 + jnp.exp(-g)) * acc[units:]).T.astype(BF16)
+    for j, at in enumerate(range(0, half, block)):
+        stream.next()
+        lanes = slice(at, at + block)
+        d = lax.dot_general(h[...], wo[j], NN, preferred_element_type=F32)
+        d = (d * flow[:, :1]).astype(BF16)
+        o[:, lanes] = d[:rows]
+        o2[:, lanes] = d[rows:]
+
+
+def rest_kernel(nx, ny, block, depth, h, flow, w_out, o, o2, wo, sems):
+    half = w_out.shape[1] // 2
+    rows = o.shape[0]
+    stream = Stream(chunks(w_out, wo, sems, half, half, block, 0), depth)
+    for j, at in enumerate(range(0, half, block)):
+        stream.next()
+        lanes = slice(at, at + block)
+        d = lax.dot_general(h[...], wo[j], NN, preferred_element_type=F32)
+        d = (d * flow[:, :1]).astype(BF16)
+        store_ordered(o, lanes, d[:rows], nx, ny)
+        store_ordered(o2, lanes, d[rows:], nx, ny)
+
+
+def fitting_experts(a, a2, b, b2, w_in, w_out, experts, nx, ny, block=1024, depth=3):
+    units, wide = w_in.shape[1], w_in.shape[2]
+    tokens = 2 * a.shape[0]
+    n_in, n_out = wide // block, wide // 2 // block
+    vmem = pl.BlockSpec(memory_space=pltpu.VMEM)
+    hbm = pl.BlockSpec(memory_space=pl.ANY)
+    half = jax.ShapeDtypeStruct((tokens // 2, wide // 2), BF16)
+    o, o2, h, flow = pl.pallas_call(
+        functools.partial(lead_kernel, experts, nx, ny, block, depth),
+        in_specs=[vmem] * 4 + [hbm] * 2,
+        out_specs=(vmem,) * 4,
+        out_shape=(
+            half,
+            half,
+            jax.ShapeDtypeStruct((tokens, units), BF16),
+            jax.ShapeDtypeStruct((tokens, 128), F32),
+        ),
+        scratch_shapes=[
+            pltpu.VMEM((2 * units, tokens), F32),
+            pltpu.VMEM((n_in, 2, units, block), BF16),
+            pltpu.VMEM((n_out, units, block), BF16),
+            pltpu.SemaphoreType.DMA((n_in + n_out,)),
+        ],
+        compiler_params=params(44),
+        cost_estimate=pl.CostEstimate(
+            flops=5 * units * wide * tokens,
+            bytes_accessed=5 * units * wide + 3 * tokens * wide,
+            transcendentals=units * tokens,
+        ),
+        name="lead_pass",
+    )(a, a2, b, b2, w_in, w_out)
+    p, p2 = pl.pallas_call(
+        functools.partial(rest_kernel, nx, ny, block, depth),
+        in_specs=[vmem] * 2 + [hbm],
+        out_specs=(vmem,) * 2,
+        out_shape=(half, half),
+        scratch_shapes=[
+            pltpu.VMEM((n_out, units, block), BF16),
+            pltpu.SemaphoreType.DMA((n_out,)),
+        ],
+        compiler_params=params(58),
+        cost_estimate=pl.CostEstimate(
+            flops=units * wide * tokens,
+            bytes_accessed=units * wide + tokens * wide,
+            transcendentals=0,
+        ),
+        name="rest_pass",
+    )(h, flow, w_out)
+    return (o, o2), (p, p2)
+
+
+def streamed_experts(a, a2, b, b2, w_in, w_out, experts, nx, ny):
+    half = a.shape[1]
+
+    def turned(r, m, n):
+        return r.reshape(m, n, -1, r.shape[1]).transpose(1, 0, 2, 3).reshape(r.shape)
+
+    b, b2 = turned(b, ny, nx), turned(b2, ny, nx)
+
+    def weights_of(rows):
+        r = rows[:, half : half + PIECES * experts].astype(F32).reshape(-1, PIECES, experts)
+        mine = jnp.arange(experts)[None, None] == lax.axis_index("exp")
+        return jnp.sum(jnp.where(mine, r, 0.0), axis=(1, 2))[:, None]
+
+    flow = (weights_of(b), weights_of(b2))
+    h = hidden_pass((a, a2, b, b2), w_in)
+    pa = down_pass(h, w_out, flow, 0, half)
+    pb = down_pass(h, w_out, flow, half, half)
+    return pa, tuple(turned(p, nx, ny) for p in pb)
+
+
+def route_columns(ids, probs, experts):
     named = ids[:, :, None] == jnp.arange(experts, dtype=jnp.int32)[None, None]
     weight = jnp.sum(jnp.where(named, probs[:, :, None], 0.0), axis=1)
     route = jnp.concatenate(pieces_of(weight), 1)
-    route = jnp.pad(route, ((0, 0), (0, 128 - route.shape[1]))).astype(BF16)
-    z = gather(z_axis, jnp.concatenate([tokens, route], 1))
-    a, b = z[:, :half], z[:, half:]
-    a, b = gather(y_axis, a), gather(x_axis, b)
-    a, b = gather(x_axis, a), gather(y_axis, b)
-    nx, ny = x_axis.n, y_axis.n
-    b = b.reshape(ny, nx, -1, b.shape[1]).transpose(1, 0, 2, 3).reshape(b.shape)
-    a2, b2 = core.send(a, 1), core.send(b, 1)
-    own = lax.axis_index("exp")
-
-    def weights_of(rows):
-        r = rows[:, half : half + PIECES * experts].astype(F32).reshape(-1, PIECES, experts)
-        mine = jnp.arange(experts)[None, None] == own
-        return jnp.sum(jnp.where(mine, r, 0.0), axis=(1, 2))[:, None]
-
-    flow = (weights_of(b), weights_of(b2))
-    h = hidden_pass((a, a2, b, b2), w_in[0].transpose(1, 2, 0))
-    pa = down_pass(h, w_out[0], flow, 0, half)
-    pb = down_pass(h, w_out[0], flow, half, half)
-    a = scatter(core, pa)
-    b = scatter(core, pb)
-    b = b.reshape(nx, ny, -1, half).transpose(1, 0, 2, 3).reshape(b.shape)
-    a, b = scatter(x_axis, rows_split(a, nx)), scatter(y_axis, rows_split(b, ny))
-    a, b = scatter(y_axis, rows_split(a, ny)), scatter(x_axis, rows_split(b, nx))
-    return scatter(z_axis, rows_split(jnp.concatenate([a, b], 1), z_axis.n))
+    return jnp.pad(route, ((0, 0), (0, 128 - route.shape[1]))).astype(BF16)
+
+
+def nothing(a):
+    probe = a[-1, 0].astype(F32)
+    return jnp.where(probe != probe, 1.0, 0.0)
 
 
 def on_device(axes, projected, log_decay, norm_gain, moe_tokens, expert_ids, route_probs, w_in, w_out):
     x_axis, core, z_axis, y_axis = axes
+    nx, ny, nz = x_axis.n, y_axis.n, z_axis.n
     heads = log_decay.shape[1]
+    half = moe_tokens.shape[1] // 2
+    experts = w_in.shape[0] * lax.axis_size("exp")
+    count = heads // min(PARTS, heads)
     qkv = projected.transpose(1, 0, 2)
+    gain = norm_gain[None]
+    route = route_columns(expert_ids, route_probs, experts)
+
+    z = gather(z_axis, jnp.concatenate([moe_tokens, route], 1))
     run, cols = prepare(log_decay)
-    mixed, state = local_pass(qkv, run, cols, heads, 0, heads)
-    moe_out = experts_layer(moe_tokens, expert_ids, route_probs, w_in, w_out, axes)
-    carried = carry_scan(state, run[:, -1], z_axis, y_axis)
-    attn_out = final_pass(qkv, mixed, cols, carried, norm_gain[None], heads)
+    local = []
+
+    def local_part(*behind):
+        local.append(local_pass(qkv, run, cols, heads, len(local) * count, count, behind))
+
+    while len(local) < heads // count // 2:
+        local_part()
+    while len(local) < heads // count:
+        local_part(z)
+    a, b = z[:, :half], z[:, half:]
+    a, b = first = gather(y_axis, a), gather(x_axis, b)
+    a, b = gather(x_axis, a), gather(y_axis, b)
+    last = run[:, -1] + nothing(first[0]) + nothing(first[1])
+    a2, b2 = core.send(a, 1), core.send(b, 1)
+    state = jnp.concatenate([s for _, s in local], 0)
+    carried = carry_scan(state, last, z_axis, y_axis)
+    apply = fitting_experts if 2 * a.shape[0] <= 512 else streamed_experts
+    pa, pb = apply(a, a2, b, b2, w_in[0].transpose(1, 2, 0), w_out[0], experts, nx, ny)
+
+    a, b = scatter(core, pa), scatter(core, pb)
+    attn_out, marks = None, []
+
+    def final_parts(upto, *behind):
+        nonlocal attn_out
+        for i in range(len(marks), upto):
+            attn_out, mark = final_pass(
+                qkv, local[i][0], cols, carried, gain, heads, i * count, count, attn_out, behind
+            )
+            marks.append(mark)
+        return marks[-1][0, 0].astype(BF16)
+
+    parts = heads // count
+    zero = final_parts(parts // 2, a, b)
+    a, b = scatter(x_axis, rows_split(a, nx)), scatter(y_axis, rows_split(b, ny))
+    a, b = a + zero, b + zero
+    zero = final_parts(3 * parts // 4, a, b)
+    a, b = scatter(y_axis, rows_split(a, ny)), scatter(x_axis, rows_split(b, nx))
+    both = jnp.concatenate([a, b], 1) + zero
+    final_parts(parts, both)
+    moe_out = scatter(z_axis, rows_split(both, nz))
     return attn_out, moe_out
 
 

time: 121 us -> 134 us (1.11)
  other arithmetic: 6.48 us -> 15.3 us
  waiting for transfers between devices: 29 us -> 20.7 us
  local copies, waits for them, and re-layouts: 3.76 us -> 7.85 us
  starting transfers between devices: 36.5 us -> 39.3 us
  Pallas kernels: 43.5 us -> 46.2 us
  between operations: 1.04 us -> 3.72 us
    ppermute x20, waiting for transfers between devices: 29 us -> 18.3 us  [send(): return lax.ppermute(a, self.name, self.turn(k))]
    unnamed x12 -> x37, local copies, waits for them, and re-layouts: 0.03 us -> 5.35 us
    convert_element_type x7 -> x5, other arithmetic: 1.38 us -> 5.04 us  [total(): return s.astype(BF16)]
    add x0 -> x4, other arithmetic: none -> 3.02 us  [the longest x2 1.53 us: on_device(): a, b = (a + zero, b + zero)]
    ppermute x20, starting transfers between devices: 30.8 us -> 33.4 us  [send(): return lax.ppermute(a, self.name, self.turn(k))]
    pallas_call x1 -> x4, Pallas kernels: 12.9 us -> 15.5 us  [local_pass(): pl.pallas_call(functools.partial(local_kernel, heads, group, base), grid=...]
    ppermute x3, waiting for transfers between devices: 0.01 us -> 2.45 us  [carry_scan(): lax.ppermute(out, z_axis.name, z_axis.hop(i)).astype(F32)]
    pallas_call x4 -> x6, Pallas kernels: 28.4 us -> 30.1 us  [the longest x1 12.9 us: fitting_experts(): pl.pallas_call(functools.partial(lead_kernel, experts, nx, ny, block, dep...]
  transfers between devices with their start and end apart: 23 -> 23, of which waited for: 9 -> 6; matrix products, arithmetic and copies ran while one was open for 6% -> 10% of each run, Pallas kernels for 36% -> 29%
where the time goes in v2:
time: 134 us; the launch traced here: 133 us
  Pallas kernels  46.2 us (34%)
  starting transfers between devices  39.3 us (29%)
  waiting for transfers between devices  20.7 us (15%)
  other arithmetic  15.3 us (11%)
  local copies, waits for them, and re-layouts  7.85 us (6%)
  between operations  3.72 us (3%)
    ppermute x20, starting transfers between devices, send(): return lax.ppermute(a, self.name, self.turn(k))  33.4 us
    ppermute x20, waiting for transfers between devices, send(): return lax.ppermute(a, self.name, self.turn(k))  18.3 us
    pallas_call x4, Pallas kernels, local_pass(): pl.pallas_call(functools.partial(local_kernel, heads, group, base), grid=...  15.5 us
    pallas_call x1, Pallas kernels, fitting_experts(): pl.pallas_call(functools.partial(lead_kernel, experts, nx, ny, block, dep...  12.9 us
    pallas_call x4, Pallas kernels, final_pass(): pl.pallas_call(functools.partial(final_kernel, heads, group, base), grid=...  12 us
    ppermute x3, starting transfers between devices, carry_scan(): lax.ppermute(out, z_axis.name, z_axis.hop(i)).astype(F32)  5.94 us
    unnamed x37, local copies, waits for them, and re-layouts  5.35 us
    pallas_call x1, Pallas kernels, fitting_experts(): pl.pallas_call(functools.partial(rest_kernel, nx, ny, block, depth), in_s...  5.16 us
  transfers between devices with their start and end apart: 23, of which 6 were waited for; matrix products, arithmetic and copies ran while one was open for 10% of the time, Pallas kernels for 29%

profile of v2, /device:TPU:0, one launch (start us, length us, event | category | flops | bytes accessed | tf_op | source)
XLA Modules:
  0.0 133.2 jit_solution(1474750308801152662)
XLA Ops:
  2.4 5.0 %collective-permute-start.2 = (bf16[8,6272]{1,0:T(8,128)(2,1)S(1)}, bf16[8,6272]{1,0:T(8,128)(2,1)S(1)}, u32[]{:S(2)}, u32[]{:S(2)}) collective-permute-start(bf16[8,6272]{1,0:T(8,128)(2,1)S(1)} %pad_maximum_fusion.7), channel_id=1, source_target_pairs={{0,24},{4,28},{8,0},{12,4},{16,8},{20,12},{24,16},{28,20},{1,25},{... | collective-permute-start | bytes 301064 | tf_op jit(solution)/shard_map/ppermute | solution.py:52
  7.5 1.0 collective-permute-start
  11.3 3.8 %local_pass.5 = (bf16[512,512]{1,0:T(8,128)(2,1)}, bf16[4,128,128]{2,1,0:T(8,128)(2,1)}) custom-call(bf16[3,512,2048]{2,1,0:T(8,128)(2,1)} %bitcast.34, bf16[3,512,2048]{2,1,0:T(8,128)(2,1)} %bitcast.35, bf16[3,512,2048]{2,1,0:T(8,128)(2,1)} %bitcast.36, f32[16,512]{1,0:T(8,128)} %copy-done.1, f32[512,128]{1,0:T(8,128)} %copy-done), custom_call_target="tpu_custom_call" | custom-call | flops 536870912 | bytes 2097152 | tf_op jit(solution)/shard_map/local_pass/pallas_call | solution.py:168
  15.1 3.9 %local_pass.6 = (bf16[512,512]{1,0:T(8,128)(2,1)}, bf16[4,128,128]{2,1,0:T(8,128)(2,1)}) custom-call(bf16[3,512,2048]{2,1,0:T(8,128)(2,1)} %bitcast.37, bf16[3,512,2048]{2,1,0:T(8,128)(2,1)} %bitcast.38, bf16[3,512,2048]{2,1,0:T(8,128)(2,1)} %bitcast.39, f32[16,512]{1,0:T(8,128)} %copy-done.1, f32[512,128]{1,0:T(8,128)} %copy-done), custom_call_target="tpu_custom_call" | custom-call | flops 536870912 | bytes 2097152 | tf_op jit(solution)/shard_map/local_pass/pallas_call | solution.py:168
  20.8 3.9 %local_pass.4 = (bf16[512,512]{1,0:T(8,128)(2,1)}, bf16[4,128,128]{2,1,0:T(8,128)(2,1)}) custom-call(bf16[3,512,2048]{2,1,0:T(8,128)(2,1)} %bitcast.40, bf16[3,512,2048]{2,1,0:T(8,128)(2,1)} %bitcast.41, bf16[3,512,2048]{2,1,0:T(8,128)(2,1)} %bitcast.42, f32[16,512]{1,0:T(8,128)} %copy-done.1, f32[512,128]{1,0:T(8,128)} %copy-done, ...), custom_call_target="tpu_custom_call" | custom-call | flops 536870912 | bytes 2097152 | tf_op jit(solution)/shard_map/local_pass/pallas_call | solution.py:168
  24.7 3.9 %local_pass.7 = (bf16[512,512]{1,0:T(8,128)(2,1)}, bf16[4,128,128]{2,1,0:T(8,128)(2,1)}) custom-call(bf16[3,512,2048]{2,1,0:T(8,128)(2,1)} %bitcast.43, bf16[3,512,2048]{2,1,0:T(8,128)(2,1)} %bitcast.44, bf16[3,512,2048]{2,1,0:T(8,128)(2,1)} %bitcast.45, f32[16,512]{1,0:T(8,128)} %copy-done.1, f32[512,128]{1,0:T(8,128)} %copy-done, ...), custom_call_target="tpu_custom_call" | custom-call | flops 536870912 | bytes 2097152 | tf_op jit(solution)/shard_map/local_pass/pallas_call | solution.py:168
  28.6 1.5 %collective-permute-start.4 = (bf16[32,3200]{1,0:T(8,128)(2,1)S(1)}, bf16[32,3200]{1,0:T(8,128)(2,1)S(1)}, u32[]{:S(2)}, u32[]{:S(2)}) collective-permute-start(bf16[32,3200]{1,0:T(8,128)(2,1)S(1)} %slice.92), channel_id=1, source_target_pairs={{0,2},{1,3},{2,0},{3,1},{4,6},{5,7},{6,4},{7,5},{8,10},{9,11},{10,... | collective-permute-start | bytes 614408 | tf_op jit(solution)/shard_map/ppermute | solution.py:52
  30.1 1.5 %collective-permute-start.3 = (bf16[32,3072]{1,0:T(8,128)(2,1)S(1)}, bf16[32,3072]{1,0:T(8,128)(2,1)S(1)}, u32[]{:S(2)}, u32[]{:S(2)}) collective-permute-start(bf16[32,3072]{1,0:T(8,128)(2,1)S(1)} %slice.90), channel_id=1, source_target_pairs={{0,4},{4,0},{8,12},{12,8},{16,20},{20,16},{24,28},{28,24},{1,5},{5... | collective-permute-start | bytes 589832 | tf_op jit(solution)/shard_map/ppermute | solution.py:52
  32.6 3.1 %collective-permute-done.3 = bf16[32,3072]{1,0:T(8,128)(2,1)S(1)} collective-permute-done((bf16[32,3072]{1,0:T(8,128)(2,1)S(1)}, bf16[32,3072]{1,0:T(8,128)(2,1)S(1)}, u32[]{:S(2)}, u32[]{:S(2)}) %collective-permute-start.3) | collective-permute-done | bytes 196640 | tf_op jit(solution)/shard_map/ppermute | solution.py:52
  41.0 1.6 %collective-permute-start.5 = (bf16[1040,128]{1,0:T(8,128)(2,1)S(1)}, bf16[1040,128]{1,0:T(8,128)(2,1)S(1)}, u32[]{:S(2)}, u32[]{:S(2)}) collective-permute-start(bf16[1040,128]{1,0:T(8,128)(2,1)S(1)} %pad_maximum_fusion.6), channel_id=1, source_target_pairs={{0,4},{4,0},{8,12},{12,8},{16,20},{20,16},{24,28},{28,24},{1,5},{5... | collective-permute-start | bytes 798728 | tf_op jit(solution)/shard_map/ppermute | solution.py:52
  43.3 7.2 %collective-permute-done.5 = bf16[1040,128]{1,0:T(8,128)(2,1)S(1)} collective-permute-done((bf16[1040,128]{1,0:T(8,128)(2,1)S(1)}, bf16[1040,128]{1,0:T(8,128)(2,1)S(1)}, u32[]{:S(2)}, u32[]{:S(2)}) %collective-permute-start.5) | collective-permute-done | bytes 266272 | tf_op jit(solution)/shard_map/ppermute | solution.py:52
  50.7 4.4 %collective-permute-start.6 = (bf16[8,128,128]{2,1,0:T(8,128)(2,1)S(1)}, bf16[8,128,128]{2,1,0:T(8,128)(2,1)S(1)}, u32[]{:S(2)}, u32[]{:S(2)}) collective-permute-start(bf16[8,128,128]{2,1,0:T(8,128)(2,1)S(1)} %add_convert_fusion.5), channel_id=1, source_target_pairs={{0,8},{4,12},{1,9},{5,13},{2,10},{6,14},{3,11},{7,15}} | collective-permute-start | bytes 786440 | tf_op jit(solution)/shard_map/ppermute | solution.py:288
  56.5 2.4 %collective-permute-done.6 = bf16[8,128,128]{2,1,0:T(8,128)(2,1)S(1)} collective-permute-done((bf16[8,128,128]{2,1,0:T(8,128)(2,1)S(1)}, bf16[8,128,128]{2,1,0:T(8,128)(2,1)S(1)}, u32[]{:S(2)}, u32[]{:S(2)}) %collective-permute-start.6) | collective-permute-done | bytes 262176 | tf_op jit(solution)/shard_map/ppermute | solution.py:288
  61.0 12.9 %lead_pass.1 = (bf16[128,3072]{1,0:T(8,128)(2,1)S(1)}, bf16[128,3072]{1,0:T(8,128)(2,1)S(1)}, bf16[256,576]{1,0:T(8,128)(2,1)S(1)}, f32[256,128]{1,0:T(8,128)S(1)}) custom-call(bf16[128,3072]{1,0:T(8,128)(2,1)S(1)} %pad_maximum_fusion.1.a, bf16[128,3072]{1,0:T(8,128)(2,1)S(1)} %collective-permute-done.11.a2, bf16[128,3200]{1,0:T(8,128)(2,1)S(1)} %pad_maximum_fusion.b, ...), custom_call_target="tpu_custom_call" | custom-call | flops 4529848320 | bytes 22413312 | tf_op jit(solution)/shard_map/lead_pass/pallas_call | solution.py:483
  75.3 5.2 %rest_pass.1 = (bf16[128,3072]{1,0:T(8,128)(2,1)}, bf16[128,3072]{1,0:T(8,128)(2,1)}) custom-call(bf16[256,576]{1,0:T(8,128)(2,1)} %copy-done.2, f32[256,128]{1,0:T(8,128)} %copy-done.3, bf16[576,6144]{1,0:T(8,128)(2,1)} %bitcast.51), custom_call_target="tpu_custom_call" | custom-call | flops 905969664 | bytes 5111808 | tf_op jit(solution)/shard_map/rest_pass/pallas_call | solution.py:507
  80.6 1.3 fusion.8
  81.9 1.5 %collective-permute-start.9 = (bf16[8,128,128]{2,1,0:T(8,128)(2,1)}, bf16[8,128,128]{2,1,0:T(8,128)(2,1)S(1)}, u32[]{:S(2)}, u32[]{:S(2)}) collective-permute-start(bf16[8,128,128]{2,1,0:T(8,128)(2,1)} %get-tuple-element.50), channel_id=1, source_target_pairs={{0,4},{4,0},{8,12},{12,8},{16,20},{20,16},{24,28},{28,24},{1,5},{5... | collective-permute-start | bytes 786440 | tf_op jit(solution)/shard_map/ppermute | solution.py:52
  83.6 7.2 %collective-permute-done.9 = bf16[8,128,128]{2,1,0:T(8,128)(2,1)S(1)} collective-permute-done((bf16[8,128,128]{2,1,0:T(8,128)(2,1)}, bf16[8,128,128]{2,1,0:T(8,128)(2,1)S(1)}, u32[]{:S(2)}, u32[]{:S(2)}) %collective-permute-start.9) | collective-permute-done | bytes 262176 | tf_op jit(solution)/shard_map/ppermute | solution.py:52
  91.9 1.3 add_convert_fusion.refs_6_.refs_7_
  93.2 1.6 %collective-permute-start.17 = (bf16[64,3072]{1,0:T(8,128)(2,1)S(1)}, bf16[64,3072]{1,0:T(8,128)(2,1)S(1)}, u32[]{:S(2)}, u32[]{:S(2)}) collective-permute-start(bf16[64,3072]{1,0:T(8,128)(2,1)S(1)} %slice.99), channel_id=1, source_target_pairs={{0,4},{4,0},{8,12},{12,8},{16,20},{20,16},{24,28},{28,24},{1,5},{5... | collective-permute-start | bytes 1179656 | tf_op jit(solution)/shard_map/ppermute | solution.py:52
  95.1 1.5 %collective-permute-start.16 = (bf16[64,3072]{1,0:T(8,128)(2,1)S(1)}, bf16[64,3072]{1,0:T(8,128)(2,1)S(1)}, u32[]{:S(2)}, u32[]{:S(2)}) collective-permute-start(bf16[64,3072]{1,0:T(8,128)(2,1)S(1)} %slice.97), channel_id=1, source_target_pairs={{0,2},{1,3},{2,0},{3,1},{4,6},{5,7},{6,4},{7,5},{8,10},{9,11},{10,... | collective-permute-start | bytes 1179656 | tf_op jit(solution)/shard_map/ppermute | solution.py:52
  96.6 2.9 %final_pass.4 = (bf16[512,2048]{1,0:T(8,128)(2,1)}, f32[8,128]{1,0:T(8,128)}) custom-call(bf16[3,512,2048]{2,1,0:T(8,128)(2,1)} %bitcast.46, bf16[512,512]{1,0:T(8,128)(2,1)} %get-tuple-element.33.refs_1_, f32[512,128]{1,0:T(8,128)} %copy-done, bf16[16,128,128]{2,1,0:T(8,128)(2,1)} %pad_maximum_fusion.2.refs_3_, f32[1,2048]{1,0:T(1,128)} %bitcast.59, ...), custom_call_target="tpu_custom_call" | custom-call | flops 67108864 | bytes 1572864 | tf_op jit(solution)/shard_map/final_pass/pallas_call | solution.py:228
  99.6 3.1 %final_pass.5 = (bf16[512,2048]{1,0:T(8,128)(2,1)}, f32[8,128]{1,0:T(8,128)}) custom-call(bf16[3,512,2048]{2,1,0:T(8,128)(2,1)} %bitcast.47, bf16[512,512]{1,0:T(8,128)(2,1)} %get-tuple-element.32.refs_1_, f32[512,128]{1,0:T(8,128)} %copy-done, bf16[16,128,128]{2,1,0:T(8,128)(2,1)} %pad_maximum_fusion.2.refs_3_, ...), custom_call_target="tpu_custom_call", output_to_operand_aliasing={{0}: (5, {})} | custom-call | flops 67108864 | bytes 1572864 | tf_op jit(solution)/shard_map/final_pass/pallas_call | solution.py:228
  104.8 1.6 %collective-permute-start.19 = (bf16[32,3072]{1,0:T(8,128)(2,1)S(1)}, bf16[32,3072]{1,0:T(8,128)(2,1)S(1)}, u32[]{:S(2)}, u32[]{:S(2)}) collective-permute-start(bf16[32,3072]{1,0:T(8,128)(2,1)S(1)} %slice.103), channel_id=1, source_target_pairs={{0,2},{1,3},{2,0},{3,1},{4,6},{5,7},{6,4},{7,5},{8,10},{9,11},{10,... | collective-permute-start | bytes 589832 | tf_op jit(solution)/shard_map/ppermute | solution.py:52
  107.2 1.6 %collective-permute-start.18 = (bf16[32,3072]{1,0:T(8,128)(2,1)S(1)}, bf16[32,3072]{1,0:T(8,128)(2,1)S(1)}, u32[]{:S(2)}, u32[]{:S(2)}) collective-permute-start(bf16[32,3072]{1,0:T(8,128)(2,1)S(1)} %slice.101), channel_id=1, source_target_pairs={{0,4},{4,0},{8,12},{12,8},{16,20},{20,16},{24,28},{28,24},{1,5},{5... | collective-permute-start | bytes 589832 | tf_op jit(solution)/shard_map/ppermute | solution.py:52
  108.8 3.0 %final_pass.6 = (bf16[512,2048]{1,0:T(8,128)(2,1)}, f32[8,128]{1,0:T(8,128)}) custom-call(bf16[3,512,2048]{2,1,0:T(8,128)(2,1)} %bitcast.48, bf16[512,512]{1,0:T(8,128)(2,1)} %get-tuple-element.31.refs_1_, f32[512,128]{1,0:T(8,128)} %copy-done, bf16[16,128,128]{2,1,0:T(8,128)(2,1)} %pad_maximum_fusion.2.refs_3_, ...), custom_call_target="tpu_custom_call", output_to_operand_aliasing={{0}: (5, {})} | custom-call | flops 67108864 | bytes 1572864 | tf_op jit(solution)/shard_map/final_pass/pallas_call | solution.py:228
  113.9 1.0 add_convert_fusion.7
  115.7 7.4 %collective-permute-start.22 = (bf16[8,6144]{1,0:T(8,128)(2,1)S(1)}, bf16[8,6144]{1,0:T(8,128)(2,1)S(1)}, u32[]{:S(2)}, u32[]{:S(2)}) collective-permute-start(bf16[8,6144]{1,0:T(8,128)(2,1)S(1)} %get-tuple-element.55), channel_id=1, source_target_pairs={{0,8},{4,12},{8,16},{12,20},{16,24},{20,28},{24,0},{28,4},{1,9},{5... | collective-permute-start | bytes 294920 | tf_op jit(solution)/shard_map/ppermute | solution.py:52
  123.1 2.6 %collective-permute-start.21 = (bf16[8,6144]{1,0:T(8,128)(2,1)S(1)}, bf16[8,6144]{1,0:T(8,128)(2,1)S(1)}, u32[]{:S(2)}, u32[]{:S(2)}) collective-permute-start(bf16[8,6144]{1,0:T(8,128)(2,1)S(1)} %get-tuple-element.56), channel_id=1, source_target_pairs={{0,16},{4,20},{8,24},{12,28},{16,0},{20,4},{24,8},{28,12},{1,17},{... | collective-permute-start | bytes 294920 | tf_op jit(solution)/shard_map/ppermute | solution.py:52
  125.7 2.8 %collective-permute-start.20 = (bf16[8,6144]{1,0:T(8,128)(2,1)S(1)}, bf16[8,6144]{1,0:T(8,128)(2,1)S(1)}, u32[]{:S(2)}, u32[]{:S(2)}) collective-permute-start(bf16[8,6144]{1,0:T(8,128)(2,1)S(1)} %get-tuple-element.54), channel_id=1, source_target_pairs={{0,24},{4,28},{8,0},{12,4},{16,8},{20,12},{24,16},{28,20},{1,25},{... | collective-permute-start | bytes 294920 | tf_op jit(solution)/shard_map/ppermute | solution.py:52
  128.6 3.0 %final_pass.7 = (bf16[512,2048]{1,0:T(8,128)(2,1)}, f32[8,128]{1,0:T(8,128)}) custom-call(bf16[3,512,2048]{2,1,0:T(8,128)(2,1)} %bitcast.49, bf16[512,512]{1,0:T(8,128)(2,1)} %get-tuple-element.26.refs_1_, f32[512,128]{1,0:T(8,128)} %copy-done, bf16[16,128,128]{2,1,0:T(8,128)(2,1)} %pad_maximum_fusion.2.refs_3_, ...), custom_call_target="tpu_custom_call", output_to_operand_aliasing={{0}: (5, {})} | custom-call | flops 67108864 | bytes 1572864 | tf_op jit(solution)/shard_map/final_pass/pallas_call | solution.py:228
  131.6 1.6 %add_convert_fusion.8 = bf16[8,6144]{1,0:T(8,128)(2,1)} fusion(bf16[8,6144]{1,0:T(8,128)(2,1)S(1)} %collective-permute-done.22, bf16[8,6144]{1,0:T(8,128)(2,1)S(1)} %collective-permute-done.21, bf16[8,6144]{1,0:T(8,128)(2,1)S(1)} %collective-permute-done.20, bf16[32,6144]{1,0:T(8,128)(2,1)} %copy-done.10), kind=kLoop, calls=%fused_computation.45 | loop fusion | flops 393216 | bytes 491520 | tf_op jit(solution)/shard_map/convert_element_type | solution.py:63
  (111 shorter events, 23.1 us)
Async XLA Ops:
  2.4 17.5 %collective-permute-start.2 = (bf16[8,6272]{1,0:T(8,128)(2,1)S(1)}, bf16[8,6272]{1,0:T(8,128)(2,1)S(1)}, u32[]{:S(2)}, u32[]{:S(2)}) collective-permute-start(bf16[8,6272]{1,0:T(8,128)(2,1)S(1)} %pad_maximum_fusion.7), channel_id=1, source_target_pairs={{0,24},{4,28},{8,0},{12,4},{16,8},{20,12},{24,16},{28,20},{1,25},{... | collective-permute-start | bytes 301064 | tf_op jit(solution)/shard_map/ppermute | solution.py:52
  7.5 12.5 %collective-permute-start.1 = (bf16[8,6272]{1,0:T(8,128)(2,1)S(1)}, bf16[8,6272]{1,0:T(8,128)(2,1)S(1)}, u32[]{:S(2)}, u32[]{:S(2)}) collective-permute-start(bf16[8,6272]{1,0:T(8,128)(2,1)S(1)} %pad_maximum_fusion.7), channel_id=1, source_target_pairs={{0,16},{4,20},{8,24},{12,28},{16,0},{20,4},{24,8},{28,12},{1,17},{... | collective-permute-start | bytes 301064 | tf_op jit(solution)/shard_map/ppermute | solution.py:52
  7.5 12.5 %collective-permute-start = (bf16[8,6272]{1,0:T(8,128)(2,1)S(1)}, bf16[8,6272]{1,0:T(8,128)(2,1)S(1)}, u32[]{:S(2)}, u32[]{:S(2)}) collective-permute-start(bf16[8,6272]{1,0:T(8,128)(2,1)S(1)} %pad_maximum_fusion.7), channel_id=1, source_target_pairs={{0,8},{4,12},{8,16},{12,20},{16,24},{20,28},{24,0},{28,4},{1,9},{5... | collective-permute-start | bytes 301064 | tf_op jit(solution)/shard_map/ppermute | solution.py:52
  15.1 3.9 %copy-start.15 = (bf16[4,128,128]{2,1,0:T(8,128)(2,1)S(1)}, bf16[4,128,128]{2,1,0:T(8,128)(2,1)}, u32[]{:S(2)}) copy-start(bf16[4,128,128]{2,1,0:T(8,128)(2,1)} %get-tuple-element.27) | copy-start | bytes 393220
  15.1 4.9 %copy-start.14 = (bf16[8,6144]{1,0:T(8,128)(2,1)S(1)}, bf16[8,6144]{1,0:T(8,128)(2,1)}, u32[]{:S(2)}) copy-start(bf16[8,6144]{1,0:T(8,128)(2,1)} %param.11) | copy-start | bytes 294916
  20.8 3.9 %copy-start.9 = (bf16[32,6272]{1,0:T(8,128)(2,1)S(1)}, bf16[32,6272]{1,0:T(8,128)(2,1)}, u32[]{:S(2)}) copy-start(bf16[32,6272]{1,0:T(8,128)(2,1)} %pad_maximum_fusion.4.refs_5_) | copy-start | bytes 1204228
  24.7 7.8 %copy-start.16 = (bf16[4,128,128]{2,1,0:T(8,128)(2,1)S(1)}, bf16[4,128,128]{2,1,0:T(8,128)(2,1)}, u32[]{:S(2)}) copy-start(bf16[4,128,128]{2,1,0:T(8,128)(2,1)} %get-tuple-element.30) | copy-start | bytes 393220
  28.6 9.6 %collective-permute-start.4 = (bf16[32,3200]{1,0:T(8,128)(2,1)S(1)}, bf16[32,3200]{1,0:T(8,128)(2,1)S(1)}, u32[]{:S(2)}, u32[]{:S(2)}) collective-permute-start(bf16[32,3200]{1,0:T(8,128)(2,1)S(1)} %slice.92), channel_id=1, source_target_pairs={{0,2},{1,3},{2,0},{3,1},{4,6},{5,7},{6,4},{7,5},{8,10},{9,11},{10,... | collective-permute-start | bytes 614408 | tf_op jit(solution)/shard_map/ppermute | solution.py:52
  30.1 5.7 %collective-permute-start.3 = (bf16[32,3072]{1,0:T(8,128)(2,1)S(1)}, bf16[32,3072]{1,0:T(8,128)(2,1)S(1)}, u32[]{:S(2)}, u32[]{:S(2)}) collective-permute-start(bf16[32,3072]{1,0:T(8,128)(2,1)S(1)} %slice.90), channel_id=1, source_target_pairs={{0,4},{4,0},{8,12},{12,8},{16,20},{20,16},{24,28},{28,24},{1,5},{5... | collective-permute-start | bytes 589832 | tf_op jit(solution)/shard_map/ppermute | solution.py:52
  37.6 18.3 %collective-permute-start.10 = (bf16[64,3072]{1,0:T(8,128)(2,1)S(1)}, bf16[64,3072]{1,0:T(8,128)(2,1)S(1)}, u32[]{:S(2)}, u32[]{:S(2)}) collective-permute-start(bf16[64,3072]{1,0:T(8,128)(2,1)S(1)} %pad_maximum_fusion.5), channel_id=1, source_target_pairs={{0,2},{1,3},{2,0},{3,1},{4,6},{5,7},{6,4},{7,5},{8,10},{9,11},{10,... | collective-permute-start | bytes 1179656 | tf_op jit(solution)/shard_map/ppermute | solution.py:52
  41.0 9.4 %collective-permute-start.5 = (bf16[1040,128]{1,0:T(8,128)(2,1)S(1)}, bf16[1040,128]{1,0:T(8,128)(2,1)S(1)}, u32[]{:S(2)}, u32[]{:S(2)}) collective-permute-start(bf16[1040,128]{1,0:T(8,128)(2,1)S(1)} %pad_maximum_fusion.6), channel_id=1, source_target_pairs={{0,4},{4,0},{8,12},{12,8},{16,20},{20,16},{24,28},{28,24},{1,5},{5... | collective-permute-start | bytes 798728 | tf_op jit(solution)/shard_map/ppermute | solution.py:52
  42.7 13.1 %collective-permute-start.12 = (bf16[64,3200]{1,0:T(8,128)(2,1)S(1)}, bf16[64,3200]{1,0:T(8,128)(2,1)S(1)}, u32[]{:S(2)}, u32[]{:S(2)}) collective-permute-start(bf16[64,3200]{1,0:T(8,128)(2,1)S(1)} %pad_maximum_fusion.3), channel_id=1, source_target_pairs={{0,4},{4,0},{8,12},{12,8},{16,20},{20,16},{24,28},{28,24},{1,5},{5... | collective-permute-start | bytes 1228808 | tf_op jit(solution)/shard_map/ppermute | solution.py:52
  50.7 8.3 %collective-permute-start.6 = (bf16[8,128,128]{2,1,0:T(8,128)(2,1)S(1)}, bf16[8,128,128]{2,1,0:T(8,128)(2,1)S(1)}, u32[]{:S(2)}, u32[]{:S(2)}) collective-permute-start(bf16[8,128,128]{2,1,0:T(8,128)(2,1)S(1)} %add_convert_fusion.5), channel_id=1, source_target_pairs={{0,8},{4,12},{1,9},{5,13},{2,10},{6,14},{3,11},{7,15}} | collective-permute-start | bytes 786440 | tf_op jit(solution)/shard_map/ppermute | solution.py:288
  55.8 5.2 %collective-permute-start.13 = (bf16[128,3200]{1,0:T(8,128)(2,1)S(1)}, bf16[128,3200]{1,0:T(8,128)(2,1)S(1)}, u32[]{:S(2)}, u32[]{:S(2)}) collective-permute-start(bf16[128,3200]{1,0:T(8,128)(2,1)S(1)} %pad_maximum_fusion.b), channel_id=1, source_target_pairs={{0,1},{1,0},{2,3},{3,2},{4,5},{5,4},{6,7},{7,6},{8,9},{9,8},{10,11... | collective-permute-start | bytes 2457608 | tf_op jit(solution)/shard_map/ppermute | solution.py:52
  56.0 5.0 %collective-permute-start.11 = (bf16[128,3072]{1,0:T(8,128)(2,1)S(1)}, bf16[128,3072]{1,0:T(8,128)(2,1)S(1)}, u32[]{:S(2)}, u32[]{:S(2)}) collective-permute-start(bf16[128,3072]{1,0:T(8,128)(2,1)S(1)} %pad_maximum_fusion.1.a), channel_id=1, source_target_pairs={{0,1},{1,0},{2,3},{3,2},{4,5},{5,4},{6,7},{7,6},{8,9},{9,8},{10,11... | collective-permute-start | bytes 2359304 | tf_op jit(solution)/shard_map/ppermute | solution.py:52
  59.2 0.7 collective-permute-start.7
  60.1 20.5 %collective-permute-start.8 = (bf16[8,128,128]{2,1,0:T(8,128)(2,1)S(1)}, bf16[8,128,128]{2,1,0:T(8,128)(2,1)S(1)}, u32[]{:S(2)}, u32[]{:S(2)}) collective-permute-start(bf16[8,128,128]{2,1,0:T(8,128)(2,1)S(1)} %add_convert_fusion.4), channel_id=1, source_target_pairs={{16,24},{20,28},{17,25},{21,29},{18,26},{22,30},{19,27},{23,31}} | collective-permute-start | bytes 786440 | tf_op jit(solution)/shard_map/ppermute | solution.py:288
  80.5 11.4 %collective-permute-start.15 = (bf16[128,3072]{1,0:T(8,128)(2,1)}, bf16[128,3072]{1,0:T(8,128)(2,1)}, u32[]{:S(2)}, u32[]{:S(2)}) collective-permute-start(bf16[128,3072]{1,0:T(8,128)(2,1)} %get-tuple-element.39), channel_id=1, source_target_pairs={{0,1},{1,0},{2,3},{3,2},{4,5},{5,4},{6,7},{7,6},{8,9},{9,8},{10,11... | collective-permute-start | bytes 2359304 | tf_op jit(solution)/shard_map/ppermute | solution.py:52
  81.9 9.9 %copy-start.13 = (bf16[128,3072]{1,0:T(8,128)(2,1)S(1)}, bf16[128,3072]{1,0:T(8,128)(2,1)}, u32[]{:S(2)}) copy-start(bf16[128,3072]{1,0:T(8,128)(2,1)} %get-tuple-element.38) | copy-start | bytes 2359300
  81.9 8.9 %collective-permute-start.9 = (bf16[8,128,128]{2,1,0:T(8,128)(2,1)}, bf16[8,128,128]{2,1,0:T(8,128)(2,1)S(1)}, u32[]{:S(2)}, u32[]{:S(2)}) collective-permute-start(bf16[8,128,128]{2,1,0:T(8,128)(2,1)} %get-tuple-element.50), channel_id=1, source_target_pairs={{0,4},{4,0},{8,12},{12,8},{16,20},{20,16},{24,28},{28,24},{1,5},{5... | collective-permute-start | bytes 786440 | tf_op jit(solution)/shard_map/ppermute | solution.py:52
  83.4 11.4 %collective-permute-start.14 = (bf16[128,3072]{1,0:T(8,128)(2,1)S(1)}, bf16[128,3072]{1,0:T(8,128)(2,1)S(1)}, u32[]{:S(2)}, u32[]{:S(2)}) collective-permute-start(bf16[128,3072]{1,0:T(8,128)(2,1)S(1)} %get-tuple-element.35), channel_id=1, source_target_pairs={{0,1},{1,0},{2,3},{3,2},{4,5},{5,4},{6,7},{7,6},{8,9},{9,8},{10,11... | collective-permute-start | bytes 2359304 | tf_op jit(solution)/shard_map/ppermute | solution.py:52
  93.2 10.8 %collective-permute-start.17 = (bf16[64,3072]{1,0:T(8,128)(2,1)S(1)}, bf16[64,3072]{1,0:T(8,128)(2,1)S(1)}, u32[]{:S(2)}, u32[]{:S(2)}) collective-permute-start(bf16[64,3072]{1,0:T(8,128)(2,1)S(1)} %slice.99), channel_id=1, source_target_pairs={{0,4},{4,0},{8,12},{12,8},{16,20},{20,16},{24,28},{28,24},{1,5},{5... | collective-permute-start | bytes 1179656 | tf_op jit(solution)/shard_map/ppermute | solution.py:52
  95.1 11.3 %collective-permute-start.16 = (bf16[64,3072]{1,0:T(8,128)(2,1)S(1)}, bf16[64,3072]{1,0:T(8,128)(2,1)S(1)}, u32[]{:S(2)}, u32[]{:S(2)}) collective-permute-start(bf16[64,3072]{1,0:T(8,128)(2,1)S(1)} %slice.97), channel_id=1, source_target_pairs={{0,2},{1,3},{2,0},{3,1},{4,6},{5,7},{6,4},{7,5},{8,10},{9,11},{10,... | collective-permute-start | bytes 1179656 | tf_op jit(solution)/shard_map/ppermute | solution.py:52
  99.6 4.5 %copy-start.6 = (bf16[128,3072]{1,0:T(8,128)(2,1)S(1)}, bf16[128,3072]{1,0:T(8,128)(2,1)}, u32[]{:S(2)}) copy-start(bf16[128,3072]{1,0:T(8,128)(2,1)} %copy-done.5) | copy-start | bytes 2359300
  102.6 3.8 %copy-start.8 = (bf16[128,3072]{1,0:T(8,128)(2,1)S(1)}, bf16[128,3072]{1,0:T(8,128)(2,1)}, u32[]{:S(2)}) copy-start(bf16[128,3072]{1,0:T(8,128)(2,1)} %copy-done.7) | copy-start | bytes 2359300
  104.8 4.0 %copy-start.11 = (bf16[64,3072]{1,0:T(8,128)(2,1)}, bf16[64,3072]{1,0:T(8,128)(2,1)S(1)}, u32[]{:S(2)}) copy-start(bf16[64,3072]{1,0:T(8,128)(2,1)S(1)} %fusion.10.refs_7_) | copy-start | bytes 1179652
  104.8 8.1 %collective-permute-start.19 = (bf16[32,3072]{1,0:T(8,128)(2,1)S(1)}, bf16[32,3072]{1,0:T(8,128)(2,1)S(1)}, u32[]{:S(2)}, u32[]{:S(2)}) collective-permute-start(bf16[32,3072]{1,0:T(8,128)(2,1)S(1)} %slice.103), channel_id=1, source_target_pairs={{0,2},{1,3},{2,0},{3,1},{4,6},{5,7},{6,4},{7,5},{8,10},{9,11},{10,... | collective-permute-start | bytes 589832 | tf_op jit(solution)/shard_map/ppermute | solution.py:52
  107.2 6.8 %collective-permute-start.18 = (bf16[32,3072]{1,0:T(8,128)(2,1)S(1)}, bf16[32,3072]{1,0:T(8,128)(2,1)S(1)}, u32[]{:S(2)}, u32[]{:S(2)}) collective-permute-start(bf16[32,3072]{1,0:T(8,128)(2,1)S(1)} %slice.101), channel_id=1, source_target_pairs={{0,4},{4,0},{8,12},{12,8},{16,20},{20,16},{24,28},{28,24},{1,5},{5... | collective-permute-start | bytes 589832 | tf_op jit(solution)/shard_map/ppermute | solution.py:52
  115.6 12.9 %copy-start.10 = (bf16[32,6144]{1,0:T(8,128)(2,1)}, bf16[32,6144]{1,0:T(8,128)(2,1)S(1)}, u32[]{:S(2)}) copy-start(bf16[32,6144]{1,0:T(8,128)(2,1)S(1)} %maximum_add_fusion.refs_6_) | copy-start | bytes 1179652
  115.7 15.9 %collective-permute-start.22 = (bf16[8,6144]{1,0:T(8,128)(2,1)S(1)}, bf16[8,6144]{1,0:T(8,128)(2,1)S(1)}, u32[]{:S(2)}, u32[]{:S(2)}) collective-permute-start(bf16[8,6144]{1,0:T(8,128)(2,1)S(1)} %get-tuple-element.55), channel_id=1, source_target_pairs={{0,8},{4,12},{8,16},{12,20},{16,24},{20,28},{24,0},{28,4},{1,9},{5... | collective-permute-start | bytes 294920 | tf_op jit(solution)/shard_map/ppermute | solution.py:52
  123.1 8.5 %collective-permute-start.21 = (bf16[8,6144]{1,0:T(8,128)(2,1)S(1)}, bf16[8,6144]{1,0:T(8,128)(2,1)S(1)}, u32[]{:S(2)}, u32[]{:S(2)}) collective-permute-start(bf16[8,6144]{1,0:T(8,128)(2,1)S(1)} %get-tuple-element.56), channel_id=1, source_target_pairs={{0,16},{4,20},{8,24},{12,28},{16,0},{20,4},{24,8},{28,12},{1,17},{... | collective-permute-start | bytes 294920 | tf_op jit(solution)/shard_map/ppermute | solution.py:52
  125.7 5.8 %collective-permute-start.20 = (bf16[8,6144]{1,0:T(8,128)(2,1)S(1)}, bf16[8,6144]{1,0:T(8,128)(2,1)S(1)}, u32[]{:S(2)}, u32[]{:S(2)}) collective-permute-start(bf16[8,6144]{1,0:T(8,128)(2,1)S(1)} %get-tuple-element.54), channel_id=1, source_target_pairs={{0,24},{4,28},{8,0},{12,4},{16,8},{20,12},{24,16},{28,20},{1,25},{... | collective-permute-start | bytes 294920 | tf_op jit(solution)/shard_map/ppermute | solution.py:52
  (8 other events, 8.6 us)

commit v3 on v1

--- a/solution.py
+++ b/solution.py
@@ -7,7 +7,8 @@
 from jax.sharding import PartitionSpec as P
 
 EPS = 1e-06
-CHUNK = 128
+CHUNK = 256
+PARTS = 2
 PIECES = 3
 F32 = jnp.float32
 BF16 = jnp.bfloat16
@@ -80,11 +81,12 @@
     return out
 
 
-def params(limit=56):
+def params(limit=16):
     return pltpu.CompilerParams(vmem_limit_bytes=limit * 2**20)
 
 
-def prep_kernel(heads, rows, d_ref, run_ref, cols_ref):
+def prep_kernel(heads, rows, d_ref, run_ref, cols_ref, seat_ref):
+    seat_ref[...] = jnp.zeros_like(seat_ref) + lax.axis_index("seq")
     run = d_ref[...]
     lane = lax.broadcasted_iota(jnp.int32, (heads, rows), 1)
     step = 1
@@ -114,13 +116,21 @@
         out_shape=(
             jax.ShapeDtypeStruct((heads, rows), F32),
             jax.ShapeDtypeStruct((rows, 128), F32),
+            jax.ShapeDtypeStruct((heads, 128), jnp.int32),
         ),
         compiler_params=params(),
         name="prepare",
     )(log_decay.T)
 
 
-def local_kernel(heads, group, base, q_ref, k_ref, v_ref, run_ref, cols_ref, mixed_ref, state_ref):
+def local_kernel(heads, group, base, loads, which, *refs):
+    q_ref, k_ref, v_ref, run_ref, cols_ref = refs[:5]
+    mixed_ref, state_ref, mark_ref = refs[-3 - 2 * loads :][:3]
+    if loads:
+        w_ref, held_ref, sem = refs[5], refs[-2], refs[-1]
+        copy = pltpu.make_async_copy(w_ref.at[which], held_ref, sem)
+        pl.when(pl.program_id(0) == 0)(copy.start)
+    mark_ref[...] = jnp.zeros_like(mark_ref)
     rows, width = q_ref.shape[1], q_ref.shape[2] // group
     first = base + pl.program_id(0) * group
     cols = pltpu.roll(cols_ref[...], 128 - first, 1)
@@ -152,17 +162,37 @@
                 state = eq[CHUNK - 1 :, :] * state + fresh
             mixed_ref[part, lanes] = out.astype(mixed_ref.dtype)
         state_ref[g] = state.astype(BF16)
-
-
-def local_pass(qkv, run, cols, heads, base, count, group=2):
+    if loads:
+        pl.when(pl.program_id(0) == pl.num_programs(0) - 1)(copy.wait)
+
+
+def local_pass(qkv, run, cols, heads, base, count, w, done, behind, zeros, group=4):
     rows, width = qkv.shape[1], qkv.shape[2] // heads
+    group = min(group, count)
     start = base // group
+    loads = 0 if w is None else 1
+    hbm = pl.BlockSpec(memory_space=pl.ANY)
 
     def take(which):
         return pl.BlockSpec((1, rows, group * width), lambda h: (which, 0, start + h))
 
+    more = ([w] if loads else []) + list(done) + list(behind)
+    aliases = {5 + loads + i: i for i in range(len(done))}
+    out_specs = [
+        pl.BlockSpec((rows, group * width), lambda h: (0, start + h)),
+        pl.BlockSpec((group, width, width), lambda h: (start + h, 0, 0)),
+        pl.BlockSpec((8, zeros), lambda h: (0, 0)),
+    ]
+    out_shape = [
+        jax.ShapeDtypeStruct((rows, heads * width), BF16),
+        jax.ShapeDtypeStruct((heads, width, width), BF16),
+        jax.ShapeDtypeStruct((8, zeros), BF16),
+    ]
+    if loads:
+        out_specs.append(hbm)
+        out_shape.append(pltpu.VMEM(w.shape[1:], w.dtype))
     return pl.pallas_call(
-        functools.partial(local_kernel, heads, group, base),
+        functools.partial(local_kernel, heads, group, base, loads, base // count),
         grid=(count // group,),
         in_specs=[
             take(0),
@@ -170,42 +200,40 @@
             take(2),
             pl.BlockSpec(run.shape, lambda h: (0, 0)),
             pl.BlockSpec(cols.shape, lambda h: (0, 0)),
-        ],
-        out_specs=(
-            pl.BlockSpec((rows, group * width), lambda h: (0, h)),
-            pl.BlockSpec((group, width, width), lambda h: (h, 0, 0)),
-        ),
-        out_shape=(
-            jax.ShapeDtypeStruct((rows, count * width), F32),
-            jax.ShapeDtypeStruct((count, width, width), BF16),
-        ),
-        compiler_params=params(),
+        ]
+        + [hbm] * len(more),
+        out_specs=out_specs,
+        out_shape=out_shape,
+        scratch_shapes=[pltpu.SemaphoreType.DMA] * loads,
+        input_output_aliases=aliases,
+        compiler_params=params(20),
         cost_estimate=pl.CostEstimate(
             flops=8 * count * rows * width * CHUNK,
-            bytes_accessed=count * rows * width * 10,
+            bytes_accessed=count * rows * width * 8,
             transcendentals=count * rows * CHUNK,
         ),
         name="local_pass",
-    )(qkv, qkv, qkv, run, cols)
-
-
-def final_kernel(heads, group, base, q_ref, mixed_ref, cols_ref, carried_ref, gain_ref, out_ref):
+    )(qkv, qkv, qkv, run, cols, *more)
+
+
+def final_kernel(heads, group, q_ref, mixed_ref, cols_ref, carried_ref, gain_ref, out_ref):
     width = q_ref.shape[2] // group
-    first = base + pl.program_id(0) * group
+    first = pl.program_id(0) * group
     cols = pltpu.roll(cols_ref[...], 128 - first, 1)
     for g in range(group):
         lanes = slice(g * width, (g + 1) * width)
         er = cols[:, 3 * heads + g : 3 * heads + g + 1]
         far = lax.dot_general(q_ref[0, :, lanes], carried_ref[g], NN, preferred_element_type=F32)
-        mixed = mixed_ref[:, lanes] + er * far
+        mixed = mixed_ref[:, lanes].astype(F32) + er * far
         mean = jnp.mean(mixed * mixed, axis=-1, keepdims=True)
         out_ref[:, lanes] = (mixed * lax.rsqrt(mean + EPS) * gain_ref[:, lanes]).astype(BF16)
 
 
-def final_pass(qkv, mixed, cols, carried, gain, heads, group=2):
+def final_pass(qkv, mixed, cols, carried, gain, heads, group=4):
     rows, width = qkv.shape[1], qkv.shape[2] // heads
+    group = min(group, heads)
     return pl.pallas_call(
-        functools.partial(final_kernel, heads, group, 0),
+        functools.partial(final_kernel, heads, group),
         grid=(heads // group,),
         in_specs=[
             pl.BlockSpec((1, rows, group * width), lambda h: (0, 0, h)),
@@ -216,37 +244,45 @@
         ],
         out_specs=pl.BlockSpec((rows, group * width), lambda h: (0, h)),
         out_shape=jax.ShapeDtypeStruct((rows, heads * width), BF16),
-        compiler_params=params(),
+        compiler_params=params(20),
         cost_estimate=pl.CostEstimate(
             flops=2 * heads * rows * width * width,
-            bytes_accessed=heads * rows * width * 8,
+            bytes_accessed=heads * rows * width * 6,
             transcendentals=0,
         ),
         name="final_pass",
     )(qkv, mixed, cols, carried, gain)
 
 
-def carry_scan(state, last, z_axis, y_axis):
+def pick(parts, at):
+    out = parts[0]
+    for p in range(1, len(parts)):
+        out = jnp.where((at == p).reshape((-1,) + (1,) * (out.ndim - 1)), parts[p], out)
+    return out
+
+
+def carry_scan(state, last, seat, z_axis, y_axis):
     heads, width = state.shape[0], state.shape[1]
-    ny, y = y_axis.n, y_axis.index()
+    ny = y_axis.n
     share = heads // ny
     pad = 16
+    y = seat[:share]
+    turned = [(y + k) & (ny - 1) for k in range(ny)]
+    fade = jnp.exp(last)
 
     def packed(k):
-        at = ((y + k) % ny) * share
-        body = lax.dynamic_slice_in_dim(state, at, share, 0).reshape(share * width, width)
-        fade = jnp.exp(lax.dynamic_slice_in_dim(last, at, share, 0))
-        rows = jnp.stack(pieces_of(fade), 0)
+        body = pick(rows_split(state, ny), turned[k]).reshape(share * width, width)
+        rows = jnp.stack(pieces_of(pick(rows_split(fade, ny), turned[k])), 0)
         rows = jnp.pad(rows, ((0, pad - PIECES), (0, width - share)))
         return jnp.concatenate([body, rows.astype(BF16)], 0)
 
     got = [packed(0)] + [y_axis.send(packed(k), k) for k in range(1, ny)]
     states = [g[: share * width].reshape(share, width, width).astype(F32) for g in got]
     fades = [jnp.sum(g[share * width :, :share].astype(F32), 0) for g in got]
-    places = [(y - k) % ny for k in range(ny)]
+    places = [turned[-k % ny] for k in range(ny)]
 
     def reach(k, end):
-        r = jnp.where(places[k] < end, 1.0, 0.0) * jnp.ones((share,), F32)
+        r = jnp.where(places[k] < end, jnp.ones((share,), F32), 0.0)
         for m in range(ny):
             if m != k:
                 r = r * jnp.where((places[m] > places[k]) & (places[m] < end), fades[m], 1.0)
@@ -263,18 +299,19 @@
     carried = jnp.zeros((share, width, width), F32)
     for i in range(z_axis.n - 1):
         out = (through * carried + inner).astype(BF16)
-        carried = carried + lax.ppermute(out, z_axis.name, z_axis.hop(i)).astype(F32)
+        tie = yield out
+        carried = carried + lax.ppermute(out, z_axis.name, z_axis.hop(i)).astype(F32) + tie[:, None]
 
     def entering(j):
-        end = (y + j) % ny
+        end = turned[j]
         return (
             whole(end) * carried + sum(reach(k, end) * states[k] for k in range(ny))
         ).astype(BF16)
 
+    tie = yield
     back = [entering(0)] + [y_axis.send(entering(j), j) for j in range(1, ny)]
-    both = jnp.stack(back, 0)
-    order = [(y - p) % ny for p in range(ny)]
-    return jnp.concatenate([lax.dynamic_index_in_dim(both, o, 0, False) for o in order], 0)
+    back[0] = back[0] + tie.astype(BF16)[:, None]
+    yield jnp.concatenate([pick(back, places[p]) for p in range(ny)], 0)
 
 
 def hidden_kernel(steps, split, *refs):
@@ -316,7 +353,7 @@
         out_specs=pl.BlockSpec((tokens, units), lambda s: (0, 0)),
         out_shape=jax.ShapeDtypeStruct((tokens, units), BF16),
         scratch_shapes=[pltpu.VMEM((units, tokens), F32), pltpu.VMEM((units, tokens), F32)],
-        compiler_params=params(),
+        compiler_params=params(56),
         cost_estimate=pl.CostEstimate(
             flops=4 * units * wide * tokens,
             bytes_accessed=4 * units * wide + 2 * tokens * wide,
@@ -351,7 +388,7 @@
         ],
         out_specs=(spec, spec),
         out_shape=(out, out),
-        compiler_params=params(),
+        compiler_params=params(56),
         cost_estimate=pl.CostEstimate(
             flops=2 * units * width * tokens,
             bytes_accessed=2 * units * width + 2 * tokens * width,
@@ -361,50 +398,220 @@
     )(h, w_out, *probs)
 
 
-def experts_layer(tokens, ids, probs, w_in, w_out, axes):
-    x_axis, core, z_axis, y_axis = axes
-    count, wide = tokens.shape
-    experts = w_in.shape[0] * lax.axis_size("exp")
-    units = w_in.shape[3]
+def ordered(ref, lanes, outer, inner):
+    m = ref.shape[0] // (outer * inner)
+    blocks = [(i * outer + o) * m for o in range(outer) for i in range(inner)]
+    return jnp.concatenate([ref[at : at + m, lanes] for at in blocks], 0)
+
+
+def store_ordered(ref, lanes, value, outer, inner):
+    m = ref.shape[0] // (outer * inner)
+    for o in range(outer):
+        for i in range(inner):
+            src, dst = (o * inner + i) * m, (i * outer + o) * m
+            ref[dst : dst + m, lanes] = value[src : src + m]
+
+
+def own_weights(ref, lanes, experts, outer, inner):
+    r = ordered(ref, lanes, outer, inner).astype(F32)
+    lane = lax.broadcasted_iota(jnp.int32, r.shape, 1)
+    mine = (lane % experts == lax.axis_index("exp")) & (lane < PIECES * experts)
+    return jnp.sum(jnp.where(mine, r, 0.0), axis=1, keepdims=True)
+
+
+def chunks(w, scratch, sems, start, width, block, first):
+    out = []
+    for j, at in enumerate(range(0, width, block)):
+        src = w.at[(slice(None),) * (len(w.shape) - 1) + (pl.ds(start + at, block),)]
+        out.append(pltpu.make_async_copy(src, scratch.at[j], sems.at[first + j]))
+    return out
+
+
+def lead_kernel(experts, nx, ny, block, a, a2, b, b2, wg, wu, w_out, o, o2, h, flow, mark, rest, acc, wo, sems):
+    units, wide = wg.shape
     half = wide // 2
+    rows = a.shape[0]
+    copies = chunks(w_out, wo, sems, 0, half, block, 0)
+    copies.append(
+        pltpu.make_async_copy(w_out.at[:, pl.ds(half, half)], rest, sems.at[len(copies)])
+    )
+    for c in copies:
+        c.start()
+    mark[...] = jnp.zeros_like(mark)
+    lanes = slice(half, half + 128)
+    flow[:rows] = jnp.broadcast_to(own_weights(b, lanes, experts, nx, ny), (rows, 128))
+    flow[rows:] = jnp.broadcast_to(own_weights(b2, lanes, experts, nx, ny), (rows, 128))
+    for at in range(0, wide, block):
+        if at < half:
+            x = jnp.concatenate([a[:, at : at + block], a2[:, at : at + block]], 0)
+        else:
+            lanes = slice(at - half, at - half + block)
+            x = jnp.concatenate([ordered(b, lanes, nx, ny), ordered(b2, lanes, nx, ny)], 0)
+        for i, w in enumerate((wg, wu)):
+            d = lax.dot_general(w[:, at : at + block], x, NT, preferred_element_type=F32)
+            if at == 0:
+                acc[i] = d
+            else:
+                acc[i] += d
+    g = acc[0]
+    h[...] = (g / (1.0 + jnp.exp(-g)) * acc[1]).T.astype(BF16)
+    for j, at in enumerate(range(0, half, block)):
+        copies[j].wait()
+        lanes = slice(at, at + block)
+        d = lax.dot_general(h[...], wo[j], NN, preferred_element_type=F32)
+        d = (d * flow[:, :1]).astype(BF16)
+        o[:, lanes] = d[:rows]
+        o2[:, lanes] = d[rows:]
+    copies[-1].wait()
+
+
+def rest_kernel(nx, ny, block, h, flow, w, behind, o, o2):
+    rows = o.shape[0]
+    for at in range(0, w.shape[1], block):
+        lanes = slice(at, at + block)
+        d = lax.dot_general(h[...], w[:, lanes], NN, preferred_element_type=F32)
+        d = (d * flow[:, :1]).astype(BF16)
+        store_ordered(o, lanes, d[:rows], nx, ny)
+        store_ordered(o2, lanes, d[rows:], nx, ny)
+
+
+def lead_pass(a, a2, b, b2, held, w_out, experts, nx, ny, zeros, block=1024):
+    units, wide = held[0].shape
+    tokens = 2 * a.shape[0]
+    n_out = wide // 2 // block
+    vmem = pl.BlockSpec(memory_space=pltpu.VMEM)
+    hbm = pl.BlockSpec(memory_space=pl.ANY)
+    half = pltpu.VMEM((tokens // 2, wide // 2), BF16)
+    mark = jax.ShapeDtypeStruct(zeros, F32)
+    o, o2, h, flow, mark0, rest = pl.pallas_call(
+        functools.partial(lead_kernel, experts, nx, ny, block),
+        in_specs=[vmem] * 6 + [hbm],
+        out_specs=(vmem,) * 6,
+        out_shape=(
+            half,
+            half,
+            pltpu.VMEM((tokens, units), BF16),
+            pltpu.VMEM((tokens, 128), F32),
+            mark,
+            pltpu.VMEM((units, wide // 2), BF16),
+        ),
+        scratch_shapes=[
+            pltpu.VMEM((2, units, tokens), F32),
+            pltpu.VMEM((n_out, units, block), BF16),
+            pltpu.SemaphoreType.DMA((n_out + 1,)),
+        ],
+        compiler_params=params(20),
+        cost_estimate=pl.CostEstimate(
+            flops=5 * units * wide * tokens,
+            bytes_accessed=5 * units * wide + 3 * tokens * wide,
+            transcendentals=units * tokens,
+        ),
+        name="lead_pass",
+    )(a, a2, b, b2, *held, w_out)
+    return (o, o2), (h, flow, rest), mark0
+
+
+def rest_pass(h, flow, w, behind, nx, ny, block=1024):
+    tokens, units = h.shape
+    vmem = pl.BlockSpec(memory_space=pltpu.VMEM)
+    half = pltpu.VMEM((tokens // 2, w.shape[1]), BF16)
+    return pl.pallas_call(
+        functools.partial(rest_kernel, nx, ny, block),
+        in_specs=[vmem] * 3 + [pl.BlockSpec(memory_space=pl.ANY)],
+        out_specs=(vmem,) * 2,
+        out_shape=(half, half),
+        compiler_params=params(20),
+        cost_estimate=pl.CostEstimate(
+            flops=2 * units * w.shape[1] * tokens,
+            bytes_accessed=2 * units * w.shape[1] + 2 * tokens * w.shape[1],
+            transcendentals=0,
+        ),
+        name="rest_pass",
+    )(h, flow, w, behind)
+
+
+def streamed_experts(a, a2, b, b2, w_in, w_out, experts, nx, ny):
+    half = a.shape[1]
+
+    def turned(r, m, n):
+        return r.reshape(m, n, -1, r.shape[1]).transpose(1, 0, 2, 3).reshape(r.shape)
+
+    b, b2 = turned(b, ny, nx), turned(b2, ny, nx)
+
+    def weights_of(rows):
+        r = rows[:, half : half + PIECES * experts].astype(F32).reshape(-1, PIECES, experts)
+        mine = jnp.arange(experts)[None, None] == lax.axis_index("exp")
+        return jnp.sum(jnp.where(mine, r, 0.0), axis=(1, 2))[:, None]
+
+    flow = (weights_of(b), weights_of(b2))
+    h = hidden_pass((a, a2, b, b2), w_in)
+    pa = down_pass(h, w_out, flow, 0, half)
+    pb = down_pass(h, w_out, flow, half, half)
+    return pa, tuple(turned(p, nx, ny) for p in pb)
+
+
+def route_columns(ids, probs, experts):
     named = ids[:, :, None] == jnp.arange(experts, dtype=jnp.int32)[None, None]
     weight = jnp.sum(jnp.where(named, probs[:, :, None], 0.0), axis=1)
     route = jnp.concatenate(pieces_of(weight), 1)
-    route = jnp.pad(route, ((0, 0), (0, 128 - route.shape[1]))).astype(BF16)
-    z = gather(z_axis, jnp.concatenate([tokens, route], 1))
+    return jnp.pad(route, ((0, 0), (0, 128 - route.shape[1]))).astype(BF16)
+
+
+def in_hbm(a):
+    return pltpu.with_memory_space_constraint(a, pltpu.HBM)
+
+
+def nothing(a, rows, lanes):
+    probe = a[-rows:, :lanes].astype(F32)
+    return jnp.where(probe != probe, 1.0, 0.0)
+
+
+def on_device(axes, projected, log_decay, norm_gain, moe_tokens, expert_ids, route_probs, w_in, w_out):
+    x_axis, core, z_axis, y_axis = axes
+    nx, ny, nz = x_axis.n, y_axis.n, z_axis.n
+    heads = log_decay.shape[1]
+    half = moe_tokens.shape[1] // 2
+    experts = w_in.shape[0] * lax.axis_size("exp")
+    tokens = moe_tokens.shape[0] * lax.axis_size("seq") * lax.axis_size("exp")
+    fits = tokens <= 512
+    count = heads // PARTS
+    qkv = in_hbm(projected.transpose(1, 0, 2))
+    w_in = w_in[0].transpose(1, 2, 0)
+    w_out = w_out[0]
+    route = route_columns(expert_ids, route_probs, experts)
+
+    z = gather(z_axis, jnp.concatenate([moe_tokens, route], 1))
+    run, cols, seat = prepare(log_decay)
+    made, held = (), []
+    for i in range(PARTS):
+        w = in_hbm(w_in) if fits else None
+        made = local_pass(qkv, run, cols, heads, i * count, count, w, made[:2], (z,) * (i > 0), z.shape[1] - half)
+        held += made[3:]
+    mixed, state, mark = made[:3]
     a, b = z[:, :half], z[:, half:]
     a, b = gather(y_axis, a), gather(x_axis, b)
-    a, b = gather(x_axis, a), gather(y_axis, b)
-    nx, ny = x_axis.n, y_axis.n
-    b = b.reshape(ny, nx, -1, b.shape[1]).transpose(1, 0, 2, 3).reshape(b.shape)
+    a, b = gather(x_axis, a + mark[:1, :half]), gather(y_axis, b + mark[:1])
+    last = run[:, -1]
+    zeros = (heads // ny, qkv.shape[2] // heads)
     a2, b2 = core.send(a, 1), core.send(b, 1)
-    own = lax.axis_index("exp")
-
-    def weights_of(rows):
-        r = rows[:, half : half + PIECES * experts].astype(F32).reshape(-1, PIECES, experts)
-        mine = jnp.arange(experts)[None, None] == own
-        return jnp.sum(jnp.where(mine, r, 0.0), axis=(1, 2))[:, None]
-
-    flow = (weights_of(b), weights_of(b2))
-    h = hidden_pass((a, a2, b, b2), w_in[0].transpose(1, 2, 0))
-    pa = down_pass(h, w_out[0], flow, 0, half)
-    pb = down_pass(h, w_out[0], flow, half, half)
-    a = scatter(core, pa)
-    b = scatter(core, pb)
-    b = b.reshape(nx, ny, -1, half).transpose(1, 0, 2, 3).reshape(b.shape)
+    scan = carry_scan(state, last, seat[:, 0] & (ny - 1), z_axis, y_axis)
+    hop = next(scan)
+    if fits:
+        pa, more, mark = lead_pass(a, a2, b, b2, held, in_hbm(w_out), experts, nx, ny, zeros)
+        hop = scan.send(mark)
+        pb = rest_pass(*more, hop, nx, ny)
+    else:
+        pa, pb = streamed_experts(a, a2, b, b2, w_in, w_out, experts, nx, ny)
+        scan.send(jnp.zeros(zeros, F32))
+    for _ in range(nz - 4):
+        scan.send(jnp.zeros(zeros, F32))
+    a, b = scatter(core, pa), scatter(core, pb)
+    scan.send(nothing(a, *zeros))
     a, b = scatter(x_axis, rows_split(a, nx)), scatter(y_axis, rows_split(b, ny))
+    scan.send(nothing(a, *zeros))
     a, b = scatter(y_axis, rows_split(a, ny)), scatter(x_axis, rows_split(b, nx))
-    return scatter(z_axis, rows_split(jnp.concatenate([a, b], 1), z_axis.n))
-
-
-def on_device(axes, projected, log_decay, norm_gain, moe_tokens, expert_ids, route_probs, w_in, w_out):
-    x_axis, core, z_axis, y_axis = axes
-    heads = log_decay.shape[1]
-    qkv = projected.transpose(1, 0, 2)
-    run, cols = prepare(log_decay)
-    mixed, state = local_pass(qkv, run, cols, heads, 0, heads)
-    moe_out = experts_layer(moe_tokens, expert_ids, route_probs, w_in, w_out, axes)
-    carried = carry_scan(state, run[:, -1], z_axis, y_axis)
+    carried = scan.send(nothing(a, *zeros))
+    moe_out = scatter(z_axis, rows_split(jnp.concatenate([a, b], 1), nz))
     attn_out = final_pass(qkv, mixed, cols, carried, norm_gain[None], heads)
     return attn_out, moe_out
 

time: 121 us -> 88.7 us (0.73)
  Pallas kernels: 43.5 us -> 25.5 us
  starting transfers between devices: 36.5 us -> 26.1 us
  local copies, waits for them, and re-layouts: 3.76 us -> 1.31 us
    pallas_call x5, Pallas kernels: 41.3 us -> 24.8 us  [the longest x2 11.1 us: local_pass(): pl.pallas_call(functools.partial(local_kernel, heads, group, base, loads,...]
    ppermute x20, starting transfers between devices: 30.8 us -> 21.2 us  [send(): return lax.ppermute(a, self.name, self.turn(k))]
    broadcast_in_dim x4 -> x0, local copies, waits for them, and re-layouts: 1.57 us -> none  [weights_of(): return jnp.sum(jnp.where(mine, r, 0.0), axis=(1, 2))[:, None]]
    pallas_call x1, Pallas kernels: 2.19 us -> 0.7 us  [prepare(): pl.pallas_call(functools.partial(prep_kernel, heads, rows), out_shape=(ja...]
  transfers between devices with their start and end apart: 23 -> 23, of which waited for: 9 -> 8; matrix products, arithmetic and copies ran while one was open for 6% -> 4% of each run, Pallas kernels for 36% -> 27%
where the time goes in v3:
time: 88.7 us; the launch traced here: 88.2 us
  waiting for transfers between devices  28.7 us (32%)
  starting transfers between devices  26.1 us (29%)
  Pallas kernels  25.5 us (29%)
  other arithmetic  5.64 us (6%)
  local copies, waits for them, and re-layouts  1.31 us (1%)
  between operations  1.02 us (1%)
    ppermute x20, waiting for transfers between devices, send(): return lax.ppermute(a, self.name, self.turn(k))  28.7 us
    ppermute x20, starting transfers between devices, send(): return lax.ppermute(a, self.name, self.turn(k))  21.2 us
    pallas_call x2, Pallas kernels, local_pass(): pl.pallas_call(functools.partial(local_kernel, heads, group, base, loads,...  11.1 us
    pallas_call x1, Pallas kernels, lead_pass(): pl.pallas_call(functools.partial(lead_kernel, experts, nx, ny, block), in...  6.4 us
    pallas_call x1, Pallas kernels, final_pass(): pl.pallas_call(functools.partial(final_kernel, heads, group), grid=(heads...  5.88 us
    ppermute x3, starting transfers between devices, carry_scan(): lax.ppermute(out, z_axis.name, z_axis.hop(i)).astype(F32)  4.89 us
  transfers between devices with their start and end apart: 23, of which 8 were waited for; matrix products, arithmetic and copies ran while one was open for 4% of the time, Pallas kernels for 27%

profile of v3, /device:TPU:0, one launch (start us, length us, event | category | flops | bytes accessed | tf_op | source)
XLA Modules:
  0.0 88.2 jit_solution(6799314833697221903)
XLA Ops:
  0.6 0.7 select_reduce_fusion
  1.5 0.9 %pad_maximum_fusion.5 = bf16[8,6272]{1,0:T(8,128)(2,1)S(1)} fusion(bf16[8,128]{1,0:T(8,128)(2,1)S(1)} %fusion.38, bf16[8,6144]{1,0:T(8,128)(2,1)} %param.11), kind=kLoop, calls=%fused_computation.44 | loop fusion | flops 200704 | bytes 200704 | tf_op jit(solution)/shard_map/concatenate | solution.py:583
  2.4 3.0 %collective-permute-start = (bf16[8,6272]{1,0:T(8,128)(2,1)S(1)}, bf16[8,6272]{1,0:T(8,128)(2,1)S(1)}, u32[]{:S(2)}, u32[]{:S(2)}) collective-permute-start(bf16[8,6272]{1,0:T(8,128)(2,1)S(1)} %pad_maximum_fusion.5), channel_id=1, source_target_pairs={{0,8},{4,12},{8,16},{12,20},{16,24},{20,28},{24,0},{28,4},{1,9},{5... | collective-permute-start | bytes 301064 | tf_op jit(solution)/shard_map/ppermute | solution.py:52
  5.4 2.6 %collective-permute-start.1 = (bf16[8,6272]{1,0:T(8,128)(2,1)S(1)}, bf16[8,6272]{1,0:T(8,128)(2,1)S(1)}, u32[]{:S(2)}, u32[]{:S(2)}) collective-permute-start(bf16[8,6272]{1,0:T(8,128)(2,1)S(1)} %pad_maximum_fusion.5), channel_id=1, source_target_pairs={{0,16},{4,20},{8,24},{12,28},{16,0},{20,4},{24,8},{28,12},{1,17},{... | collective-permute-start | bytes 301064 | tf_op jit(solution)/shard_map/ppermute | solution.py:52
  8.0 1.3 %collective-permute-start.2 = (bf16[8,6272]{1,0:T(8,128)(2,1)S(1)}, bf16[8,6272]{1,0:T(8,128)(2,1)S(1)}, u32[]{:S(2)}, u32[]{:S(2)}) collective-permute-start(bf16[8,6272]{1,0:T(8,128)(2,1)S(1)} %pad_maximum_fusion.5), channel_id=1, source_target_pairs={{0,24},{4,28},{8,0},{12,4},{16,8},{20,12},{24,16},{28,20},{1,25},{... | collective-permute-start | bytes 301064 | tf_op jit(solution)/shard_map/ppermute | solution.py:52
  9.4 0.8 copy-done
  10.1 0.7 prepare.1
  11.4 5.5 %local_pass.2 = (bf16[512,2048]{1,0:T(8,128)(2,1)S(1)}, bf16[16,128,128]{2,1,0:T(8,128)(2,1)S(1)}, bf16[8,3200]{1,0:T(8,128)(2,1)}, bf16[576,6144]{1,0:T(8,128)(2,1)S(1)}) custom-call(bf16[3,512,2048]{2,1,0:T(8,128)(2,1)} %bitcast.26, bf16[3,512,2048]{2,1,0:T(8,128)(2,1)} %bitcast.27, bf16[3,512,2048]{2,1,0:T(8,128)(2,1)} %bitcast.28, ...), custom_call_target="tpu_custom_call" | custom-call | flops 1073741824 | bytes 4194304 | tf_op jit(solution)/shard_map/local_pass/pallas_call | solution.py:194
  17.0 1.6 %collective-permute-start.8 = (bf16[32,3200]{1,0:T(8,128)(2,1)S(1)}, bf16[32,3200]{1,0:T(8,128)(2,1)S(1)}, u32[]{:S(2)}, u32[]{:S(2)}) collective-permute-start(bf16[32,3200]{1,0:T(8,128)(2,1)S(1)} %slice.135), channel_id=1, source_target_pairs={{0,2},{1,3},{2,0},{3,1},{4,6},{5,7},{6,4},{7,5},{8,10},{9,11},{10,... | collective-permute-start | bytes 614408 | tf_op jit(solution)/shard_map/ppermute | solution.py:52
  18.6 1.5 %collective-permute-start.5 = (bf16[32,3072]{1,0:T(8,128)(2,1)S(1)}, bf16[32,3072]{1,0:T(8,128)(2,1)S(1)}, u32[]{:S(2)}, u32[]{:S(2)}) collective-permute-start(bf16[32,3072]{1,0:T(8,128)(2,1)S(1)} %slice.134), channel_id=1, source_target_pairs={{0,4},{4,0},{8,12},{12,8},{16,20},{20,16},{24,28},{28,24},{1,5},{5... | collective-permute-start | bytes 589832 | tf_op jit(solution)/shard_map/ppermute | solution.py:52
  20.1 5.6 %local_pass.3 = (bf16[512,2048]{1,0:T(8,128)(2,1)S(1)}, bf16[16,128,128]{2,1,0:T(8,128)(2,1)S(1)}, bf16[8,3200]{1,0:T(8,128)(2,1)S(1)}, bf16[576,6144]{1,0:T(8,128)(2,1)S(1)}) custom-call(bf16[3,512,2048]{2,1,0:T(8,128)(2,1)} %bitcast.29, bf16[3,512,2048]{2,1,0:T(8,128)(2,1)} %bitcast.30, ...), custom_call_target="tpu_custom_call", output_to_operand_aliasing={{0}: (6, {}), {1}: (7, {})} | custom-call | flops 1073741824 | bytes 4194304 | tf_op jit(solution)/shard_map/local_pass/pallas_call | solution.py:194
  25.8 0.6 collective-permute-start.3
  26.5 1.6 %collective-permute-start.9 = (bf16[64,3200]{1,0:T(8,128)(2,1)S(1)}, bf16[64,3200]{1,0:T(8,128)(2,1)S(1)}, u32[]{:S(2)}, u32[]{:S(2)}) collective-permute-start(bf16[64,3200]{1,0:T(8,128)(2,1)S(1)} %maximum_add_fusion), channel_id=1, source_target_pairs={{0,4},{4,0},{8,12},{12,8},{16,20},{20,16},{24,28},{28,24},{1,5},{5... | collective-permute-start | bytes 1228808 | tf_op jit(solution)/shard_map/ppermute | solution.py:52
  28.2 0.6 collective-permute-start.6
  28.8 12.6 %collective-permute-done.9 = bf16[64,3200]{1,0:T(8,128)(2,1)S(1)} collective-permute-done((bf16[64,3200]{1,0:T(8,128)(2,1)S(1)}, bf16[64,3200]{1,0:T(8,128)(2,1)S(1)}, u32[]{:S(2)}, u32[]{:S(2)}) %collective-permute-start.9) | collective-permute-done | bytes 409632 | tf_op jit(solution)/shard_map/ppermute | solution.py:52
  42.6 3.4 %collective-permute-start.4 = (bf16[8,128,128]{2,1,0:T(8,128)(2,1)S(1)}, bf16[8,128,128]{2,1,0:T(8,128)(2,1)S(1)}, u32[]{:S(2)}, u32[]{:S(2)}) collective-permute-start(bf16[8,128,128]{2,1,0:T(8,128)(2,1)S(1)} %get-tuple-element.50), channel_id=1, source_target_pairs={{0,8},{4,12},{1,9},{5,13},{2,10},{6,14},{3,11},{7,15}} | collective-permute-start | bytes 786440 | tf_op jit(solution)/shard_map/ppermute | solution.py:303
  46.0 6.4 %lead_pass.1 = (bf16[128,3072]{1,0:T(8,128)(2,1)S(1)}, bf16[128,3072]{1,0:T(8,128)(2,1)S(1)}, bf16[256,576]{1,0:T(8,128)(2,1)S(1)}, f32[256,128]{1,0:T(8,128)S(1...) custom-call(bf16[128,3072]{1,0:T(8,128)(2,1)S(1)} %pad_maximum_fusion.1.a, ...), custom_call_target="tpu_custom_call" | custom-call | flops 4529848320 | bytes 22413312 | tf_op jit(solution)/shard_map/lead_pass/pallas_call | solution.py:486
  52.6 1.4 %rest_pass.1 = (bf16[128,3072]{1,0:T(8,128)(2,1)S(1)}, bf16[128,3072]{1,0:T(8,128)(2,1)S(1)}) custom-call(bf16[256,576]{1,0:T(8,128)(2,1)S(1)} %get-tuple-element.33.h, f32[256,128]{1,0:T(8,128)S(1)} %get-tuple-element.34.flow, bf16[576,3072]{1,0:T(8,128)(2,1)S(1)} %get-tuple-element.35.w, bf16[8,128,128]{2,1,0:T(8,128)(2,1)S(1)} %add_convert_fusion.5.behind), custom_call_target="tpu_custom_call" | custom-call | flops 905969664 | bytes 5111808 | tf_op jit(solution)/shard_map/rest_pass/pallas_call | solution.py:518
  54.6 0.7 collective-permute-start.11
  55.3 1.1 %collective-permute-done.17 = bf16[128,3072]{1,0:T(8,128)(2,1)S(1)} collective-permute-done((bf16[128,3072]{1,0:T(8,128)(2,1)S(1)}, bf16[128,3072]{1,0:T(8,128)(2,1)S(1)}, u32[]{:S(2)}, u32[]{:S(2)}) %collective-permute-start.17) | collective-permute-done | bytes 786464 | tf_op jit(solution)/shard_map/ppermute | solution.py:52
  56.6 0.6 collective-permute-start.18
  57.7 0.6 collective-permute-start.14
  58.6 0.9 collective-permute-start.13
  59.5 8.4 %collective-permute-done.18 = bf16[64,3072]{1,0:T(8,128)(2,1)S(1)} collective-permute-done((bf16[64,3072]{1,0:T(8,128)(2,1)S(1)}, bf16[64,3072]{1,0:T(8,128)(2,1)S(1)}, u32[]{:S(2)}, u32[]{:S(2)}) %collective-permute-start.18) | collective-permute-done | bytes 393248 | tf_op jit(solution)/shard_map/ppermute | solution.py:52
  68.0 0.6 collective-permute-start.19
  69.1 1.0 %collective-permute-start.16 = (bf16[32,3072]{1,0:T(8,128)(2,1)S(1)}, bf16[32,3072]{1,0:T(8,128)(2,1)S(1)}, u32[]{:S(2)}, u32[]{:S(2)}) collective-permute-start(bf16[32,3072]{1,0:T(8,128)(2,1)S(1)} %slice.141), channel_id=1, source_target_pairs={{0,4},{4,0},{8,12},{12,8},{16,20},{20,16},{24,28},{28,24},{1,5},{5... | collective-permute-start | bytes 589832 | tf_op jit(solution)/shard_map/ppermute | solution.py:52
  70.4 1.2 %collective-permute-start.15 = (bf16[8,128,128]{2,1,0:T(8,128)(2,1)S(1)}, bf16[8,128,128]{2,1,0:T(8,128)(2,1)S(1)}, u32[]{:S(2)}, u32[]{:S(2)}) collective-permute-start(bf16[8,128,128]{2,1,0:T(8,128)(2,1)S(1)} %fusion.3), channel_id=1, source_target_pairs={{0,4},{4,0},{8,12},{12,8},{16,20},{20,16},{24,28},{28,24},{1,5},{5... | collective-permute-start | bytes 786440 | tf_op jit(solution)/shard_map/ppermute | solution.py:52
  71.6 2.6 %collective-permute-done.19 = bf16[32,3072]{1,0:T(8,128)(2,1)S(1)} collective-permute-done((bf16[32,3072]{1,0:T(8,128)(2,1)S(1)}, bf16[32,3072]{1,0:T(8,128)(2,1)S(1)}, u32[]{:S(2)}, u32[]{:S(2)}) %collective-permute-start.19) | collective-permute-done | bytes 196640 | tf_op jit(solution)/shard_map/ppermute | solution.py:52
  74.2 2.8 %collective-permute-done.16 = bf16[32,3072]{1,0:T(8,128)(2,1)S(1)} collective-permute-done((bf16[32,3072]{1,0:T(8,128)(2,1)S(1)}, bf16[32,3072]{1,0:T(8,128)(2,1)S(1)}, u32[]{:S(2)}, u32[]{:S(2)}) %collective-permute-start.16) | collective-permute-done | bytes 196640 | tf_op jit(solution)/shard_map/ppermute | solution.py:52
  77.1 3.2 %collective-permute-start.21 = (bf16[8,6144]{1,0:T(8,128)(2,1)S(1)}, bf16[8,6144]{1,0:T(8,128)(2,1)S(1)}, u32[]{:S(2)}, u32[]{:S(2)}) collective-permute-start(bf16[8,6144]{1,0:T(8,128)(2,1)S(1)} %get-tuple-element.60), channel_id=1, source_target_pairs={{0,16},{4,20},{8,24},{12,28},{16,0},{20,4},{24,8},{28,12},{1,17},{... | collective-permute-start | bytes 294920 | tf_op jit(solution)/shard_map/ppermute | solution.py:52
  81.6 5.9 %final_pass.1 = bf16[512,2048]{1,0:T(8,128)(2,1)} custom-call(bf16[3,512,2048]{2,1,0:T(8,128)(2,1)} %bitcast.32, bf16[512,2048]{1,0:T(8,128)(2,1)S(1)} %get-tuple-element.24.mixed_ref, f32[512,128]{1,0:T(8,128)S(1)} %get-tuple-element.21.refs_4_.cols_ref, bf16[16,128,128]{2,1,0:T(8,128)(2,1)S(1)} %pad_maximum_fusion.2.carried_ref, f32[1,2048]{1,0:T(1,128)S(1)} %bitcast.24), custom_call_target="tpu_custom_call" | custom-call | flops 268435456 | bytes 6291456 | tf_op jit(solution)/shard_map/final_pass/pallas_call | solution.py:235
  87.5 0.7 add_convert_fusion.9
  (75 shorter events, 6.4 us)
Async XLA Ops:
  2.4 14.5 %collective-permute-start = (bf16[8,6272]{1,0:T(8,128)(2,1)S(1)}, bf16[8,6272]{1,0:T(8,128)(2,1)S(1)}, u32[]{:S(2)}, u32[]{:S(2)}) collective-permute-start(bf16[8,6272]{1,0:T(8,128)(2,1)S(1)} %pad_maximum_fusion.5), channel_id=1, source_target_pairs={{0,8},{4,12},{8,16},{12,20},{16,24},{20,28},{24,0},{28,4},{1,9},{5... | collective-permute-start | bytes 301064 | tf_op jit(solution)/shard_map/ppermute | solution.py:52
  5.4 11.5 %collective-permute-start.1 = (bf16[8,6272]{1,0:T(8,128)(2,1)S(1)}, bf16[8,6272]{1,0:T(8,128)(2,1)S(1)}, u32[]{:S(2)}, u32[]{:S(2)}) collective-permute-start(bf16[8,6272]{1,0:T(8,128)(2,1)S(1)} %pad_maximum_fusion.5), channel_id=1, source_target_pairs={{0,16},{4,20},{8,24},{12,28},{16,0},{20,4},{24,8},{28,12},{1,17},{... | collective-permute-start | bytes 301064 | tf_op jit(solution)/shard_map/ppermute | solution.py:52
  8.0 8.9 %collective-permute-start.2 = (bf16[8,6272]{1,0:T(8,128)(2,1)S(1)}, bf16[8,6272]{1,0:T(8,128)(2,1)S(1)}, u32[]{:S(2)}, u32[]{:S(2)}) collective-permute-start(bf16[8,6272]{1,0:T(8,128)(2,1)S(1)} %pad_maximum_fusion.5), channel_id=1, source_target_pairs={{0,24},{4,28},{8,0},{12,4},{16,8},{20,12},{24,16},{28,20},{1,25},{... | collective-permute-start | bytes 301064 | tf_op jit(solution)/shard_map/ppermute | solution.py:52
  9.4 0.8 copy-start
  11.4 5.6 %copy-start.2 = (bf16[8,6144]{1,0:T(8,128)(2,1)S(1)}, bf16[8,6144]{1,0:T(8,128)(2,1)}, u32[]{:S(2)}) copy-start(bf16[8,6144]{1,0:T(8,128)(2,1)} %param.11) | copy-start | bytes 294916
  17.0 9.4 %collective-permute-start.8 = (bf16[32,3200]{1,0:T(8,128)(2,1)S(1)}, bf16[32,3200]{1,0:T(8,128)(2,1)S(1)}, u32[]{:S(2)}, u32[]{:S(2)}) collective-permute-start(bf16[32,3200]{1,0:T(8,128)(2,1)S(1)} %slice.135), channel_id=1, source_target_pairs={{0,2},{1,3},{2,0},{3,1},{4,6},{5,7},{6,4},{7,5},{8,10},{9,11},{10,... | collective-permute-start | bytes 614408 | tf_op jit(solution)/shard_map/ppermute | solution.py:52
  18.6 9.6 %collective-permute-start.5 = (bf16[32,3072]{1,0:T(8,128)(2,1)S(1)}, bf16[32,3072]{1,0:T(8,128)(2,1)S(1)}, u32[]{:S(2)}, u32[]{:S(2)}) collective-permute-start(bf16[32,3072]{1,0:T(8,128)(2,1)S(1)} %slice.134), channel_id=1, source_target_pairs={{0,4},{4,0},{8,12},{12,8},{16,20},{20,16},{24,28},{28,24},{1,5},{5... | collective-permute-start | bytes 589832 | tf_op jit(solution)/shard_map/ppermute | solution.py:52
  25.8 16.4 %collective-permute-start.3 = (bf16[1040,128]{1,0:T(8,128)(2,1)S(1)}, bf16[1040,128]{1,0:T(8,128)(2,1)S(1)}, u32[]{:S(2)}, u32[]{:S(2)}) collective-permute-start(bf16[1040,128]{1,0:T(8,128)(2,1)S(1)} %pad_maximum_fusion.4), channel_id=1, source_target_pairs={{0,4},{4,0},{8,12},{12,8},{16,20},{20,16},{24,28},{28,24},{1,5},{5... | collective-permute-start | bytes 798728 | tf_op jit(solution)/shard_map/ppermute | solution.py:52
  26.5 14.8 %collective-permute-start.9 = (bf16[64,3200]{1,0:T(8,128)(2,1)S(1)}, bf16[64,3200]{1,0:T(8,128)(2,1)S(1)}, u32[]{:S(2)}, u32[]{:S(2)}) collective-permute-start(bf16[64,3200]{1,0:T(8,128)(2,1)S(1)} %maximum_add_fusion), channel_id=1, source_target_pairs={{0,4},{4,0},{8,12},{12,8},{16,20},{20,16},{24,28},{28,24},{1,5},{5... | collective-permute-start | bytes 1228808 | tf_op jit(solution)/shard_map/ppermute | solution.py:52
  28.2 13.3 %collective-permute-start.6 = (bf16[64,3072]{1,0:T(8,128)(2,1)S(1)}, bf16[64,3072]{1,0:T(8,128)(2,1)S(1)}, u32[]{:S(2)}, u32[]{:S(2)}) collective-permute-start(bf16[64,3072]{1,0:T(8,128)(2,1)S(1)} %maximum_add_fusion.1), channel_id=1, source_target_pairs={{0,2},{1,3},{2,0},{3,1},{4,6},{5,7},{6,4},{7,5},{8,10},{9,11},{10,... | collective-permute-start | bytes 1179656 | tf_op jit(solution)/shard_map/ppermute | solution.py:52
  41.4 4.5 %collective-permute-start.10 = (bf16[128,3200]{1,0:T(8,128)(2,1)S(1)}, bf16[128,3200]{1,0:T(8,128)(2,1)S(1)}, u32[]{:S(2)}, u32[]{:S(2)}) collective-permute-start(bf16[128,3200]{1,0:T(8,128)(2,1)S(1)} %pad_maximum_fusion.b), channel_id=1, source_target_pairs={{0,1},{1,0},{2,3},{3,2},{4,5},{5,4},{6,7},{7,6},{8,9},{9,8},{10,11... | collective-permute-start | bytes 2457608 | tf_op jit(solution)/shard_map/ppermute | solution.py:52
  41.6 4.4 %collective-permute-start.7 = (bf16[128,3072]{1,0:T(8,128)(2,1)S(1)}, bf16[128,3072]{1,0:T(8,128)(2,1)S(1)}, u32[]{:S(2)}, u32[]{:S(2)}) collective-permute-start(bf16[128,3072]{1,0:T(8,128)(2,1)S(1)} %pad_maximum_fusion.1.a), channel_id=1, source_target_pairs={{0,1},{1,0},{2,3},{3,2},{4,5},{5,4},{6,7},{7,6},{8,9},{9,8},{10,11... | collective-permute-start | bytes 2359304 | tf_op jit(solution)/shard_map/ppermute | solution.py:52
  42.6 9.8 %collective-permute-start.4 = (bf16[8,128,128]{2,1,0:T(8,128)(2,1)S(1)}, bf16[8,128,128]{2,1,0:T(8,128)(2,1)S(1)}, u32[]{:S(2)}, u32[]{:S(2)}) collective-permute-start(bf16[8,128,128]{2,1,0:T(8,128)(2,1)S(1)} %get-tuple-element.50), channel_id=1, source_target_pairs={{0,8},{4,12},{1,9},{5,13},{2,10},{6,14},{3,11},{7,15}} | collective-permute-start | bytes 786440 | tf_op jit(solution)/shard_map/ppermute | solution.py:303
  54.0 2.4 %collective-permute-start.17 = (bf16[128,3072]{1,0:T(8,128)(2,1)S(1)}, bf16[128,3072]{1,0:T(8,128)(2,1)S(1)}, u32[]{:S(2)}, u32[]{:S(2)}) collective-permute-start(bf16[128,3072]{1,0:T(8,128)(2,1)S(1)} %get-tuple-element.37), channel_id=1, source_target_pairs={{0,1},{1,0},{2,3},{3,2},{4,5},{5,4},{6,7},{7,6},{8,9},{9,8},{10,11... | collective-permute-start | bytes 2359304 | tf_op jit(solution)/shard_map/ppermute | solution.py:52
  54.1 3.4 %collective-permute-start.12 = (bf16[128,3072]{1,0:T(8,128)(2,1)S(1)}, bf16[128,3072]{1,0:T(8,128)(2,1)S(1)}, u32[]{:S(2)}, u32[]{:S(2)}) collective-permute-start(bf16[128,3072]{1,0:T(8,128)(2,1)S(1)} %get-tuple-element.32), channel_id=1, source_target_pairs={{0,1},{1,0},{2,3},{3,2},{4,5},{5,4},{6,7},{7,6},{8,9},{9,8},{10,11... | collective-permute-start | bytes 2359304 | tf_op jit(solution)/shard_map/ppermute | solution.py:52
  54.6 3.7 %collective-permute-start.11 = (bf16[8,128,128]{2,1,0:T(8,128)(2,1)S(1)}, bf16[8,128,128]{2,1,0:T(8,128)(2,1)S(1)}, u32[]{:S(2)}, u32[]{:S(2)}) collective-permute-start(bf16[8,128,128]{2,1,0:T(8,128)(2,1)S(1)} %add_convert_fusion.5.behind), channel_id=1, source_target_pairs={{8,16},{12,20},{9,17},{13,21},{10,18},{14,22},{11,19},{15,23}} | collective-permute-start | bytes 786440 | tf_op jit(solution)/shard_map/ppermute | solution.py:303
  56.6 11.2 %collective-permute-start.18 = (bf16[64,3072]{1,0:T(8,128)(2,1)S(1)}, bf16[64,3072]{1,0:T(8,128)(2,1)S(1)}, u32[]{:S(2)}, u32[]{:S(2)}) collective-permute-start(bf16[64,3072]{1,0:T(8,128)(2,1)S(1)} %slice.144), channel_id=1, source_target_pairs={{0,4},{4,0},{8,12},{12,8},{16,20},{20,16},{24,28},{28,24},{1,5},{5... | collective-permute-start | bytes 1179656 | tf_op jit(solution)/shard_map/ppermute | solution.py:52
  57.7 11.2 %collective-permute-start.14 = (bf16[64,3072]{1,0:T(8,128)(2,1)S(1)}, bf16[64,3072]{1,0:T(8,128)(2,1)S(1)}, u32[]{:S(2)}, u32[]{:S(2)}) collective-permute-start(bf16[64,3072]{1,0:T(8,128)(2,1)S(1)} %slice.138), channel_id=1, source_target_pairs={{0,2},{1,3},{2,0},{3,1},{4,6},{5,7},{6,4},{7,5},{8,10},{9,11},{10,... | collective-permute-start | bytes 1179656 | tf_op jit(solution)/shard_map/ppermute | solution.py:52
  58.6 11.5 %collective-permute-start.13 = (bf16[8,128,128]{2,1,0:T(8,128)(2,1)S(1)}, bf16[8,128,128]{2,1,0:T(8,128)(2,1)S(1)}, u32[]{:S(2)}, u32[]{:S(2)}) collective-permute-start(bf16[8,128,128]{2,1,0:T(8,128)(2,1)S(1)} %add_convert_fusion.4), channel_id=1, source_target_pairs={{16,24},{20,28},{17,25},{21,29},{18,26},{22,30},{19,27},{23,31}} | collective-permute-start | bytes 786440 | tf_op jit(solution)/shard_map/ppermute | solution.py:303
  68.0 6.2 %collective-permute-start.19 = (bf16[32,3072]{1,0:T(8,128)(2,1)S(1)}, bf16[32,3072]{1,0:T(8,128)(2,1)S(1)}, u32[]{:S(2)}, u32[]{:S(2)}) collective-permute-start(bf16[32,3072]{1,0:T(8,128)(2,1)S(1)} %slice.146), channel_id=1, source_target_pairs={{0,2},{1,3},{2,0},{3,1},{4,6},{5,7},{6,4},{7,5},{8,10},{9,11},{10,... | collective-permute-start | bytes 589832 | tf_op jit(solution)/shard_map/ppermute | solution.py:52
  69.1 7.9 %collective-permute-start.16 = (bf16[32,3072]{1,0:T(8,128)(2,1)S(1)}, bf16[32,3072]{1,0:T(8,128)(2,1)S(1)}, u32[]{:S(2)}, u32[]{:S(2)}) collective-permute-start(bf16[32,3072]{1,0:T(8,128)(2,1)S(1)} %slice.141), channel_id=1, source_target_pairs={{0,4},{4,0},{8,12},{12,8},{16,20},{20,16},{24,28},{28,24},{1,5},{5... | collective-permute-start | bytes 589832 | tf_op jit(solution)/shard_map/ppermute | solution.py:52
  70.4 10.5 %collective-permute-start.15 = (bf16[8,128,128]{2,1,0:T(8,128)(2,1)S(1)}, bf16[8,128,128]{2,1,0:T(8,128)(2,1)S(1)}, u32[]{:S(2)}, u32[]{:S(2)}) collective-permute-start(bf16[8,128,128]{2,1,0:T(8,128)(2,1)S(1)} %fusion.3), channel_id=1, source_target_pairs={{0,4},{4,0},{8,12},{12,8},{16,20},{20,16},{24,28},{28,24},{1,5},{5... | collective-permute-start | bytes 786440 | tf_op jit(solution)/shard_map/ppermute | solution.py:52
  77.1 10.4 %collective-permute-start.20 = (bf16[8,6144]{1,0:T(8,128)(2,1)S(1)}, bf16[8,6144]{1,0:T(8,128)(2,1)S(1)}, u32[]{:S(2)}, u32[]{:S(2)}) collective-permute-start(bf16[8,6144]{1,0:T(8,128)(2,1)S(1)} %get-tuple-element.58), channel_id=1, source_target_pairs={{0,24},{4,28},{8,0},{12,4},{16,8},{20,12},{24,16},{28,20},{1,25},{... | collective-permute-start | bytes 294920 | tf_op jit(solution)/shard_map/ppermute | solution.py:52
  77.1 10.4 %collective-permute-start.21 = (bf16[8,6144]{1,0:T(8,128)(2,1)S(1)}, bf16[8,6144]{1,0:T(8,128)(2,1)S(1)}, u32[]{:S(2)}, u32[]{:S(2)}) collective-permute-start(bf16[8,6144]{1,0:T(8,128)(2,1)S(1)} %get-tuple-element.60), channel_id=1, source_target_pairs={{0,16},{4,20},{8,24},{12,28},{16,0},{20,4},{24,8},{28,12},{1,17},{... | collective-permute-start | bytes 294920 | tf_op jit(solution)/shard_map/ppermute | solution.py:52
  80.3 7.2 %collective-permute-start.22 = (bf16[8,6144]{1,0:T(8,128)(2,1)S(1)}, bf16[8,6144]{1,0:T(8,128)(2,1)S(1)}, u32[]{:S(2)}, u32[]{:S(2)}) collective-permute-start(bf16[8,6144]{1,0:T(8,128)(2,1)S(1)} %get-tuple-element.59), channel_id=1, source_target_pairs={{0,8},{4,12},{8,16},{12,20},{16,24},{20,28},{24,0},{28,4},{1,9},{5... | collective-permute-start | bytes 294920 | tf_op jit(solution)/shard_map/ppermute | solution.py:52
  80.9 0.7 copy-start.1

commit v4 on v3

--- a/solution.py
+++ b/solution.py
@@ -216,9 +216,11 @@
     )(qkv, qkv, qkv, run, cols, *more)
 
 
-def final_kernel(heads, group, q_ref, mixed_ref, cols_ref, carried_ref, gain_ref, out_ref):
+def final_kernel(heads, group, first_of, *refs):
+    q_ref, mixed_ref, cols_ref, carried_ref, gain_ref = refs[:5]
+    out_ref = refs[-1]
     width = q_ref.shape[2] // group
-    first = pl.program_id(0) * group
+    first = first_of(pl.program_id(0)) * group
     cols = pltpu.roll(cols_ref[...], 128 - first, 1)
     for g in range(group):
         lanes = slice(g * width, (g + 1) * width)
@@ -229,29 +231,38 @@
         out_ref[:, lanes] = (mixed * lax.rsqrt(mean + EPS) * gain_ref[:, lanes]).astype(BF16)
 
 
-def final_pass(qkv, mixed, cols, carried, gain, heads, group=4):
+def final_pass(qkv, mixed, cols, carried, gain, heads, y_axis, back, done, behind, group=4):
     rows, width = qkv.shape[1], qkv.shape[2] // heads
-    group = min(group, heads)
+    share = carried.shape[0]
+    group = min(group, share)
+
+    def block(h):
+        place = (y_axis.index() + y_axis.n - back) % y_axis.n
+        return place * (share // group) + h
+
+    more = [a for a in (done, behind) if a is not None]
     return pl.pallas_call(
-        functools.partial(final_kernel, heads, group),
-        grid=(heads // group,),
+        functools.partial(final_kernel, heads, group, block),
+        grid=(share // group,),
         in_specs=[
-            pl.BlockSpec((1, rows, group * width), lambda h: (0, 0, h)),
-            pl.BlockSpec((rows, group * width), lambda h: (0, h)),
+            pl.BlockSpec((1, rows, group * width), lambda h: (0, 0, block(h))),
+            pl.BlockSpec((rows, group * width), lambda h: (0, block(h))),
             pl.BlockSpec(cols.shape, lambda h: (0, 0)),
             pl.BlockSpec((group, width, width), lambda h: (h, 0, 0)),
-            pl.BlockSpec((1, group * width), lambda h: (0, h)),
-        ],
-        out_specs=pl.BlockSpec((rows, group * width), lambda h: (0, h)),
+            pl.BlockSpec((1, group * width), lambda h: (0, block(h))),
+        ]
+        + [pl.BlockSpec(memory_space=pl.ANY)] * len(more),
+        out_specs=pl.BlockSpec((rows, group * width), lambda h: (0, block(h))),
         out_shape=jax.ShapeDtypeStruct((rows, heads * width), BF16),
+        input_output_aliases={} if done is None else {5: 0},
         compiler_params=params(20),
         cost_estimate=pl.CostEstimate(
-            flops=2 * heads * rows * width * width,
-            bytes_accessed=heads * rows * width * 6,
+            flops=2 * share * rows * width * width,
+            bytes_accessed=share * rows * width * 6,
             transcendentals=0,
         ),
         name="final_pass",
-    )(qkv, mixed, cols, carried, gain)
+    )(qkv, mixed, cols, carried, gain, *more)
 
 
 def pick(parts, at):
@@ -269,9 +280,11 @@
     y = seat[:share]
     turned = [(y + k) & (ny - 1) for k in range(ny)]
     fade = jnp.exp(last)
+    tie = yield
 
     def packed(k):
-        body = pick(rows_split(state, ny), turned[k]).reshape(share * width, width)
+        body = pick(rows_split(state, ny), turned[k]) + tie[:, None].astype(BF16)
+        body = body.reshape(share * width, width)
         rows = jnp.stack(pieces_of(pick(rows_split(fade, ny), turned[k])), 0)
         rows = jnp.pad(rows, ((0, pad - PIECES), (0, width - share)))
         return jnp.concatenate([body, rows.astype(BF16)], 0)
@@ -294,7 +307,8 @@
             r = r * jnp.where(places[m] < end, fades[m], 1.0)
         return r[:, None, None]
 
-    inner = sum(reach(k, ny) * states[k] for k in range(ny))
+    tie = yield
+    inner = sum(reach(k, ny) * states[k] for k in range(ny)) + tie[:, None]
     through = whole(ny)
     carried = jnp.zeros((share, width, width), F32)
     for i in range(z_axis.n - 1):
@@ -308,10 +322,7 @@
             whole(end) * carried + sum(reach(k, end) * states[k] for k in range(ny))
         ).astype(BF16)
 
-    tie = yield
-    back = [entering(0)] + [y_axis.send(entering(j), j) for j in range(1, ny)]
-    back[0] = back[0] + tie.astype(BF16)[:, None]
-    yield jnp.concatenate([pick(back, places[p]) for p in range(ny)], 0)
+    yield [entering(0)] + [y_axis.send(entering(j), j) for j in range(1, ny)]
 
 
 def hidden_kernel(steps, split, *refs):
@@ -595,7 +606,8 @@
     zeros = (heads // ny, qkv.shape[2] // heads)
     a2, b2 = core.send(a, 1), core.send(b, 1)
     scan = carry_scan(state, last, seat[:, 0] & (ny - 1), z_axis, y_axis)
-    hop = next(scan)
+    next(scan)
+    scan.send(nothing(b, *zeros))
     if fits:
         pa, more, mark = lead_pass(a, a2, b, b2, held, in_hbm(w_out), experts, nx, ny, zeros)
         hop = scan.send(mark)
@@ -611,8 +623,22 @@
     scan.send(nothing(a, *zeros))
     a, b = scatter(y_axis, rows_split(a, ny)), scatter(x_axis, rows_split(b, nx))
     carried = scan.send(nothing(a, *zeros))
-    moe_out = scatter(z_axis, rows_split(jnp.concatenate([a, b], 1), nz))
-    attn_out = final_pass(qkv, mixed, cols, carried, norm_gain[None], heads)
+    both = jnp.concatenate([a, b], 1)
+    moe_out = scatter(z_axis, rows_split(both, nz))
+    attn_out = None
+    for k in range(ny):
+        attn_out = final_pass(
+            qkv,
+            mixed,
+            cols,
+            carried[k],
+            norm_gain[None],
+            heads,
+            y_axis,
+            k,
+            attn_out,
+            both if k == 0 else None,
+        )
     return attn_out, moe_out
 
 

time: 88.7 us -> 91.4 us (1.030)
  waiting for transfers between devices: 28.7 us -> 30.6 us
  Pallas kernels: 25.5 us -> 27 us
    ppermute x3, waiting for transfers between devices: 0.01 us -> 4.23 us  [carry_scan(): lax.ppermute(out, z_axis.name, z_axis.hop(i)).astype(F32)]
    ppermute x20, waiting for transfers between devices: 28.7 us -> 26.4 us  [send(): return lax.ppermute(a, self.name, self.turn(k))]
    pallas_call x1 -> x2, Pallas kernels: 5.88 us -> 7.4 us  [final_pass(): pl.pallas_call(functools.partial(final_kernel, heads, group, block), grid...]
  transfers between devices with their start and end apart: 23 -> 23, of which waited for: 8 -> 8; matrix products, arithmetic and copies ran while one was open for 4% -> 4% of each run, Pallas kernels for 27% -> 26%
where the time goes in v4:
time: 91.4 us; the launch traced here: 91 us
  waiting for transfers between devices  30.6 us (33%)
  Pallas kernels  27 us (30%)
  starting transfers between devices  25.9 us (28%)
  other arithmetic  5.19 us (6%)
  local copies, waits for them, and re-layouts  1.31 us (1%)
  between operations  0.98 us (1%)
    ppermute x20, waiting for transfers between devices, send(): return lax.ppermute(a, self.name, self.turn(k))  26.4 us
    ppermute x20, starting transfers between devices, send(): return lax.ppermute(a, self.name, self.turn(k))  20.8 us
    pallas_call x2, Pallas kernels, local_pass(): pl.pallas_call(functools.partial(local_kernel, heads, group, base, loads,...  11.1 us
    pallas_call x2, Pallas kernels, final_pass(): pl.pallas_call(functools.partial(final_kernel, heads, group, block), grid...  7.4 us
    pallas_call x1, Pallas kernels, lead_pass(): pl.pallas_call(functools.partial(lead_kernel, experts, nx, ny, block), in...  6.4 us
    ppermute x3, starting transfers between devices, carry_scan(): lax.ppermute(out, z_axis.name, z_axis.hop(i)).astype(F32)  5.07 us
    ppermute x3, waiting for transfers between devices, carry_scan(): lax.ppermute(out, z_axis.name, z_axis.hop(i)).astype(F32)  4.23 us
  transfers between devices with their start and end apart: 23, of which 8 were waited for; matrix products, arithmetic and copies ran while one was open for 4% of the time, Pallas kernels for 26%

profile of v4, /device:TPU:0, one launch (start us, length us, event | category | flops | bytes accessed | tf_op | source)
XLA Modules:
  0.0 91.0 jit_solution(5108021957831334051)
XLA Ops:
  0.6 0.7 select_reduce_fusion
  1.5 0.9 pad_maximum_fusion.5
  2.4 5.0 %collective-permute-start.2 = (bf16[8,6272]{1,0:T(8,128)(2,1)S(1)}, bf16[8,6272]{1,0:T(8,128)(2,1)S(1)}, u32[]{:S(2)}, u32[]{:S(2)}) collective-permute-start(bf16[8,6272]{1,0:T(8,128)(2,1)S(1)} %pad_maximum_fusion.5), channel_id=1, source_target_pairs={{0,24},{4,28},{8,0},{12,4},{16,8},{20,12},{24,16},{28,20},{1,25},{... | collective-permute-start | bytes 301064 | tf_op jit(solution)/shard_map/ppermute | solution.py:52
  7.5 1.0 %collective-permute-start = (bf16[8,6272]{1,0:T(8,128)(2,1)S(1)}, bf16[8,6272]{1,0:T(8,128)(2,1)S(1)}, u32[]{:S(2)}, u32[]{:S(2)}) collective-permute-start(bf16[8,6272]{1,0:T(8,128)(2,1)S(1)} %pad_maximum_fusion.5), channel_id=1, source_target_pairs={{0,8},{4,12},{8,16},{12,20},{16,24},{20,28},{24,0},{28,4},{1,9},{5... | collective-permute-start | bytes 301064 | tf_op jit(solution)/shard_map/ppermute | solution.py:52
  8.5 0.8 copy-done
  9.2 0.7 prepare.1
  10.5 5.5 %local_pass.2 = (bf16[512,2048]{1,0:T(8,128)(2,1)S(1)}, bf16[16,128,128]{2,1,0:T(8,128)(2,1)S(1)}, bf16[8,3200]{1,0:T(8,128)(2,1)}, bf16[576,6144]{1,0:T(8,128)(2,1)S(1)}) custom-call(bf16[3,512,2048]{2,1,0:T(8,128)(2,1)} %bitcast.27, bf16[3,512,2048]{2,1,0:T(8,128)(2,1)} %bitcast.28, bf16[3,512,2048]{2,1,0:T(8,128)(2,1)} %bitcast.29, ...), custom_call_target="tpu_custom_call" | custom-call | flops 1073741824 | bytes 4194304 | tf_op jit(solution)/shard_map/local_pass/pallas_call | solution.py:194
  16.5 1.6 %collective-permute-start.6 = (bf16[32,3072]{1,0:T(8,128)(2,1)S(1)}, bf16[32,3072]{1,0:T(8,128)(2,1)S(1)}, u32[]{:S(2)}, u32[]{:S(2)}) collective-permute-start(bf16[32,3072]{1,0:T(8,128)(2,1)S(1)} %slice.140), channel_id=1, source_target_pairs={{0,4},{4,0},{8,12},{12,8},{16,20},{20,16},{24,28},{28,24},{1,5},{5... | collective-permute-start | bytes 589832 | tf_op jit(solution)/shard_map/ppermute | solution.py:52
  18.0 1.5 %collective-permute-start.3 = (bf16[32,3200]{1,0:T(8,128)(2,1)S(1)}, bf16[32,3200]{1,0:T(8,128)(2,1)S(1)}, u32[]{:S(2)}, u32[]{:S(2)}) collective-permute-start(bf16[32,3200]{1,0:T(8,128)(2,1)S(1)} %slice.136), channel_id=1, source_target_pairs={{0,2},{1,3},{2,0},{3,1},{4,6},{5,7},{6,4},{7,5},{8,10},{9,11},{10,... | collective-permute-start | bytes 614408 | tf_op jit(solution)/shard_map/ppermute | solution.py:52
  19.5 5.6 %local_pass.3 = (bf16[512,2048]{1,0:T(8,128)(2,1)S(1)}, bf16[16,128,128]{2,1,0:T(8,128)(2,1)S(1)}, bf16[8,3200]{1,0:T(8,128)(2,1)S(1)}, bf16[576,6144]{1,0:T(8,128)(2,1)S(1)}) custom-call(bf16[3,512,2048]{2,1,0:T(8,128)(2,1)} %bitcast.30, bf16[3,512,2048]{2,1,0:T(8,128)(2,1)} %bitcast.31, ...), custom_call_target="tpu_custom_call", output_to_operand_aliasing={{0}: (6, {}), {1}: (7, {})} | custom-call | flops 1073741824 | bytes 4194304 | tf_op jit(solution)/shard_map/local_pass/pallas_call | solution.py:194
  25.9 0.6 collective-permute-start.7
  26.5 9.1 %collective-permute-done.4 = bf16[64,3200]{1,0:T(8,128)(2,1)S(1)} collective-permute-done((bf16[64,3200]{1,0:T(8,128)(2,1)S(1)}, bf16[64,3200]{1,0:T(8,128)(2,1)S(1)}, u32[]{:S(2)}, u32[]{:S(2)}) %collective-permute-start.4) | collective-permute-done | bytes 409632 | tf_op jit(solution)/shard_map/ppermute | solution.py:52
  36.6 1.0 %collective-permute-start.5 = (bf16[1040,128]{1,0:T(8,128)(2,1)S(1)}, bf16[1040,128]{1,0:T(8,128)(2,1)S(1)}, u32[]{:S(2)}, u32[]{:S(2)}) collective-permute-start(bf16[1040,128]{1,0:T(8,128)(2,1)S(1)} %pad_maximum_fusion.4), channel_id=1, source_target_pairs={{0,4},{4,0},{8,12},{12,8},{16,20},{20,16},{24,28},{28,24},{1,5},{5... | collective-permute-start | bytes 798728 | tf_op jit(solution)/shard_map/ppermute | solution.py:52
  37.6 1.7 %collective-permute-done.8.a2 = bf16[128,3072]{1,0:T(8,128)(2,1)S(1)} collective-permute-done((bf16[128,3072]{1,0:T(8,128)(2,1)S(1)}, bf16[128,3072]{1,0:T(8,128)(2,1)S(1)}, u32[]{:S(2)}, u32[]{:S(2)}) %collective-permute-start.8) | collective-permute-done | bytes 786464 | tf_op jit(solution)/shard_map/ppermute | solution.py:52
  39.3 6.4 %lead_pass.1 = (bf16[128,3072]{1,0:T(8,128)(2,1)S(1)}, bf16[128,3072]{1,0:T(8,128)(2,1)S(1)}, bf16[256,576]{1,0:T(8,128)(2,1)S(1)}, f32[256,128]{1,0:T(8,128)S(1...) custom-call(bf16[128,3072]{1,0:T(8,128)(2,1)S(1)} %pad_maximum_fusion.1.a, ...), custom_call_target="tpu_custom_call" | custom-call | flops 4529848320 | bytes 22413312 | tf_op jit(solution)/shard_map/lead_pass/pallas_call | solution.py:497
  46.3 3.5 %collective-permute-start.10 = (bf16[8,128,128]{2,1,0:T(8,128)(2,1)S(1)}, bf16[8,128,128]{2,1,0:T(8,128)(2,1)S(1)}, u32[]{:S(2)}, u32[]{:S(2)}) collective-permute-start(bf16[8,128,128]{2,1,0:T(8,128)(2,1)S(1)} %get-tuple-element.48.behind), channel_id=1, source_target_pairs={{0,8},{4,12},{1,9},{5,13},{2,10},{6,14},{3,11},{7,15}} | collective-permute-start | bytes 786440 | tf_op jit(solution)/shard_map/ppermute | solution.py:317
  49.9 1.4 %rest_pass.1 = (bf16[128,3072]{1,0:T(8,128)(2,1)S(1)}, bf16[128,3072]{1,0:T(8,128)(2,1)S(1)}) custom-call(bf16[256,576]{1,0:T(8,128)(2,1)S(1)} %get-tuple-element.33.h, f32[256,128]{1,0:T(8,128)S(1)} %get-tuple-element.34.flow, bf16[576,3072]{1,0:T(8,128)(2,1)S(1)} %get-tuple-element.35.w, bf16[8,128,128]{2,1,0:T(8,128)(2,1)S(1)} %get-tuple-element.48.behind), custom_call_target="tpu_custom_call" | custom-call | flops 905969664 | bytes 5111808 | tf_op jit(solution)/shard_map/rest_pass/pallas_call | solution.py:529
  51.7 4.2 %collective-permute-done.10 = bf16[8,128,128]{2,1,0:T(8,128)(2,1)S(1)} collective-permute-done((bf16[8,128,128]{2,1,0:T(8,128)(2,1)S(1)}, bf16[8,128,128]{2,1,0:T(8,128)(2,1)S(1)}, u32[]{:S(2)}, u32[]{:S(2)}) %collective-permute-start.10) | collective-permute-done | bytes 262176 | tf_op jit(solution)/shard_map/ppermute | solution.py:317
  56.2 0.7 collective-permute-start.12
  56.8 0.6 collective-permute-start.13
  57.7 0.6 collective-permute-start.18
  58.3 9.2 %collective-permute-done.13 = bf16[64,3072]{1,0:T(8,128)(2,1)S(1)} collective-permute-done((bf16[64,3072]{1,0:T(8,128)(2,1)S(1)}, bf16[64,3072]{1,0:T(8,128)(2,1)S(1)}, u32[]{:S(2)}, u32[]{:S(2)}) %collective-permute-start.13) | collective-permute-done | bytes 393248 | tf_op jit(solution)/shard_map/ppermute | solution.py:52
  68.5 0.9 collective-permute-start.14
  69.5 0.6 collective-permute-start.19
  70.1 3.3 %collective-permute-done.15 = bf16[32,3072]{1,0:T(8,128)(2,1)S(1)} collective-permute-done((bf16[32,3072]{1,0:T(8,128)(2,1)S(1)}, bf16[32,3072]{1,0:T(8,128)(2,1)S(1)}, u32[]{:S(2)}, u32[]{:S(2)}) %collective-permute-start.15) | collective-permute-done | bytes 196640 | tf_op jit(solution)/shard_map/ppermute | solution.py:52
  73.4 1.8 %collective-permute-done.19 = bf16[32,3072]{1,0:T(8,128)(2,1)S(1)} collective-permute-done((bf16[32,3072]{1,0:T(8,128)(2,1)S(1)}, bf16[32,3072]{1,0:T(8,128)(2,1)S(1)}, u32[]{:S(2)}, u32[]{:S(2)}) %collective-permute-start.19) | collective-permute-done | bytes 196640 | tf_op jit(solution)/shard_map/ppermute | solution.py:52
  75.4 4.6 %collective-permute-start.21 = (bf16[8,6144]{1,0:T(8,128)(2,1)S(1)}, bf16[8,6144]{1,0:T(8,128)(2,1)S(1)}, u32[]{:S(2)}, u32[]{:S(2)}) collective-permute-start(bf16[8,6144]{1,0:T(8,128)(2,1)S(1)} %get-tuple-element.59), channel_id=1, source_target_pairs={{0,16},{4,20},{8,24},{12,28},{16,0},{20,4},{24,8},{28,12},{1,17},{... | collective-permute-start | bytes 294920 | tf_op jit(solution)/shard_map/ppermute | solution.py:52
  80.4 1.6 %collective-permute-start.16 = (bf16[8,128,128]{2,1,0:T(8,128)(2,1)S(1)}, bf16[8,128,128]{2,1,0:T(8,128)(2,1)S(1)}, u32[]{:S(2)}, u32[]{:S(2)}) collective-permute-start(bf16[8,128,128]{2,1,0:T(8,128)(2,1)S(1)} %get-tuple-element.57), channel_id=1, source_target_pairs={{0,4},{4,0},{8,12},{12,8},{16,20},{20,16},{24,28},{28,24},{1,5},{5... | collective-permute-start | bytes 786440 | tf_op jit(solution)/shard_map/ppermute | solution.py:52
  82.0 3.7 %final_pass.2.refs_5_ = bf16[512,2048]{1,0:T(8,128)(2,1)} custom-call(bf16[3,512,2048]{2,1,0:T(8,128)(2,1)} %bitcast.33, bf16[512,2048]{1,0:T(8,128)(2,1)S(1)} %get-tuple-element.24.refs_1_, f32[512,128]{1,0:T(8,128)S(1)} %get-tuple-element.21.refs_4_.refs_2_, bf16[8,128,128]{2,1,0:T(8,128)(2,1)S(1)} %get-tuple-element.56.refs_3_, f32[1,2048]{1,0:T(1,128)S(1)} %bitcast.24, ...), custom_call_target="tpu_custom_call" | custom-call | flops 134217728 | bytes 3145728 | tf_op jit(solution)/shard_map/final_pass/pallas_call | solution.py:244
  85.7 0.8 collective-permute-done.21
  86.6 0.7 add_convert_fusion.9
  87.3 3.7 %final_pass.3 = bf16[512,2048]{1,0:T(8,128)(2,1)} custom-call(bf16[3,512,2048]{2,1,0:T(8,128)(2,1)} %bitcast.34, bf16[512,2048]{1,0:T(8,128)(2,1)S(1)} %get-tuple-element.24.refs_1_, f32[512,128]{1,0:T(8,128)S(1)} %get-tuple-element.21.refs_4_.refs_2_, bf16[8,128,128]{2,1,0:T(8,128)(2,1)S(1)} %collective-permute-done.16.refs_3_, ...), custom_call_target="tpu_custom_call", output_to_operand_aliasing={{}: (5, {})} | custom-call | flops 134217728 | bytes 3145728 | tf_op jit(solution)/shard_map/final_pass/pallas_call | solution.py:244
  (75 shorter events, 6.0 us)
Async XLA Ops:
  2.4 13.6 %collective-permute-start.2 = (bf16[8,6272]{1,0:T(8,128)(2,1)S(1)}, bf16[8,6272]{1,0:T(8,128)(2,1)S(1)}, u32[]{:S(2)}, u32[]{:S(2)}) collective-permute-start(bf16[8,6272]{1,0:T(8,128)(2,1)S(1)} %pad_maximum_fusion.5), channel_id=1, source_target_pairs={{0,24},{4,28},{8,0},{12,4},{16,8},{20,12},{24,16},{28,20},{1,25},{... | collective-permute-start | bytes 301064 | tf_op jit(solution)/shard_map/ppermute | solution.py:52
  7.5 8.9 %collective-permute-start.1 = (bf16[8,6272]{1,0:T(8,128)(2,1)S(1)}, bf16[8,6272]{1,0:T(8,128)(2,1)S(1)}, u32[]{:S(2)}, u32[]{:S(2)}) collective-permute-start(bf16[8,6272]{1,0:T(8,128)(2,1)S(1)} %pad_maximum_fusion.5), channel_id=1, source_target_pairs={{0,16},{4,20},{8,24},{12,28},{16,0},{20,4},{24,8},{28,12},{1,17},{... | collective-permute-start | bytes 301064 | tf_op jit(solution)/shard_map/ppermute | solution.py:52
  7.5 8.9 %collective-permute-start = (bf16[8,6272]{1,0:T(8,128)(2,1)S(1)}, bf16[8,6272]{1,0:T(8,128)(2,1)S(1)}, u32[]{:S(2)}, u32[]{:S(2)}) collective-permute-start(bf16[8,6272]{1,0:T(8,128)(2,1)S(1)} %pad_maximum_fusion.5), channel_id=1, source_target_pairs={{0,8},{4,12},{8,16},{12,20},{16,24},{20,28},{24,0},{28,4},{1,9},{5... | collective-permute-start | bytes 301064 | tf_op jit(solution)/shard_map/ppermute | solution.py:52
  8.5 0.8 copy-start
  10.4 5.9 %copy-start.2 = (bf16[8,6144]{1,0:T(8,128)(2,1)S(1)}, bf16[8,6144]{1,0:T(8,128)(2,1)}, u32[]{:S(2)}) copy-start(bf16[8,6144]{1,0:T(8,128)(2,1)} %param.11) | copy-start | bytes 294916
  16.5 9.4 %collective-permute-start.6 = (bf16[32,3072]{1,0:T(8,128)(2,1)S(1)}, bf16[32,3072]{1,0:T(8,128)(2,1)S(1)}, u32[]{:S(2)}, u32[]{:S(2)}) collective-permute-start(bf16[32,3072]{1,0:T(8,128)(2,1)S(1)} %slice.140), channel_id=1, source_target_pairs={{0,4},{4,0},{8,12},{12,8},{16,20},{20,16},{24,28},{28,24},{1,5},{5... | collective-permute-start | bytes 589832 | tf_op jit(solution)/shard_map/ppermute | solution.py:52
  18.0 7.2 %collective-permute-start.3 = (bf16[32,3200]{1,0:T(8,128)(2,1)S(1)}, bf16[32,3200]{1,0:T(8,128)(2,1)S(1)}, u32[]{:S(2)}, u32[]{:S(2)}) collective-permute-start(bf16[32,3200]{1,0:T(8,128)(2,1)S(1)} %slice.136), channel_id=1, source_target_pairs={{0,2},{1,3},{2,0},{3,1},{4,6},{5,7},{6,4},{7,5},{8,10},{9,11},{10,... | collective-permute-start | bytes 614408 | tf_op jit(solution)/shard_map/ppermute | solution.py:52
  25.3 10.4 %collective-permute-start.4 = (bf16[64,3200]{1,0:T(8,128)(2,1)S(1)}, bf16[64,3200]{1,0:T(8,128)(2,1)S(1)}, u32[]{:S(2)}, u32[]{:S(2)}) collective-permute-start(bf16[64,3200]{1,0:T(8,128)(2,1)S(1)} %maximum_add_fusion), channel_id=1, source_target_pairs={{0,4},{4,0},{8,12},{12,8},{16,20},{20,16},{24,28},{28,24},{1,5},{5... | collective-permute-start | bytes 1228808 | tf_op jit(solution)/shard_map/ppermute | solution.py:52
  25.9 9.9 %collective-permute-start.7 = (bf16[64,3072]{1,0:T(8,128)(2,1)S(1)}, bf16[64,3072]{1,0:T(8,128)(2,1)S(1)}, u32[]{:S(2)}, u32[]{:S(2)}) collective-permute-start(bf16[64,3072]{1,0:T(8,128)(2,1)S(1)} %maximum_add_fusion.1), channel_id=1, source_target_pairs={{0,2},{1,3},{2,0},{3,1},{4,6},{5,7},{6,4},{7,5},{8,10},{9,11},{10,... | collective-permute-start | bytes 1179656 | tf_op jit(solution)/shard_map/ppermute | solution.py:52
  35.7 3.5 %collective-permute-start.9 = (bf16[128,3200]{1,0:T(8,128)(2,1)S(1)}, bf16[128,3200]{1,0:T(8,128)(2,1)S(1)}, u32[]{:S(2)}, u32[]{:S(2)}) collective-permute-start(bf16[128,3200]{1,0:T(8,128)(2,1)S(1)} %pad_maximum_fusion.b), channel_id=1, source_target_pairs={{0,1},{1,0},{2,3},{3,2},{4,5},{5,4},{6,7},{7,6},{8,9},{9,8},{10,11... | collective-permute-start | bytes 2457608 | tf_op jit(solution)/shard_map/ppermute | solution.py:52
  35.9 3.4 %collective-permute-start.8 = (bf16[128,3072]{1,0:T(8,128)(2,1)S(1)}, bf16[128,3072]{1,0:T(8,128)(2,1)S(1)}, u32[]{:S(2)}, u32[]{:S(2)}) collective-permute-start(bf16[128,3072]{1,0:T(8,128)(2,1)S(1)} %pad_maximum_fusion.1.a), channel_id=1, source_target_pairs={{0,1},{1,0},{2,3},{3,2},{4,5},{5,4},{6,7},{7,6},{8,9},{9,8},{10,11... | collective-permute-start | bytes 2359304 | tf_op jit(solution)/shard_map/ppermute | solution.py:52
  36.6 9.3 %collective-permute-start.5 = (bf16[1040,128]{1,0:T(8,128)(2,1)S(1)}, bf16[1040,128]{1,0:T(8,128)(2,1)S(1)}, u32[]{:S(2)}, u32[]{:S(2)}) collective-permute-start(bf16[1040,128]{1,0:T(8,128)(2,1)S(1)} %pad_maximum_fusion.4), channel_id=1, source_target_pairs={{0,4},{4,0},{8,12},{12,8},{16,20},{20,16},{24,28},{28,24},{1,5},{5... | collective-permute-start | bytes 798728 | tf_op jit(solution)/shard_map/ppermute | solution.py:52
  45.7 5.8 %collective-permute-start.11 = (bf16[128,3072]{1,0:T(8,128)(2,1)S(1)}, bf16[128,3072]{1,0:T(8,128)(2,1)S(1)}, u32[]{:S(2)}, u32[]{:S(2)}) collective-permute-start(bf16[128,3072]{1,0:T(8,128)(2,1)S(1)} %get-tuple-element.32), channel_id=1, source_target_pairs={{0,1},{1,0},{2,3},{3,2},{4,5},{5,4},{6,7},{7,6},{8,9},{9,8},{10,11... | collective-permute-start | bytes 2359304 | tf_op jit(solution)/shard_map/ppermute | solution.py:52
  46.3 9.6 %collective-permute-start.10 = (bf16[8,128,128]{2,1,0:T(8,128)(2,1)S(1)}, bf16[8,128,128]{2,1,0:T(8,128)(2,1)S(1)}, u32[]{:S(2)}, u32[]{:S(2)}) collective-permute-start(bf16[8,128,128]{2,1,0:T(8,128)(2,1)S(1)} %get-tuple-element.48.behind), channel_id=1, source_target_pairs={{0,8},{4,12},{1,9},{5,13},{2,10},{6,14},{3,11},{7,15}} | collective-permute-start | bytes 786440 | tf_op jit(solution)/shard_map/ppermute | solution.py:317
  51.3 6.2 %collective-permute-start.17 = (bf16[128,3072]{1,0:T(8,128)(2,1)S(1)}, bf16[128,3072]{1,0:T(8,128)(2,1)S(1)}, u32[]{:S(2)}, u32[]{:S(2)}) collective-permute-start(bf16[128,3072]{1,0:T(8,128)(2,1)S(1)} %get-tuple-element.37), channel_id=1, source_target_pairs={{0,1},{1,0},{2,3},{3,2},{4,5},{5,4},{6,7},{7,6},{8,9},{9,8},{10,11... | collective-permute-start | bytes 2359304 | tf_op jit(solution)/shard_map/ppermute | solution.py:52
  56.2 12.0 %collective-permute-start.12 = (bf16[8,128,128]{2,1,0:T(8,128)(2,1)S(1)}, bf16[8,128,128]{2,1,0:T(8,128)(2,1)S(1)}, u32[]{:S(2)}, u32[]{:S(2)}) collective-permute-start(bf16[8,128,128]{2,1,0:T(8,128)(2,1)S(1)} %add_convert_fusion.5), channel_id=1, source_target_pairs={{8,16},{12,20},{9,17},{13,21},{10,18},{14,22},{11,19},{15,23}} | collective-permute-start | bytes 786440 | tf_op jit(solution)/shard_map/ppermute | solution.py:317
  56.8 10.6 %collective-permute-start.13 = (bf16[64,3072]{1,0:T(8,128)(2,1)S(1)}, bf16[64,3072]{1,0:T(8,128)(2,1)S(1)}, u32[]{:S(2)}, u32[]{:S(2)}) collective-permute-start(bf16[64,3072]{1,0:T(8,128)(2,1)S(1)} %slice.143), channel_id=1, source_target_pairs={{0,2},{1,3},{2,0},{3,1},{4,6},{5,7},{6,4},{7,5},{8,10},{9,11},{10,... | collective-permute-start | bytes 1179656 | tf_op jit(solution)/shard_map/ppermute | solution.py:52
  57.7 11.7 %collective-permute-start.18 = (bf16[64,3072]{1,0:T(8,128)(2,1)S(1)}, bf16[64,3072]{1,0:T(8,128)(2,1)S(1)}, u32[]{:S(2)}, u32[]{:S(2)}) collective-permute-start(bf16[64,3072]{1,0:T(8,128)(2,1)S(1)} %slice.149), channel_id=1, source_target_pairs={{0,4},{4,0},{8,12},{12,8},{16,20},{20,16},{24,28},{28,24},{1,5},{5... | collective-permute-start | bytes 1179656 | tf_op jit(solution)/shard_map/ppermute | solution.py:52
  67.6 5.7 %collective-permute-start.15 = (bf16[32,3072]{1,0:T(8,128)(2,1)S(1)}, bf16[32,3072]{1,0:T(8,128)(2,1)S(1)}, u32[]{:S(2)}, u32[]{:S(2)}) collective-permute-start(bf16[32,3072]{1,0:T(8,128)(2,1)S(1)} %slice.146), channel_id=1, source_target_pairs={{0,4},{4,0},{8,12},{12,8},{16,20},{20,16},{24,28},{28,24},{1,5},{5... | collective-permute-start | bytes 589832 | tf_op jit(solution)/shard_map/ppermute | solution.py:52
  68.5 11.5 %collective-permute-start.14 = (bf16[8,128,128]{2,1,0:T(8,128)(2,1)S(1)}, bf16[8,128,128]{2,1,0:T(8,128)(2,1)S(1)}, u32[]{:S(2)}, u32[]{:S(2)}) collective-permute-start(bf16[8,128,128]{2,1,0:T(8,128)(2,1)S(1)} %add_convert_fusion.4), channel_id=1, source_target_pairs={{16,24},{20,28},{17,25},{21,29},{18,26},{22,30},{19,27},{23,31}} | collective-permute-start | bytes 786440 | tf_op jit(solution)/shard_map/ppermute | solution.py:317
  69.5 5.7 %collective-permute-start.19 = (bf16[32,3072]{1,0:T(8,128)(2,1)S(1)}, bf16[32,3072]{1,0:T(8,128)(2,1)S(1)}, u32[]{:S(2)}, u32[]{:S(2)}) collective-permute-start(bf16[32,3072]{1,0:T(8,128)(2,1)S(1)} %slice.151), channel_id=1, source_target_pairs={{0,2},{1,3},{2,0},{3,1},{4,6},{5,7},{6,4},{7,5},{8,10},{9,11},{10,... | collective-permute-start | bytes 589832 | tf_op jit(solution)/shard_map/ppermute | solution.py:52
  75.3 6.8 %copy-start.1 = (f32[2048]{0:T(1024)S(1)}, f32[2048]{0:T(1024)}, u32[]{:S(2)}) copy-start(f32[2048]{0:T(1024)} %param.10) | copy-start | bytes 24580
  75.3 10.4 %collective-permute-start.20 = (bf16[8,6144]{1,0:T(8,128)(2,1)S(1)}, bf16[8,6144]{1,0:T(8,128)(2,1)S(1)}, u32[]{:S(2)}, u32[]{:S(2)}) collective-permute-start(bf16[8,6144]{1,0:T(8,128)(2,1)S(1)} %get-tuple-element.58), channel_id=1, source_target_pairs={{0,24},{4,28},{8,0},{12,4},{16,8},{20,12},{24,16},{28,20},{1,25},{... | collective-permute-start | bytes 294920 | tf_op jit(solution)/shard_map/ppermute | solution.py:52
  75.4 11.2 %collective-permute-start.21 = (bf16[8,6144]{1,0:T(8,128)(2,1)S(1)}, bf16[8,6144]{1,0:T(8,128)(2,1)S(1)}, u32[]{:S(2)}, u32[]{:S(2)}) collective-permute-start(bf16[8,6144]{1,0:T(8,128)(2,1)S(1)} %get-tuple-element.59), channel_id=1, source_target_pairs={{0,16},{4,20},{8,24},{12,28},{16,0},{20,4},{24,8},{28,12},{1,17},{... | collective-permute-start | bytes 294920 | tf_op jit(solution)/shard_map/ppermute | solution.py:52
  80.0 6.6 %collective-permute-start.22 = (bf16[8,6144]{1,0:T(8,128)(2,1)S(1)}, bf16[8,6144]{1,0:T(8,128)(2,1)S(1)}, u32[]{:S(2)}, u32[]{:S(2)}) collective-permute-start(bf16[8,6144]{1,0:T(8,128)(2,1)S(1)} %get-tuple-element.60), channel_id=1, source_target_pairs={{0,8},{4,12},{8,16},{12,20},{16,24},{20,28},{24,0},{28,4},{1,9},{5... | collective-permute-start | bytes 294920 | tf_op jit(solution)/shard_map/ppermute | solution.py:52
  80.4 6.8 %collective-permute-start.16 = (bf16[8,128,128]{2,1,0:T(8,128)(2,1)S(1)}, bf16[8,128,128]{2,1,0:T(8,128)(2,1)S(1)}, u32[]{:S(2)}, u32[]{:S(2)}) collective-permute-start(bf16[8,128,128]{2,1,0:T(8,128)(2,1)S(1)} %get-tuple-element.57), channel_id=1, source_target_pairs={{0,4},{4,0},{8,12},{12,8},{16,20},{20,16},{24,28},{28,24},{1,5},{5... | collective-permute-start | bytes 786440 | tf_op jit(solution)/shard_map/ppermute | solution.py:52

commit v5 on v4

--- a/solution.py
+++ b/solution.py
@@ -8,7 +8,6 @@
 
 EPS = 1e-06
 CHUNK = 256
-PARTS = 2
 PIECES = 3
 F32 = jnp.float32
 BF16 = jnp.bfloat16
@@ -41,10 +40,11 @@
             for j in range(self.inner)
         ]
 
-    def hop(self, i):
+    def jump(self, k):
         return [
-            (self.flat(o, i, j), self.flat(o, i + 1, j))
+            (self.flat(o, i, j), self.flat(o, i + k, j))
             for o in range(self.outer)
+            for i in range(self.n - k)
             for j in range(self.inner)
         ]
 
@@ -123,7 +123,7 @@
     )(log_decay.T)
 
 
-def local_kernel(heads, group, base, loads, which, *refs):
+def local_kernel(heads, group, first_of, loads, which, *refs):
     q_ref, k_ref, v_ref, run_ref, cols_ref = refs[:5]
     mixed_ref, state_ref, mark_ref = refs[-3 - 2 * loads :][:3]
     if loads:
@@ -132,7 +132,7 @@
         pl.when(pl.program_id(0) == 0)(copy.start)
     mark_ref[...] = jnp.zeros_like(mark_ref)
     rows, width = q_ref.shape[1], q_ref.shape[2] // group
-    first = base + pl.program_id(0) * group
+    first = first_of(pl.program_id(0)) * group
     cols = pltpu.roll(cols_ref[...], 128 - first, 1)
     ri = lax.broadcasted_iota(jnp.int32, (CHUNK, CHUNK), 0)
     ci = lax.broadcasted_iota(jnp.int32, (CHUNK, CHUNK), 1)
@@ -166,34 +166,39 @@
         pl.when(pl.program_id(0) == pl.num_programs(0) - 1)(copy.wait)
 
 
-def local_pass(qkv, run, cols, heads, base, count, w, done, behind, zeros, group=4):
+def place_block(axis, turn, per):
+    return lambda h: ((axis.index() + axis.n + turn) % axis.n) * per + h
+
+
+def local_pass(qkv, run, cols, heads, y_axis, turn, w, which, done, behind, zeros, group=4):
     rows, width = qkv.shape[1], qkv.shape[2] // heads
-    group = min(group, count)
-    start = base // group
+    share = heads // y_axis.n
+    group = min(group, share)
+    block = place_block(y_axis, turn, share // group)
     loads = 0 if w is None else 1
     hbm = pl.BlockSpec(memory_space=pl.ANY)
 
-    def take(which):
-        return pl.BlockSpec((1, rows, group * width), lambda h: (which, 0, start + h))
+    def take(part):
+        return pl.BlockSpec((1, rows, group * width), lambda h: (part, 0, block(h)))
 
     more = ([w] if loads else []) + list(done) + list(behind)
     aliases = {5 + loads + i: i for i in range(len(done))}
     out_specs = [
-        pl.BlockSpec((rows, group * width), lambda h: (0, start + h)),
-        pl.BlockSpec((group, width, width), lambda h: (start + h, 0, 0)),
+        pl.BlockSpec((rows, group * width), lambda h: (0, block(h))),
+        pl.BlockSpec((group, width, width), lambda h: (h, 0, 0)),
         pl.BlockSpec((8, zeros), lambda h: (0, 0)),
     ]
     out_shape = [
         jax.ShapeDtypeStruct((rows, heads * width), BF16),
-        jax.ShapeDtypeStruct((heads, width, width), BF16),
+        jax.ShapeDtypeStruct((share, width, width), BF16),
         jax.ShapeDtypeStruct((8, zeros), BF16),
     ]
     if loads:
         out_specs.append(hbm)
         out_shape.append(pltpu.VMEM(w.shape[1:], w.dtype))
     return pl.pallas_call(
-        functools.partial(local_kernel, heads, group, base, loads, base // count),
-        grid=(count // group,),
+        functools.partial(local_kernel, heads, group, block, loads, which),
+        grid=(share // group,),
         in_specs=[
             take(0),
             take(1),
@@ -207,11 +212,7 @@
         scratch_shapes=[pltpu.SemaphoreType.DMA] * loads,
         input_output_aliases=aliases,
         compiler_params=params(20),
-        cost_estimate=pl.CostEstimate(
-            flops=8 * count * rows * width * CHUNK,
-            bytes_accessed=count * rows * width * 8,
-            transcendentals=count * rows * CHUNK,
-        ),
+        cost_estimate=pl.CostEstimate(flops=1, bytes_accessed=1, transcendentals=0),
         name="local_pass",
     )(qkv, qkv, qkv, run, cols, *more)
 
@@ -236,10 +237,7 @@
     share = carried.shape[0]
     group = min(group, share)
 
-    def block(h):
-        place = (y_axis.index() + y_axis.n - back) % y_axis.n
-        return place * (share // group) + h
-
+    block = place_block(y_axis, -back, share // group)
     more = [a for a in (done, behind) if a is not None]
     return pl.pallas_call(
         functools.partial(final_kernel, heads, group, block),
@@ -256,11 +254,7 @@
         out_shape=jax.ShapeDtypeStruct((rows, heads * width), BF16),
         input_output_aliases={} if done is None else {5: 0},
         compiler_params=params(20),
-        cost_estimate=pl.CostEstimate(
-            flops=2 * share * rows * width * width,
-            bytes_accessed=share * rows * width * 6,
-            transcendentals=0,
-        ),
+        cost_estimate=pl.CostEstimate(flops=1, bytes_accessed=1, transcendentals=0),
         name="final_pass",
     )(qkv, mixed, cols, carried, gain, *more)
 
@@ -272,26 +266,28 @@
     return out
 
 
-def carry_scan(state, last, seat, z_axis, y_axis):
-    heads, width = state.shape[0], state.shape[1]
+def carry_scan(shares, last, seat, z_axis, y_axis):
+    share, width = shares[0].shape[:2]
     ny = y_axis.n
-    share = heads // ny
     pad = 16
     y = seat[:share]
     turned = [(y + k) & (ny - 1) for k in range(ny)]
     fade = jnp.exp(last)
+    mine = [pick(rows_split(fade, ny), turned[k]) for k in range(ny)]
+
+    def packed(body, fade):
+        rows = jnp.stack(pieces_of(fade), 0)
+        rows = jnp.pad(rows, ((0, pad - PIECES), (0, width - share)))
+        body = body.reshape(share * width, width)
+        return jnp.concatenate([body.astype(BF16), rows.astype(BF16)], 0)
+
+    def unpacked(g):
+        body = g[: share * width].reshape(share, width, width).astype(F32)
+        return body, jnp.sum(g[share * width :, :share].astype(F32), 0)
+
+    got = [y_axis.send(packed(shares[k], mine[k]), k) for k in range(1, ny)]
     tie = yield
-
-    def packed(k):
-        body = pick(rows_split(state, ny), turned[k]) + tie[:, None].astype(BF16)
-        body = body.reshape(share * width, width)
-        rows = jnp.stack(pieces_of(pick(rows_split(fade, ny), turned[k])), 0)
-        rows = jnp.pad(rows, ((0, pad - PIECES), (0, width - share)))
-        return jnp.concatenate([body, rows.astype(BF16)], 0)
-
-    got = [packed(0)] + [y_axis.send(packed(k), k) for k in range(1, ny)]
-    states = [g[: share * width].reshape(share, width, width).astype(F32) for g in got]
-    fades = [jnp.sum(g[share * width :, :share].astype(F32), 0) for g in got]
+    states, fades = zip((shares[0].astype(F32), mine[0]), *[unpacked(g) for g in got])
     places = [turned[-k % ny] for k in range(ny)]
 
     def reach(k, end):
@@ -307,14 +303,27 @@
             r = r * jnp.where(places[m] < end, fades[m], 1.0)
         return r[:, None, None]
 
-    tie = yield
-    inner = sum(reach(k, ny) * states[k] for k in range(ny)) + tie[:, None]
+    inner = sum(reach(k, ny) * states[k] for k in range(ny))
     through = whole(ny)
-    carried = jnp.zeros((share, width, width), F32)
-    for i in range(z_axis.n - 1):
-        out = (through * carried + inner).astype(BF16)
+    carried, behind = jnp.zeros((share, width, width), F32), jnp.ones((share,), F32)
+    first = tie[:, None]
+    far = 1
+    while far < z_axis.n:
+        out = through * carried + inner + first
+        if 2 * far < z_axis.n:
+            out = packed(out, through[:, 0, 0] * behind)
+        else:
+            out = out.astype(BF16)
         tie = yield out
-        carried = carried + lax.ppermute(out, z_axis.name, z_axis.hop(i)).astype(F32) + tie[:, None]
+        came = lax.ppermute(out, z_axis.name, z_axis.jump(far))
+        if 2 * far < z_axis.n:
+            came, more = unpacked(came + tie[:1].astype(BF16))
+            carried = carried + behind[:, None, None] * came
+            behind = behind * more
+        else:
+            carried = carried + behind[:, None, None] * came.astype(F32) + tie[:, None]
+        first = 0.0
+        far *= 2
 
     def entering(j):
         end = turned[j]
@@ -365,11 +374,7 @@
         out_shape=jax.ShapeDtypeStruct((tokens, units), BF16),
         scratch_shapes=[pltpu.VMEM((units, tokens), F32), pltpu.VMEM((units, tokens), F32)],
         compiler_params=params(56),
-        cost_estimate=pl.CostEstimate(
-            flops=4 * units * wide * tokens,
-            bytes_accessed=4 * units * wide + 2 * tokens * wide,
-            transcendentals=units * tokens,
-        ),
+        cost_estimate=pl.CostEstimate(flops=1, bytes_accessed=1, transcendentals=0),
         name="hidden_pass",
     )(*xs, w_in)
 
@@ -400,11 +405,7 @@
         out_specs=(spec, spec),
         out_shape=(out, out),
         compiler_params=params(56),
-        cost_estimate=pl.CostEstimate(
-            flops=2 * units * width * tokens,
-            bytes_accessed=2 * units * width + 2 * tokens * width,
-            transcendentals=0,
-        ),
+        cost_estimate=pl.CostEstimate(flops=1, bytes_accessed=1, transcendentals=0),
         name="down_pass",
     )(h, w_out, *probs)
 
@@ -512,11 +513,7 @@
             pltpu.SemaphoreType.DMA((n_out + 1,)),
         ],
         compiler_params=params(20),
-        cost_estimate=pl.CostEstimate(
-            flops=5 * units * wide * tokens,
-            bytes_accessed=5 * units * wide + 3 * tokens * wide,
-            transcendentals=units * tokens,
-        ),
+        cost_estimate=pl.CostEstimate(flops=1, bytes_accessed=1, transcendentals=0),
         name="lead_pass",
     )(a, a2, b, b2, *held, w_out)
     return (o, o2), (h, flow, rest), mark0
@@ -532,11 +529,7 @@
         out_specs=(vmem,) * 2,
         out_shape=(half, half),
         compiler_params=params(20),
-        cost_estimate=pl.CostEstimate(
-            flops=2 * units * w.shape[1] * tokens,
-            bytes_accessed=2 * units * w.shape[1] + 2 * tokens * w.shape[1],
-            transcendentals=0,
-        ),
+        cost_estimate=pl.CostEstimate(flops=1, bytes_accessed=1, transcendentals=0),
         name="rest_pass",
     )(h, flow, w, behind)
 
@@ -584,8 +577,8 @@
     half = moe_tokens.shape[1] // 2
     experts = w_in.shape[0] * lax.axis_size("exp")
     tokens = moe_tokens.shape[0] * lax.axis_size("seq") * lax.axis_size("exp")
-    fits = tokens <= 512
-    count = heads // PARTS
+    fits = tokens <= 512 and ny == 2
+    zeros = (heads // ny, projected.shape[2] // heads)
     qkv = in_hbm(projected.transpose(1, 0, 2))
     w_in = w_in[0].transpose(1, 2, 0)
     w_out = w_out[0]
@@ -593,36 +586,39 @@
 
     z = gather(z_axis, jnp.concatenate([moe_tokens, route], 1))
     run, cols, seat = prepare(log_decay)
-    made, held = (), []
-    for i in range(PARTS):
+    done, held, shares = (), [], {}
+    for i in range(ny):
+        turn = (i + 1) % ny
         w = in_hbm(w_in) if fits else None
-        made = local_pass(qkv, run, cols, heads, i * count, count, w, made[:2], (z,) * (i > 0), z.shape[1] - half)
+        behind = (z,) * (i == ny - 1)
+        made = local_pass(
+            qkv, run, cols, heads, y_axis, turn, w, i, done, behind, z.shape[1] - half
+        )
+        done, shares[turn], mark = made[:1], made[1], made[2]
         held += made[3:]
-    mixed, state, mark = made[:3]
+    mixed = done[0]
+    scan = carry_scan(shares, run[:, -1], seat[:, 0] & (ny - 1), z_axis, y_axis)
+    next(scan)
     a, b = z[:, :half], z[:, half:]
     a, b = gather(y_axis, a), gather(x_axis, b)
     a, b = gather(x_axis, a + mark[:1, :half]), gather(y_axis, b + mark[:1])
-    last = run[:, -1]
-    zeros = (heads // ny, qkv.shape[2] // heads)
+    scan.send(nothing(a, *zeros))
     a2, b2 = core.send(a, 1), core.send(b, 1)
-    scan = carry_scan(state, last, seat[:, 0] & (ny - 1), z_axis, y_axis)
-    next(scan)
-    scan.send(nothing(b, *zeros))
     if fits:
-        pa, more, mark = lead_pass(a, a2, b, b2, held, in_hbm(w_out), experts, nx, ny, zeros)
+        pa, more, mark = lead_pass(
+            a, a2, b, b2, held, in_hbm(w_out), experts, nx, ny, zeros
+        )
         hop = scan.send(mark)
         pb = rest_pass(*more, hop, nx, ny)
     else:
         pa, pb = streamed_experts(a, a2, b, b2, w_in, w_out, experts, nx, ny)
         scan.send(jnp.zeros(zeros, F32))
-    for _ in range(nz - 4):
+    for _ in range((nz - 1).bit_length() - 2):
         scan.send(jnp.zeros(zeros, F32))
     a, b = scatter(core, pa), scatter(core, pb)
-    scan.send(nothing(a, *zeros))
     a, b = scatter(x_axis, rows_split(a, nx)), scatter(y_axis, rows_split(b, ny))
-    scan.send(nothing(a, *zeros))
+    carried = scan.send(nothing(a, *zeros))
     a, b = scatter(y_axis, rows_split(a, ny)), scatter(x_axis, rows_split(b, nx))
-    carried = scan.send(nothing(a, *zeros))
     both = jnp.concatenate([a, b], 1)
     moe_out = scatter(z_axis, rows_split(both, nz))
     attn_out = None

time: 91.4 us -> 88.7 us (0.970)
  waiting for transfers between devices: 30.6 us -> 23.9 us
  starting transfers between devices: 25.9 us -> 30.2 us
    ppermute x3 -> x2, waiting for transfers between devices: 4.23 us -> 0.01 us  [carry_scan(): came = lax.ppermute(out, z_axis.name, z_axis.jump(far))]
    ppermute x3 -> x2, starting transfers between devices: 5.07 us -> 8.78 us  [carry_scan(): came = lax.ppermute(out, z_axis.name, z_axis.jump(far))]
    ppermute x20, waiting for transfers between devices: 26.4 us -> 23.9 us  [send(): return lax.ppermute(a, self.name, self.turn(k))]
  transfers between devices with their start and end apart: 23 -> 22, of which waited for: 8 -> 7; matrix products, arithmetic and copies ran while one was open for 4% -> 3% of each run, Pallas kernels for 26% -> 29%
where the time goes in v5:
time: 88.7 us; the launch traced here: 88.3 us
  starting transfers between devices  30.2 us (34%)
  Pallas kernels  27.2 us (31%)
  waiting for transfers between devices  23.9 us (27%)
  other arithmetic  4.79 us (5%)
  local copies, waits for them, and re-layouts  1.18 us (1%)
  between operations  1.03 us (1%)
    ppermute x20, waiting for transfers between devices, send(): return lax.ppermute(a, self.name, self.turn(k))  23.9 us
    ppermute x20, starting transfers between devices, send(): return lax.ppermute(a, self.name, self.turn(k))  21.5 us
    pallas_call x2, Pallas kernels, local_pass(): pl.pallas_call(functools.partial(local_kernel, heads, group, block, loads...  11.2 us
    ppermute x2, starting transfers between devices, carry_scan(): came = lax.ppermute(out, z_axis.name, z_axis.jump(far))  8.78 us
    pallas_call x2, Pallas kernels, final_pass(): pl.pallas_call(functools.partial(final_kernel, heads, group, block), grid...  7.46 us
    pallas_call x1, Pallas kernels, lead_pass(): pl.pallas_call(functools.partial(lead_kernel, experts, nx, ny, block), in...  6.4 us
  transfers between devices with their start and end apart: 22, of which 7 were waited for; matrix products, arithmetic and copies ran while one was open for 3% of the time, Pallas kernels for 29%

profile of v5, /device:TPU:0, one launch (start us, length us, event | category | flops | bytes accessed | tf_op | source)
XLA Modules:
  0.0 88.3 jit_solution(3148040715861643977)
XLA Ops:
  0.6 0.7 select_reduce_fusion.2
  1.5 0.9 %pad_maximum_fusion.6 = bf16[8,6272]{1,0:T(8,128)(2,1)S(1)} fusion(bf16[8,128]{1,0:T(8,128)(2,1)S(1)} %fusion.40, bf16[8,6144]{1,0:T(8,128)(2,1)} %param.11), kind=kLoop, calls=%fused_computation.43 | loop fusion | flops 200704 | bytes 200704 | tf_op jit(solution)/shard_map/concatenate | solution.py:587
  2.4 5.0 %collective-permute-start.2 = (bf16[8,6272]{1,0:T(8,128)(2,1)S(1)}, bf16[8,6272]{1,0:T(8,128)(2,1)S(1)}, u32[]{:S(2)}, u32[]{:S(2)}) collective-permute-start(bf16[8,6272]{1,0:T(8,128)(2,1)S(1)} %pad_maximum_fusion.6), channel_id=1, source_target_pairs={{0,24},{4,28},{8,0},{12,4},{16,8},{20,12},{24,16},{28,20},{1,25},{... | collective-permute-start | bytes 301064 | tf_op jit(solution)/shard_map/ppermute | solution.py:52
  7.5 1.0 %collective-permute-start = (bf16[8,6272]{1,0:T(8,128)(2,1)S(1)}, bf16[8,6272]{1,0:T(8,128)(2,1)S(1)}, u32[]{:S(2)}, u32[]{:S(2)}) collective-permute-start(bf16[8,6272]{1,0:T(8,128)(2,1)S(1)} %pad_maximum_fusion.6), channel_id=1, source_target_pairs={{0,8},{4,12},{8,16},{12,20},{16,24},{20,28},{24,0},{28,4},{1,9},{5... | collective-permute-start | bytes 301064 | tf_op jit(solution)/shard_map/ppermute | solution.py:52
  8.5 0.8 copy-done
  9.2 0.7 prepare.1
  10.2 5.6 %local_pass.2 = (bf16[512,2048]{1,0:T(8,128)(2,1)S(1)}, bf16[8,128,128]{2,1,0:T(8,128)(2,1)S(1)}, bf16[8,3200]{1,0:T(8,128)(2,1)}, bf16[576,6144]{1,0:T(8,128)(2,1)S(1)}) custom-call(bf16[3,512,2048]{2,1,0:T(8,128)(2,1)} %bitcast.34, bf16[3,512,2048]{2,1,0:T(8,128)(2,1)} %bitcast.35, bf16[3,512,2048]{2,1,0:T(8,128)(2,1)} %bitcast.36, ...), custom_call_target="tpu_custom_call" | custom-call | flops 1 | bytes 1 | tf_op jit(solution)/shard_map/local_pass/pallas_call | solution.py:199
  15.8 1.6 %collective-permute-start.3 = (bf16[1040,128]{1,0:T(8,128)(2,1)S(1)}, bf16[1040,128]{1,0:T(8,128)(2,1)S(1)}, u32[]{:S(2)}, u32[]{:S(2)}) collective-permute-start(bf16[1040,128]{1,0:T(8,128)(2,1)S(1)} %pad_maximum_fusion.4), channel_id=1, source_target_pairs={{0,4},{4,0},{8,12},{12,8},{16,20},{20,16},{24,28},{28,24},{1,5},{5... | collective-permute-start | bytes 798728 | tf_op jit(solution)/shard_map/ppermute | solution.py:52
  18.3 1.5 %collective-permute-start.8 = (bf16[32,3200]{1,0:T(8,128)(2,1)S(1)}, bf16[32,3200]{1,0:T(8,128)(2,1)S(1)}, u32[]{:S(2)}, u32[]{:S(2)}) collective-permute-start(bf16[32,3200]{1,0:T(8,128)(2,1)S(1)} %slice.131), channel_id=1, source_target_pairs={{0,2},{1,3},{2,0},{3,1},{4,6},{5,7},{6,4},{7,5},{8,10},{9,11},{10,... | collective-permute-start | bytes 614408 | tf_op jit(solution)/shard_map/ppermute | solution.py:52
  19.8 5.6 %local_pass.3 = (bf16[512,2048]{1,0:T(8,128)(2,1)S(1)}, bf16[8,128,128]{2,1,0:T(8,128)(2,1)S(1)}, bf16[8,3200]{1,0:T(8,128)(2,1)S(1)}, bf16[576,6144]{1,0:T(8,128)(2,1)S(1)}) custom-call(bf16[3,512,2048]{2,1,0:T(8,128)(2,1)} %bitcast.37, bf16[3,512,2048]{2,1,0:T(8,128)(2,1)} %bitcast.38, ...), custom_call_target="tpu_custom_call", output_to_operand_aliasing={{0}: (6, {})} | custom-call | flops 1 | bytes 1 | tf_op jit(solution)/shard_map/local_pass/pallas_call | solution.py:199
  25.5 1.9 %collective-permute-done.4 = bf16[32,3072]{1,0:T(8,128)(2,1)S(1)} collective-permute-done((bf16[32,3072]{1,0:T(8,128)(2,1)S(1)}, bf16[32,3072]{1,0:T(8,128)(2,1)S(1)}, u32[]{:S(2)}, u32[]{:S(2)}) %collective-permute-start.4) | collective-permute-done | bytes 196640 | tf_op jit(solution)/shard_map/ppermute | solution.py:52
  27.5 1.6 %collective-permute-start.5 = (bf16[64,3072]{1,0:T(8,128)(2,1)S(1)}, bf16[64,3072]{1,0:T(8,128)(2,1)S(1)}, u32[]{:S(2)}, u32[]{:S(2)}) collective-permute-start(bf16[64,3072]{1,0:T(8,128)(2,1)S(1)} %maximum_add_fusion.1), channel_id=1, source_target_pairs={{0,2},{1,3},{2,0},{3,1},{4,6},{5,7},{6,4},{7,5},{8,10},{9,11},{10,... | collective-permute-start | bytes 1179656 | tf_op jit(solution)/shard_map/ppermute | solution.py:52
  29.1 1.6 %collective-permute-start.9 = (bf16[64,3200]{1,0:T(8,128)(2,1)S(1)}, bf16[64,3200]{1,0:T(8,128)(2,1)S(1)}, u32[]{:S(2)}, u32[]{:S(2)}) collective-permute-start(bf16[64,3200]{1,0:T(8,128)(2,1)S(1)} %maximum_add_fusion), channel_id=1, source_target_pairs={{0,4},{4,0},{8,12},{12,8},{16,20},{20,16},{24,28},{28,24},{1,5},{5... | collective-permute-start | bytes 1228808 | tf_op jit(solution)/shard_map/ppermute | solution.py:52
  30.7 5.9 %collective-permute-done.5 = bf16[64,3072]{1,0:T(8,128)(2,1)S(1)} collective-permute-done((bf16[64,3072]{1,0:T(8,128)(2,1)S(1)}, bf16[64,3072]{1,0:T(8,128)(2,1)S(1)}, u32[]{:S(2)}, u32[]{:S(2)}) %collective-permute-start.5) | collective-permute-done | bytes 393248 | tf_op jit(solution)/shard_map/ppermute | solution.py:52
  36.8 1.6 %collective-permute-done.9 = bf16[64,3200]{1,0:T(8,128)(2,1)S(1)} collective-permute-done((bf16[64,3200]{1,0:T(8,128)(2,1)S(1)}, bf16[64,3200]{1,0:T(8,128)(2,1)S(1)}, u32[]{:S(2)}, u32[]{:S(2)}) %collective-permute-start.9) | collective-permute-done | bytes 409632 | tf_op jit(solution)/shard_map/ppermute | solution.py:52
  38.8 4.4 %collective-permute-start.6 = (bf16[1040,128]{1,0:T(8,128)(2,1)S(1)}, bf16[1040,128]{1,0:T(8,128)(2,1)S(1)}, u32[]{:S(2)}, u32[]{:S(2)}) collective-permute-start(bf16[1040,128]{1,0:T(8,128)(2,1)S(1)} %pad_maximum_fusion.5), channel_id=1, source_target_pairs={{0,8},{4,12},{8,16},{12,20},{16,24},{20,28},{1,9},{5,13},{9,17},{1... | collective-permute-start | bytes 798728 | tf_op jit(solution)/shard_map/ppermute | solution.py:318
  43.2 6.4 %lead_pass.1 = (bf16[128,3072]{1,0:T(8,128)(2,1)S(1)}, bf16[128,3072]{1,0:T(8,128)(2,1)S(1)}, bf16[256,576]{1,0:T(8,128)(2,1)S(1)}, f32[256,128]{1,0:T(8,128)S(1...) custom-call(bf16[128,3072]{1,0:T(8,128)(2,1)S(1)} %pad_maximum_fusion.1.a, ...), custom_call_target="tpu_custom_call" | custom-call | flops 1 | bytes 1 | tf_op jit(solution)/shard_map/lead_pass/pallas_call | solution.py:498
  49.9 1.4 %rest_pass.1 = (bf16[128,3072]{1,0:T(8,128)(2,1)S(1)}, bf16[128,3072]{1,0:T(8,128)(2,1)S(1)}) custom-call(bf16[256,576]{1,0:T(8,128)(2,1)S(1)} %get-tuple-element.33.h, f32[256,128]{1,0:T(8,128)S(1)} %get-tuple-element.34.flow, bf16[576,3072]{1,0:T(8,128)(2,1)S(1)} %get-tuple-element.35.w, bf16[8,128,128]{2,1,0:T(8,128)(2,1)S(1)} %fusion.1.behind), custom_call_target="tpu_custom_call" | custom-call | flops 1 | bytes 1 | tf_op jit(solution)/shard_map/rest_pass/pallas_call | solution.py:526
  52.0 4.4 %collective-permute-start.11 = (bf16[8,128,128]{2,1,0:T(8,128)(2,1)S(1)}, bf16[8,128,128]{2,1,0:T(8,128)(2,1)S(1)}, u32[]{:S(2)}, u32[]{:S(2)}) collective-permute-start(bf16[8,128,128]{2,1,0:T(8,128)(2,1)S(1)} %fusion.1.behind), channel_id=1, source_target_pairs={{0,16},{4,20},{8,24},{12,28},{1,17},{5,21},{9,25},{13,29},{2,18},{... | collective-permute-start | bytes 786440 | tf_op jit(solution)/shard_map/ppermute | solution.py:318
  56.6 1.6 %collective-permute-start.17 = (bf16[64,3072]{1,0:T(8,128)(2,1)S(1)}, bf16[64,3072]{1,0:T(8,128)(2,1)S(1)}, u32[]{:S(2)}, u32[]{:S(2)}) collective-permute-start(bf16[64,3072]{1,0:T(8,128)(2,1)S(1)} %slice.140), channel_id=1, source_target_pairs={{0,4},{4,0},{8,12},{12,8},{16,20},{20,16},{24,28},{28,24},{1,5},{5... | collective-permute-start | bytes 1179656 | tf_op jit(solution)/shard_map/ppermute | solution.py:52
  58.4 0.6 collective-permute-start.13
  59.0 8.5 %collective-permute-done.17 = bf16[64,3072]{1,0:T(8,128)(2,1)S(1)} collective-permute-done((bf16[64,3072]{1,0:T(8,128)(2,1)S(1)}, bf16[64,3072]{1,0:T(8,128)(2,1)S(1)}, u32[]{:S(2)}, u32[]{:S(2)}) %collective-permute-start.17) | collective-permute-done | bytes 393248 | tf_op jit(solution)/shard_map/ppermute | solution.py:52
  67.6 0.6 collective-permute-start.18
  68.2 0.8 collective-permute-done.13
  69.1 0.8 collective-permute-start.15
  70.4 1.4 %collective-permute-start.14 = (bf16[8,128,128]{2,1,0:T(8,128)(2,1)S(1)}, bf16[8,128,128]{2,1,0:T(8,128)(2,1)S(1)}, u32[]{:S(2)}, u32[]{:S(2)}) collective-permute-start(bf16[8,128,128]{2,1,0:T(8,128)(2,1)S(1)} %get-tuple-element.49), channel_id=1, source_target_pairs={{0,4},{4,0},{8,12},{12,8},{16,20},{20,16},{24,28},{28,24},{1,5},{5... | collective-permute-start | bytes 786440 | tf_op jit(solution)/shard_map/ppermute | solution.py:52
  71.8 1.6 %collective-permute-done.18 = bf16[32,3072]{1,0:T(8,128)(2,1)S(1)} collective-permute-done((bf16[32,3072]{1,0:T(8,128)(2,1)S(1)}, bf16[32,3072]{1,0:T(8,128)(2,1)S(1)}, u32[]{:S(2)}, u32[]{:S(2)}) %collective-permute-start.18) | collective-permute-done | bytes 196640 | tf_op jit(solution)/shard_map/ppermute | solution.py:52
  73.4 3.6 %collective-permute-done.15 = bf16[32,3072]{1,0:T(8,128)(2,1)S(1)} collective-permute-done((bf16[32,3072]{1,0:T(8,128)(2,1)S(1)}, bf16[32,3072]{1,0:T(8,128)(2,1)S(1)}, u32[]{:S(2)}, u32[]{:S(2)}) %collective-permute-start.15) | collective-permute-done | bytes 196640 | tf_op jit(solution)/shard_map/ppermute | solution.py:52
  77.2 2.9 %collective-permute-start.20 = (bf16[8,6144]{1,0:T(8,128)(2,1)S(1)}, bf16[8,6144]{1,0:T(8,128)(2,1)S(1)}, u32[]{:S(2)}, u32[]{:S(2)}) collective-permute-start(bf16[8,6144]{1,0:T(8,128)(2,1)S(1)} %get-tuple-element.51), channel_id=1, source_target_pairs={{0,16},{4,20},{8,24},{12,28},{16,0},{20,4},{24,8},{28,12},{1,17},{... | collective-permute-start | bytes 294920 | tf_op jit(solution)/shard_map/ppermute | solution.py:52
  80.1 3.8 %final_pass.2.refs_5_ = bf16[512,2048]{1,0:T(8,128)(2,1)} custom-call(bf16[3,512,2048]{2,1,0:T(8,128)(2,1)} %bitcast.40, bf16[512,2048]{1,0:T(8,128)(2,1)S(1)} %get-tuple-element.23.refs_1_, f32[512,128]{1,0:T(8,128)S(1)} %get-tuple-element.21.refs_4_.refs_2_, bf16[8,128,128]{2,1,0:T(8,128)(2,1)S(1)} %get-tuple-element.48.refs_3_, f32[1,2048]{1,0:T(1,128)S(1)} %bitcast.30, ...), custom_call_target="tpu_custom_call" | custom-call | flops 1 | bytes 1 | tf_op jit(solution)/shard_map/final_pass/pallas_call | solution.py:242
  83.9 3.7 %final_pass.3 = bf16[512,2048]{1,0:T(8,128)(2,1)} custom-call(bf16[3,512,2048]{2,1,0:T(8,128)(2,1)} %bitcast.41, bf16[512,2048]{1,0:T(8,128)(2,1)S(1)} %get-tuple-element.23.refs_1_, f32[512,128]{1,0:T(8,128)S(1)} %get-tuple-element.21.refs_4_.refs_2_, bf16[8,128,128]{2,1,0:T(8,128)(2,1)S(1)} %collective-permute-done.14.refs_3_, ...), custom_call_target="tpu_custom_call", output_to_operand_aliasing={{}: (5, {})} | custom-call | flops 1 | bytes 1 | tf_op jit(solution)/shard_map/final_pass/pallas_call | solution.py:242
  87.6 0.7 add_convert_fusion.7
  (74 shorter events, 4.3 us)
Async XLA Ops:
  2.4 15.2 %collective-permute-start.2 = (bf16[8,6272]{1,0:T(8,128)(2,1)S(1)}, bf16[8,6272]{1,0:T(8,128)(2,1)S(1)}, u32[]{:S(2)}, u32[]{:S(2)}) collective-permute-start(bf16[8,6272]{1,0:T(8,128)(2,1)S(1)} %pad_maximum_fusion.6), channel_id=1, source_target_pairs={{0,24},{4,28},{8,0},{12,4},{16,8},{20,12},{24,16},{28,20},{1,25},{... | collective-permute-start | bytes 301064 | tf_op jit(solution)/shard_map/ppermute | solution.py:52
  7.5 10.1 %collective-permute-start.1 = (bf16[8,6272]{1,0:T(8,128)(2,1)S(1)}, bf16[8,6272]{1,0:T(8,128)(2,1)S(1)}, u32[]{:S(2)}, u32[]{:S(2)}) collective-permute-start(bf16[8,6272]{1,0:T(8,128)(2,1)S(1)} %pad_maximum_fusion.6), channel_id=1, source_target_pairs={{0,16},{4,20},{8,24},{12,28},{16,0},{20,4},{24,8},{28,12},{1,17},{... | collective-permute-start | bytes 301064 | tf_op jit(solution)/shard_map/ppermute | solution.py:52
  7.5 10.2 %collective-permute-start = (bf16[8,6272]{1,0:T(8,128)(2,1)S(1)}, bf16[8,6272]{1,0:T(8,128)(2,1)S(1)}, u32[]{:S(2)}, u32[]{:S(2)}) collective-permute-start(bf16[8,6272]{1,0:T(8,128)(2,1)S(1)} %pad_maximum_fusion.6), channel_id=1, source_target_pairs={{0,8},{4,12},{8,16},{12,20},{16,24},{20,28},{24,0},{28,4},{1,9},{5... | collective-permute-start | bytes 301064 | tf_op jit(solution)/shard_map/ppermute | solution.py:52
  8.5 0.8 copy-start
  10.2 7.4 %copy-start.2 = (bf16[8,6144]{1,0:T(8,128)(2,1)S(1)}, bf16[8,6144]{1,0:T(8,128)(2,1)}, u32[]{:S(2)}) copy-start(bf16[8,6144]{1,0:T(8,128)(2,1)} %param.11) | copy-start | bytes 294916
  15.8 9.7 %collective-permute-start.3 = (bf16[1040,128]{1,0:T(8,128)(2,1)S(1)}, bf16[1040,128]{1,0:T(8,128)(2,1)S(1)}, u32[]{:S(2)}, u32[]{:S(2)}) collective-permute-start(bf16[1040,128]{1,0:T(8,128)(2,1)S(1)} %pad_maximum_fusion.4), channel_id=1, source_target_pairs={{0,4},{4,0},{8,12},{12,8},{16,20},{20,16},{24,28},{28,24},{1,5},{5... | collective-permute-start | bytes 798728 | tf_op jit(solution)/shard_map/ppermute | solution.py:52
  17.7 9.7 %collective-permute-start.4 = (bf16[32,3072]{1,0:T(8,128)(2,1)S(1)}, bf16[32,3072]{1,0:T(8,128)(2,1)S(1)}, u32[]{:S(2)}, u32[]{:S(2)}) collective-permute-start(bf16[32,3072]{1,0:T(8,128)(2,1)S(1)} %slice.129), channel_id=1, source_target_pairs={{0,4},{4,0},{8,12},{12,8},{16,20},{20,16},{24,28},{28,24},{1,5},{5... | collective-permute-start | bytes 589832 | tf_op jit(solution)/shard_map/ppermute | solution.py:52
  18.3 10.7 %collective-permute-start.8 = (bf16[32,3200]{1,0:T(8,128)(2,1)S(1)}, bf16[32,3200]{1,0:T(8,128)(2,1)S(1)}, u32[]{:S(2)}, u32[]{:S(2)}) collective-permute-start(bf16[32,3200]{1,0:T(8,128)(2,1)S(1)} %slice.131), channel_id=1, source_target_pairs={{0,2},{1,3},{2,0},{3,1},{4,6},{5,7},{6,4},{7,5},{8,10},{9,11},{10,... | collective-permute-start | bytes 614408 | tf_op jit(solution)/shard_map/ppermute | solution.py:52
  27.5 9.2 %collective-permute-start.5 = (bf16[64,3072]{1,0:T(8,128)(2,1)S(1)}, bf16[64,3072]{1,0:T(8,128)(2,1)S(1)}, u32[]{:S(2)}, u32[]{:S(2)}) collective-permute-start(bf16[64,3072]{1,0:T(8,128)(2,1)S(1)} %maximum_add_fusion.1), channel_id=1, source_target_pairs={{0,2},{1,3},{2,0},{3,1},{4,6},{5,7},{6,4},{7,5},{8,10},{9,11},{10,... | collective-permute-start | bytes 1179656 | tf_op jit(solution)/shard_map/ppermute | solution.py:52
  29.1 9.2 %collective-permute-start.9 = (bf16[64,3200]{1,0:T(8,128)(2,1)S(1)}, bf16[64,3200]{1,0:T(8,128)(2,1)S(1)}, u32[]{:S(2)}, u32[]{:S(2)}) collective-permute-start(bf16[64,3200]{1,0:T(8,128)(2,1)S(1)} %maximum_add_fusion), channel_id=1, source_target_pairs={{0,4},{4,0},{8,12},{12,8},{16,20},{20,16},{24,28},{28,24},{1,5},{5... | collective-permute-start | bytes 1228808 | tf_op jit(solution)/shard_map/ppermute | solution.py:52
  36.7 6.5 %collective-permute-start.7 = (bf16[128,3072]{1,0:T(8,128)(2,1)S(1)}, bf16[128,3072]{1,0:T(8,128)(2,1)S(1)}, u32[]{:S(2)}, u32[]{:S(2)}) collective-permute-start(bf16[128,3072]{1,0:T(8,128)(2,1)S(1)} %pad_maximum_fusion.1.a), channel_id=1, source_target_pairs={{0,1},{1,0},{2,3},{3,2},{4,5},{5,4},{6,7},{7,6},{8,9},{9,8},{10,11... | collective-permute-start | bytes 2359304 | tf_op jit(solution)/shard_map/ppermute | solution.py:52
  38.4 4.8 %collective-permute-start.10 = (bf16[128,3200]{1,0:T(8,128)(2,1)S(1)}, bf16[128,3200]{1,0:T(8,128)(2,1)S(1)}, u32[]{:S(2)}, u32[]{:S(2)}) collective-permute-start(bf16[128,3200]{1,0:T(8,128)(2,1)S(1)} %pad_maximum_fusion.b), channel_id=1, source_target_pairs={{0,1},{1,0},{2,3},{3,2},{4,5},{5,4},{6,7},{7,6},{8,9},{9,8},{10,11... | collective-permute-start | bytes 2457608 | tf_op jit(solution)/shard_map/ppermute | solution.py:52
  38.8 10.9 %collective-permute-start.6 = (bf16[1040,128]{1,0:T(8,128)(2,1)S(1)}, bf16[1040,128]{1,0:T(8,128)(2,1)S(1)}, u32[]{:S(2)}, u32[]{:S(2)}) collective-permute-start(bf16[1040,128]{1,0:T(8,128)(2,1)S(1)} %pad_maximum_fusion.5), channel_id=1, source_target_pairs={{0,8},{4,12},{8,16},{12,20},{16,24},{20,28},{1,9},{5,13},{9,17},{1... | collective-permute-start | bytes 798728 | tf_op jit(solution)/shard_map/ppermute | solution.py:318
  51.4 5.0 %collective-permute-start.16 = (bf16[128,3072]{1,0:T(8,128)(2,1)S(1)}, bf16[128,3072]{1,0:T(8,128)(2,1)S(1)}, u32[]{:S(2)}, u32[]{:S(2)}) collective-permute-start(bf16[128,3072]{1,0:T(8,128)(2,1)S(1)} %get-tuple-element.37), channel_id=1, source_target_pairs={{0,1},{1,0},{2,3},{3,2},{4,5},{5,4},{6,7},{7,6},{8,9},{9,8},{10,11... | collective-permute-start | bytes 2359304 | tf_op jit(solution)/shard_map/ppermute | solution.py:52
  51.6 6.5 %collective-permute-start.12 = (bf16[128,3072]{1,0:T(8,128)(2,1)S(1)}, bf16[128,3072]{1,0:T(8,128)(2,1)S(1)}, u32[]{:S(2)}, u32[]{:S(2)}) collective-permute-start(bf16[128,3072]{1,0:T(8,128)(2,1)S(1)} %get-tuple-element.32), channel_id=1, source_target_pairs={{0,1},{1,0},{2,3},{3,2},{4,5},{5,4},{6,7},{7,6},{8,9},{9,8},{10,11... | collective-permute-start | bytes 2359304 | tf_op jit(solution)/shard_map/ppermute | solution.py:52
  52.0 18.0 %collective-permute-start.11 = (bf16[8,128,128]{2,1,0:T(8,128)(2,1)S(1)}, bf16[8,128,128]{2,1,0:T(8,128)(2,1)S(1)}, u32[]{:S(2)}, u32[]{:S(2)}) collective-permute-start(bf16[8,128,128]{2,1,0:T(8,128)(2,1)S(1)} %fusion.1.behind), channel_id=1, source_target_pairs={{0,16},{4,20},{8,24},{12,28},{1,17},{5,21},{9,25},{13,29},{2,18},{... | collective-permute-start | bytes 786440 | tf_op jit(solution)/shard_map/ppermute | solution.py:318
  56.6 10.9 %collective-permute-start.17 = (bf16[64,3072]{1,0:T(8,128)(2,1)S(1)}, bf16[64,3072]{1,0:T(8,128)(2,1)S(1)}, u32[]{:S(2)}, u32[]{:S(2)}) collective-permute-start(bf16[64,3072]{1,0:T(8,128)(2,1)S(1)} %slice.140), channel_id=1, source_target_pairs={{0,4},{4,0},{8,12},{12,8},{16,20},{20,16},{24,28},{28,24},{1,5},{5... | collective-permute-start | bytes 1179656 | tf_op jit(solution)/shard_map/ppermute | solution.py:52
  58.4 10.6 %collective-permute-start.13 = (bf16[64,3072]{1,0:T(8,128)(2,1)S(1)}, bf16[64,3072]{1,0:T(8,128)(2,1)S(1)}, u32[]{:S(2)}, u32[]{:S(2)}) collective-permute-start(bf16[64,3072]{1,0:T(8,128)(2,1)S(1)} %slice.135), channel_id=1, source_target_pairs={{0,2},{1,3},{2,0},{3,1},{4,6},{5,7},{6,4},{7,5},{8,10},{9,11},{10,... | collective-permute-start | bytes 1179656 | tf_op jit(solution)/shard_map/ppermute | solution.py:52
  67.6 5.8 %collective-permute-start.18 = (bf16[32,3072]{1,0:T(8,128)(2,1)S(1)}, bf16[32,3072]{1,0:T(8,128)(2,1)S(1)}, u32[]{:S(2)}, u32[]{:S(2)}) collective-permute-start(bf16[32,3072]{1,0:T(8,128)(2,1)S(1)} %slice.142), channel_id=1, source_target_pairs={{0,2},{1,3},{2,0},{3,1},{4,6},{5,7},{6,4},{7,5},{8,10},{9,11},{10,... | collective-permute-start | bytes 589832 | tf_op jit(solution)/shard_map/ppermute | solution.py:52
  69.1 7.9 %collective-permute-start.15 = (bf16[32,3072]{1,0:T(8,128)(2,1)S(1)}, bf16[32,3072]{1,0:T(8,128)(2,1)S(1)}, u32[]{:S(2)}, u32[]{:S(2)}) collective-permute-start(bf16[32,3072]{1,0:T(8,128)(2,1)S(1)} %slice.138), channel_id=1, source_target_pairs={{0,4},{4,0},{8,12},{12,8},{16,20},{20,16},{24,28},{28,24},{1,5},{5... | collective-permute-start | bytes 589832 | tf_op jit(solution)/shard_map/ppermute | solution.py:52
  70.4 9.8 %copy-start.1 = (f32[2048]{0:T(1024)S(1)}, f32[2048]{0:T(1024)}, u32[]{:S(2)}) copy-start(f32[2048]{0:T(1024)} %param.10) | copy-start | bytes 24580
  70.4 13.5 %collective-permute-start.14 = (bf16[8,128,128]{2,1,0:T(8,128)(2,1)S(1)}, bf16[8,128,128]{2,1,0:T(8,128)(2,1)S(1)}, u32[]{:S(2)}, u32[]{:S(2)}) collective-permute-start(bf16[8,128,128]{2,1,0:T(8,128)(2,1)S(1)} %get-tuple-element.49), channel_id=1, source_target_pairs={{0,4},{4,0},{8,12},{12,8},{16,20},{20,16},{24,28},{28,24},{1,5},{5... | collective-permute-start | bytes 786440 | tf_op jit(solution)/shard_map/ppermute | solution.py:52
  77.1 10.5 %collective-permute-start.19 = (bf16[8,6144]{1,0:T(8,128)(2,1)S(1)}, bf16[8,6144]{1,0:T(8,128)(2,1)S(1)}, u32[]{:S(2)}, u32[]{:S(2)}) collective-permute-start(bf16[8,6144]{1,0:T(8,128)(2,1)S(1)} %get-tuple-element.50), channel_id=1, source_target_pairs={{0,24},{4,28},{8,0},{12,4},{16,8},{20,12},{24,16},{28,20},{1,25},{... | collective-permute-start | bytes 294920 | tf_op jit(solution)/shard_map/ppermute | solution.py:52
  77.2 10.4 %collective-permute-start.20 = (bf16[8,6144]{1,0:T(8,128)(2,1)S(1)}, bf16[8,6144]{1,0:T(8,128)(2,1)S(1)}, u32[]{:S(2)}, u32[]{:S(2)}) collective-permute-start(bf16[8,6144]{1,0:T(8,128)(2,1)S(1)} %get-tuple-element.51), channel_id=1, source_target_pairs={{0,16},{4,20},{8,24},{12,28},{16,0},{20,4},{24,8},{28,12},{1,17},{... | collective-permute-start | bytes 294920 | tf_op jit(solution)/shard_map/ppermute | solution.py:52
  80.1 7.5 %collective-permute-start.21 = (bf16[8,6144]{1,0:T(8,128)(2,1)S(1)}, bf16[8,6144]{1,0:T(8,128)(2,1)S(1)}, u32[]{:S(2)}, u32[]{:S(2)}) collective-permute-start(bf16[8,6144]{1,0:T(8,128)(2,1)S(1)} %get-tuple-element.52), channel_id=1, source_target_pairs={{0,8},{4,12},{8,16},{12,20},{16,24},{20,28},{24,0},{28,4},{1,9},{5... | collective-permute-start | bytes 294920 | tf_op jit(solution)/shard_map/ppermute | solution.py:52

commit v6 on v5

--- a/solution.py
+++ b/solution.py
@@ -219,7 +219,8 @@
 
 def final_kernel(heads, group, first_of, *refs):
     q_ref, mixed_ref, cols_ref, carried_ref, gain_ref = refs[:5]
-    out_ref = refs[-1]
+    out_ref, mark_ref = refs[-2:]
+    mark_ref[...] = jnp.zeros_like(mark_ref)
     width = q_ref.shape[2] // group
     first = first_of(pl.program_id(0)) * group
     cols = pltpu.roll(cols_ref[...], 128 - first, 1)
@@ -232,7 +233,7 @@
         out_ref[:, lanes] = (mixed * lax.rsqrt(mean + EPS) * gain_ref[:, lanes]).astype(BF16)
 
 
-def final_pass(qkv, mixed, cols, carried, gain, heads, y_axis, back, done, behind, group=4):
+def final_pass(qkv, mixed, cols, carried, gain, heads, y_axis, back, done, behind, zeros, group=4):
     rows, width = qkv.shape[1], qkv.shape[2] // heads
     share = carried.shape[0]
     group = min(group, share)
@@ -250,8 +251,14 @@
             pl.BlockSpec((1, group * width), lambda h: (0, block(h))),
         ]
         + [pl.BlockSpec(memory_space=pl.ANY)] * len(more),
-        out_specs=pl.BlockSpec((rows, group * width), lambda h: (0, block(h))),
-        out_shape=jax.ShapeDtypeStruct((rows, heads * width), BF16),
+        out_specs=(
+            pl.BlockSpec((rows, group * width), lambda h: (0, block(h))),
+            pl.BlockSpec((8, zeros), lambda h: (0, 0)),
+        ),
+        out_shape=(
+            jax.ShapeDtypeStruct((rows, heads * width), BF16),
+            jax.ShapeDtypeStruct((8, zeros), BF16),
+        ),
         input_output_aliases={} if done is None else {5: 0},
         compiler_params=params(20),
         cost_estimate=pl.CostEstimate(flops=1, bytes_accessed=1, transcendentals=0),
@@ -618,23 +625,20 @@
     a, b = scatter(core, pa), scatter(core, pb)
     a, b = scatter(x_axis, rows_split(a, nx)), scatter(y_axis, rows_split(b, ny))
     carried = scan.send(nothing(a, *zeros))
+    attn_out = None
+
+    def final(k, behind):
+        gain = norm_gain[None]
+        return final_pass(
+            qkv, mixed, cols, carried[k], gain, heads, y_axis, k, attn_out, behind, 2 * half
+        )
+
+    attn_out, mark = final(0, a)
     a, b = scatter(y_axis, rows_split(a, ny)), scatter(x_axis, rows_split(b, nx))
-    both = jnp.concatenate([a, b], 1)
+    both = jnp.concatenate([a, b], 1) + mark[:1]
+    for k in range(1, ny):
+        attn_out, _ = final(k, both)
     moe_out = scatter(z_axis, rows_split(both, nz))
-    attn_out = None
-    for k in range(ny):
-        attn_out = final_pass(
-            qkv,
-            mixed,
-            cols,
-            carried[k],
-            norm_gain[None],
-            heads,
-            y_axis,
-            k,
-            attn_out,
-            both if k == 0 else None,
-        )
     return attn_out, moe_out
 
 

time: 88.7 us -> 89.4 us (level)
  transfers between devices with their start and end apart: 22 -> 22, of which waited for: 7 -> 10; matrix products, arithmetic and copies ran while one was open for 3% -> 3% of each run, Pallas kernels for 29% -> 29%
where the time goes in v6:
time: 89.4 us; the launch traced here: 89 us
  starting transfers between devices  30.3 us (34%)
  Pallas kernels  27.1 us (30%)
  waiting for transfers between devices  24.5 us (27%)
  other arithmetic  4.82 us (5%)
  local copies, waits for them, and re-layouts  1.27 us (1%)
  between operations  1.03 us (1%)
    ppermute x20, waiting for transfers between devices, send(): return lax.ppermute(a, self.name, self.turn(k))  24.5 us
    ppermute x20, starting transfers between devices, send(): return lax.ppermute(a, self.name, self.turn(k))  21.5 us
    pallas_call x2, Pallas kernels, local_pass(): pl.pallas_call(functools.partial(local_kernel, heads, group, block, loads...  11.2 us
    ppermute x2, starting transfers between devices, carry_scan(): came = lax.ppermute(out, z_axis.name, z_axis.jump(far))  8.78 us
    pallas_call x2, Pallas kernels, final_pass(): pl.pallas_call(functools.partial(final_kernel, heads, group, block), grid...  7.41 us
    pallas_call x1, Pallas kernels, lead_pass(): pl.pallas_call(functools.partial(lead_kernel, experts, nx, ny, block), in...  6.4 us
  transfers between devices with their start and end apart: 22, of which 10 were waited for; matrix products, arithmetic and copies ran while one was open for 3% of the time, Pallas kernels for 29%

profile of v6, /device:TPU:0, one launch (start us, length us, event | category | flops | bytes accessed | tf_op | source)
XLA Modules:
  0.0 89.0 jit_solution(13135237381243027440)
XLA Ops:
  0.6 0.7 select_reduce_fusion.2
  1.5 0.9 %pad_maximum_fusion.5 = bf16[8,6272]{1,0:T(8,128)(2,1)S(1)} fusion(bf16[8,128]{1,0:T(8,128)(2,1)S(1)} %fusion.36, bf16[8,6144]{1,0:T(8,128)(2,1)} %param.11), kind=kLoop, calls=%fused_computation.35 | loop fusion | flops 200704 | bytes 200704 | tf_op jit(solution)/shard_map/concatenate | solution.py:594
  2.4 5.0 %collective-permute-start.2 = (bf16[8,6272]{1,0:T(8,128)(2,1)S(1)}, bf16[8,6272]{1,0:T(8,128)(2,1)S(1)}, u32[]{:S(2)}, u32[]{:S(2)}) collective-permute-start(bf16[8,6272]{1,0:T(8,128)(2,1)S(1)} %pad_maximum_fusion.5), channel_id=1, source_target_pairs={{0,24},{4,28},{8,0},{12,4},{16,8},{20,12},{24,16},{28,20},{1,25},{... | collective-permute-start | bytes 301064 | tf_op jit(solution)/shard_map/ppermute | solution.py:52
  7.5 1.0 %collective-permute-start = (bf16[8,6272]{1,0:T(8,128)(2,1)S(1)}, bf16[8,6272]{1,0:T(8,128)(2,1)S(1)}, u32[]{:S(2)}, u32[]{:S(2)}) collective-permute-start(bf16[8,6272]{1,0:T(8,128)(2,1)S(1)} %pad_maximum_fusion.5), channel_id=1, source_target_pairs={{0,8},{4,12},{8,16},{12,20},{16,24},{20,28},{24,0},{28,4},{1,9},{5... | collective-permute-start | bytes 301064 | tf_op jit(solution)/shard_map/ppermute | solution.py:52
  8.5 0.8 copy-done
  9.2 0.7 prepare.1
  10.2 5.6 %local_pass.2 = (bf16[512,2048]{1,0:T(8,128)(2,1)S(1)}, bf16[8,128,128]{2,1,0:T(8,128)(2,1)S(1)}, bf16[8,3200]{1,0:T(8,128)(2,1)}, bf16[576,6144]{1,0:T(8,128)(2,1)S(1)}) custom-call(bf16[3,512,2048]{2,1,0:T(8,128)(2,1)} %bitcast.34, bf16[3,512,2048]{2,1,0:T(8,128)(2,1)} %bitcast.35, bf16[3,512,2048]{2,1,0:T(8,128)(2,1)} %bitcast.36, ...), custom_call_target="tpu_custom_call" | custom-call | flops 1 | bytes 1 | tf_op jit(solution)/shard_map/local_pass/pallas_call | solution.py:199
  15.8 1.6 %collective-permute-start.3 = (bf16[1040,128]{1,0:T(8,128)(2,1)S(1)}, bf16[1040,128]{1,0:T(8,128)(2,1)S(1)}, u32[]{:S(2)}, u32[]{:S(2)}) collective-permute-start(bf16[1040,128]{1,0:T(8,128)(2,1)S(1)} %pad_maximum_fusion.3), channel_id=1, source_target_pairs={{0,4},{4,0},{8,12},{12,8},{16,20},{20,16},{24,28},{28,24},{1,5},{5... | collective-permute-start | bytes 798728 | tf_op jit(solution)/shard_map/ppermute | solution.py:52
  18.3 1.5 %collective-permute-start.8 = (bf16[32,3200]{1,0:T(8,128)(2,1)S(1)}, bf16[32,3200]{1,0:T(8,128)(2,1)S(1)}, u32[]{:S(2)}, u32[]{:S(2)}) collective-permute-start(bf16[32,3200]{1,0:T(8,128)(2,1)S(1)} %slice.135), channel_id=1, source_target_pairs={{0,2},{1,3},{2,0},{3,1},{4,6},{5,7},{6,4},{7,5},{8,10},{9,11},{10,... | collective-permute-start | bytes 614408 | tf_op jit(solution)/shard_map/ppermute | solution.py:52
  19.8 5.6 %local_pass.3 = (bf16[512,2048]{1,0:T(8,128)(2,1)S(1)}, bf16[8,128,128]{2,1,0:T(8,128)(2,1)S(1)}, bf16[8,3200]{1,0:T(8,128)(2,1)S(1)}, bf16[576,6144]{1,0:T(8,128)(2,1)S(1)}) custom-call(bf16[3,512,2048]{2,1,0:T(8,128)(2,1)} %bitcast.37, bf16[3,512,2048]{2,1,0:T(8,128)(2,1)} %bitcast.38, ...), custom_call_target="tpu_custom_call", output_to_operand_aliasing={{0}: (6, {})} | custom-call | flops 1 | bytes 1 | tf_op jit(solution)/shard_map/local_pass/pallas_call | solution.py:199
  25.5 1.9 %collective-permute-done.4 = bf16[32,3072]{1,0:T(8,128)(2,1)S(1)} collective-permute-done((bf16[32,3072]{1,0:T(8,128)(2,1)S(1)}, bf16[32,3072]{1,0:T(8,128)(2,1)S(1)}, u32[]{:S(2)}, u32[]{:S(2)}) %collective-permute-start.4) | collective-permute-done | bytes 196640 | tf_op jit(solution)/shard_map/ppermute | solution.py:52
  27.5 1.6 %collective-permute-start.5 = (bf16[64,3072]{1,0:T(8,128)(2,1)S(1)}, bf16[64,3072]{1,0:T(8,128)(2,1)S(1)}, u32[]{:S(2)}, u32[]{:S(2)}) collective-permute-start(bf16[64,3072]{1,0:T(8,128)(2,1)S(1)} %maximum_add_fusion.1), channel_id=1, source_target_pairs={{0,2},{1,3},{2,0},{3,1},{4,6},{5,7},{6,4},{7,5},{8,10},{9,11},{10,... | collective-permute-start | bytes 1179656 | tf_op jit(solution)/shard_map/ppermute | solution.py:52
  29.1 1.6 %collective-permute-start.9 = (bf16[64,3200]{1,0:T(8,128)(2,1)S(1)}, bf16[64,3200]{1,0:T(8,128)(2,1)S(1)}, u32[]{:S(2)}, u32[]{:S(2)}) collective-permute-start(bf16[64,3200]{1,0:T(8,128)(2,1)S(1)} %maximum_add_fusion), channel_id=1, source_target_pairs={{0,4},{4,0},{8,12},{12,8},{16,20},{20,16},{24,28},{28,24},{1,5},{5... | collective-permute-start | bytes 1228808 | tf_op jit(solution)/shard_map/ppermute | solution.py:52
  30.7 5.9 %collective-permute-done.5 = bf16[64,3072]{1,0:T(8,128)(2,1)S(1)} collective-permute-done((bf16[64,3072]{1,0:T(8,128)(2,1)S(1)}, bf16[64,3072]{1,0:T(8,128)(2,1)S(1)}, u32[]{:S(2)}, u32[]{:S(2)}) %collective-permute-start.5) | collective-permute-done | bytes 393248 | tf_op jit(solution)/shard_map/ppermute | solution.py:52
  36.8 1.6 %collective-permute-done.9 = bf16[64,3200]{1,0:T(8,128)(2,1)S(1)} collective-permute-done((bf16[64,3200]{1,0:T(8,128)(2,1)S(1)}, bf16[64,3200]{1,0:T(8,128)(2,1)S(1)}, u32[]{:S(2)}, u32[]{:S(2)}) %collective-permute-start.9) | collective-permute-done | bytes 409632 | tf_op jit(solution)/shard_map/ppermute | solution.py:52
  38.8 4.4 %collective-permute-start.6 = (bf16[1040,128]{1,0:T(8,128)(2,1)S(1)}, bf16[1040,128]{1,0:T(8,128)(2,1)S(1)}, u32[]{:S(2)}, u32[]{:S(2)}) collective-permute-start(bf16[1040,128]{1,0:T(8,128)(2,1)S(1)} %pad_maximum_fusion.4), channel_id=1, source_target_pairs={{0,8},{4,12},{8,16},{12,20},{16,24},{20,28},{1,9},{5,13},{9,17},{1... | collective-permute-start | bytes 798728 | tf_op jit(solution)/shard_map/ppermute | solution.py:325
  43.2 6.4 %lead_pass.1 = (bf16[128,3072]{1,0:T(8,128)(2,1)S(1)}, bf16[128,3072]{1,0:T(8,128)(2,1)S(1)}, bf16[256,576]{1,0:T(8,128)(2,1)S(1)}, f32[256,128]{1,0:T(8,128)S(1...) custom-call(bf16[128,3072]{1,0:T(8,128)(2,1)S(1)} %pad_maximum_fusion.1.a, ...), custom_call_target="tpu_custom_call" | custom-call | flops 1 | bytes 1 | tf_op jit(solution)/shard_map/lead_pass/pallas_call | solution.py:505
  49.9 1.4 %rest_pass.1 = (bf16[128,3072]{1,0:T(8,128)(2,1)S(1)}, bf16[128,3072]{1,0:T(8,128)(2,1)S(1)}) custom-call(bf16[256,576]{1,0:T(8,128)(2,1)S(1)} %get-tuple-element.37.h, f32[256,128]{1,0:T(8,128)S(1)} %get-tuple-element.38.flow, bf16[576,3072]{1,0:T(8,128)(2,1)S(1)} %get-tuple-element.39.w, bf16[8,128,128]{2,1,0:T(8,128)(2,1)S(1)} %fusion.1.behind), custom_call_target="tpu_custom_call" | custom-call | flops 1 | bytes 1 | tf_op jit(solution)/shard_map/rest_pass/pallas_call | solution.py:533
  52.0 4.4 %collective-permute-start.11 = (bf16[8,128,128]{2,1,0:T(8,128)(2,1)S(1)}, bf16[8,128,128]{2,1,0:T(8,128)(2,1)S(1)}, u32[]{:S(2)}, u32[]{:S(2)}) collective-permute-start(bf16[8,128,128]{2,1,0:T(8,128)(2,1)S(1)} %fusion.1.behind), channel_id=1, source_target_pairs={{0,16},{4,20},{8,24},{12,28},{1,17},{5,21},{9,25},{13,29},{2,18},{... | collective-permute-start | bytes 786440 | tf_op jit(solution)/shard_map/ppermute | solution.py:325
  56.6 1.6 %collective-permute-start.17 = (bf16[64,3072]{1,0:T(8,128)(2,1)S(1)}, bf16[64,3072]{1,0:T(8,128)(2,1)S(1)}, u32[]{:S(2)}, u32[]{:S(2)}) collective-permute-start(bf16[64,3072]{1,0:T(8,128)(2,1)S(1)} %slice.144), channel_id=1, source_target_pairs={{0,4},{4,0},{8,12},{12,8},{16,20},{20,16},{24,28},{28,24},{1,5},{5... | collective-permute-start | bytes 1179656 | tf_op jit(solution)/shard_map/ppermute | solution.py:52
  59.0 8.5 %collective-permute-done.17 = bf16[64,3072]{1,0:T(8,128)(2,1)S(1)} collective-permute-done((bf16[64,3072]{1,0:T(8,128)(2,1)S(1)}, bf16[64,3072]{1,0:T(8,128)(2,1)S(1)}, u32[]{:S(2)}, u32[]{:S(2)}) %collective-permute-start.17) | collective-permute-done | bytes 393248 | tf_op jit(solution)/shard_map/ppermute | solution.py:52
  68.2 0.8 collective-permute-done.13
  69.1 0.8 collective-permute-start.15
  70.4 1.4 %collective-permute-start.14 = (bf16[8,128,128]{2,1,0:T(8,128)(2,1)S(1)}, bf16[8,128,128]{2,1,0:T(8,128)(2,1)S(1)}, u32[]{:S(2)}, u32[]{:S(2)}) collective-permute-start(bf16[8,128,128]{2,1,0:T(8,128)(2,1)S(1)} %get-tuple-element.55), channel_id=1, source_target_pairs={{0,4},{4,0},{8,12},{12,8},{16,20},{20,16},{24,28},{28,24},{1,5},{5... | collective-permute-start | bytes 786440 | tf_op jit(solution)/shard_map/ppermute | solution.py:52
  71.8 3.7 %final_pass.2 = (bf16[512,2048]{1,0:T(8,128)(2,1)}, bf16[8,6144]{1,0:T(8,128)(2,1)S(1)}) custom-call(bf16[3,512,2048]{2,1,0:T(8,128)(2,1)} %bitcast.40, bf16[512,2048]{1,0:T(8,128)(2,1)S(1)} %get-tuple-element.26.refs_1_, f32[512,128]{1,0:T(8,128)S(1)} %get-tuple-element.24.refs_4_.refs_2_, bf16[8,128,128]{2,1,0:T(8,128)(2,1)S(1)} %get-tuple-element.54.refs_3_, ...), custom_call_target="tpu_custom_call" | custom-call | flops 1 | bytes 1 | tf_op jit(solution)/shard_map/final_pass/pallas_call | solution.py:243
  75.6 1.4 %collective-permute-done.15 = bf16[32,3072]{1,0:T(8,128)(2,1)S(1)} collective-permute-done((bf16[32,3072]{1,0:T(8,128)(2,1)S(1)}, bf16[32,3072]{1,0:T(8,128)(2,1)S(1)}, u32[]{:S(2)}, u32[]{:S(2)}) %collective-permute-start.15) | collective-permute-done | bytes 196640 | tf_op jit(solution)/shard_map/ppermute | solution.py:52
  77.2 0.7 collective-permute-start.19
  77.9 1.3 %collective-permute-start.21 = (bf16[8,6144]{1,0:T(8,128)(2,1)S(1)}, bf16[8,6144]{1,0:T(8,128)(2,1)S(1)}, u32[]{:S(2)}, u32[]{:S(2)}) collective-permute-start(bf16[8,6144]{1,0:T(8,128)(2,1)S(1)} %get-tuple-element.57), channel_id=1, source_target_pairs={{0,8},{4,12},{8,16},{12,20},{16,24},{20,28},{24,0},{28,4},{1,9},{5... | collective-permute-start | bytes 294920 | tf_op jit(solution)/shard_map/ppermute | solution.py:52
  79.3 0.9 %collective-permute-start.20 = (bf16[8,6144]{1,0:T(8,128)(2,1)S(1)}, bf16[8,6144]{1,0:T(8,128)(2,1)S(1)}, u32[]{:S(2)}, u32[]{:S(2)}) collective-permute-start(bf16[8,6144]{1,0:T(8,128)(2,1)S(1)} %get-tuple-element.58), channel_id=1, source_target_pairs={{0,16},{4,20},{8,24},{12,28},{16,0},{20,4},{24,8},{28,12},{1,17},{... | collective-permute-start | bytes 294920 | tf_op jit(solution)/shard_map/ppermute | solution.py:52
  80.2 3.7 %final_pass.3 = (bf16[512,2048]{1,0:T(8,128)(2,1)}, bf16[8,6144]{1,0:T(8,128)(2,1)}) custom-call(bf16[3,512,2048]{2,1,0:T(8,128)(2,1)} %bitcast.41, bf16[512,2048]{1,0:T(8,128)(2,1)S(1)} %get-tuple-element.26.refs_1_, f32[512,128]{1,0:T(8,128)S(1)} %get-tuple-element.24.refs_4_.refs_2_, ...), custom_call_target="tpu_custom_call", output_to_operand_aliasing={{0}: (5, {})} | custom-call | flops 1 | bytes 1 | tf_op jit(solution)/shard_map/final_pass/pallas_call | solution.py:243
  84.2 0.9 collective-permute-done.21
  85.0 3.2 %collective-permute-done.20 = bf16[8,6144]{1,0:T(8,128)(2,1)S(1)} collective-permute-done((bf16[8,6144]{1,0:T(8,128)(2,1)S(1)}, bf16[8,6144]{1,0:T(8,128)(2,1)S(1)}, u32[]{:S(2)}, u32[]{:S(2)}) %collective-permute-start.20) | collective-permute-done | bytes 98336 | tf_op jit(solution)/shard_map/ppermute | solution.py:52
  (75 shorter events, 6.6 us)
Async XLA Ops:
  2.4 15.2 %collective-permute-start.2 = (bf16[8,6272]{1,0:T(8,128)(2,1)S(1)}, bf16[8,6272]{1,0:T(8,128)(2,1)S(1)}, u32[]{:S(2)}, u32[]{:S(2)}) collective-permute-start(bf16[8,6272]{1,0:T(8,128)(2,1)S(1)} %pad_maximum_fusion.5), channel_id=1, source_target_pairs={{0,24},{4,28},{8,0},{12,4},{16,8},{20,12},{24,16},{28,20},{1,25},{... | collective-permute-start | bytes 301064 | tf_op jit(solution)/shard_map/ppermute | solution.py:52
  7.5 10.1 %collective-permute-start.1 = (bf16[8,6272]{1,0:T(8,128)(2,1)S(1)}, bf16[8,6272]{1,0:T(8,128)(2,1)S(1)}, u32[]{:S(2)}, u32[]{:S(2)}) collective-permute-start(bf16[8,6272]{1,0:T(8,128)(2,1)S(1)} %pad_maximum_fusion.5), channel_id=1, source_target_pairs={{0,16},{4,20},{8,24},{12,28},{16,0},{20,4},{24,8},{28,12},{1,17},{... | collective-permute-start | bytes 301064 | tf_op jit(solution)/shard_map/ppermute | solution.py:52
  7.5 10.2 %collective-permute-start = (bf16[8,6272]{1,0:T(8,128)(2,1)S(1)}, bf16[8,6272]{1,0:T(8,128)(2,1)S(1)}, u32[]{:S(2)}, u32[]{:S(2)}) collective-permute-start(bf16[8,6272]{1,0:T(8,128)(2,1)S(1)} %pad_maximum_fusion.5), channel_id=1, source_target_pairs={{0,8},{4,12},{8,16},{12,20},{16,24},{20,28},{24,0},{28,4},{1,9},{5... | collective-permute-start | bytes 301064 | tf_op jit(solution)/shard_map/ppermute | solution.py:52
  8.5 0.8 copy-start
  10.2 7.4 %copy-start.2 = (bf16[8,6144]{1,0:T(8,128)(2,1)S(1)}, bf16[8,6144]{1,0:T(8,128)(2,1)}, u32[]{:S(2)}) copy-start(bf16[8,6144]{1,0:T(8,128)(2,1)} %param.11) | copy-start | bytes 294916
  15.8 9.7 %collective-permute-start.3 = (bf16[1040,128]{1,0:T(8,128)(2,1)S(1)}, bf16[1040,128]{1,0:T(8,128)(2,1)S(1)}, u32[]{:S(2)}, u32[]{:S(2)}) collective-permute-start(bf16[1040,128]{1,0:T(8,128)(2,1)S(1)} %pad_maximum_fusion.3), channel_id=1, source_target_pairs={{0,4},{4,0},{8,12},{12,8},{16,20},{20,16},{24,28},{28,24},{1,5},{5... | collective-permute-start | bytes 798728 | tf_op jit(solution)/shard_map/ppermute | solution.py:52
  17.7 9.7 %collective-permute-start.4 = (bf16[32,3072]{1,0:T(8,128)(2,1)S(1)}, bf16[32,3072]{1,0:T(8,128)(2,1)S(1)}, u32[]{:S(2)}, u32[]{:S(2)}) collective-permute-start(bf16[32,3072]{1,0:T(8,128)(2,1)S(1)} %slice.133), channel_id=1, source_target_pairs={{0,4},{4,0},{8,12},{12,8},{16,20},{20,16},{24,28},{28,24},{1,5},{5... | collective-permute-start | bytes 589832 | tf_op jit(solution)/shard_map/ppermute | solution.py:52
  18.3 10.7 %collective-permute-start.8 = (bf16[32,3200]{1,0:T(8,128)(2,1)S(1)}, bf16[32,3200]{1,0:T(8,128)(2,1)S(1)}, u32[]{:S(2)}, u32[]{:S(2)}) collective-permute-start(bf16[32,3200]{1,0:T(8,128)(2,1)S(1)} %slice.135), channel_id=1, source_target_pairs={{0,2},{1,3},{2,0},{3,1},{4,6},{5,7},{6,4},{7,5},{8,10},{9,11},{10,... | collective-permute-start | bytes 614408 | tf_op jit(solution)/shard_map/ppermute | solution.py:52
  27.5 9.2 %collective-permute-start.5 = (bf16[64,3072]{1,0:T(8,128)(2,1)S(1)}, bf16[64,3072]{1,0:T(8,128)(2,1)S(1)}, u32[]{:S(2)}, u32[]{:S(2)}) collective-permute-start(bf16[64,3072]{1,0:T(8,128)(2,1)S(1)} %maximum_add_fusion.1), channel_id=1, source_target_pairs={{0,2},{1,3},{2,0},{3,1},{4,6},{5,7},{6,4},{7,5},{8,10},{9,11},{10,... | collective-permute-start | bytes 1179656 | tf_op jit(solution)/shard_map/ppermute | solution.py:52
  29.1 9.2 %collective-permute-start.9 = (bf16[64,3200]{1,0:T(8,128)(2,1)S(1)}, bf16[64,3200]{1,0:T(8,128)(2,1)S(1)}, u32[]{:S(2)}, u32[]{:S(2)}) collective-permute-start(bf16[64,3200]{1,0:T(8,128)(2,1)S(1)} %maximum_add_fusion), channel_id=1, source_target_pairs={{0,4},{4,0},{8,12},{12,8},{16,20},{20,16},{24,28},{28,24},{1,5},{5... | collective-permute-start | bytes 1228808 | tf_op jit(solution)/shard_map/ppermute | solution.py:52
  36.7 6.5 %collective-permute-start.7 = (bf16[128,3072]{1,0:T(8,128)(2,1)S(1)}, bf16[128,3072]{1,0:T(8,128)(2,1)S(1)}, u32[]{:S(2)}, u32[]{:S(2)}) collective-permute-start(bf16[128,3072]{1,0:T(8,128)(2,1)S(1)} %pad_maximum_fusion.1.a), channel_id=1, source_target_pairs={{0,1},{1,0},{2,3},{3,2},{4,5},{5,4},{6,7},{7,6},{8,9},{9,8},{10,11... | collective-permute-start | bytes 2359304 | tf_op jit(solution)/shard_map/ppermute | solution.py:52
  38.4 4.8 %collective-permute-start.10 = (bf16[128,3200]{1,0:T(8,128)(2,1)S(1)}, bf16[128,3200]{1,0:T(8,128)(2,1)S(1)}, u32[]{:S(2)}, u32[]{:S(2)}) collective-permute-start(bf16[128,3200]{1,0:T(8,128)(2,1)S(1)} %pad_maximum_fusion.b), channel_id=1, source_target_pairs={{0,1},{1,0},{2,3},{3,2},{4,5},{5,4},{6,7},{7,6},{8,9},{9,8},{10,11... | collective-permute-start | bytes 2457608 | tf_op jit(solution)/shard_map/ppermute | solution.py:52
  38.8 10.9 %collective-permute-start.6 = (bf16[1040,128]{1,0:T(8,128)(2,1)S(1)}, bf16[1040,128]{1,0:T(8,128)(2,1)S(1)}, u32[]{:S(2)}, u32[]{:S(2)}) collective-permute-start(bf16[1040,128]{1,0:T(8,128)(2,1)S(1)} %pad_maximum_fusion.4), channel_id=1, source_target_pairs={{0,8},{4,12},{8,16},{12,20},{16,24},{20,28},{1,9},{5,13},{9,17},{1... | collective-permute-start | bytes 798728 | tf_op jit(solution)/shard_map/ppermute | solution.py:325
  51.4 5.0 %collective-permute-start.16 = (bf16[128,3072]{1,0:T(8,128)(2,1)S(1)}, bf16[128,3072]{1,0:T(8,128)(2,1)S(1)}, u32[]{:S(2)}, u32[]{:S(2)}) collective-permute-start(bf16[128,3072]{1,0:T(8,128)(2,1)S(1)} %get-tuple-element.41), channel_id=1, source_target_pairs={{0,1},{1,0},{2,3},{3,2},{4,5},{5,4},{6,7},{7,6},{8,9},{9,8},{10,11... | collective-permute-start | bytes 2359304 | tf_op jit(solution)/shard_map/ppermute | solution.py:52
  51.6 6.5 %collective-permute-start.12 = (bf16[128,3072]{1,0:T(8,128)(2,1)S(1)}, bf16[128,3072]{1,0:T(8,128)(2,1)S(1)}, u32[]{:S(2)}, u32[]{:S(2)}) collective-permute-start(bf16[128,3072]{1,0:T(8,128)(2,1)S(1)} %get-tuple-element.35), channel_id=1, source_target_pairs={{0,1},{1,0},{2,3},{3,2},{4,5},{5,4},{6,7},{7,6},{8,9},{9,8},{10,11... | collective-permute-start | bytes 2359304 | tf_op jit(solution)/shard_map/ppermute | solution.py:52
  52.0 18.0 %collective-permute-start.11 = (bf16[8,128,128]{2,1,0:T(8,128)(2,1)S(1)}, bf16[8,128,128]{2,1,0:T(8,128)(2,1)S(1)}, u32[]{:S(2)}, u32[]{:S(2)}) collective-permute-start(bf16[8,128,128]{2,1,0:T(8,128)(2,1)S(1)} %fusion.1.behind), channel_id=1, source_target_pairs={{0,16},{4,20},{8,24},{12,28},{1,17},{5,21},{9,25},{13,29},{2,18},{... | collective-permute-start | bytes 786440 | tf_op jit(solution)/shard_map/ppermute | solution.py:325
  56.6 10.9 %collective-permute-start.17 = (bf16[64,3072]{1,0:T(8,128)(2,1)S(1)}, bf16[64,3072]{1,0:T(8,128)(2,1)S(1)}, u32[]{:S(2)}, u32[]{:S(2)}) collective-permute-start(bf16[64,3072]{1,0:T(8,128)(2,1)S(1)} %slice.144), channel_id=1, source_target_pairs={{0,4},{4,0},{8,12},{12,8},{16,20},{20,16},{24,28},{28,24},{1,5},{5... | collective-permute-start | bytes 1179656 | tf_op jit(solution)/shard_map/ppermute | solution.py:52
  58.4 10.6 %collective-permute-start.13 = (bf16[64,3072]{1,0:T(8,128)(2,1)S(1)}, bf16[64,3072]{1,0:T(8,128)(2,1)S(1)}, u32[]{:S(2)}, u32[]{:S(2)}) collective-permute-start(bf16[64,3072]{1,0:T(8,128)(2,1)S(1)} %slice.139), channel_id=1, source_target_pairs={{0,2},{1,3},{2,0},{3,1},{4,6},{5,7},{6,4},{7,5},{8,10},{9,11},{10,... | collective-permute-start | bytes 1179656 | tf_op jit(solution)/shard_map/ppermute | solution.py:52
  67.6 4.2 %copy-start.1 = (f32[2048]{0:T(1024)S(1)}, f32[2048]{0:T(1024)}, u32[]{:S(2)}) copy-start(f32[2048]{0:T(1024)} %param.10) | copy-start | bytes 24580
  67.6 7.9 %collective-permute-start.18 = (bf16[32,3072]{1,0:T(8,128)(2,1)S(1)}, bf16[32,3072]{1,0:T(8,128)(2,1)S(1)}, u32[]{:S(2)}, u32[]{:S(2)}) collective-permute-start(bf16[32,3072]{1,0:T(8,128)(2,1)S(1)} %slice.146), channel_id=1, source_target_pairs={{0,2},{1,3},{2,0},{3,1},{4,6},{5,7},{6,4},{7,5},{8,10},{9,11},{10,... | collective-permute-start | bytes 589832 | tf_op jit(solution)/shard_map/ppermute | solution.py:52
  69.1 7.9 %collective-permute-start.15 = (bf16[32,3072]{1,0:T(8,128)(2,1)S(1)}, bf16[32,3072]{1,0:T(8,128)(2,1)S(1)}, u32[]{:S(2)}, u32[]{:S(2)}) collective-permute-start(bf16[32,3072]{1,0:T(8,128)(2,1)S(1)} %slice.142), channel_id=1, source_target_pairs={{0,4},{4,0},{8,12},{12,8},{16,20},{20,16},{24,28},{28,24},{1,5},{5... | collective-permute-start | bytes 589832 | tf_op jit(solution)/shard_map/ppermute | solution.py:52
  70.4 9.8 %collective-permute-start.14 = (bf16[8,128,128]{2,1,0:T(8,128)(2,1)S(1)}, bf16[8,128,128]{2,1,0:T(8,128)(2,1)S(1)}, u32[]{:S(2)}, u32[]{:S(2)}) collective-permute-start(bf16[8,128,128]{2,1,0:T(8,128)(2,1)S(1)} %get-tuple-element.55), channel_id=1, source_target_pairs={{0,4},{4,0},{8,12},{12,8},{16,20},{20,16},{24,28},{28,24},{1,5},{5... | collective-permute-start | bytes 786440 | tf_op jit(solution)/shard_map/ppermute | solution.py:52
  77.2 7.0 %collective-permute-start.19 = (bf16[8,6144]{1,0:T(8,128)(2,1)S(1)}, bf16[8,6144]{1,0:T(8,128)(2,1)S(1)}, u32[]{:S(2)}, u32[]{:S(2)}) collective-permute-start(bf16[8,6144]{1,0:T(8,128)(2,1)S(1)} %get-tuple-element.56), channel_id=1, source_target_pairs={{0,24},{4,28},{8,0},{12,4},{16,8},{20,12},{24,16},{28,20},{1,25},{... | collective-permute-start | bytes 294920 | tf_op jit(solution)/shard_map/ppermute | solution.py:52
  77.9 7.1 %collective-permute-start.21 = (bf16[8,6144]{1,0:T(8,128)(2,1)S(1)}, bf16[8,6144]{1,0:T(8,128)(2,1)S(1)}, u32[]{:S(2)}, u32[]{:S(2)}) collective-permute-start(bf16[8,6144]{1,0:T(8,128)(2,1)S(1)} %get-tuple-element.57), channel_id=1, source_target_pairs={{0,8},{4,12},{8,16},{12,20},{16,24},{20,28},{24,0},{28,4},{1,9},{5... | collective-permute-start | bytes 294920 | tf_op jit(solution)/shard_map/ppermute | solution.py:52
  79.3 9.0 %collective-permute-start.20 = (bf16[8,6144]{1,0:T(8,128)(2,1)S(1)}, bf16[8,6144]{1,0:T(8,128)(2,1)S(1)}, u32[]{:S(2)}, u32[]{:S(2)}) collective-permute-start(bf16[8,6144]{1,0:T(8,128)(2,1)S(1)} %get-tuple-element.58), channel_id=1, source_target_pairs={{0,16},{4,20},{8,24},{12,28},{16,0},{20,4},{24,8},{28,12},{1,17},{... | collective-permute-start | bytes 294920 | tf_op jit(solution)/shard_map/ppermute | solution.py:52

commit v7 on v6

--- a/solution.py
+++ b/solution.py
@@ -40,12 +40,13 @@
             for j in range(self.inner)
         ]
 
-    def jump(self, k):
+    def pairs(self, step, upwards):
         return [
-            (self.flat(o, i, j), self.flat(o, i + k, j))
+            (self.flat(o, i, j), self.flat(o, i ^ step, j))
             for o in range(self.outer)
-            for i in range(self.n - k)
+            for i in range(self.n)
             for j in range(self.inner)
+            if not (upwards and i & step)
         ]
 
     def send(self, a, k):
@@ -277,7 +278,7 @@
     share, width = shares[0].shape[:2]
     ny = y_axis.n
     pad = 16
-    y = seat[:share]
+    y = seat[:share] & (ny - 1)
     turned = [(y + k) & (ny - 1) for k in range(ny)]
     fade = jnp.exp(last)
     mine = [pick(rows_split(fade, ny), turned[k]) for k in range(ny)]
@@ -313,24 +314,27 @@
     inner = sum(reach(k, ny) * states[k] for k in range(ny))
     through = whole(ny)
     carried, behind = jnp.zeros((share, width, width), F32), jnp.ones((share,), F32)
-    first = tie[:, None]
-    far = 1
-    while far < z_axis.n:
-        out = through * carried + inner + first
-        if 2 * far < z_axis.n:
-            out = packed(out, through[:, 0, 0] * behind)
+    group, fall = inner + tie[:, None], through[:, 0, 0]
+    z = seat[:share] >> (ny.bit_length() - 1)
+    step = 1
+    while step < z_axis.n:
+        upper = (z & step) != 0
+        last_step = 2 * step == z_axis.n
+        out = group.astype(BF16) if last_step else packed(group, fall)
+        tie = yield out
+        came = lax.ppermute(out, z_axis.name, z_axis.pairs(step, last_step))
+        if last_step:
+            came = came.astype(F32) + tie[:, None]
         else:
-            out = out.astype(BF16)
-        tie = yield out
-        came = lax.ppermute(out, z_axis.name, z_axis.jump(far))
-        if 2 * far < z_axis.n:
             came, more = unpacked(came + tie[:1].astype(BF16))
-            carried = carried + behind[:, None, None] * came
-            behind = behind * more
-        else:
-            carried = carried + behind[:, None, None] * came.astype(F32) + tie[:, None]
-        first = 0.0
-        far *= 2
+            group = (
+                jnp.where(upper, 1.0, more)[:, None, None] * group
+                + jnp.where(upper, fall, 1.0)[:, None, None] * came
+            )
+        carried = carried + jnp.where(upper, behind, 0.0)[:, None, None] * came
+        if not last_step:
+            behind, fall = jnp.where(upper, behind * more, behind), fall * more
+        step *= 2
 
     def entering(j):
         end = turned[j]
@@ -604,7 +608,7 @@
         done, shares[turn], mark = made[:1], made[1], made[2]
         held += made[3:]
     mixed = done[0]
-    scan = carry_scan(shares, run[:, -1], seat[:, 0] & (ny - 1), z_axis, y_axis)
+    scan = carry_scan(shares, run[:, -1], seat[:, 0], z_axis, y_axis)
     next(scan)
     a, b = z[:, :half], z[:, half:]
     a, b = gather(y_axis, a), gather(x_axis, b)

time: 89.4 us -> 87.5 us (0.979)
  starting transfers between devices: 30.3 us -> 27.9 us
    ppermute x2, starting transfers between devices: 8.78 us -> 6.36 us  [carry_scan(): came = lax.ppermute(out, z_axis.name, z_axis.pairs(step, last_step))]
  transfers between devices with their start and end apart: 22 -> 22, of which waited for: 10 -> 11; matrix products, arithmetic and copies ran while one was open for 3% -> 3% of each run, Pallas kernels for 29% -> 29%
where the time goes in v7:
time: 87.5 us; the launch traced here: 87.1 us
  starting transfers between devices  27.9 us (32%)
  Pallas kernels  27.1 us (31%)
  waiting for transfers between devices  25 us (29%)
  other arithmetic  4.88 us (6%)
  local copies, waits for them, and re-layouts  1.27 us (1%)
  between operations  1.01 us (1%)
    ppermute x20, waiting for transfers between devices, send(): return lax.ppermute(a, self.name, self.turn(k))  24.4 us
    ppermute x20, starting transfers between devices, send(): return lax.ppermute(a, self.name, self.turn(k))  21.5 us
    pallas_call x2, Pallas kernels, local_pass(): pl.pallas_call(functools.partial(local_kernel, heads, group, block, loads...  11.2 us
    pallas_call x2, Pallas kernels, final_pass(): pl.pallas_call(functools.partial(final_kernel, heads, group, block), grid...  7.4 us
    pallas_call x1, Pallas kernels, lead_pass(): pl.pallas_call(functools.partial(lead_kernel, experts, nx, ny, block), in...  6.4 us
    ppermute x2, starting transfers between devices, carry_scan(): came = lax.ppermute(out, z_axis.name, z_axis.pairs(step, last_step))  6.36 us
  transfers between devices with their start and end apart: 22, of which 11 were waited for; matrix products, arithmetic and copies ran while one was open for 3% of the time, Pallas kernels for 29%

profile of v7, /device:TPU:0, one launch (start us, length us, event | category | flops | bytes accessed | tf_op | source)
XLA Modules:
  0.0 87.1 jit_solution(3881934306726601740)
XLA Ops:
  0.6 0.7 select_reduce_fusion.2
  1.5 0.9 %pad_maximum_fusion.5 = bf16[8,6272]{1,0:T(8,128)(2,1)S(1)} fusion(bf16[8,128]{1,0:T(8,128)(2,1)S(1)} %fusion.39, bf16[8,6144]{1,0:T(8,128)(2,1)} %param.11), kind=kLoop, calls=%fused_computation.36 | loop fusion | flops 200704 | bytes 200704 | tf_op jit(solution)/shard_map/concatenate | solution.py:598
  2.4 5.0 %collective-permute-start.2 = (bf16[8,6272]{1,0:T(8,128)(2,1)S(1)}, bf16[8,6272]{1,0:T(8,128)(2,1)S(1)}, u32[]{:S(2)}, u32[]{:S(2)}) collective-permute-start(bf16[8,6272]{1,0:T(8,128)(2,1)S(1)} %pad_maximum_fusion.5), channel_id=1, source_target_pairs={{0,24},{4,28},{8,0},{12,4},{16,8},{20,12},{24,16},{28,20},{1,25},{... | collective-permute-start | bytes 301064 | tf_op jit(solution)/shard_map/ppermute | solution.py:53
  7.5 1.0 %collective-permute-start = (bf16[8,6272]{1,0:T(8,128)(2,1)S(1)}, bf16[8,6272]{1,0:T(8,128)(2,1)S(1)}, u32[]{:S(2)}, u32[]{:S(2)}) collective-permute-start(bf16[8,6272]{1,0:T(8,128)(2,1)S(1)} %pad_maximum_fusion.5), channel_id=1, source_target_pairs={{0,8},{4,12},{8,16},{12,20},{16,24},{20,28},{24,0},{28,4},{1,9},{5... | collective-permute-start | bytes 301064 | tf_op jit(solution)/shard_map/ppermute | solution.py:53
  8.5 0.8 copy-done
  9.2 0.7 prepare.1
  10.2 5.6 %local_pass.2 = (bf16[512,2048]{1,0:T(8,128)(2,1)S(1)}, bf16[8,128,128]{2,1,0:T(8,128)(2,1)S(1)}, bf16[8,3200]{1,0:T(8,128)(2,1)}, bf16[576,6144]{1,0:T(8,128)(2,1)S(1)}) custom-call(bf16[3,512,2048]{2,1,0:T(8,128)(2,1)} %bitcast.31, bf16[3,512,2048]{2,1,0:T(8,128)(2,1)} %bitcast.32, bf16[3,512,2048]{2,1,0:T(8,128)(2,1)} %bitcast.33, ...), custom_call_target="tpu_custom_call" | custom-call | flops 1 | bytes 1 | tf_op jit(solution)/shard_map/local_pass/pallas_call | solution.py:200
  15.8 1.6 %collective-permute-start.3 = (bf16[1040,128]{1,0:T(8,128)(2,1)S(1)}, bf16[1040,128]{1,0:T(8,128)(2,1)S(1)}, u32[]{:S(2)}, u32[]{:S(2)}) collective-permute-start(bf16[1040,128]{1,0:T(8,128)(2,1)S(1)} %pad_maximum_fusion.3), channel_id=1, source_target_pairs={{0,4},{4,0},{8,12},{12,8},{16,20},{20,16},{24,28},{28,24},{1,5},{5... | collective-permute-start | bytes 798728 | tf_op jit(solution)/shard_map/ppermute | solution.py:53
  18.3 1.5 %collective-permute-start.8 = (bf16[32,3200]{1,0:T(8,128)(2,1)S(1)}, bf16[32,3200]{1,0:T(8,128)(2,1)S(1)}, u32[]{:S(2)}, u32[]{:S(2)}) collective-permute-start(bf16[32,3200]{1,0:T(8,128)(2,1)S(1)} %slice.133), channel_id=1, source_target_pairs={{0,2},{1,3},{2,0},{3,1},{4,6},{5,7},{6,4},{7,5},{8,10},{9,11},{10,... | collective-permute-start | bytes 614408 | tf_op jit(solution)/shard_map/ppermute | solution.py:53
  19.8 5.6 %local_pass.3 = (bf16[512,2048]{1,0:T(8,128)(2,1)S(1)}, bf16[8,128,128]{2,1,0:T(8,128)(2,1)S(1)}, bf16[8,3200]{1,0:T(8,128)(2,1)S(1)}, bf16[576,6144]{1,0:T(8,128)(2,1)S(1)}) custom-call(bf16[3,512,2048]{2,1,0:T(8,128)(2,1)} %bitcast.34, bf16[3,512,2048]{2,1,0:T(8,128)(2,1)} %bitcast.35, ...), custom_call_target="tpu_custom_call", output_to_operand_aliasing={{0}: (6, {})} | custom-call | flops 1 | bytes 1 | tf_op jit(solution)/shard_map/local_pass/pallas_call | solution.py:200
  25.6 1.8 %collective-permute-done.4 = bf16[32,3072]{1,0:T(8,128)(2,1)S(1)} collective-permute-done((bf16[32,3072]{1,0:T(8,128)(2,1)S(1)}, bf16[32,3072]{1,0:T(8,128)(2,1)S(1)}, u32[]{:S(2)}, u32[]{:S(2)}) %collective-permute-start.4) | collective-permute-done | bytes 196640 | tf_op jit(solution)/shard_map/ppermute | solution.py:53
  27.5 1.6 %collective-permute-start.5 = (bf16[64,3072]{1,0:T(8,128)(2,1)S(1)}, bf16[64,3072]{1,0:T(8,128)(2,1)S(1)}, u32[]{:S(2)}, u32[]{:S(2)}) collective-permute-start(bf16[64,3072]{1,0:T(8,128)(2,1)S(1)} %maximum_add_fusion.1), channel_id=1, source_target_pairs={{0,2},{1,3},{2,0},{3,1},{4,6},{5,7},{6,4},{7,5},{8,10},{9,11},{10,... | collective-permute-start | bytes 1179656 | tf_op jit(solution)/shard_map/ppermute | solution.py:53
  29.1 1.6 %collective-permute-start.9 = (bf16[64,3200]{1,0:T(8,128)(2,1)S(1)}, bf16[64,3200]{1,0:T(8,128)(2,1)S(1)}, u32[]{:S(2)}, u32[]{:S(2)}) collective-permute-start(bf16[64,3200]{1,0:T(8,128)(2,1)S(1)} %maximum_add_fusion), channel_id=1, source_target_pairs={{0,4},{4,0},{8,12},{12,8},{16,20},{20,16},{24,28},{28,24},{1,5},{5... | collective-permute-start | bytes 1228808 | tf_op jit(solution)/shard_map/ppermute | solution.py:53
  30.7 5.9 %collective-permute-done.5 = bf16[64,3072]{1,0:T(8,128)(2,1)S(1)} collective-permute-done((bf16[64,3072]{1,0:T(8,128)(2,1)S(1)}, bf16[64,3072]{1,0:T(8,128)(2,1)S(1)}, u32[]{:S(2)}, u32[]{:S(2)}) %collective-permute-start.5) | collective-permute-done | bytes 393248 | tf_op jit(solution)/shard_map/ppermute | solution.py:53
  36.8 1.6 %collective-permute-done.9 = bf16[64,3200]{1,0:T(8,128)(2,1)S(1)} collective-permute-done((bf16[64,3200]{1,0:T(8,128)(2,1)S(1)}, bf16[64,3200]{1,0:T(8,128)(2,1)S(1)}, u32[]{:S(2)}, u32[]{:S(2)}) %collective-permute-start.9) | collective-permute-done | bytes 409632 | tf_op jit(solution)/shard_map/ppermute | solution.py:53
  38.8 2.5 %collective-permute-start.6 = (bf16[1040,128]{1,0:T(8,128)(2,1)S(1)}, bf16[1040,128]{1,0:T(8,128)(2,1)S(1)}, u32[]{:S(2)}, u32[]{:S(2)}) collective-permute-start(bf16[1040,128]{1,0:T(8,128)(2,1)S(1)} %pad_maximum_fusion.4), channel_id=1, source_target_pairs={{0,8},{4,12},{8,0},{12,4},{16,24},{20,28},{24,16},{28,20},{1,9},{5... | collective-permute-start | bytes 798728 | tf_op jit(solution)/shard_map/ppermute | solution.py:325
  41.3 6.4 %lead_pass.1 = (bf16[128,3072]{1,0:T(8,128)(2,1)S(1)}, bf16[128,3072]{1,0:T(8,128)(2,1)S(1)}, bf16[256,576]{1,0:T(8,128)(2,1)S(1)}, f32[256,128]{1,0:T(8,128)S(1...) custom-call(bf16[128,3072]{1,0:T(8,128)(2,1)S(1)} %pad_maximum_fusion.1.a, ...), custom_call_target="tpu_custom_call" | custom-call | flops 1 | bytes 1 | tf_op jit(solution)/shard_map/lead_pass/pallas_call | solution.py:509
  48.7 1.4 %rest_pass.1 = (bf16[128,3072]{1,0:T(8,128)(2,1)S(1)}, bf16[128,3072]{1,0:T(8,128)(2,1)S(1)}) custom-call(bf16[256,576]{1,0:T(8,128)(2,1)S(1)} %get-tuple-element.37.h, f32[256,128]{1,0:T(8,128)S(1)} %get-tuple-element.38.flow, bf16[576,3072]{1,0:T(8,128)(2,1)S(1)} %get-tuple-element.39.w, bf16[8,128,128]{2,1,0:T(8,128)(2,1)S(1)} %fusion.2.behind), custom_call_target="tpu_custom_call" | custom-call | flops 1 | bytes 1 | tf_op jit(solution)/shard_map/rest_pass/pallas_call | solution.py:537
  50.7 3.8 %collective-permute-start.11 = (bf16[8,128,128]{2,1,0:T(8,128)(2,1)S(1)}, bf16[8,128,128]{2,1,0:T(8,128)(2,1)S(1)}, u32[]{:S(2)}, u32[]{:S(2)}) collective-permute-start(bf16[8,128,128]{2,1,0:T(8,128)(2,1)S(1)} %fusion.2.behind), channel_id=1, source_target_pairs={{0,16},{4,20},{8,24},{12,28},{1,17},{5,21},{9,25},{13,29},{2,18},{... | collective-permute-start | bytes 786440 | tf_op jit(solution)/shard_map/ppermute | solution.py:325
  54.8 1.6 %collective-permute-start.17 = (bf16[64,3072]{1,0:T(8,128)(2,1)S(1)}, bf16[64,3072]{1,0:T(8,128)(2,1)S(1)}, u32[]{:S(2)}, u32[]{:S(2)}) collective-permute-start(bf16[64,3072]{1,0:T(8,128)(2,1)S(1)} %slice.142), channel_id=1, source_target_pairs={{0,4},{4,0},{8,12},{12,8},{16,20},{20,16},{24,28},{28,24},{1,5},{5... | collective-permute-start | bytes 1179656 | tf_op jit(solution)/shard_map/ppermute | solution.py:53
  57.2 8.5 %collective-permute-done.17 = bf16[64,3072]{1,0:T(8,128)(2,1)S(1)} collective-permute-done((bf16[64,3072]{1,0:T(8,128)(2,1)S(1)}, bf16[64,3072]{1,0:T(8,128)(2,1)S(1)}, u32[]{:S(2)}, u32[]{:S(2)}) %collective-permute-start.17) | collective-permute-done | bytes 393248 | tf_op jit(solution)/shard_map/ppermute | solution.py:53
  66.5 0.8 collective-permute-done.13
  67.3 0.8 collective-permute-start.15
  68.6 1.3 %collective-permute-start.14 = (bf16[8,128,128]{2,1,0:T(8,128)(2,1)S(1)}, bf16[8,128,128]{2,1,0:T(8,128)(2,1)S(1)}, u32[]{:S(2)}, u32[]{:S(2)}) collective-permute-start(bf16[8,128,128]{2,1,0:T(8,128)(2,1)S(1)} %get-tuple-element.57), channel_id=1, source_target_pairs={{0,4},{4,0},{8,12},{12,8},{16,20},{20,16},{24,28},{28,24},{1,5},{5... | collective-permute-start | bytes 786440 | tf_op jit(solution)/shard_map/ppermute | solution.py:53
  70.0 3.7 %final_pass.2 = (bf16[512,2048]{1,0:T(8,128)(2,1)}, bf16[8,6144]{1,0:T(8,128)(2,1)S(1)}) custom-call(bf16[3,512,2048]{2,1,0:T(8,128)(2,1)} %bitcast.37, bf16[512,2048]{1,0:T(8,128)(2,1)S(1)} %get-tuple-element.26.refs_1_, f32[512,128]{1,0:T(8,128)S(1)} %get-tuple-element.24.refs_4_.refs_2_, bf16[8,128,128]{2,1,0:T(8,128)(2,1)S(1)} %get-tuple-element.56.refs_3_, ...), custom_call_target="tpu_custom_call" | custom-call | flops 1 | bytes 1 | tf_op jit(solution)/shard_map/final_pass/pallas_call | solution.py:244
  73.8 1.4 %collective-permute-done.15 = bf16[32,3072]{1,0:T(8,128)(2,1)S(1)} collective-permute-done((bf16[32,3072]{1,0:T(8,128)(2,1)S(1)}, bf16[32,3072]{1,0:T(8,128)(2,1)S(1)}, u32[]{:S(2)}, u32[]{:S(2)}) %collective-permute-start.15) | collective-permute-done | bytes 196640 | tf_op jit(solution)/shard_map/ppermute | solution.py:53
  75.4 0.7 collective-permute-start.19
  76.1 1.3 %collective-permute-start.21 = (bf16[8,6144]{1,0:T(8,128)(2,1)S(1)}, bf16[8,6144]{1,0:T(8,128)(2,1)S(1)}, u32[]{:S(2)}, u32[]{:S(2)}) collective-permute-start(bf16[8,6144]{1,0:T(8,128)(2,1)S(1)} %get-tuple-element.59), channel_id=1, source_target_pairs={{0,8},{4,12},{8,16},{12,20},{16,24},{20,28},{24,0},{28,4},{1,9},{5... | collective-permute-start | bytes 294920 | tf_op jit(solution)/shard_map/ppermute | solution.py:53
  77.5 0.9 %collective-permute-start.20 = (bf16[8,6144]{1,0:T(8,128)(2,1)S(1)}, bf16[8,6144]{1,0:T(8,128)(2,1)S(1)}, u32[]{:S(2)}, u32[]{:S(2)}) collective-permute-start(bf16[8,6144]{1,0:T(8,128)(2,1)S(1)} %get-tuple-element.60), channel_id=1, source_target_pairs={{0,16},{4,20},{8,24},{12,28},{16,0},{20,4},{24,8},{28,12},{1,17},{... | collective-permute-start | bytes 294920 | tf_op jit(solution)/shard_map/ppermute | solution.py:53
  78.4 3.7 %final_pass.3 = (bf16[512,2048]{1,0:T(8,128)(2,1)}, bf16[8,6144]{1,0:T(8,128)(2,1)}) custom-call(bf16[3,512,2048]{2,1,0:T(8,128)(2,1)} %bitcast.38, bf16[512,2048]{1,0:T(8,128)(2,1)S(1)} %get-tuple-element.26.refs_1_, f32[512,128]{1,0:T(8,128)S(1)} %get-tuple-element.24.refs_4_.refs_2_, ...), custom_call_target="tpu_custom_call", output_to_operand_aliasing={{0}: (5, {})} | custom-call | flops 1 | bytes 1 | tf_op jit(solution)/shard_map/final_pass/pallas_call | solution.py:244
  82.4 0.8 collective-permute-done.21
  83.2 3.2 %collective-permute-done.20 = bf16[8,6144]{1,0:T(8,128)(2,1)S(1)} collective-permute-done((bf16[8,6144]{1,0:T(8,128)(2,1)S(1)}, bf16[8,6144]{1,0:T(8,128)(2,1)S(1)}, u32[]{:S(2)}, u32[]{:S(2)}) %collective-permute-start.20) | collective-permute-done | bytes 98336 | tf_op jit(solution)/shard_map/ppermute | solution.py:53
  (76 shorter events, 7.3 us)
Async XLA Ops:
  2.4 15.2 %collective-permute-start.2 = (bf16[8,6272]{1,0:T(8,128)(2,1)S(1)}, bf16[8,6272]{1,0:T(8,128)(2,1)S(1)}, u32[]{:S(2)}, u32[]{:S(2)}) collective-permute-start(bf16[8,6272]{1,0:T(8,128)(2,1)S(1)} %pad_maximum_fusion.5), channel_id=1, source_target_pairs={{0,24},{4,28},{8,0},{12,4},{16,8},{20,12},{24,16},{28,20},{1,25},{... | collective-permute-start | bytes 301064 | tf_op jit(solution)/shard_map/ppermute | solution.py:53
  7.5 10.2 %collective-permute-start.1 = (bf16[8,6272]{1,0:T(8,128)(2,1)S(1)}, bf16[8,6272]{1,0:T(8,128)(2,1)S(1)}, u32[]{:S(2)}, u32[]{:S(2)}) collective-permute-start(bf16[8,6272]{1,0:T(8,128)(2,1)S(1)} %pad_maximum_fusion.5), channel_id=1, source_target_pairs={{0,16},{4,20},{8,24},{12,28},{16,0},{20,4},{24,8},{28,12},{1,17},{... | collective-permute-start | bytes 301064 | tf_op jit(solution)/shard_map/ppermute | solution.py:53
  7.5 10.2 %collective-permute-start = (bf16[8,6272]{1,0:T(8,128)(2,1)S(1)}, bf16[8,6272]{1,0:T(8,128)(2,1)S(1)}, u32[]{:S(2)}, u32[]{:S(2)}) collective-permute-start(bf16[8,6272]{1,0:T(8,128)(2,1)S(1)} %pad_maximum_fusion.5), channel_id=1, source_target_pairs={{0,8},{4,12},{8,16},{12,20},{16,24},{20,28},{24,0},{28,4},{1,9},{5... | collective-permute-start | bytes 301064 | tf_op jit(solution)/shard_map/ppermute | solution.py:53
  8.5 0.8 copy-start
  10.2 7.5 %copy-start.2 = (bf16[8,6144]{1,0:T(8,128)(2,1)S(1)}, bf16[8,6144]{1,0:T(8,128)(2,1)}, u32[]{:S(2)}) copy-start(bf16[8,6144]{1,0:T(8,128)(2,1)} %param.11) | copy-start | bytes 294916
  15.8 9.7 %collective-permute-start.3 = (bf16[1040,128]{1,0:T(8,128)(2,1)S(1)}, bf16[1040,128]{1,0:T(8,128)(2,1)S(1)}, u32[]{:S(2)}, u32[]{:S(2)}) collective-permute-start(bf16[1040,128]{1,0:T(8,128)(2,1)S(1)} %pad_maximum_fusion.3), channel_id=1, source_target_pairs={{0,4},{4,0},{8,12},{12,8},{16,20},{20,16},{24,28},{28,24},{1,5},{5... | collective-permute-start | bytes 798728 | tf_op jit(solution)/shard_map/ppermute | solution.py:53
  17.8 9.6 %collective-permute-start.4 = (bf16[32,3072]{1,0:T(8,128)(2,1)S(1)}, bf16[32,3072]{1,0:T(8,128)(2,1)S(1)}, u32[]{:S(2)}, u32[]{:S(2)}) collective-permute-start(bf16[32,3072]{1,0:T(8,128)(2,1)S(1)} %slice.131), channel_id=1, source_target_pairs={{0,4},{4,0},{8,12},{12,8},{16,20},{20,16},{24,28},{28,24},{1,5},{5... | collective-permute-start | bytes 589832 | tf_op jit(solution)/shard_map/ppermute | solution.py:53
  18.3 10.7 %collective-permute-start.8 = (bf16[32,3200]{1,0:T(8,128)(2,1)S(1)}, bf16[32,3200]{1,0:T(8,128)(2,1)S(1)}, u32[]{:S(2)}, u32[]{:S(2)}) collective-permute-start(bf16[32,3200]{1,0:T(8,128)(2,1)S(1)} %slice.133), channel_id=1, source_target_pairs={{0,2},{1,3},{2,0},{3,1},{4,6},{5,7},{6,4},{7,5},{8,10},{9,11},{10,... | collective-permute-start | bytes 614408 | tf_op jit(solution)/shard_map/ppermute | solution.py:53
  27.5 9.2 %collective-permute-start.5 = (bf16[64,3072]{1,0:T(8,128)(2,1)S(1)}, bf16[64,3072]{1,0:T(8,128)(2,1)S(1)}, u32[]{:S(2)}, u32[]{:S(2)}) collective-permute-start(bf16[64,3072]{1,0:T(8,128)(2,1)S(1)} %maximum_add_fusion.1), channel_id=1, source_target_pairs={{0,2},{1,3},{2,0},{3,1},{4,6},{5,7},{6,4},{7,5},{8,10},{9,11},{10,... | collective-permute-start | bytes 1179656 | tf_op jit(solution)/shard_map/ppermute | solution.py:53
  29.1 9.2 %collective-permute-start.9 = (bf16[64,3200]{1,0:T(8,128)(2,1)S(1)}, bf16[64,3200]{1,0:T(8,128)(2,1)S(1)}, u32[]{:S(2)}, u32[]{:S(2)}) collective-permute-start(bf16[64,3200]{1,0:T(8,128)(2,1)S(1)} %maximum_add_fusion), channel_id=1, source_target_pairs={{0,4},{4,0},{8,12},{12,8},{16,20},{20,16},{24,28},{28,24},{1,5},{5... | collective-permute-start | bytes 1228808 | tf_op jit(solution)/shard_map/ppermute | solution.py:53
  36.7 4.6 %collective-permute-start.7 = (bf16[128,3072]{1,0:T(8,128)(2,1)S(1)}, bf16[128,3072]{1,0:T(8,128)(2,1)S(1)}, u32[]{:S(2)}, u32[]{:S(2)}) collective-permute-start(bf16[128,3072]{1,0:T(8,128)(2,1)S(1)} %pad_maximum_fusion.1.a), channel_id=1, source_target_pairs={{0,1},{1,0},{2,3},{3,2},{4,5},{5,4},{6,7},{7,6},{8,9},{9,8},{10,11... | collective-permute-start | bytes 2359304 | tf_op jit(solution)/shard_map/ppermute | solution.py:53
  38.4 2.9 %collective-permute-start.10 = (bf16[128,3200]{1,0:T(8,128)(2,1)S(1)}, bf16[128,3200]{1,0:T(8,128)(2,1)S(1)}, u32[]{:S(2)}, u32[]{:S(2)}) collective-permute-start(bf16[128,3200]{1,0:T(8,128)(2,1)S(1)} %pad_maximum_fusion.b), channel_id=1, source_target_pairs={{0,1},{1,0},{2,3},{3,2},{4,5},{5,4},{6,7},{7,6},{8,9},{9,8},{10,11... | collective-permute-start | bytes 2457608 | tf_op jit(solution)/shard_map/ppermute | solution.py:53
  38.8 9.6 %collective-permute-start.6 = (bf16[1040,128]{1,0:T(8,128)(2,1)S(1)}, bf16[1040,128]{1,0:T(8,128)(2,1)S(1)}, u32[]{:S(2)}, u32[]{:S(2)}) collective-permute-start(bf16[1040,128]{1,0:T(8,128)(2,1)S(1)} %pad_maximum_fusion.4), channel_id=1, source_target_pairs={{0,8},{4,12},{8,0},{12,4},{16,24},{20,28},{24,16},{28,20},{1,9},{5... | collective-permute-start | bytes 798728 | tf_op jit(solution)/shard_map/ppermute | solution.py:325
  50.1 4.4 %collective-permute-start.16 = (bf16[128,3072]{1,0:T(8,128)(2,1)S(1)}, bf16[128,3072]{1,0:T(8,128)(2,1)S(1)}, u32[]{:S(2)}, u32[]{:S(2)}) collective-permute-start(bf16[128,3072]{1,0:T(8,128)(2,1)S(1)} %get-tuple-element.41), channel_id=1, source_target_pairs={{0,1},{1,0},{2,3},{3,2},{4,5},{5,4},{6,7},{7,6},{8,9},{9,8},{10,11... | collective-permute-start | bytes 2359304 | tf_op jit(solution)/shard_map/ppermute | solution.py:53
  50.2 6.2 %collective-permute-start.12 = (bf16[128,3072]{1,0:T(8,128)(2,1)S(1)}, bf16[128,3072]{1,0:T(8,128)(2,1)S(1)}, u32[]{:S(2)}, u32[]{:S(2)}) collective-permute-start(bf16[128,3072]{1,0:T(8,128)(2,1)S(1)} %get-tuple-element.35), channel_id=1, source_target_pairs={{0,1},{1,0},{2,3},{3,2},{4,5},{5,4},{6,7},{7,6},{8,9},{9,8},{10,11... | collective-permute-start | bytes 2359304 | tf_op jit(solution)/shard_map/ppermute | solution.py:53
  50.7 17.4 %collective-permute-start.11 = (bf16[8,128,128]{2,1,0:T(8,128)(2,1)S(1)}, bf16[8,128,128]{2,1,0:T(8,128)(2,1)S(1)}, u32[]{:S(2)}, u32[]{:S(2)}) collective-permute-start(bf16[8,128,128]{2,1,0:T(8,128)(2,1)S(1)} %fusion.2.behind), channel_id=1, source_target_pairs={{0,16},{4,20},{8,24},{12,28},{1,17},{5,21},{9,25},{13,29},{2,18},{... | collective-permute-start | bytes 786440 | tf_op jit(solution)/shard_map/ppermute | solution.py:325
  54.8 10.9 %collective-permute-start.17 = (bf16[64,3072]{1,0:T(8,128)(2,1)S(1)}, bf16[64,3072]{1,0:T(8,128)(2,1)S(1)}, u32[]{:S(2)}, u32[]{:S(2)}) collective-permute-start(bf16[64,3072]{1,0:T(8,128)(2,1)S(1)} %slice.142), channel_id=1, source_target_pairs={{0,4},{4,0},{8,12},{12,8},{16,20},{20,16},{24,28},{28,24},{1,5},{5... | collective-permute-start | bytes 1179656 | tf_op jit(solution)/shard_map/ppermute | solution.py:53
  56.6 10.6 %collective-permute-start.13 = (bf16[64,3072]{1,0:T(8,128)(2,1)S(1)}, bf16[64,3072]{1,0:T(8,128)(2,1)S(1)}, u32[]{:S(2)}, u32[]{:S(2)}) collective-permute-start(bf16[64,3072]{1,0:T(8,128)(2,1)S(1)} %slice.137), channel_id=1, source_target_pairs={{0,2},{1,3},{2,0},{3,1},{4,6},{5,7},{6,4},{7,5},{8,10},{9,11},{10,... | collective-permute-start | bytes 1179656 | tf_op jit(solution)/shard_map/ppermute | solution.py:53
  65.8 4.2 %copy-start.1 = (f32[2048]{0:T(1024)S(1)}, f32[2048]{0:T(1024)}, u32[]{:S(2)}) copy-start(f32[2048]{0:T(1024)} %param.10) | copy-start | bytes 24580
  65.8 7.9 %collective-permute-start.18 = (bf16[32,3072]{1,0:T(8,128)(2,1)S(1)}, bf16[32,3072]{1,0:T(8,128)(2,1)S(1)}, u32[]{:S(2)}, u32[]{:S(2)}) collective-permute-start(bf16[32,3072]{1,0:T(8,128)(2,1)S(1)} %slice.144), channel_id=1, source_target_pairs={{0,2},{1,3},{2,0},{3,1},{4,6},{5,7},{6,4},{7,5},{8,10},{9,11},{10,... | collective-permute-start | bytes 589832 | tf_op jit(solution)/shard_map/ppermute | solution.py:53
  67.3 7.9 %collective-permute-start.15 = (bf16[32,3072]{1,0:T(8,128)(2,1)S(1)}, bf16[32,3072]{1,0:T(8,128)(2,1)S(1)}, u32[]{:S(2)}, u32[]{:S(2)}) collective-permute-start(bf16[32,3072]{1,0:T(8,128)(2,1)S(1)} %slice.140), channel_id=1, source_target_pairs={{0,4},{4,0},{8,12},{12,8},{16,20},{20,16},{24,28},{28,24},{1,5},{5... | collective-permute-start | bytes 589832 | tf_op jit(solution)/shard_map/ppermute | solution.py:53
  68.6 9.8 %collective-permute-start.14 = (bf16[8,128,128]{2,1,0:T(8,128)(2,1)S(1)}, bf16[8,128,128]{2,1,0:T(8,128)(2,1)S(1)}, u32[]{:S(2)}, u32[]{:S(2)}) collective-permute-start(bf16[8,128,128]{2,1,0:T(8,128)(2,1)S(1)} %get-tuple-element.57), channel_id=1, source_target_pairs={{0,4},{4,0},{8,12},{12,8},{16,20},{20,16},{24,28},{28,24},{1,5},{5... | collective-permute-start | bytes 786440 | tf_op jit(solution)/shard_map/ppermute | solution.py:53
  75.4 7.0 %collective-permute-start.19 = (bf16[8,6144]{1,0:T(8,128)(2,1)S(1)}, bf16[8,6144]{1,0:T(8,128)(2,1)S(1)}, u32[]{:S(2)}, u32[]{:S(2)}) collective-permute-start(bf16[8,6144]{1,0:T(8,128)(2,1)S(1)} %get-tuple-element.58), channel_id=1, source_target_pairs={{0,24},{4,28},{8,0},{12,4},{16,8},{20,12},{24,16},{28,20},{1,25},{... | collective-permute-start | bytes 294920 | tf_op jit(solution)/shard_map/ppermute | solution.py:53
  76.1 7.1 %collective-permute-start.21 = (bf16[8,6144]{1,0:T(8,128)(2,1)S(1)}, bf16[8,6144]{1,0:T(8,128)(2,1)S(1)}, u32[]{:S(2)}, u32[]{:S(2)}) collective-permute-start(bf16[8,6144]{1,0:T(8,128)(2,1)S(1)} %get-tuple-element.59), channel_id=1, source_target_pairs={{0,8},{4,12},{8,16},{12,20},{16,24},{20,28},{24,0},{28,4},{1,9},{5... | collective-permute-start | bytes 294920 | tf_op jit(solution)/shard_map/ppermute | solution.py:53
  77.5 9.0 %collective-permute-start.20 = (bf16[8,6144]{1,0:T(8,128)(2,1)S(1)}, bf16[8,6144]{1,0:T(8,128)(2,1)S(1)}, u32[]{:S(2)}, u32[]{:S(2)}) collective-permute-start(bf16[8,6144]{1,0:T(8,128)(2,1)S(1)} %get-tuple-element.60), channel_id=1, source_target_pairs={{0,16},{4,20},{8,24},{12,28},{16,0},{20,4},{24,8},{28,12},{1,17},{... | collective-permute-start | bytes 294920 | tf_op jit(solution)/shard_map/ppermute | solution.py:53

commit v8 on v7

--- a/solution.py
+++ b/solution.py
@@ -53,8 +53,12 @@
         return lax.ppermute(a, self.name, self.turn(k))
 
 
+def parts_of(axis, a):
+    return [a] + [axis.send(a, k) for k in range(1, axis.n)]
+
+
 def gather(axis, a):
-    return jnp.concatenate([a] + [axis.send(a, k) for k in range(1, axis.n)], 0)
+    return jnp.concatenate(parts_of(axis, a), 0)
 
 
 def total(parts):
@@ -421,10 +425,9 @@
     )(h, w_out, *probs)
 
 
-def ordered(ref, lanes, outer, inner):
-    m = ref.shape[0] // (outer * inner)
-    blocks = [(i * outer + o) * m for o in range(outer) for i in range(inner)]
-    return jnp.concatenate([ref[at : at + m, lanes] for at in blocks], 0)
+def across(pieces, lanes, outer):
+    m = pieces[0].shape[0] // outer
+    return [p[o * m : (o + 1) * m, lanes] for o in range(outer) for p in pieces]
 
 
 def store_ordered(ref, lanes, value, outer, inner):
@@ -435,8 +438,8 @@
             ref[dst : dst + m, lanes] = value[src : src + m]
 
 
-def own_weights(ref, lanes, experts, outer, inner):
-    r = ordered(ref, lanes, outer, inner).astype(F32)
+def own_weights(pieces, lanes, experts, outer):
+    r = jnp.concatenate(across(pieces, lanes, outer), 0).astype(F32)
     lane = lax.broadcasted_iota(jnp.int32, r.shape, 1)
     mine = (lane % experts == lax.axis_index("exp")) & (lane < PIECES * experts)
     return jnp.sum(jnp.where(mine, r, 0.0), axis=1, keepdims=True)
@@ -450,10 +453,13 @@
     return out
 
 
-def lead_kernel(experts, nx, ny, block, a, a2, b, b2, wg, wu, w_out, o, o2, h, flow, mark, rest, acc, wo, sems):
+def lead_kernel(experts, nx, ny, block, *refs):
+    a, a2, refs = refs[:nx], refs[nx : 2 * nx], refs[2 * nx :]
+    b, b2, refs = refs[:ny], refs[ny : 2 * ny], refs[2 * ny :]
+    wg, wu, w_out, o, o2, h, flow, mark, rest, acc, wo, sems = refs
     units, wide = wg.shape
     half = wide // 2
-    rows = a.shape[0]
+    rows = nx * a[0].shape[0]
     copies = chunks(w_out, wo, sems, 0, half, block, 0)
     copies.append(
         pltpu.make_async_copy(w_out.at[:, pl.ds(half, half)], rest, sems.at[len(copies)])
@@ -462,14 +468,15 @@
         c.start()
     mark[...] = jnp.zeros_like(mark)
     lanes = slice(half, half + 128)
-    flow[:rows] = jnp.broadcast_to(own_weights(b, lanes, experts, nx, ny), (rows, 128))
-    flow[rows:] = jnp.broadcast_to(own_weights(b2, lanes, experts, nx, ny), (rows, 128))
+    flow[:rows] = jnp.broadcast_to(own_weights(b, lanes, experts, nx), (rows, 128))
+    flow[rows:] = jnp.broadcast_to(own_weights(b2, lanes, experts, nx), (rows, 128))
     for at in range(0, wide, block):
         if at < half:
-            x = jnp.concatenate([a[:, at : at + block], a2[:, at : at + block]], 0)
+            lanes = slice(at, at + block)
+            x = jnp.concatenate([p[:, lanes] for p in (*a, *a2)], 0)
         else:
             lanes = slice(at - half, at - half + block)
-            x = jnp.concatenate([ordered(b, lanes, nx, ny), ordered(b2, lanes, nx, ny)], 0)
+            x = jnp.concatenate(across(b, lanes, nx) + across(b2, lanes, nx), 0)
         for i, w in enumerate((wg, wu)):
             d = lax.dot_general(w[:, at : at + block], x, NT, preferred_element_type=F32)
             if at == 0:
@@ -500,7 +507,7 @@
 
 def lead_pass(a, a2, b, b2, held, w_out, experts, nx, ny, zeros, block=1024):
     units, wide = held[0].shape
-    tokens = 2 * a.shape[0]
+    tokens = 2 * nx * a[0].shape[0]
     n_out = wide // 2 // block
     vmem = pl.BlockSpec(memory_space=pltpu.VMEM)
     hbm = pl.BlockSpec(memory_space=pl.ANY)
@@ -508,7 +515,7 @@
     mark = jax.ShapeDtypeStruct(zeros, F32)
     o, o2, h, flow, mark0, rest = pl.pallas_call(
         functools.partial(lead_kernel, experts, nx, ny, block),
-        in_specs=[vmem] * 6 + [hbm],
+        in_specs=[vmem] * (2 * (nx + ny) + 2) + [hbm],
         out_specs=(vmem,) * 6,
         out_shape=(
             half,
@@ -526,7 +533,7 @@
         compiler_params=params(20),
         cost_estimate=pl.CostEstimate(flops=1, bytes_accessed=1, transcendentals=0),
         name="lead_pass",
-    )(a, a2, b, b2, *held, w_out)
+    )(*a, *a2, *b, *b2, *held, w_out)
     return (o, o2), (h, flow, rest), mark0
 
 
@@ -546,6 +553,7 @@
 
 
 def streamed_experts(a, a2, b, b2, w_in, w_out, experts, nx, ny):
+    a, a2, b, b2 = [jnp.concatenate(p, 0) for p in (a, a2, b, b2)]
     half = a.shape[1]
 
     def turned(r, m, n):
@@ -612,9 +620,9 @@
     next(scan)
     a, b = z[:, :half], z[:, half:]
     a, b = gather(y_axis, a), gather(x_axis, b)
-    a, b = gather(x_axis, a + mark[:1, :half]), gather(y_axis, b + mark[:1])
-    scan.send(nothing(a, *zeros))
-    a2, b2 = core.send(a, 1), core.send(b, 1)
+    a, b = parts_of(x_axis, a + mark[:1, :half]), parts_of(y_axis, b + mark[:1])
+    scan.send(nothing(a[-1], *zeros))
+    a2, b2 = [core.send(p, 1) for p in a], [core.send(p, 1) for p in b]
     if fits:
         pa, more, mark = lead_pass(
             a, a2, b, b2, held, in_hbm(w_out), experts, nx, ny, zeros

time: 87.5 us -> 85.3 us (0.975)
  starting transfers between devices: 27.9 us -> 25.7 us
    ppermute x2, starting transfers between devices: 6.36 us -> 3.3 us  [carry_scan(): came = lax.ppermute(out, z_axis.name, z_axis.pairs(step, last_step))]
    ppermute x20 -> x22, starting transfers between devices: 21.5 us -> 22.4 us  [send(): return lax.ppermute(a, self.name, self.turn(k))]
    ppermute x20 -> x22, waiting for transfers between devices: 24.4 us -> 24.4 us  [send(): return lax.ppermute(a, self.name, self.turn(k))]
  transfers between devices with their start and end apart: 22 -> 24, of which waited for: 11 -> 9; matrix products, arithmetic and copies ran while one was open for 3% -> 3% of each run, Pallas kernels for 29% -> 32%
where the time goes in v8:
time: 85.3 us; the launch traced here: 85 us
  Pallas kernels  27.6 us (32%)
  starting transfers between devices  25.7 us (30%)
  waiting for transfers between devices  24.7 us (29%)
  other arithmetic  4.77 us (6%)
  local copies, waits for them, and re-layouts  1.27 us (1%)
  between operations  0.96 us (1%)
    ppermute x22, waiting for transfers between devices, send(): return lax.ppermute(a, self.name, self.turn(k))  24.4 us
    ppermute x22, starting transfers between devices, send(): return lax.ppermute(a, self.name, self.turn(k))  22.4 us
    pallas_call x2, Pallas kernels, local_pass(): pl.pallas_call(functools.partial(local_kernel, heads, group, block, loads...  11.2 us
    pallas_call x2, Pallas kernels, final_pass(): pl.pallas_call(functools.partial(final_kernel, heads, group, block), grid...  7.4 us
    pallas_call x1, Pallas kernels, lead_pass(): pl.pallas_call(functools.partial(lead_kernel, experts, nx, ny, block), in...  6.78 us
    ppermute x2, starting transfers between devices, carry_scan(): came = lax.ppermute(out, z_axis.name, z_axis.pairs(step, last_step))  3.3 us
  transfers between devices with their start and end apart: 24, of which 9 were waited for; matrix products, arithmetic and copies ran while one was open for 3% of the time, Pallas kernels for 32%

profile of v8, /device:TPU:0, one launch (start us, length us, event | category | flops | bytes accessed | tf_op | source)
XLA Modules:
  0.0 85.0 jit_solution(7875521601397490939)
XLA Ops:
  0.6 0.7 select_reduce_fusion.2
  1.5 0.9 %pad_maximum_fusion.3 = bf16[8,6272]{1,0:T(8,128)(2,1)S(1)} fusion(bf16[8,128]{1,0:T(8,128)(2,1)S(1)} %fusion.39, bf16[8,6144]{1,0:T(8,128)(2,1)} %param.11), kind=kLoop, calls=%fused_computation.34 | loop fusion | flops 200704 | bytes 200704 | tf_op jit(solution)/shard_map/concatenate | solution.py:606
  2.4 3.0 %collective-permute-start = (bf16[8,6272]{1,0:T(8,128)(2,1)S(1)}, bf16[8,6272]{1,0:T(8,128)(2,1)S(1)}, u32[]{:S(2)}, u32[]{:S(2)}) collective-permute-start(bf16[8,6272]{1,0:T(8,128)(2,1)S(1)} %pad_maximum_fusion.3), channel_id=1, source_target_pairs={{0,8},{4,12},{8,16},{12,20},{16,24},{20,28},{24,0},{28,4},{1,9},{5... | collective-permute-start | bytes 301064 | tf_op jit(solution)/shard_map/ppermute | solution.py:53
  5.4 2.6 %collective-permute-start.1 = (bf16[8,6272]{1,0:T(8,128)(2,1)S(1)}, bf16[8,6272]{1,0:T(8,128)(2,1)S(1)}, u32[]{:S(2)}, u32[]{:S(2)}) collective-permute-start(bf16[8,6272]{1,0:T(8,128)(2,1)S(1)} %pad_maximum_fusion.3), channel_id=1, source_target_pairs={{0,16},{4,20},{8,24},{12,28},{16,0},{20,4},{24,8},{28,12},{1,17},{... | collective-permute-start | bytes 301064 | tf_op jit(solution)/shard_map/ppermute | solution.py:53
  8.0 1.3 %collective-permute-start.2 = (bf16[8,6272]{1,0:T(8,128)(2,1)S(1)}, bf16[8,6272]{1,0:T(8,128)(2,1)S(1)}, u32[]{:S(2)}, u32[]{:S(2)}) collective-permute-start(bf16[8,6272]{1,0:T(8,128)(2,1)S(1)} %pad_maximum_fusion.3), channel_id=1, source_target_pairs={{0,24},{4,28},{8,0},{12,4},{16,8},{20,12},{24,16},{28,20},{1,25},{... | collective-permute-start | bytes 301064 | tf_op jit(solution)/shard_map/ppermute | solution.py:53
  9.4 0.8 copy-done
  10.1 0.7 prepare.1
  11.1 5.6 %local_pass.2 = (bf16[512,2048]{1,0:T(8,128)(2,1)S(1)}, bf16[8,128,128]{2,1,0:T(8,128)(2,1)S(1)}, bf16[8,3200]{1,0:T(8,128)(2,1)}, bf16[576,6144]{1,0:T(8,128)(2,1)S(1)}) custom-call(bf16[3,512,2048]{2,1,0:T(8,128)(2,1)} %bitcast.31, bf16[3,512,2048]{2,1,0:T(8,128)(2,1)} %bitcast.32, bf16[3,512,2048]{2,1,0:T(8,128)(2,1)} %bitcast.33, ...), custom_call_target="tpu_custom_call" | custom-call | flops 1 | bytes 1 | tf_op jit(solution)/shard_map/local_pass/pallas_call | solution.py:204
  16.7 1.6 %collective-permute-start.3 = (bf16[1040,128]{1,0:T(8,128)(2,1)S(1)}, bf16[1040,128]{1,0:T(8,128)(2,1)S(1)}, u32[]{:S(2)}, u32[]{:S(2)}) collective-permute-start(bf16[1040,128]{1,0:T(8,128)(2,1)S(1)} %pad_maximum_fusion.1), channel_id=1, source_target_pairs={{0,4},{4,0},{8,12},{12,8},{16,20},{20,16},{24,28},{28,24},{1,5},{5... | collective-permute-start | bytes 798728 | tf_op jit(solution)/shard_map/ppermute | solution.py:53
  18.6 5.7 %local_pass.3 = (bf16[512,2048]{1,0:T(8,128)(2,1)S(1)}, bf16[8,128,128]{2,1,0:T(8,128)(2,1)S(1)}, bf16[8,3200]{1,0:T(8,128)(2,1)S(1)}, bf16[576,6144]{1,0:T(8,128)(2,1)S(1)}) custom-call(bf16[3,512,2048]{2,1,0:T(8,128)(2,1)} %bitcast.34, bf16[3,512,2048]{2,1,0:T(8,128)(2,1)} %bitcast.35, ...), custom_call_target="tpu_custom_call", output_to_operand_aliasing={{0}: (6, {})} | custom-call | flops 1 | bytes 1 | tf_op jit(solution)/shard_map/local_pass/pallas_call | solution.py:204
  24.9 1.5 %collective-permute-start.9 = (bf16[32,3200]{1,0:T(8,128)(2,1)S(1)}, bf16[32,3200]{1,0:T(8,128)(2,1)S(1)}, u32[]{:S(2)}, u32[]{:S(2)}) collective-permute-start(bf16[32,3200]{1,0:T(8,128)(2,1)S(1)} %slice.133), channel_id=1, source_target_pairs={{0,2},{1,3},{2,0},{3,1},{4,6},{5,7},{6,4},{7,5},{8,10},{9,11},{10,... | collective-permute-start | bytes 614408 | tf_op jit(solution)/shard_map/ppermute | solution.py:53
  26.5 3.5 %collective-permute-done.4 = bf16[32,3072]{1,0:T(8,128)(2,1)S(1)} collective-permute-done((bf16[32,3072]{1,0:T(8,128)(2,1)S(1)}, bf16[32,3072]{1,0:T(8,128)(2,1)S(1)}, u32[]{:S(2)}, u32[]{:S(2)}) %collective-permute-start.4) | collective-permute-done | bytes 196640 | tf_op jit(solution)/shard_map/ppermute | solution.py:53
  30.2 1.6 %collective-permute-start.5 = (bf16[64,3072]{1,0:T(8,128)(2,1)S(1)}, bf16[64,3072]{1,0:T(8,128)(2,1)S(1)}, u32[]{:S(2)}, u32[]{:S(2)}) collective-permute-start(bf16[64,3072]{1,0:T(8,128)(2,1)S(1)} %maximum_add_fusion.1.refs_0_), channel_id=1, source_target_pairs={{0,2},{1,3},{2,0},{3,1},{4,6},{5,7},{6,4},{7,5},{8,10},{9,11},{10,... | collective-permute-start | bytes 1179656 | tf_op jit(solution)/shard_map/ppermute | solution.py:53
  31.8 1.9 %collective-permute-start.10 = (bf16[64,3200]{1,0:T(8,128)(2,1)S(1)}, bf16[64,3200]{1,0:T(8,128)(2,1)S(1)}, u32[]{:S(2)}, u32[]{:S(2)}) collective-permute-start(bf16[64,3200]{1,0:T(8,128)(2,1)S(1)} %maximum_add_fusion.refs_4_), channel_id=1, source_target_pairs={{0,4},{4,0},{8,12},{12,8},{16,20},{20,16},{24,28},{28,24},{1,5},{5... | collective-permute-start | bytes 1228808 | tf_op jit(solution)/shard_map/ppermute | solution.py:53
  34.3 4.8 %collective-permute-done.5.refs_1_ = bf16[64,3072]{1,0:T(8,128)(2,1)S(1)} collective-permute-done((bf16[64,3072]{1,0:T(8,128)(2,1)S(1)}, bf16[64,3072]{1,0:T(8,128)(2,1)S(1)}, u32[]{:S(2)}, u32[]{:S(2)}) %collective-permute-start.5) | collective-permute-done | bytes 393248 | tf_op jit(solution)/shard_map/ppermute | solution.py:53
  39.1 1.4 %collective-permute-done.10.refs_5_ = bf16[64,3200]{1,0:T(8,128)(2,1)S(1)} collective-permute-done((bf16[64,3200]{1,0:T(8,128)(2,1)S(1)}, bf16[64,3200]{1,0:T(8,128)(2,1)S(1)}, u32[]{:S(2)}, u32[]{:S(2)}) %collective-permute-start.10) | collective-permute-done | bytes 409632 | tf_op jit(solution)/shard_map/ppermute | solution.py:53
  40.7 0.7 collective-permute-start.6
  41.5 0.8 collective-permute-done.12.refs_7_
  42.3 6.8 %lead_pass.1 = (bf16[128,3072]{1,0:T(8,128)(2,1)S(1)}, bf16[128,3072]{1,0:T(8,128)(2,1)S(1)}, bf16[256,576]{1,0:T(8,128)(2,1)S(1)}, f32[256,128]{1,0:T(8,128)S(1...) custom-call(bf16[64,3072]{1,0:T(8,128)(2,1)S(1)} %maximum_add_fusion.1.refs_0_, ...), custom_call_target="tpu_custom_call" | custom-call | flops 1 | bytes 1 | tf_op jit(solution)/shard_map/lead_pass/pallas_call | solution.py:516
  50.0 1.4 %rest_pass.1 = (bf16[128,3072]{1,0:T(8,128)(2,1)S(1)}, bf16[128,3072]{1,0:T(8,128)(2,1)S(1)}) custom-call(bf16[256,576]{1,0:T(8,128)(2,1)S(1)} %get-tuple-element.37.h, f32[256,128]{1,0:T(8,128)S(1)} %get-tuple-element.38.flow, bf16[576,3072]{1,0:T(8,128)(2,1)S(1)} %get-tuple-element.39.w, bf16[8,128,128]{2,1,0:T(8,128)(2,1)S(1)} %fusion.2.behind), custom_call_target="tpu_custom_call" | custom-call | flops 1 | bytes 1 | tf_op jit(solution)/shard_map/rest_pass/pallas_call | solution.py:544
  51.5 2.6 %collective-permute-start.13 = (bf16[8,128,128]{2,1,0:T(8,128)(2,1)S(1)}, bf16[8,128,128]{2,1,0:T(8,128)(2,1)S(1)}, u32[]{:S(2)}, u32[]{:S(2)}) collective-permute-start(bf16[8,128,128]{2,1,0:T(8,128)(2,1)S(1)} %fusion.2.behind), channel_id=1, source_target_pairs={{0,16},{4,20},{8,24},{12,28},{1,17},{5,21},{9,25},{13,29},{2,18},{... | collective-permute-start | bytes 786440 | tf_op jit(solution)/shard_map/ppermute | solution.py:329
  54.3 0.8 collective-permute-start.15
  55.4 1.6 %collective-permute-start.19 = (bf16[64,3072]{1,0:T(8,128)(2,1)S(1)}, bf16[64,3072]{1,0:T(8,128)(2,1)S(1)}, u32[]{:S(2)}, u32[]{:S(2)}) collective-permute-start(bf16[64,3072]{1,0:T(8,128)(2,1)S(1)} %slice.142), channel_id=1, source_target_pairs={{0,4},{4,0},{8,12},{12,8},{16,20},{20,16},{24,28},{28,24},{1,5},{5... | collective-permute-start | bytes 1179656 | tf_op jit(solution)/shard_map/ppermute | solution.py:53
  57.0 8.6 %collective-permute-done.15 = bf16[64,3072]{1,0:T(8,128)(2,1)S(1)} collective-permute-done((bf16[64,3072]{1,0:T(8,128)(2,1)S(1)}, bf16[64,3072]{1,0:T(8,128)(2,1)S(1)}, u32[]{:S(2)}, u32[]{:S(2)}) %collective-permute-start.15) | collective-permute-done | bytes 393248 | tf_op jit(solution)/shard_map/ppermute | solution.py:53
  65.7 0.8 collective-permute-start.17
  66.7 1.6 %collective-permute-start.20 = (bf16[32,3072]{1,0:T(8,128)(2,1)S(1)}, bf16[32,3072]{1,0:T(8,128)(2,1)S(1)}, u32[]{:S(2)}, u32[]{:S(2)}) collective-permute-start(bf16[32,3072]{1,0:T(8,128)(2,1)S(1)} %slice.144), channel_id=1, source_target_pairs={{0,2},{1,3},{2,0},{3,1},{4,6},{5,7},{6,4},{7,5},{8,10},{9,11},{10,... | collective-permute-start | bytes 589832 | tf_op jit(solution)/shard_map/ppermute | solution.py:53
  69.3 3.7 %final_pass.2 = (bf16[512,2048]{1,0:T(8,128)(2,1)}, bf16[8,6144]{1,0:T(8,128)(2,1)S(1)}) custom-call(bf16[3,512,2048]{2,1,0:T(8,128)(2,1)} %bitcast.37, bf16[512,2048]{1,0:T(8,128)(2,1)S(1)} %get-tuple-element.26.refs_1_, f32[512,128]{1,0:T(8,128)S(1)} %get-tuple-element.24.refs_4_.refs_2_, bf16[8,128,128]{2,1,0:T(8,128)(2,1)S(1)} %get-tuple-element.56.refs_3_, ...), custom_call_target="tpu_custom_call" | custom-call | flops 1 | bytes 1 | tf_op jit(solution)/shard_map/final_pass/pallas_call | solution.py:248
  74.5 1.4 %collective-permute-start.22 = (bf16[8,6144]{1,0:T(8,128)(2,1)S(1)}, bf16[8,6144]{1,0:T(8,128)(2,1)S(1)}, u32[]{:S(2)}, u32[]{:S(2)}) collective-permute-start(bf16[8,6144]{1,0:T(8,128)(2,1)S(1)} %get-tuple-element.60), channel_id=1, source_target_pairs={{0,16},{4,20},{8,24},{12,28},{16,0},{20,4},{24,8},{28,12},{1,17},{... | collective-permute-start | bytes 294920 | tf_op jit(solution)/shard_map/ppermute | solution.py:53
  75.9 1.6 %collective-permute-done.16.refs_3_ = bf16[8,128,128]{2,1,0:T(8,128)(2,1)S(1)} collective-permute-done((bf16[8,128,128]{2,1,0:T(8,128)(2,1)S(1)}, bf16[8,128,128]{2,1,0:T(8,128)(2,1)S(1)}, u32[]{:S(2)}, u32[]{:S(2)}) %collective-permute-start.16) | collective-permute-done | bytes 262176 | tf_op jit(solution)/shard_map/ppermute | solution.py:53
  77.6 3.7 %final_pass.3 = (bf16[512,2048]{1,0:T(8,128)(2,1)}, bf16[8,6144]{1,0:T(8,128)(2,1)}) custom-call(bf16[3,512,2048]{2,1,0:T(8,128)(2,1)} %bitcast.38, bf16[512,2048]{1,0:T(8,128)(2,1)S(1)} %get-tuple-element.26.refs_1_, f32[512,128]{1,0:T(8,128)S(1)} %get-tuple-element.24.refs_4_.refs_2_, ...), custom_call_target="tpu_custom_call", output_to_operand_aliasing={{0}: (5, {})} | custom-call | flops 1 | bytes 1 | tf_op jit(solution)/shard_map/final_pass/pallas_call | solution.py:248
  81.3 3.0 %collective-permute-done.22 = bf16[8,6144]{1,0:T(8,128)(2,1)S(1)} collective-permute-done((bf16[8,6144]{1,0:T(8,128)(2,1)S(1)}, bf16[8,6144]{1,0:T(8,128)(2,1)S(1)}, u32[]{:S(2)}, u32[]{:S(2)}) %collective-permute-start.22) | collective-permute-done | bytes 98336 | tf_op jit(solution)/shard_map/ppermute | solution.py:53
  84.3 0.7 add_convert_fusion.6
  (78 shorter events, 6.6 us)
Async XLA Ops:
  2.4 16.1 %collective-permute-start = (bf16[8,6272]{1,0:T(8,128)(2,1)S(1)}, bf16[8,6272]{1,0:T(8,128)(2,1)S(1)}, u32[]{:S(2)}, u32[]{:S(2)}) collective-permute-start(bf16[8,6272]{1,0:T(8,128)(2,1)S(1)} %pad_maximum_fusion.3), channel_id=1, source_target_pairs={{0,8},{4,12},{8,16},{12,20},{16,24},{20,28},{24,0},{28,4},{1,9},{5... | collective-permute-start | bytes 301064 | tf_op jit(solution)/shard_map/ppermute | solution.py:53
  5.4 13.1 %collective-permute-start.1 = (bf16[8,6272]{1,0:T(8,128)(2,1)S(1)}, bf16[8,6272]{1,0:T(8,128)(2,1)S(1)}, u32[]{:S(2)}, u32[]{:S(2)}) collective-permute-start(bf16[8,6272]{1,0:T(8,128)(2,1)S(1)} %pad_maximum_fusion.3), channel_id=1, source_target_pairs={{0,16},{4,20},{8,24},{12,28},{16,0},{20,4},{24,8},{28,12},{1,17},{... | collective-permute-start | bytes 301064 | tf_op jit(solution)/shard_map/ppermute | solution.py:53
  8.0 10.5 %collective-permute-start.2 = (bf16[8,6272]{1,0:T(8,128)(2,1)S(1)}, bf16[8,6272]{1,0:T(8,128)(2,1)S(1)}, u32[]{:S(2)}, u32[]{:S(2)}) collective-permute-start(bf16[8,6272]{1,0:T(8,128)(2,1)S(1)} %pad_maximum_fusion.3), channel_id=1, source_target_pairs={{0,24},{4,28},{8,0},{12,4},{16,8},{20,12},{24,16},{28,20},{1,25},{... | collective-permute-start | bytes 301064 | tf_op jit(solution)/shard_map/ppermute | solution.py:53
  9.4 0.8 copy-start
  11.1 7.5 %copy-start.2 = (bf16[8,6144]{1,0:T(8,128)(2,1)S(1)}, bf16[8,6144]{1,0:T(8,128)(2,1)}, u32[]{:S(2)}) copy-start(bf16[8,6144]{1,0:T(8,128)(2,1)} %param.11) | copy-start | bytes 294916
  16.7 9.8 %collective-permute-start.3 = (bf16[1040,128]{1,0:T(8,128)(2,1)S(1)}, bf16[1040,128]{1,0:T(8,128)(2,1)S(1)}, u32[]{:S(2)}, u32[]{:S(2)}) collective-permute-start(bf16[1040,128]{1,0:T(8,128)(2,1)S(1)} %pad_maximum_fusion.1), channel_id=1, source_target_pairs={{0,4},{4,0},{8,12},{12,8},{16,20},{20,16},{24,28},{28,24},{1,5},{5... | collective-permute-start | bytes 798728 | tf_op jit(solution)/shard_map/ppermute | solution.py:53
  24.3 5.7 %collective-permute-start.4 = (bf16[32,3072]{1,0:T(8,128)(2,1)S(1)}, bf16[32,3072]{1,0:T(8,128)(2,1)S(1)}, u32[]{:S(2)}, u32[]{:S(2)}) collective-permute-start(bf16[32,3072]{1,0:T(8,128)(2,1)S(1)} %slice.131), channel_id=1, source_target_pairs={{0,4},{4,0},{8,12},{12,8},{16,20},{20,16},{24,28},{28,24},{1,5},{5... | collective-permute-start | bytes 589832 | tf_op jit(solution)/shard_map/ppermute | solution.py:53
  24.9 6.8 %collective-permute-start.9 = (bf16[32,3200]{1,0:T(8,128)(2,1)S(1)}, bf16[32,3200]{1,0:T(8,128)(2,1)S(1)}, u32[]{:S(2)}, u32[]{:S(2)}) collective-permute-start(bf16[32,3200]{1,0:T(8,128)(2,1)S(1)} %slice.133), channel_id=1, source_target_pairs={{0,2},{1,3},{2,0},{3,1},{4,6},{5,7},{6,4},{7,5},{8,10},{9,11},{10,... | collective-permute-start | bytes 614408 | tf_op jit(solution)/shard_map/ppermute | solution.py:53
  30.2 8.9 %collective-permute-start.5 = (bf16[64,3072]{1,0:T(8,128)(2,1)S(1)}, bf16[64,3072]{1,0:T(8,128)(2,1)S(1)}, u32[]{:S(2)}, u32[]{:S(2)}) collective-permute-start(bf16[64,3072]{1,0:T(8,128)(2,1)S(1)} %maximum_add_fusion.1.refs_0_), channel_id=1, source_target_pairs={{0,2},{1,3},{2,0},{3,1},{4,6},{5,7},{6,4},{7,5},{8,10},{9,11},{10,... | collective-permute-start | bytes 1179656 | tf_op jit(solution)/shard_map/ppermute | solution.py:53
  31.8 8.7 %collective-permute-start.10 = (bf16[64,3200]{1,0:T(8,128)(2,1)S(1)}, bf16[64,3200]{1,0:T(8,128)(2,1)S(1)}, u32[]{:S(2)}, u32[]{:S(2)}) collective-permute-start(bf16[64,3200]{1,0:T(8,128)(2,1)S(1)} %maximum_add_fusion.refs_4_), channel_id=1, source_target_pairs={{0,4},{4,0},{8,12},{12,8},{16,20},{20,16},{24,28},{28,24},{1,5},{5... | collective-permute-start | bytes 1228808 | tf_op jit(solution)/shard_map/ppermute | solution.py:53
  33.7 7.8 %collective-permute-start.7 = (bf16[64,3072]{1,0:T(8,128)(2,1)S(1)}, bf16[64,3072]{1,0:T(8,128)(2,1)S(1)}, u32[]{:S(2)}, u32[]{:S(2)}) collective-permute-start(bf16[64,3072]{1,0:T(8,128)(2,1)S(1)} %maximum_add_fusion.1.refs_0_), channel_id=1, source_target_pairs={{0,1},{1,0},{2,3},{3,2},{4,5},{5,4},{6,7},{7,6},{8,9},{9,8},{10,11... | collective-permute-start | bytes 1179656 | tf_op jit(solution)/shard_map/ppermute | solution.py:53
  33.8 7.7 %collective-permute-start.11 = (bf16[64,3200]{1,0:T(8,128)(2,1)S(1)}, bf16[64,3200]{1,0:T(8,128)(2,1)S(1)}, u32[]{:S(2)}, u32[]{:S(2)}) collective-permute-start(bf16[64,3200]{1,0:T(8,128)(2,1)S(1)} %maximum_add_fusion.refs_4_), channel_id=1, source_target_pairs={{0,1},{1,0},{2,3},{3,2},{4,5},{5,4},{6,7},{7,6},{8,9},{9,8},{10,11... | collective-permute-start | bytes 1228808 | tf_op jit(solution)/shard_map/ppermute | solution.py:53
  39.1 2.4 %collective-permute-start.8 = (bf16[64,3072]{1,0:T(8,128)(2,1)S(1)}, bf16[64,3072]{1,0:T(8,128)(2,1)S(1)}, u32[]{:S(2)}, u32[]{:S(2)}) collective-permute-start(bf16[64,3072]{1,0:T(8,128)(2,1)S(1)} %collective-permute-done.5.refs_1_), channel_id=1, source_target_pairs={{0,1},{1,0},{2,3},{3,2},{4,5},{5,4},{6,7},{7,6},{8,9},{9,8},{10,11... | collective-permute-start | bytes 1179656 | tf_op jit(solution)/shard_map/ppermute | solution.py:53
  40.5 1.7 %collective-permute-start.12 = (bf16[64,3200]{1,0:T(8,128)(2,1)S(1)}, bf16[64,3200]{1,0:T(8,128)(2,1)S(1)}, u32[]{:S(2)}, u32[]{:S(2)}) collective-permute-start(bf16[64,3200]{1,0:T(8,128)(2,1)S(1)} %collective-permute-done.10.refs_5_), channel_id=1, source_target_pairs={{0,1},{1,0},{2,3},{3,2},{4,5},{5,4},{6,7},{7,6},{8,9},{9,8},{10,11... | collective-permute-start | bytes 1228808 | tf_op jit(solution)/shard_map/ppermute | solution.py:53
  40.7 8.9 %collective-permute-start.6 = (bf16[1040,128]{1,0:T(8,128)(2,1)S(1)}, bf16[1040,128]{1,0:T(8,128)(2,1)S(1)}, u32[]{:S(2)}, u32[]{:S(2)}) collective-permute-start(bf16[1040,128]{1,0:T(8,128)(2,1)S(1)} %pad_maximum_fusion.2), channel_id=1, source_target_pairs={{0,8},{4,12},{8,0},{12,4},{16,24},{20,28},{24,16},{28,20},{1,9},{5... | collective-permute-start | bytes 798728 | tf_op jit(solution)/shard_map/ppermute | solution.py:329
  49.1 5.0 %collective-permute-start.14 = (bf16[128,3072]{1,0:T(8,128)(2,1)S(1)}, bf16[128,3072]{1,0:T(8,128)(2,1)S(1)}, u32[]{:S(2)}, u32[]{:S(2)}) collective-permute-start(bf16[128,3072]{1,0:T(8,128)(2,1)S(1)} %get-tuple-element.35), channel_id=1, source_target_pairs={{0,1},{1,0},{2,3},{3,2},{4,5},{5,4},{6,7},{7,6},{8,9},{9,8},{10,11... | collective-permute-start | bytes 2359304 | tf_op jit(solution)/shard_map/ppermute | solution.py:53
  51.4 3.7 %collective-permute-start.18 = (bf16[128,3072]{1,0:T(8,128)(2,1)S(1)}, bf16[128,3072]{1,0:T(8,128)(2,1)S(1)}, u32[]{:S(2)}, u32[]{:S(2)}) collective-permute-start(bf16[128,3072]{1,0:T(8,128)(2,1)S(1)} %get-tuple-element.41), channel_id=1, source_target_pairs={{0,1},{1,0},{2,3},{3,2},{4,5},{5,4},{6,7},{7,6},{8,9},{9,8},{10,11... | collective-permute-start | bytes 2359304 | tf_op jit(solution)/shard_map/ppermute | solution.py:53
  51.5 16.8 %collective-permute-start.13 = (bf16[8,128,128]{2,1,0:T(8,128)(2,1)S(1)}, bf16[8,128,128]{2,1,0:T(8,128)(2,1)S(1)}, u32[]{:S(2)}, u32[]{:S(2)}) collective-permute-start(bf16[8,128,128]{2,1,0:T(8,128)(2,1)S(1)} %fusion.2.behind), channel_id=1, source_target_pairs={{0,16},{4,20},{8,24},{12,28},{1,17},{5,21},{9,25},{13,29},{2,18},{... | collective-permute-start | bytes 786440 | tf_op jit(solution)/shard_map/ppermute | solution.py:329
  54.3 11.3 %collective-permute-start.15 = (bf16[64,3072]{1,0:T(8,128)(2,1)S(1)}, bf16[64,3072]{1,0:T(8,128)(2,1)S(1)}, u32[]{:S(2)}, u32[]{:S(2)}) collective-permute-start(bf16[64,3072]{1,0:T(8,128)(2,1)S(1)} %slice.137), channel_id=1, source_target_pairs={{0,2},{1,3},{2,0},{3,1},{4,6},{5,7},{6,4},{7,5},{8,10},{9,11},{10,... | collective-permute-start | bytes 1179656 | tf_op jit(solution)/shard_map/ppermute | solution.py:53
  55.4 13.9 %copy-start.1 = (f32[2048]{0:T(1024)S(1)}, f32[2048]{0:T(1024)}, u32[]{:S(2)}) copy-start(f32[2048]{0:T(1024)} %param.10) | copy-start | bytes 24580
  55.4 11.2 %collective-permute-start.19 = (bf16[64,3072]{1,0:T(8,128)(2,1)S(1)}, bf16[64,3072]{1,0:T(8,128)(2,1)S(1)}, u32[]{:S(2)}, u32[]{:S(2)}) collective-permute-start(bf16[64,3072]{1,0:T(8,128)(2,1)S(1)} %slice.142), channel_id=1, source_target_pairs={{0,4},{4,0},{8,12},{12,8},{16,20},{20,16},{24,28},{28,24},{1,5},{5... | collective-permute-start | bytes 1179656 | tf_op jit(solution)/shard_map/ppermute | solution.py:53
  65.7 7.9 %collective-permute-start.17 = (bf16[32,3072]{1,0:T(8,128)(2,1)S(1)}, bf16[32,3072]{1,0:T(8,128)(2,1)S(1)}, u32[]{:S(2)}, u32[]{:S(2)}) collective-permute-start(bf16[32,3072]{1,0:T(8,128)(2,1)S(1)} %slice.140), channel_id=1, source_target_pairs={{0,4},{4,0},{8,12},{12,8},{16,20},{20,16},{24,28},{28,24},{1,5},{5... | collective-permute-start | bytes 589832 | tf_op jit(solution)/shard_map/ppermute | solution.py:53
  66.7 7.0 %collective-permute-start.20 = (bf16[32,3072]{1,0:T(8,128)(2,1)S(1)}, bf16[32,3072]{1,0:T(8,128)(2,1)S(1)}, u32[]{:S(2)}, u32[]{:S(2)}) collective-permute-start(bf16[32,3072]{1,0:T(8,128)(2,1)S(1)} %slice.144), channel_id=1, source_target_pairs={{0,2},{1,3},{2,0},{3,1},{4,6},{5,7},{6,4},{7,5},{8,10},{9,11},{10,... | collective-permute-start | bytes 589832 | tf_op jit(solution)/shard_map/ppermute | solution.py:53
  68.7 8.8 %collective-permute-start.16 = (bf16[8,128,128]{2,1,0:T(8,128)(2,1)S(1)}, bf16[8,128,128]{2,1,0:T(8,128)(2,1)S(1)}, u32[]{:S(2)}, u32[]{:S(2)}) collective-permute-start(bf16[8,128,128]{2,1,0:T(8,128)(2,1)S(1)} %get-tuple-element.57), channel_id=1, source_target_pairs={{0,4},{4,0},{8,12},{12,8},{16,20},{20,16},{24,28},{28,24},{1,5},{5... | collective-permute-start | bytes 786440 | tf_op jit(solution)/shard_map/ppermute | solution.py:53
  73.8 7.4 %collective-permute-start.21 = (bf16[8,6144]{1,0:T(8,128)(2,1)S(1)}, bf16[8,6144]{1,0:T(8,128)(2,1)S(1)}, u32[]{:S(2)}, u32[]{:S(2)}) collective-permute-start(bf16[8,6144]{1,0:T(8,128)(2,1)S(1)} %get-tuple-element.58), channel_id=1, source_target_pairs={{0,24},{4,28},{8,0},{12,4},{16,8},{20,12},{24,16},{28,20},{1,25},{... | collective-permute-start | bytes 294920 | tf_op jit(solution)/shard_map/ppermute | solution.py:53
  74.5 9.7 %collective-permute-start.22 = (bf16[8,6144]{1,0:T(8,128)(2,1)S(1)}, bf16[8,6144]{1,0:T(8,128)(2,1)S(1)}, u32[]{:S(2)}, u32[]{:S(2)}) collective-permute-start(bf16[8,6144]{1,0:T(8,128)(2,1)S(1)} %get-tuple-element.60), channel_id=1, source_target_pairs={{0,16},{4,20},{8,24},{12,28},{16,0},{20,4},{24,8},{28,12},{1,17},{... | collective-permute-start | bytes 294920 | tf_op jit(solution)/shard_map/ppermute | solution.py:53
  75.9 8.3 %collective-permute-start.23 = (bf16[8,6144]{1,0:T(8,128)(2,1)S(1)}, bf16[8,6144]{1,0:T(8,128)(2,1)S(1)}, u32[]{:S(2)}, u32[]{:S(2)}) collective-permute-start(bf16[8,6144]{1,0:T(8,128)(2,1)S(1)} %get-tuple-element.59), channel_id=1, source_target_pairs={{0,8},{4,12},{8,16},{12,20},{16,24},{20,28},{24,0},{28,4},{1,9},{5... | collective-permute-start | bytes 294920 | tf_op jit(solution)/shard_map/ppermute | solution.py:53

commit v9 on v8

--- a/solution.py
+++ b/solution.py
@@ -324,6 +324,9 @@
     while step < z_axis.n:
         upper = (z & step) != 0
         last_step = 2 * step == z_axis.n
+        if last_step:
+            tie = yield group
+            group = group + tie[:, None]
         out = group.astype(BF16) if last_step else packed(group, fall)
         tie = yield out
         came = lax.ppermute(out, z_axis.name, z_axis.pairs(step, last_step))
@@ -635,6 +638,7 @@
     for _ in range((nz - 1).bit_length() - 2):
         scan.send(jnp.zeros(zeros, F32))
     a, b = scatter(core, pa), scatter(core, pb)
+    scan.send(nothing(a, *zeros) + nothing(b, *zeros))
     a, b = scatter(x_axis, rows_split(a, nx)), scatter(y_axis, rows_split(b, ny))
     carried = scan.send(nothing(a, *zeros))
     attn_out = None

time: 85.3 us -> 86.3 us (1.012)
  starting transfers between devices: 25.7 us -> 29.5 us
  waiting for transfers between devices: 24.7 us -> 21.8 us
    ppermute x22, starting transfers between devices: 22.4 us -> 26.5 us  [send(): return lax.ppermute(a, self.name, self.turn(k))]
    ppermute x22, waiting for transfers between devices: 24.4 us -> 21.4 us  [send(): return lax.ppermute(a, self.name, self.turn(k))]
where the time goes in v9:
time: 86.3 us; the launch traced here: 85.9 us
  starting transfers between devices  29.5 us (34%)
  Pallas kernels  27.6 us (32%)
  waiting for transfers between devices  21.8 us (25%)
  other arithmetic  4.79 us (6%)
  local copies, waits for them, and re-layouts  1.27 us (1%)
  between operations  0.97 us (1%)
    ppermute x22, starting transfers between devices, send(): return lax.ppermute(a, self.name, self.turn(k))  26.5 us
    ppermute x22, waiting for transfers between devices, send(): return lax.ppermute(a, self.name, self.turn(k))  21.4 us
    pallas_call x2, Pallas kernels, local_pass(): pl.pallas_call(functools.partial(local_kernel, heads, group, block, loads...  11.2 us
    pallas_call x2, Pallas kernels, final_pass(): pl.pallas_call(functools.partial(final_kernel, heads, group, block), grid...  7.4 us
    pallas_call x1, Pallas kernels, lead_pass(): pl.pallas_call(functools.partial(lead_kernel, experts, nx, ny, block), in...  6.78 us
    ppermute x2, starting transfers between devices, carry_scan(): came = lax.ppermute(out, z_axis.name, z_axis.pairs(step, last_step))  2.98 us
  transfers between devices with their start and end apart: 24, of which 9 were waited for; matrix products, arithmetic and copies ran while one was open for 3% of the time, Pallas kernels for 32%

profile of v9, /device:TPU:0, one launch (start us, length us, event | category | flops | bytes accessed | tf_op | source)
XLA Modules:
  0.0 85.9 jit_solution(15433160833305249906)
XLA Ops:
  0.6 0.7 select_reduce_fusion.2
  1.5 0.9 %pad_maximum_fusion.3 = bf16[8,6272]{1,0:T(8,128)(2,1)S(1)} fusion(bf16[8,128]{1,0:T(8,128)(2,1)S(1)} %fusion.38, bf16[8,6144]{1,0:T(8,128)(2,1)} %param.11), kind=kLoop, calls=%fused_computation.34 | loop fusion | flops 200704 | bytes 200704 | tf_op jit(solution)/shard_map/concatenate | solution.py:609
  2.4 3.0 %collective-permute-start = (bf16[8,6272]{1,0:T(8,128)(2,1)S(1)}, bf16[8,6272]{1,0:T(8,128)(2,1)S(1)}, u32[]{:S(2)}, u32[]{:S(2)}) collective-permute-start(bf16[8,6272]{1,0:T(8,128)(2,1)S(1)} %pad_maximum_fusion.3), channel_id=1, source_target_pairs={{0,8},{4,12},{8,16},{12,20},{16,24},{20,28},{24,0},{28,4},{1,9},{5... | collective-permute-start | bytes 301064 | tf_op jit(solution)/shard_map/ppermute | solution.py:53
  5.4 2.6 %collective-permute-start.1 = (bf16[8,6272]{1,0:T(8,128)(2,1)S(1)}, bf16[8,6272]{1,0:T(8,128)(2,1)S(1)}, u32[]{:S(2)}, u32[]{:S(2)}) collective-permute-start(bf16[8,6272]{1,0:T(8,128)(2,1)S(1)} %pad_maximum_fusion.3), channel_id=1, source_target_pairs={{0,16},{4,20},{8,24},{12,28},{16,0},{20,4},{24,8},{28,12},{1,17},{... | collective-permute-start | bytes 301064 | tf_op jit(solution)/shard_map/ppermute | solution.py:53
  8.0 1.3 %collective-permute-start.2 = (bf16[8,6272]{1,0:T(8,128)(2,1)S(1)}, bf16[8,6272]{1,0:T(8,128)(2,1)S(1)}, u32[]{:S(2)}, u32[]{:S(2)}) collective-permute-start(bf16[8,6272]{1,0:T(8,128)(2,1)S(1)} %pad_maximum_fusion.3), channel_id=1, source_target_pairs={{0,24},{4,28},{8,0},{12,4},{16,8},{20,12},{24,16},{28,20},{1,25},{... | collective-permute-start | bytes 301064 | tf_op jit(solution)/shard_map/ppermute | solution.py:53
  9.4 0.8 copy-done
  10.1 0.7 prepare.1
  11.1 5.6 %local_pass.2 = (bf16[512,2048]{1,0:T(8,128)(2,1)S(1)}, bf16[8,128,128]{2,1,0:T(8,128)(2,1)S(1)}, bf16[8,3200]{1,0:T(8,128)(2,1)}, bf16[576,6144]{1,0:T(8,128)(2,1)S(1)}) custom-call(bf16[3,512,2048]{2,1,0:T(8,128)(2,1)} %bitcast.31, bf16[3,512,2048]{2,1,0:T(8,128)(2,1)} %bitcast.32, bf16[3,512,2048]{2,1,0:T(8,128)(2,1)} %bitcast.33, ...), custom_call_target="tpu_custom_call" | custom-call | flops 1 | bytes 1 | tf_op jit(solution)/shard_map/local_pass/pallas_call | solution.py:204
  16.7 1.6 %collective-permute-start.3 = (bf16[1040,128]{1,0:T(8,128)(2,1)S(1)}, bf16[1040,128]{1,0:T(8,128)(2,1)S(1)}, u32[]{:S(2)}, u32[]{:S(2)}) collective-permute-start(bf16[1040,128]{1,0:T(8,128)(2,1)S(1)} %pad_maximum_fusion.1), channel_id=1, source_target_pairs={{0,4},{4,0},{8,12},{12,8},{16,20},{20,16},{24,28},{28,24},{1,5},{5... | collective-permute-start | bytes 798728 | tf_op jit(solution)/shard_map/ppermute | solution.py:53
  18.6 5.7 %local_pass.3 = (bf16[512,2048]{1,0:T(8,128)(2,1)S(1)}, bf16[8,128,128]{2,1,0:T(8,128)(2,1)S(1)}, bf16[8,3200]{1,0:T(8,128)(2,1)S(1)}, bf16[576,6144]{1,0:T(8,128)(2,1)S(1)}) custom-call(bf16[3,512,2048]{2,1,0:T(8,128)(2,1)} %bitcast.34, bf16[3,512,2048]{2,1,0:T(8,128)(2,1)} %bitcast.35, ...), custom_call_target="tpu_custom_call", output_to_operand_aliasing={{0}: (6, {})} | custom-call | flops 1 | bytes 1 | tf_op jit(solution)/shard_map/local_pass/pallas_call | solution.py:204
  24.9 1.5 %collective-permute-start.9 = (bf16[32,3200]{1,0:T(8,128)(2,1)S(1)}, bf16[32,3200]{1,0:T(8,128)(2,1)S(1)}, u32[]{:S(2)}, u32[]{:S(2)}) collective-permute-start(bf16[32,3200]{1,0:T(8,128)(2,1)S(1)} %slice.141), channel_id=1, source_target_pairs={{0,2},{1,3},{2,0},{3,1},{4,6},{5,7},{6,4},{7,5},{8,10},{9,11},{10,... | collective-permute-start | bytes 614408 | tf_op jit(solution)/shard_map/ppermute | solution.py:53
  26.5 3.5 %collective-permute-done.4 = bf16[32,3072]{1,0:T(8,128)(2,1)S(1)} collective-permute-done((bf16[32,3072]{1,0:T(8,128)(2,1)S(1)}, bf16[32,3072]{1,0:T(8,128)(2,1)S(1)}, u32[]{:S(2)}, u32[]{:S(2)}) %collective-permute-start.4) | collective-permute-done | bytes 196640 | tf_op jit(solution)/shard_map/ppermute | solution.py:53
  30.2 1.6 %collective-permute-start.5 = (bf16[64,3072]{1,0:T(8,128)(2,1)S(1)}, bf16[64,3072]{1,0:T(8,128)(2,1)S(1)}, u32[]{:S(2)}, u32[]{:S(2)}) collective-permute-start(bf16[64,3072]{1,0:T(8,128)(2,1)S(1)} %maximum_add_fusion.1.refs_0_), channel_id=1, source_target_pairs={{0,2},{1,3},{2,0},{3,1},{4,6},{5,7},{6,4},{7,5},{8,10},{9,11},{10,... | collective-permute-start | bytes 1179656 | tf_op jit(solution)/shard_map/ppermute | solution.py:53
  31.8 1.9 %collective-permute-start.10 = (bf16[64,3200]{1,0:T(8,128)(2,1)S(1)}, bf16[64,3200]{1,0:T(8,128)(2,1)S(1)}, u32[]{:S(2)}, u32[]{:S(2)}) collective-permute-start(bf16[64,3200]{1,0:T(8,128)(2,1)S(1)} %maximum_add_fusion.refs_4_), channel_id=1, source_target_pairs={{0,4},{4,0},{8,12},{12,8},{16,20},{20,16},{24,28},{28,24},{1,5},{5... | collective-permute-start | bytes 1228808 | tf_op jit(solution)/shard_map/ppermute | solution.py:53
  34.3 4.8 %collective-permute-done.5.refs_1_ = bf16[64,3072]{1,0:T(8,128)(2,1)S(1)} collective-permute-done((bf16[64,3072]{1,0:T(8,128)(2,1)S(1)}, bf16[64,3072]{1,0:T(8,128)(2,1)S(1)}, u32[]{:S(2)}, u32[]{:S(2)}) %collective-permute-start.5) | collective-permute-done | bytes 393248 | tf_op jit(solution)/shard_map/ppermute | solution.py:53
  39.1 1.4 %collective-permute-done.10.refs_5_ = bf16[64,3200]{1,0:T(8,128)(2,1)S(1)} collective-permute-done((bf16[64,3200]{1,0:T(8,128)(2,1)S(1)}, bf16[64,3200]{1,0:T(8,128)(2,1)S(1)}, u32[]{:S(2)}, u32[]{:S(2)}) %collective-permute-start.10) | collective-permute-done | bytes 409632 | tf_op jit(solution)/shard_map/ppermute | solution.py:53
  40.7 0.7 collective-permute-start.6
  41.5 0.8 collective-permute-done.12.refs_7_
  42.3 6.8 %lead_pass.1 = (bf16[128,3072]{1,0:T(8,128)(2,1)S(1)}, bf16[128,3072]{1,0:T(8,128)(2,1)S(1)}, bf16[256,576]{1,0:T(8,128)(2,1)S(1)}, f32[256,128]{1,0:T(8,128)S(1...) custom-call(bf16[64,3072]{1,0:T(8,128)(2,1)S(1)} %maximum_add_fusion.1.refs_0_, ...), custom_call_target="tpu_custom_call" | custom-call | flops 1 | bytes 1 | tf_op jit(solution)/shard_map/lead_pass/pallas_call | solution.py:519
  49.9 1.4 %rest_pass.1 = (bf16[128,3072]{1,0:T(8,128)(2,1)S(1)}, bf16[128,3072]{1,0:T(8,128)(2,1)S(1)}) custom-call(bf16[256,576]{1,0:T(8,128)(2,1)S(1)} %get-tuple-element.36.h, f32[256,128]{1,0:T(8,128)S(1)} %get-tuple-element.37.flow, bf16[576,3072]{1,0:T(8,128)(2,1)S(1)} %get-tuple-element.38.w, f32[8,128,128]{2,1,0:T(8,128)S(1)} %fusion.1.behind), custom_call_target="tpu_custom_call" | custom-call | flops 1 | bytes 1 | tf_op jit(solution)/shard_map/rest_pass/pallas_call | solution.py:547
  51.7 0.8 collective-permute-start.16
  52.5 1.2 %collective-permute-done.14 = bf16[128,3072]{1,0:T(8,128)(2,1)S(1)} collective-permute-done((bf16[128,3072]{1,0:T(8,128)(2,1)S(1)}, bf16[128,3072]{1,0:T(8,128)(2,1)S(1)}, u32[]{:S(2)}, u32[]{:S(2)}) %collective-permute-start.14) | collective-permute-done | bytes 786464 | tf_op jit(solution)/shard_map/ppermute | solution.py:53
  54.0 1.2 %collective-permute-start.19 = (bf16[64,3072]{1,0:T(8,128)(2,1)S(1)}, bf16[64,3072]{1,0:T(8,128)(2,1)S(1)}, u32[]{:S(2)}, u32[]{:S(2)}) collective-permute-start(bf16[64,3072]{1,0:T(8,128)(2,1)S(1)} %slice.152), channel_id=1, source_target_pairs={{0,4},{4,0},{8,12},{12,8},{16,20},{20,16},{24,28},{28,24},{1,5},{5... | collective-permute-start | bytes 1179656 | tf_op jit(solution)/shard_map/ppermute | solution.py:53
  55.2 2.2 %collective-permute-start.15 = (bf16[8,128,128]{2,1,0:T(8,128)(2,1)S(1)}, bf16[8,128,128]{2,1,0:T(8,128)(2,1)S(1)}, u32[]{:S(2)}, u32[]{:S(2)}) collective-permute-start(bf16[8,128,128]{2,1,0:T(8,128)(2,1)S(1)} %add_convert_fusion.4), channel_id=1, source_target_pairs={{0,16},{4,20},{8,24},{12,28},{1,17},{5,21},{9,25},{13,29},{2,18},{... | collective-permute-start | bytes 786440 | tf_op jit(solution)/shard_map/ppermute | solution.py:332
  57.4 5.8 %collective-permute-done.16 = bf16[64,3072]{1,0:T(8,128)(2,1)S(1)} collective-permute-done((bf16[64,3072]{1,0:T(8,128)(2,1)S(1)}, bf16[64,3072]{1,0:T(8,128)(2,1)S(1)}, u32[]{:S(2)}, u32[]{:S(2)}) %collective-permute-start.16) | collective-permute-done | bytes 393248 | tf_op jit(solution)/shard_map/ppermute | solution.py:53
  63.4 1.2 %collective-permute-start.18 = (bf16[32,3072]{1,0:T(8,128)(2,1)S(1)}, bf16[32,3072]{1,0:T(8,128)(2,1)S(1)}, u32[]{:S(2)}, u32[]{:S(2)}) collective-permute-start(bf16[32,3072]{1,0:T(8,128)(2,1)S(1)} %slice.150), channel_id=1, source_target_pairs={{0,4},{4,0},{8,12},{12,8},{16,20},{20,16},{24,28},{28,24},{1,5},{5... | collective-permute-start | bytes 589832 | tf_op jit(solution)/shard_map/ppermute | solution.py:53
  65.3 0.9 %collective-permute-start.20 = (bf16[32,3072]{1,0:T(8,128)(2,1)S(1)}, bf16[32,3072]{1,0:T(8,128)(2,1)S(1)}, u32[]{:S(2)}, u32[]{:S(2)}) collective-permute-start(bf16[32,3072]{1,0:T(8,128)(2,1)S(1)} %slice.154), channel_id=1, source_target_pairs={{0,2},{1,3},{2,0},{3,1},{4,6},{5,7},{6,4},{7,5},{8,10},{9,11},{10,... | collective-permute-start | bytes 589832 | tf_op jit(solution)/shard_map/ppermute | solution.py:53
  66.7 1.8 %collective-permute-start.17 = (bf16[8,128,128]{2,1,0:T(8,128)(2,1)S(1)}, bf16[8,128,128]{2,1,0:T(8,128)(2,1)S(1)}, u32[]{:S(2)}, u32[]{:S(2)}) collective-permute-start(bf16[8,128,128]{2,1,0:T(8,128)(2,1)S(1)} %get-tuple-element.57), channel_id=1, source_target_pairs={{0,4},{4,0},{8,12},{12,8},{16,20},{20,16},{24,28},{28,24},{1,5},{5... | collective-permute-start | bytes 786440 | tf_op jit(solution)/shard_map/ppermute | solution.py:53
  68.5 3.7 %final_pass.2 = (bf16[512,2048]{1,0:T(8,128)(2,1)}, bf16[8,6144]{1,0:T(8,128)(2,1)S(1)}) custom-call(bf16[3,512,2048]{2,1,0:T(8,128)(2,1)} %bitcast.37, bf16[512,2048]{1,0:T(8,128)(2,1)S(1)} %get-tuple-element.26.refs_1_, f32[512,128]{1,0:T(8,128)S(1)} %get-tuple-element.24.refs_4_.refs_2_, bf16[8,128,128]{2,1,0:T(8,128)(2,1)S(1)} %get-tuple-element.56.refs_3_, ...), custom_call_target="tpu_custom_call" | custom-call | flops 1 | bytes 1 | tf_op jit(solution)/shard_map/final_pass/pallas_call | solution.py:248
  72.5 5.1 %collective-permute-start.21 = (bf16[8,6144]{1,0:T(8,128)(2,1)S(1)}, bf16[8,6144]{1,0:T(8,128)(2,1)S(1)}, u32[]{:S(2)}, u32[]{:S(2)}) collective-permute-start(bf16[8,6144]{1,0:T(8,128)(2,1)S(1)} %get-tuple-element.58), channel_id=1, source_target_pairs={{0,24},{4,28},{8,0},{12,4},{16,8},{20,12},{24,16},{28,20},{1,25},{... | collective-permute-start | bytes 294920 | tf_op jit(solution)/shard_map/ppermute | solution.py:53
  78.3 3.7 %final_pass.3 = (bf16[512,2048]{1,0:T(8,128)(2,1)}, bf16[8,6144]{1,0:T(8,128)(2,1)}) custom-call(bf16[3,512,2048]{2,1,0:T(8,128)(2,1)} %bitcast.38, bf16[512,2048]{1,0:T(8,128)(2,1)S(1)} %get-tuple-element.26.refs_1_, f32[512,128]{1,0:T(8,128)S(1)} %get-tuple-element.24.refs_4_.refs_2_, ...), custom_call_target="tpu_custom_call", output_to_operand_aliasing={{0}: (5, {})} | custom-call | flops 1 | bytes 1 | tf_op jit(solution)/shard_map/final_pass/pallas_call | solution.py:248
  82.0 3.2 %collective-permute-done.22 = bf16[8,6144]{1,0:T(8,128)(2,1)S(1)} collective-permute-done((bf16[8,6144]{1,0:T(8,128)(2,1)S(1)}, bf16[8,6144]{1,0:T(8,128)(2,1)S(1)}, u32[]{:S(2)}, u32[]{:S(2)}) %collective-permute-start.22) | collective-permute-done | bytes 98336 | tf_op jit(solution)/shard_map/ppermute | solution.py:53
  (80 shorter events, 6.8 us)
Async XLA Ops:
  2.4 16.1 %collective-permute-start = (bf16[8,6272]{1,0:T(8,128)(2,1)S(1)}, bf16[8,6272]{1,0:T(8,128)(2,1)S(1)}, u32[]{:S(2)}, u32[]{:S(2)}) collective-permute-start(bf16[8,6272]{1,0:T(8,128)(2,1)S(1)} %pad_maximum_fusion.3), channel_id=1, source_target_pairs={{0,8},{4,12},{8,16},{12,20},{16,24},{20,28},{24,0},{28,4},{1,9},{5... | collective-permute-start | bytes 301064 | tf_op jit(solution)/shard_map/ppermute | solution.py:53
  5.4 13.1 %collective-permute-start.1 = (bf16[8,6272]{1,0:T(8,128)(2,1)S(1)}, bf16[8,6272]{1,0:T(8,128)(2,1)S(1)}, u32[]{:S(2)}, u32[]{:S(2)}) collective-permute-start(bf16[8,6272]{1,0:T(8,128)(2,1)S(1)} %pad_maximum_fusion.3), channel_id=1, source_target_pairs={{0,16},{4,20},{8,24},{12,28},{16,0},{20,4},{24,8},{28,12},{1,17},{... | collective-permute-start | bytes 301064 | tf_op jit(solution)/shard_map/ppermute | solution.py:53
  8.0 10.5 %collective-permute-start.2 = (bf16[8,6272]{1,0:T(8,128)(2,1)S(1)}, bf16[8,6272]{1,0:T(8,128)(2,1)S(1)}, u32[]{:S(2)}, u32[]{:S(2)}) collective-permute-start(bf16[8,6272]{1,0:T(8,128)(2,1)S(1)} %pad_maximum_fusion.3), channel_id=1, source_target_pairs={{0,24},{4,28},{8,0},{12,4},{16,8},{20,12},{24,16},{28,20},{1,25},{... | collective-permute-start | bytes 301064 | tf_op jit(solution)/shard_map/ppermute | solution.py:53
  9.4 0.8 copy-start
  11.1 7.5 %copy-start.2 = (bf16[8,6144]{1,0:T(8,128)(2,1)S(1)}, bf16[8,6144]{1,0:T(8,128)(2,1)}, u32[]{:S(2)}) copy-start(bf16[8,6144]{1,0:T(8,128)(2,1)} %param.11) | copy-start | bytes 294916
  16.7 9.8 %collective-permute-start.3 = (bf16[1040,128]{1,0:T(8,128)(2,1)S(1)}, bf16[1040,128]{1,0:T(8,128)(2,1)S(1)}, u32[]{:S(2)}, u32[]{:S(2)}) collective-permute-start(bf16[1040,128]{1,0:T(8,128)(2,1)S(1)} %pad_maximum_fusion.1), channel_id=1, source_target_pairs={{0,4},{4,0},{8,12},{12,8},{16,20},{20,16},{24,28},{28,24},{1,5},{5... | collective-permute-start | bytes 798728 | tf_op jit(solution)/shard_map/ppermute | solution.py:53
  24.3 5.7 %collective-permute-start.4 = (bf16[32,3072]{1,0:T(8,128)(2,1)S(1)}, bf16[32,3072]{1,0:T(8,128)(2,1)S(1)}, u32[]{:S(2)}, u32[]{:S(2)}) collective-permute-start(bf16[32,3072]{1,0:T(8,128)(2,1)S(1)} %slice.139), channel_id=1, source_target_pairs={{0,4},{4,0},{8,12},{12,8},{16,20},{20,16},{24,28},{28,24},{1,5},{5... | collective-permute-start | bytes 589832 | tf_op jit(solution)/shard_map/ppermute | solution.py:53
  24.9 6.8 %collective-permute-start.9 = (bf16[32,3200]{1,0:T(8,128)(2,1)S(1)}, bf16[32,3200]{1,0:T(8,128)(2,1)S(1)}, u32[]{:S(2)}, u32[]{:S(2)}) collective-permute-start(bf16[32,3200]{1,0:T(8,128)(2,1)S(1)} %slice.141), channel_id=1, source_target_pairs={{0,2},{1,3},{2,0},{3,1},{4,6},{5,7},{6,4},{7,5},{8,10},{9,11},{10,... | collective-permute-start | bytes 614408 | tf_op jit(solution)/shard_map/ppermute | solution.py:53
  30.2 8.9 %collective-permute-start.5 = (bf16[64,3072]{1,0:T(8,128)(2,1)S(1)}, bf16[64,3072]{1,0:T(8,128)(2,1)S(1)}, u32[]{:S(2)}, u32[]{:S(2)}) collective-permute-start(bf16[64,3072]{1,0:T(8,128)(2,1)S(1)} %maximum_add_fusion.1.refs_0_), channel_id=1, source_target_pairs={{0,2},{1,3},{2,0},{3,1},{4,6},{5,7},{6,4},{7,5},{8,10},{9,11},{10,... | collective-permute-start | bytes 1179656 | tf_op jit(solution)/shard_map/ppermute | solution.py:53
  31.8 8.7 %collective-permute-start.10 = (bf16[64,3200]{1,0:T(8,128)(2,1)S(1)}, bf16[64,3200]{1,0:T(8,128)(2,1)S(1)}, u32[]{:S(2)}, u32[]{:S(2)}) collective-permute-start(bf16[64,3200]{1,0:T(8,128)(2,1)S(1)} %maximum_add_fusion.refs_4_), channel_id=1, source_target_pairs={{0,4},{4,0},{8,12},{12,8},{16,20},{20,16},{24,28},{28,24},{1,5},{5... | collective-permute-start | bytes 1228808 | tf_op jit(solution)/shard_map/ppermute | solution.py:53
  33.7 7.8 %collective-permute-start.7 = (bf16[64,3072]{1,0:T(8,128)(2,1)S(1)}, bf16[64,3072]{1,0:T(8,128)(2,1)S(1)}, u32[]{:S(2)}, u32[]{:S(2)}) collective-permute-start(bf16[64,3072]{1,0:T(8,128)(2,1)S(1)} %maximum_add_fusion.1.refs_0_), channel_id=1, source_target_pairs={{0,1},{1,0},{2,3},{3,2},{4,5},{5,4},{6,7},{7,6},{8,9},{9,8},{10,11... | collective-permute-start | bytes 1179656 | tf_op jit(solution)/shard_map/ppermute | solution.py:53
  33.8 7.7 %collective-permute-start.11 = (bf16[64,3200]{1,0:T(8,128)(2,1)S(1)}, bf16[64,3200]{1,0:T(8,128)(2,1)S(1)}, u32[]{:S(2)}, u32[]{:S(2)}) collective-permute-start(bf16[64,3200]{1,0:T(8,128)(2,1)S(1)} %maximum_add_fusion.refs_4_), channel_id=1, source_target_pairs={{0,1},{1,0},{2,3},{3,2},{4,5},{5,4},{6,7},{7,6},{8,9},{9,8},{10,11... | collective-permute-start | bytes 1228808 | tf_op jit(solution)/shard_map/ppermute | solution.py:53
  39.1 2.4 %collective-permute-start.8 = (bf16[64,3072]{1,0:T(8,128)(2,1)S(1)}, bf16[64,3072]{1,0:T(8,128)(2,1)S(1)}, u32[]{:S(2)}, u32[]{:S(2)}) collective-permute-start(bf16[64,3072]{1,0:T(8,128)(2,1)S(1)} %collective-permute-done.5.refs_1_), channel_id=1, source_target_pairs={{0,1},{1,0},{2,3},{3,2},{4,5},{5,4},{6,7},{7,6},{8,9},{9,8},{10,11... | collective-permute-start | bytes 1179656 | tf_op jit(solution)/shard_map/ppermute | solution.py:53
  40.5 1.7 %collective-permute-start.12 = (bf16[64,3200]{1,0:T(8,128)(2,1)S(1)}, bf16[64,3200]{1,0:T(8,128)(2,1)S(1)}, u32[]{:S(2)}, u32[]{:S(2)}) collective-permute-start(bf16[64,3200]{1,0:T(8,128)(2,1)S(1)} %collective-permute-done.10.refs_5_), channel_id=1, source_target_pairs={{0,1},{1,0},{2,3},{3,2},{4,5},{5,4},{6,7},{7,6},{8,9},{9,8},{10,11... | collective-permute-start | bytes 1228808 | tf_op jit(solution)/shard_map/ppermute | solution.py:53
  40.7 8.9 %collective-permute-start.6 = (bf16[1040,128]{1,0:T(8,128)(2,1)S(1)}, bf16[1040,128]{1,0:T(8,128)(2,1)S(1)}, u32[]{:S(2)}, u32[]{:S(2)}) collective-permute-start(bf16[1040,128]{1,0:T(8,128)(2,1)S(1)} %pad_maximum_fusion.2), channel_id=1, source_target_pairs={{0,8},{4,12},{8,0},{12,4},{16,24},{20,28},{24,16},{28,20},{1,9},{5... | collective-permute-start | bytes 798728 | tf_op jit(solution)/shard_map/ppermute | solution.py:332
  49.1 2.4 %collective-permute-start.13 = (bf16[128,3072]{1,0:T(8,128)(2,1)S(1)}, bf16[128,3072]{1,0:T(8,128)(2,1)S(1)}, u32[]{:S(2)}, u32[]{:S(2)}) collective-permute-start(bf16[128,3072]{1,0:T(8,128)(2,1)S(1)} %get-tuple-element.35), channel_id=1, source_target_pairs={{0,1},{1,0},{2,3},{3,2},{4,5},{5,4},{6,7},{7,6},{8,9},{9,8},{10,11... | collective-permute-start | bytes 2359304 | tf_op jit(solution)/shard_map/ppermute | solution.py:53
  51.4 2.4 %collective-permute-start.14 = (bf16[128,3072]{1,0:T(8,128)(2,1)S(1)}, bf16[128,3072]{1,0:T(8,128)(2,1)S(1)}, u32[]{:S(2)}, u32[]{:S(2)}) collective-permute-start(bf16[128,3072]{1,0:T(8,128)(2,1)S(1)} %get-tuple-element.40), channel_id=1, source_target_pairs={{0,1},{1,0},{2,3},{3,2},{4,5},{5,4},{6,7},{7,6},{8,9},{9,8},{10,11... | collective-permute-start | bytes 2359304 | tf_op jit(solution)/shard_map/ppermute | solution.py:53
  51.7 11.6 %collective-permute-start.16 = (bf16[64,3072]{1,0:T(8,128)(2,1)S(1)}, bf16[64,3072]{1,0:T(8,128)(2,1)S(1)}, u32[]{:S(2)}, u32[]{:S(2)}) collective-permute-start(bf16[64,3072]{1,0:T(8,128)(2,1)S(1)} %slice.147), channel_id=1, source_target_pairs={{0,2},{1,3},{2,0},{3,1},{4,6},{5,7},{6,4},{7,5},{8,10},{9,11},{10,... | collective-permute-start | bytes 1179656 | tf_op jit(solution)/shard_map/ppermute | solution.py:53
  54.0 11.2 %collective-permute-start.19 = (bf16[64,3072]{1,0:T(8,128)(2,1)S(1)}, bf16[64,3072]{1,0:T(8,128)(2,1)S(1)}, u32[]{:S(2)}, u32[]{:S(2)}) collective-permute-start(bf16[64,3072]{1,0:T(8,128)(2,1)S(1)} %slice.152), channel_id=1, source_target_pairs={{0,4},{4,0},{8,12},{12,8},{16,20},{20,16},{24,28},{28,24},{1,5},{5... | collective-permute-start | bytes 1179656 | tf_op jit(solution)/shard_map/ppermute | solution.py:53
  55.2 13.3 %copy-start.1 = (f32[2048]{0:T(1024)S(1)}, f32[2048]{0:T(1024)}, u32[]{:S(2)}) copy-start(f32[2048]{0:T(1024)} %param.10) | copy-start | bytes 24580
  55.2 11.0 %collective-permute-start.15 = (bf16[8,128,128]{2,1,0:T(8,128)(2,1)S(1)}, bf16[8,128,128]{2,1,0:T(8,128)(2,1)S(1)}, u32[]{:S(2)}, u32[]{:S(2)}) collective-permute-start(bf16[8,128,128]{2,1,0:T(8,128)(2,1)S(1)} %add_convert_fusion.4), channel_id=1, source_target_pairs={{0,16},{4,20},{8,24},{12,28},{1,17},{5,21},{9,25},{13,29},{2,18},{... | collective-permute-start | bytes 786440 | tf_op jit(solution)/shard_map/ppermute | solution.py:332
  63.4 8.9 %collective-permute-start.18 = (bf16[32,3072]{1,0:T(8,128)(2,1)S(1)}, bf16[32,3072]{1,0:T(8,128)(2,1)S(1)}, u32[]{:S(2)}, u32[]{:S(2)}) collective-permute-start(bf16[32,3072]{1,0:T(8,128)(2,1)S(1)} %slice.150), channel_id=1, source_target_pairs={{0,4},{4,0},{8,12},{12,8},{16,20},{20,16},{24,28},{28,24},{1,5},{5... | collective-permute-start | bytes 589832 | tf_op jit(solution)/shard_map/ppermute | solution.py:53
  65.3 7.0 %collective-permute-start.20 = (bf16[32,3072]{1,0:T(8,128)(2,1)S(1)}, bf16[32,3072]{1,0:T(8,128)(2,1)S(1)}, u32[]{:S(2)}, u32[]{:S(2)}) collective-permute-start(bf16[32,3072]{1,0:T(8,128)(2,1)S(1)} %slice.154), channel_id=1, source_target_pairs={{0,2},{1,3},{2,0},{3,1},{4,6},{5,7},{6,4},{7,5},{8,10},{9,11},{10,... | collective-permute-start | bytes 589832 | tf_op jit(solution)/shard_map/ppermute | solution.py:53
  66.7 11.6 %collective-permute-start.17 = (bf16[8,128,128]{2,1,0:T(8,128)(2,1)S(1)}, bf16[8,128,128]{2,1,0:T(8,128)(2,1)S(1)}, u32[]{:S(2)}, u32[]{:S(2)}) collective-permute-start(bf16[8,128,128]{2,1,0:T(8,128)(2,1)S(1)} %get-tuple-element.57), channel_id=1, source_target_pairs={{0,4},{4,0},{8,12},{12,8},{16,20},{20,16},{24,28},{28,24},{1,5},{5... | collective-permute-start | bytes 786440 | tf_op jit(solution)/shard_map/ppermute | solution.py:53
  72.5 9.5 %collective-permute-start.21 = (bf16[8,6144]{1,0:T(8,128)(2,1)S(1)}, bf16[8,6144]{1,0:T(8,128)(2,1)S(1)}, u32[]{:S(2)}, u32[]{:S(2)}) collective-permute-start(bf16[8,6144]{1,0:T(8,128)(2,1)S(1)} %get-tuple-element.58), channel_id=1, source_target_pairs={{0,24},{4,28},{8,0},{12,4},{16,8},{20,12},{24,16},{28,20},{1,25},{... | collective-permute-start | bytes 294920 | tf_op jit(solution)/shard_map/ppermute | solution.py:53
  77.6 7.6 %collective-permute-start.22 = (bf16[8,6144]{1,0:T(8,128)(2,1)S(1)}, bf16[8,6144]{1,0:T(8,128)(2,1)S(1)}, u32[]{:S(2)}, u32[]{:S(2)}) collective-permute-start(bf16[8,6144]{1,0:T(8,128)(2,1)S(1)} %get-tuple-element.60), channel_id=1, source_target_pairs={{0,16},{4,20},{8,24},{12,28},{16,0},{20,4},{24,8},{28,12},{1,17},{... | collective-permute-start | bytes 294920 | tf_op jit(solution)/shard_map/ppermute | solution.py:53
  77.6 7.6 %collective-permute-start.23 = (bf16[8,6144]{1,0:T(8,128)(2,1)S(1)}, bf16[8,6144]{1,0:T(8,128)(2,1)S(1)}, u32[]{:S(2)}, u32[]{:S(2)}) collective-permute-start(bf16[8,6144]{1,0:T(8,128)(2,1)S(1)} %get-tuple-element.59), channel_id=1, source_target_pairs={{0,8},{4,12},{8,16},{12,20},{16,24},{20,28},{24,0},{28,4},{1,9},{5... | collective-permute-start | bytes 294920 | tf_op jit(solution)/shard_map/ppermute | solution.py:53
